TPU v7x, 32 devices: a whole 2x2x4 slice. The times are simulated.
32 devices in a mesh: groups: 2 (over x), seq: 16 (over z, y, core).
Axes of the slice: x: 2, y: 2, z: 4, core: 2. Of those that a mesh axis runs over, the one named last changes fastest.
Arguments:
- prompt_query: bfloat16 [4096, 4096], P(('groups', 'seq')), parts along dimension 0, may hold values from -16 to 16
- prompt_key: bfloat16 [4096, 4096], P(('groups', 'seq')), parts along dimension 0, may hold values from -16 to 16
- prompt_value: bfloat16 [4096, 4096], P(('groups', 'seq')), parts along dimension 0, may hold values from -6 to 6
- response_embed: bfloat16 [1024, 4096], P('groups'), parts along dimension 0, may hold values from -32 to 32
- mask_embed: bfloat16 [4096], replicated, may hold values from -6 to 6
- commit_step: int32 [1024], P('groups'), parts along dimension 0, may hold values from 1 to 4
- block_index: int32 [2], P('groups'), parts along dimension 0, may hold values from 0 to 7
- attention_gain: bfloat16 [4096], replicated, may hold values from 0.099609375 to 1.8984375
- residual_gain: bfloat16 [4096], replicated, may hold values from 0.099609375 to 1.8984375
- query_weight: bfloat16 [4096, 4096], P(None, 'seq'), may hold values from -0.125 to 0.125
- key_weight: bfloat16 [4096, 4096], P(None, 'seq'), may hold values from -0.09375 to 0.09375
- value_weight: bfloat16 [4096, 4096], P(None, 'seq'), may hold values from -1.5 to 1.5
- output_weight: bfloat16 [4096, 4096], P('seq'), may hold values from -0.09375 to 0.09375
Outputs:
- prompt_context: bfloat16 [4096, 4096], P(('groups', 'seq')), parts along dimension 0
- response_residual: bfloat16 [4, 1024, 4096], P(None, ('groups', 'seq')), parts along dimension 1
- response_normed: bfloat16 [4, 1024, 4096], P(None, ('groups', 'seq')), parts along dimension 1
There are 2 independent parts, one for each index of `groups`. A program takes and returns all parts, laid end to end along the dimension named above; an argument that names none is the same for every part. Nothing has to cross between parts.
All inputs are finite; a program needn't handle non-finite values.
Results may differ from a plain program's by a relative error of at most 0.018.
Values may be sent and summed in bfloat16 or wider, within the bound.
No kernel may reach another device: no remote copies, remote signals or barrier semaphores. Data moves between devices by JAX's collectives and lax.ppermute only.
A program may use at most 128 MiB of HBM per device.

v0:
```python
import functools
import math

import jax
import jax.numpy as jnp
from jax import lax
from jax.experimental import pallas as pl
from jax.experimental.pallas import tpu as pltpu
from jax.sharding import PartitionSpec as P


HD = 128
STEPS = 4
ROPE_BASE = 500000.0
NORM_EPS = 1e-05
SCORE_SCALE = math.log2(math.e) / math.sqrt(HD)

F32 = jnp.float32
BF16 = jnp.bfloat16


def call(body, grid, in_specs, out_specs, out_shape, scratch=(), flops=0, moved=0, exps=0):
    return pl.pallas_call(
        body,
        grid=grid,
        in_specs=in_specs,
        out_specs=out_specs,
        out_shape=out_shape,
        scratch_shapes=list(scratch),
        cost_estimate=pl.CostEstimate(flops=flops, bytes_accessed=moved, transcendentals=exps),
    )


def whole(shape):
    return pl.BlockSpec(shape, lambda *_: (0,) * len(shape))


def tables(positions):
    half = HD // 2
    exponent = jnp.arange(half, dtype=F32) * (2.0 / HD)
    inv_freq = ROPE_BASE ** (-exponent)
    angles = positions.astype(F32)[:, None] * inv_freq[None, :]
    cosine, sine = jnp.cos(angles), jnp.sin(angles)
    return jnp.concatenate([cosine, cosine], 1), jnp.concatenate([-sine, sine], 1)


def rope(u, cosine, sine):
    return u * cosine + pltpu.roll(u, HD // 2, 1) * sine


def pack_kv_body(k_ref, v_ref, cos_ref, sin_ref, out_ref):
    cosine, sine = cos_ref[...], sin_ref[...]
    width = out_ref.shape[3]
    for dest in range(out_ref.shape[0]):
        for lane in range(0, width, HD):
            column = dest * width + lane
            out_ref[dest, 0, :, lane : lane + HD] = rope(
                k_ref[:, column : column + HD].astype(F32), cosine, sine
            ).astype(BF16)
        out_ref[dest, 1] = v_ref[:, dest * width : (dest + 1) * width]


def pack_q_body(me_ref, q_ref, cos_ref, sin_ref, *out_refs):
    cosine, sine = cos_ref[...] * SCORE_SCALE, sin_ref[...] * SCORE_SCALE
    width = out_refs[0].shape[1]
    for k, out_ref in enumerate(out_refs):
        start = (me_ref[0] ^ k) * width
        for lane in range(0, width, HD):
            u = q_ref[:, pl.ds(pl.multiple_of(start + lane, HD), HD)].astype(F32)
            out_ref[:, lane : lane + HD] = rope(u, cosine, sine).astype(BF16)


def normed(rows, gain):
    rows = rows.astype(F32)
    return (
        rows * lax.rsqrt(jnp.mean(rows * rows, axis=-1, keepdims=True) + NORM_EPS) * gain.astype(F32)
    ).astype(BF16)


def project_body(
    embed_ref, mask_ref, gain_ref, wq_ref, wk_ref, wv_ref, cos_ref, sin_ref,
    qe_ref, qm_ref, ke_ref, km_ref, ve_ref, vm_ref, mq, mk,
):
    gain = gain_ref[...]

    @pl.when(pl.program_id(0) == 0)
    def _():
        mask_row = normed(jnp.broadcast_to(mask_ref[...], (16, mask_ref.shape[1])), gain)
        mq[...] = jnp.dot(mask_row, wq_ref[...], preferred_element_type=F32)
        mk[...] = jnp.dot(mask_row, wk_ref[...], preferred_element_type=F32)
        vm_ref[...] = jnp.dot(mask_row, wv_ref[...], preferred_element_type=F32).astype(BF16)

    rows = normed(embed_ref[...], gain)
    count = rows.shape[0]
    q = jnp.dot(rows, wq_ref[...], preferred_element_type=F32)
    k = jnp.dot(rows, wk_ref[...], preferred_element_type=F32)
    ve_ref[...] = jnp.dot(rows, wv_ref[...], preferred_element_type=F32).astype(BF16)
    cosine, sine = cos_ref[...], sin_ref[...]
    for lane in range(0, q.shape[1], HD):
        at = slice(lane, lane + HD)
        qe_ref[:, at] = (rope(q[:, at], cosine, sine) * SCORE_SCALE).astype(BF16)
        ke_ref[:, at] = rope(k[:, at], cosine, sine).astype(BF16)
        one_q = jnp.broadcast_to(mq[0:1, at], (count, HD))
        one_k = jnp.broadcast_to(mk[0:1, at], (count, HD))
        qm_ref[:, at] = (rope(one_q, cosine, sine) * SCORE_SCALE).astype(BF16)
        km_ref[:, at] = rope(one_k, cosine, sine).astype(BF16)


def scores(q, k):
    return lax.dot_general(q, k, (((1,), (1,)), ((), ())), preferred_element_type=F32)


def merge(state, s, v):
    top = jnp.max(s, axis=-1, keepdims=True)
    if state is None:
        w = jnp.exp2(s - top)
        return (
            top,
            jnp.sum(w, axis=-1, keepdims=True),
            jnp.dot(w.astype(BF16), v, preferred_element_type=F32),
        )
    old, total, acc = state
    top = jnp.maximum(old, top)
    keep = jnp.exp2(old - top)
    w = jnp.exp2(s - top)
    total = total * keep + jnp.sum(w, axis=-1, keepdims=True)
    acc = acc * keep + jnp.dot(w.astype(BF16), v, preferred_element_type=F32)
    return top, total, acc


def over_prompt(state, q, kv_ref, chunk):
    sources, _, rows, width = kv_ref.shape
    for first in range(0, sources, chunk):
        k = kv_ref[first : first + chunk, 0].reshape(chunk * rows, width)
        v = kv_ref[first : first + chunk, 1].reshape(chunk * rows, width)
        state = merge(state, scores(q, k), v)
    return state


def response_body(chunk, low_ref, kv_ref, qe_ref, qm_ref, ke_ref, km_ref, ve_ref, vm_ref, commit_ref, *refs):
    out_refs, scratch_ref = refs[:-1], refs[-1]
    lows = len(out_refs)
    steps, highs, per, _ = out_refs[0].shape
    resp = qe_ref.shape[0]
    both = over_prompt(None, jnp.concatenate([qm_ref[...], qe_ref[...]], 0), kv_ref, chunk)
    mask_value = jnp.broadcast_to(vm_ref[0:1], ve_ref.shape)
    span = min(resp, chunk * kv_ref.shape[2])
    for step in range(steps):
        shown = commit_ref[...] <= step
        one = commit_ref[:, 0:1] <= step
        q = jnp.where(shown, qe_ref[...], qm_ref[...])
        k = jnp.where(shown, ke_ref[...], km_ref[...])
        v = jnp.where(shown, ve_ref[...], mask_value)
        state = (
            jnp.where(one, both[0][resp:], both[0][:resp]),
            jnp.where(one, both[1][resp:], both[1][:resp]),
            jnp.where(shown, both[2][resp:], both[2][:resp]),
        )
        for first in range(0, resp, span):
            state = merge(state, scores(q, k[first : first + span]), v[first : first + span])
        _, total, acc = state
        scratch_ref[...] = acc / total
        for high in range(highs):
            for k in range(lows):
                at = (high * lows + (low_ref[0] ^ k)) * per
                out_refs[k][step, high] = scratch_ref[pl.ds(pl.multiple_of(at, per), per), :].astype(BF16)


def prompt_body(chunk, group, me_ref, kv_ref, km_ref, vm_ref, *refs):
    q_refs, out_ref, queries = refs[: kv_ref.shape[0]], refs[-2], refs[-1]
    rows = out_ref.shape[1]
    for k, ref in enumerate(q_refs):
        queries[k * rows : (k + 1) * rows] = ref[...]

    @pl.loop(0, len(q_refs) // group)
    def _(turn):
        q = queries[pl.ds(pl.multiple_of(turn * (group * rows), group * rows), group * rows), :]
        s = scores(q, km_ref[...])
        top = jnp.max(s, axis=-1, keepdims=True)
        total = jnp.sum(jnp.exp2(s - top), axis=-1, keepdims=True)
        state = over_prompt((top, total, total * vm_ref[0:1].astype(F32)), q, kv_ref, chunk)
        context = (state[2] / state[1]).astype(BF16)
        for k in range(group):
            out_ref[me_ref[0] ^ (turn * group + k)] = context[k * rows : (k + 1) * rows]


def output_body(lows, place_ref, *refs):
    x_refs, w_refs, outs = refs[:lows], refs[lows : 2 * lows], refs[2 * lows :]
    steps, highs, per, width = x_refs[0].shape
    sends, keeps = outs[:steps], outs[steps:]
    bit = place_ref[1]
    total = None
    for x_ref, w_ref in zip(x_refs, w_refs):
        x = x_ref[...].reshape(steps * highs * per, width)
        term = jnp.dot(x, w_ref[...], preferred_element_type=F32)
        total = term if total is None else total + term
    for step in range(steps):
        for high in range(0, highs, 2):
            at = (step * highs + high) * per
            first, second = total[at : at + per], total[at + per : at + 2 * per]
            keeps[step][high // 2] = jnp.where(bit == 0, first, second)
            sends[step][high // 2] = jnp.where(bit == 0, second, first).astype(BF16)


def halve_body(place_ref, keep_ref, got_ref, send_ref, kept_ref):
    bit = place_ref[0]
    for pair in range(send_ref.shape[0]):
        first = keep_ref[2 * pair] + got_ref[2 * pair].astype(F32)
        second = keep_ref[2 * pair + 1] + got_ref[2 * pair + 1].astype(F32)
        kept_ref[pair] = jnp.where(bit == 0, first, second)
        send_ref[pair] = jnp.where(bit == 0, second, first).astype(BF16)


def finish_body(steps, place_ref, embed_ref, mask_ref, gain_ref, commit_ref, *refs):
    keeps, gots, (residual_ref, normed_ref) = refs[:steps], refs[steps : 2 * steps], refs[2 * steps :]
    gain = gain_ref[...].astype(F32)
    for step in range(steps):
        shown = commit_ref[:, 0:1] <= step
        rows = jnp.where(shown, embed_ref[...].astype(F32), mask_ref[...].astype(F32))
        hidden = rows + (keeps[step][0] + gots[step][0].astype(F32))
        residual_ref[step] = hidden.astype(BF16)
        scale = lax.rsqrt(jnp.mean(hidden * hidden, axis=-1, keepdims=True) + NORM_EPS)
        normed_ref[step] = (hidden * scale * gain).astype(BF16)


def unpack_body(in_ref, out_ref):
    width = in_ref.shape[2]
    for source in range(in_ref.shape[0]):
        out_ref[:, source * width : (source + 1) * width] = in_ref[source]


def per_device(
    prompt_query,
    prompt_key,
    prompt_value,
    response_embed,
    mask_embed,
    commit_step,
    block_index,
    attention_gain,
    residual_gain,
    query_weight,
    key_weight,
    value_weight,
    output_weight,
):
    rows, head_cols = prompt_query.shape
    resp, model = response_embed.shape
    n = lax.axis_size("seq")
    me = lax.axis_index("seq")
    width = query_weight.shape[1]
    heads = width // HD
    prompt_len = rows * n
    lows = min(4, n)
    highs = n // lows
    per = resp // n

    def swap(x, bit):
        return lax.ppermute(x, "seq", [(i, i ^ bit) for i in range(n)])

    dests = max(1, n // 4)
    cos_p, sin_p = tables(me * rows + jnp.arange(rows, dtype=jnp.int32))
    kv_send = call(
        pack_kv_body,
        (n // dests,),
        [
            pl.BlockSpec((rows, dests * width), lambda j: (0, j)),
            pl.BlockSpec((rows, dests * width), lambda j: (0, j)),
            whole((rows, HD)),
            whole((rows, HD)),
        ],
        pl.BlockSpec((dests, 2, rows, width), lambda j: (j, 0, 0, 0)),
        jax.ShapeDtypeStruct((n, 2, rows, width), BF16),
        flops=6 * rows * head_cols,
        moved=8 * rows * head_cols,
    )(prompt_key, prompt_value, cos_p, sin_p)
    kv = lax.all_to_all(kv_send, "seq", 0, 0, tiled=True)
    where = me.astype(jnp.int32).reshape(1)
    q_parts = pl.pallas_call(
        pack_q_body,
        grid_spec=pltpu.PrefetchScalarGridSpec(
            num_scalar_prefetch=1,
            grid=(1,),
            in_specs=[whole((rows, head_cols)), whole((rows, HD)), whole((rows, HD))],
            out_specs=[whole((rows, width))] * n,
        ),
        out_shape=[jax.ShapeDtypeStruct((rows, width), BF16)] * n,
        name="pack_q",
        cost_estimate=pl.CostEstimate(
            flops=6 * rows * head_cols, bytes_accessed=4 * rows * head_cols, transcendentals=0
        ),
    )(where, prompt_query, cos_p, sin_p)
    q_heads = [q_parts[0]]
    for k in range(1, n):
        q_heads.append(swap(q_parts[k], k))

    weights = [output_weight]
    if lows == 4:
        weights.append(swap(output_weight, 2))
    near = swap(output_weight, 1)
    if lows == 4:
        last = swap(weights[1], 1)
        weights = [output_weight, near, weights[1], last]
    else:
        weights = [output_weight, near]

    cos_r, sin_r = tables(prompt_len + block_index[0] * resp + jnp.arange(resp, dtype=jnp.int32))
    commit = jnp.broadcast_to(commit_step[:, None], (resp, HD))
    block = min(resp, 128)
    row_block = pl.BlockSpec((block, width), lambda i: (i, 0))
    wide = jax.ShapeDtypeStruct((resp, width), BF16)
    qe, qm, ke, km, ve, vm = call(
        project_body,
        (resp // block,),
        [
            pl.BlockSpec((block, model), lambda i: (i, 0)),
            whole((1, model)),
            whole((1, model)),
            whole((model, width)),
            whole((model, width)),
            whole((model, width)),
            pl.BlockSpec((block, HD), lambda i: (i, 0)),
            pl.BlockSpec((block, HD), lambda i: (i, 0)),
        ],
        [row_block] * 5 + [whole((16, width))],
        [wide] * 5 + [jax.ShapeDtypeStruct((16, width), BF16)],
        scratch=[pltpu.VMEM((16, width), F32)] * 2,
        flops=6 * resp * model * width,
        moved=2 * resp * model + 6 * model * width,
    )(
        response_embed, mask_embed[None, :], attention_gain[None, :],
        query_weight, key_weight, value_weight, cos_r, sin_r,
    )

    chunk = max(1, min(n, 256 // rows))
    kv_block = pl.BlockSpec((n, 2, rows, HD), lambda h, *_: (0, 0, 0, h))
    key_block = pl.BlockSpec((resp, HD), lambda h, *_: (0, h))
    vm_block = pl.BlockSpec((16, HD), lambda h, *_: (0, h))
    low = me & (lows - 1)
    high = me >> (lows.bit_length() - 1)
    place = jnp.stack([low, high & 1]).astype(jnp.int32)
    context = pl.pallas_call(
        functools.partial(response_body, chunk),
        grid_spec=pltpu.PrefetchScalarGridSpec(
            num_scalar_prefetch=1,
            grid=(heads,),
            in_specs=[kv_block] + [key_block] * 5 + [vm_block, whole((resp, HD))],
            out_specs=[pl.BlockSpec((STEPS, highs, per, HD), lambda h, *_: (0, 0, 0, h))] * lows,
            scratch_shapes=[pltpu.VMEM((resp, HD), F32)],
        ),
        out_shape=[jax.ShapeDtypeStruct((STEPS, highs, per, width), BF16)] * lows,
        name="response_attention",
        cost_estimate=pl.CostEstimate(
            flops=4 * resp * width * (2 * prompt_len + STEPS * resp),
            bytes_accessed=4 * prompt_len * width,
            transcendentals=heads * resp * (2 * prompt_len + STEPS * resp),
        ),
    )(place, kv, qe, qm, ke, km, ve, vm, commit)
    plane_context = [context[0]]
    for k in range(1, lows):
        plane_context.append(swap(context[k], k))

    columns = min(model, 512)
    out_block = pl.BlockSpec((highs // 2, per, columns), lambda j, *_: (0, 0, j))
    half = (highs // 2, per, model)
    parts = pl.pallas_call(
        functools.partial(output_body, lows),
        grid_spec=pltpu.PrefetchScalarGridSpec(
            num_scalar_prefetch=1,
            grid=(model // columns,),
            in_specs=[whole((STEPS, highs, per, width))] * lows
            + [pl.BlockSpec((width, columns), lambda j, *_: (0, j))] * lows,
            out_specs=[out_block] * (2 * STEPS),
        ),
        out_shape=[jax.ShapeDtypeStruct(half, BF16)] * STEPS + [jax.ShapeDtypeStruct(half, F32)] * STEPS,
        name="output_projection",
        cost_estimate=pl.CostEstimate(
            flops=2 * STEPS * resp * model * width, bytes_accessed=2 * lows * width * model, transcendentals=0
        ),
    )(place, *plane_context, *weights)
    sends, keeps = parts[:STEPS], parts[STEPS:]

    level = 0
    while True:
        gots = []
        for step in range(STEPS):
            gots.append(swap(sends[step], lows << level))
        count = keeps[0].shape[0]
        if count == 1:
            break
        level += 1
        bit = ((high >> level) & 1).astype(jnp.int32).reshape(1)
        sends, kept = [], []
        for step in range(STEPS):
            columns = min(model, 2048)
            get = pl.BlockSpec((count, per, columns), lambda j, *_: (0, 0, j))
            put = pl.BlockSpec((count // 2, per, columns), lambda j, *_: (0, 0, j))
            one, two = pl.pallas_call(
                halve_body,
                grid_spec=pltpu.PrefetchScalarGridSpec(
                    num_scalar_prefetch=1,
                    grid=(model // columns,),
                    in_specs=[get, get],
                    out_specs=[put, put],
                ),
                out_shape=[
                    jax.ShapeDtypeStruct((count // 2, per, model), BF16),
                    jax.ShapeDtypeStruct((count // 2, per, model), F32),
                ],
                name="halve",
                cost_estimate=pl.CostEstimate(
                    flops=count * per * model, bytes_accessed=9 * count * per * model, transcendentals=0
                ),
            )(bit, keeps[step], gots[step])
            sends.append(one)
            kept.append(two)
        keeps = kept

    group = max(1, min(n, 1024 // rows))
    prompt_context = None
    for head in range(heads):
        of_head = functools.partial(lambda head, *_: (0, head), head)
        of_kv = functools.partial(lambda head, *_: (0, 0, 0, head), head)
        earlier = [] if prompt_context is None else [prompt_context]
        prompt_context = pl.pallas_call(
            functools.partial(prompt_body, chunk, group),
            grid_spec=pltpu.PrefetchScalarGridSpec(
                num_scalar_prefetch=1,
                grid=(1,),
                in_specs=[
                    pl.BlockSpec((n, 2, rows, HD), of_kv),
                    pl.BlockSpec((resp, HD), of_head),
                    pl.BlockSpec((16, HD), of_head),
                ]
                + [pl.BlockSpec((rows, HD), of_head)] * n
                + [pl.BlockSpec(memory_space=pl.ANY)] * len(earlier),
                out_specs=pl.BlockSpec((n, rows, HD), functools.partial(lambda head, *_: (0, 0, head), head)),
                scratch_shapes=[pltpu.VMEM((n * rows, HD), BF16)],
            ),
            out_shape=jax.ShapeDtypeStruct((n, rows, width), BF16),
            name="prompt_attention",
            input_output_aliases={n + 4: 0} if earlier else {},
            cost_estimate=pl.CostEstimate(
                flops=4 * prompt_len * HD * (prompt_len + resp),
                bytes_accessed=8 * prompt_len * HD,
                transcendentals=prompt_len * (prompt_len + resp),
            ),
        )(where, kv, km, vm, *q_heads, *earlier)
    back = lax.all_to_all(prompt_context, "seq", 0, 0, tiled=True)

    row_block = pl.BlockSpec((per, model), lambda i, at: (at[0], 0))
    sums = pl.BlockSpec((1, per, model), lambda i, at: (0, 0, 0))
    result = pl.BlockSpec((STEPS, per, model), lambda i, at: (0, 0, 0))
    residual, normed_rows = pl.pallas_call(
        functools.partial(finish_body, STEPS),
        grid_spec=pltpu.PrefetchScalarGridSpec(
            num_scalar_prefetch=1,
            grid=(1,),
            in_specs=[
                row_block,
                pl.BlockSpec((1, model), lambda i, at: (0, 0)),
                pl.BlockSpec((1, model), lambda i, at: (0, 0)),
                pl.BlockSpec((per, HD), lambda i, at: (at[0], 0)),
            ]
            + [sums] * (2 * STEPS),
            out_specs=[result, result],
        ),
        out_shape=[jax.ShapeDtypeStruct((STEPS, per, model), BF16)] * 2,
        name="finish",
    )(
        where, response_embed, mask_embed[None, :], residual_gain[None, :],
        commit, *keeps, *gots,
    )
    columns = max(1, n // 4)
    prompt_out = call(
        unpack_body,
        (n // columns,),
        [pl.BlockSpec((columns, rows, width), lambda j: (j, 0, 0))],
        pl.BlockSpec((rows, columns * width), lambda j: (0, j)),
        jax.ShapeDtypeStruct((rows, head_cols), BF16),
        moved=4 * rows * head_cols,
    )(back)
    return prompt_out, residual, normed_rows


def solution(mesh):
    return jax.shard_map(
        per_device,
        mesh=mesh,
        in_specs=(
            P(("groups", "seq"), None),
            P(("groups", "seq"), None),
            P(("groups", "seq"), None),
            P("groups", None),
            P(),
            P("groups"),
            P("groups"),
            P(),
            P(),
            P(None, "seq"),
            P(None, "seq"),
            P(None, "seq"),
            P("seq", None),
        ),
        out_specs=(
            P(("groups", "seq"), None),
            P(None, ("groups", "seq"), None),
            P(None, ("groups", "seq"), None),
        ),
        check_vma=False,
    )
```

profile of v0, /device:TPU:0, one launch (start us, length us, event | category | flops | bytes accessed | tf_op | source)
XLA Modules:
  0.0 287.9 jit_solution(9494308621188958012)
XLA Ops:
  1.7 4.1 %shard_map.148 = bf16[16,2,128,256]{3,2,1,0:T(8,128)(2,1)} custom-call(bf16[128,4096]{1,0:T(8,128)(2,1)} %k_ref.1, bf16[128,4096]{1,0:T(8,128)(2,1)} %v_ref.1, f32[128,128]{1,0:T(8,128)} %get-tuple-element.97.cos_ref, f32[128,128]{1,0:T(8,128)} %get-tuple-element.98.sin_ref), custom_call_target="tpu_custom_call" | custom-call | flops 3145728 | bytes 4194304 | tf_op jit(solution)/shard_map/pallas_call | solution.py:263
  5.8 7.6 %all-to-all-start = ((bf16[16,2,128,256]{3,2,1,0:T(8,128)(2,1)}), bf16[16,2,128,256]{3,2,1,0:T(8,128)(2,1)S(1)}, u32[]{:S(2)}, u32[]{:S(2)}) async-start(bf16[16,2,128,256]{3,2,1,0:T(8,128)(2,1)} %shard_map.148), calls=%async_computation | async-start | bytes 4194304 | tf_op jit(solution)/shard_map/all_to_all | solution.py:277
  13.4 1.9 collective-permute-start.19
  15.3 2.7 pack_q.1
  18.3 1.6 collective-permute-start.2
  20.3 64.3 %collective-permute-done.19.refs_6_ = bf16[256,4096]{1,0:T(8,128)(2,1)} collective-permute-done((bf16[256,4096]{1,0:T(8,128)(2,1)}, bf16[256,4096]{1,0:T(8,128)(2,1)}, u32[]{:S(2)}, u32[]{:S(2)}) %collective-permute-start.19) | collective-permute-done | bytes 2097184 | tf_op jit(solution)/shard_map/ppermute | solution.py:259
  85.2 1.5 collective-permute-start.3
  87.2 1.5 collective-permute-start.5
  88.7 1.4 collective-permute-done.3.refs_4_
  91.1 2.4 collective-permute-start.7
  93.4 1.1 collective-permute-start.8
  94.5 1.0 fusion
  96.7 3.1 %collective-permute-start.9 = (bf16[128,256]{1,0:T(8,128)(2,1)}, bf16[128,256]{1,0:T(8,128)(2,1)S(1)}, u32[]{:S(2)}, u32[]{:S(2)}) collective-permute-start(bf16[128,256]{1,0:T(8,128)(2,1)} %get-tuple-element.59), channel_id=1, source_target_pairs={{0,10},{1,11},{2,8},{3,9},{4,14},{5,15},{6,12},{7,13},{8,2},{9,3},... | collective-permute-start | bytes 196616 | tf_op jit(solution)/shard_map/ppermute | solution.py:259
  99.8 0.9 collective-permute-start.10
  101.4 3.9 %collective-permute-start.11 = (bf16[128,256]{1,0:T(8,128)(2,1)}, bf16[128,256]{1,0:T(8,128)(2,1)S(1)}, u32[]{:S(2)}, u32[]{:S(2)}) collective-permute-start(bf16[128,256]{1,0:T(8,128)(2,1)} %get-tuple-element.61), channel_id=1, source_target_pairs={{0,12},{1,13},{2,14},{3,15},{4,8},{5,9},{6,10},{7,11},{8,4},{9,5},... | collective-permute-start | bytes 196616 | tf_op jit(solution)/shard_map/ppermute | solution.py:259
  105.3 1.0 pad_maximum_fusion
  106.3 0.9 collective-permute-done.9.refs_10_
  107.8 1.3 collective-permute-done.10.refs_11_
  109.0 3.5 %collective-permute-start.13 = (bf16[128,256]{1,0:T(8,128)(2,1)S(1)}, bf16[128,256]{1,0:T(8,128)(2,1)S(1)}, u32[]{:S(2)}, u32[]{:S(2)}) collective-permute-start(bf16[128,256]{1,0:T(8,128)(2,1)S(1)} %copy-done.21), channel_id=1, source_target_pairs={{0,14},{1,15},{2,12},{3,13},{4,10},{5,11},{6,8},{7,9},{8,6},{9,7},... | collective-permute-start | bytes 196616 | tf_op jit(solution)/shard_map/ppermute | solution.py:259
  113.3 10.4 %shard_map.149 = (bf16[512,256]{1,0:T(8,128)(2,1)}, bf16[512,256]{1,0:T(8,128)(2,1)}, bf16[512,256]{1,0:T(8,128)(2,1)}, bf16[512,256]{1,0:T(8,128)(2,1)}, bf16[5...) custom-call(bf16[512,4096]{1,0:T(8,128)(2,1)} %embed_ref.3, bf16[1,4096]{1,0:T(2,128)(2,1)} %broadcast_in_dim.8.mask_ref, ...), custom_call_target="tpu_custom_call" | custom-call | flops 3221225472 | bytes 10485760 | tf_op jit(solution)/shard_map/pallas_call | solution.py:312
  125.3 8.8 %prompt_attention.2.refs_16_ = bf16[16,128,256]{2,1,0:T(8,128)(2,1)} custom-call(s32[1]{0:T(128)} %bitcast.me_ref.place_ref, bf16[16,2,128,256]{3,2,1,0:T(8,128)(2,1)} %copy-done.1, bf16[512,256]{1,0:T(8,128)(2,1)} %get-tuple-element.47.km_ref, bf16[16,256]{1,0:T(8,128)(2,1)} %get-tuple-element.48.vm_ref, bf16[128,256]{1,0:T(8,128)(2,1)} %get-tuple-element.49.refs_0_, ...), custom_call_target="tpu_custom_call" | custom-call | flops 2684354560 | bytes 2097152 | tf_op jit(solution)/shard_map/prompt_attention/pallas_call | solution.py:425
  134.1 9.0 %prompt_attention.3 = bf16[16,128,256]{2,1,0:T(8,128)(2,1)} custom-call(s32[1]{0:T(128)} %bitcast.me_ref.place_ref, bf16[16,2,128,256]{3,2,1,0:T(8,128)(2,1)} %copy-done.1, bf16[512,256]{1,0:T(8,128)(2,1)} %get-tuple-element.47.km_ref, bf16[16,256]{1,0:T(8,128)(2,1)} %get-tuple-element.48.vm_ref, ...), custom_call_target="tpu_custom_call", output_to_operand_aliasing={{}: (20, {})} | custom-call | flops 2684354560 | bytes 2097152 | tf_op jit(solution)/shard_map/prompt_attention/pallas_call | solution.py:425
  143.2 5.3 %all-to-all-start.1 = ((bf16[16,128,256]{2,1,0:T(8,128)(2,1)}), bf16[16,128,256]{2,1,0:T(8,128)(2,1)S(1)}, u32[]{:S(2)}, u32[]{:S(2)}) async-start(bf16[16,128,256]{2,1,0:T(8,128)(2,1)} %prompt_attention.3), calls=%async_computation.1 | async-start | bytes 2097152 | tf_op jit(solution)/shard_map/all_to_all | solution.py:449
  149.1 0.8 broadcast_in_dim.11.commit_ref
  149.9 17.4 %response_attention.1 = (bf16[4,4,32,256]{3,2,1,0:T(8,128)(2,1)}, bf16[4,4,32,256]{3,2,1,0:T(8,128)(2,1)}, bf16[4,4,32,256]{3,2,1,0:T(8,128)(2,1)}, bf16[4,4,32,256]{3,2,1,0:T(8,128)(2,1)}) custom-call(s32[2]{0:T(128)} %pad_add_fusion.low_ref.place_ref, bf16[16,2,128,256]{3,2,1,0:T(8,128)(2,1)} %copy-done.1, bf16[512,256]{1,0:T(8,128)(2,1)} %get-tuple-element.65.qe_ref, ...), custom_call_target="tpu_custom_call" | custom-call | flops 3221225472 | bytes 2097152 | tf_op jit(solution)/shard_map/response_attention/pallas_call | solution.py:342
  167.8 1.6 collective-permute-start.16
  169.4 8.1 %collective-permute-done.16.refs_2_ = bf16[4,4,32,256]{3,2,1,0:T(8,128)(2,1)S(1)} collective-permute-done((bf16[4,4,32,256]{3,2,1,0:T(8,128)(2,1)}, bf16[4,4,32,256]{3,2,1,0:T(8,128)(2,1)S(1)}, u32[]{:S(2)}, u32[]{:S(2)}) %collective-permute-start.16) | collective-permute-done | bytes 262176 | tf_op jit(solution)/shard_map/ppermute | solution.py:259
  177.5 5.4 %collective-permute-done.17.refs_3_ = bf16[4,4,32,256]{3,2,1,0:T(8,128)(2,1)S(1)} collective-permute-done((bf16[4,4,32,256]{3,2,1,0:T(8,128)(2,1)}, bf16[4,4,32,256]{3,2,1,0:T(8,128)(2,1)S(1)}, u32[]{:S(2)}, u32[]{:S(2)}) %collective-permute-start.17) | collective-permute-done | bytes 262176 | tf_op jit(solution)/shard_map/ppermute | solution.py:259
  183.6 11.2 %output_projection.1 = (bf16[2,32,4096]{2,1,0:T(8,128)(2,1)}, bf16[2,32,4096]{2,1,0:T(8,128)(2,1)}, bf16[2,32,4096]{2,1,0:T(8,128)(2,1)}, bf16[2,32,4096]{2,1,0:...) custom-call(s32[2]{0:T(128)} %pad_add_fusion.low_ref.place_ref, ...), custom_call_target="tpu_custom_call" | custom-call | flops 4294967296 | bytes 8388608 | tf_op jit(solution)/shard_map/output_projection/pallas_call | solution.py:366
  194.8 1.9 collective-permute-start.21
  196.9 1.8 collective-permute-start.23
  198.9 11.0 %collective-permute-done.21.got_ref = bf16[2,32,4096]{2,1,0:T(8,128)(2,1)S(1)} collective-permute-done((bf16[2,32,4096]{2,1,0:T(8,128)(2,1)}, bf16[2,32,4096]{2,1,0:T(8,128)(2,1)S(1)}, u32[]{:S(2)}, u32[]{:S(2)}) %collective-permute-start.21) | collective-permute-done | bytes 524320 | tf_op jit(solution)/shard_map/ppermute | solution.py:259
  209.9 0.8 copy-done.5
  210.7 2.2 halve.4
  212.9 2.7 collective-permute-start.25
  215.5 11.2 %collective-permute-done.22.got_ref = bf16[2,32,4096]{2,1,0:T(8,128)(2,1)S(1)} collective-permute-done((bf16[2,32,4096]{2,1,0:T(8,128)(2,1)}, bf16[2,32,4096]{2,1,0:T(8,128)(2,1)S(1)}, u32[]{:S(2)}, u32[]{:S(2)}) %collective-permute-start.22) | collective-permute-done | bytes 524320 | tf_op jit(solution)/shard_map/ppermute | solution.py:259
  227.5 2.2 halve.5
  229.7 1.4 collective-permute-start.26
  231.1 12.5 %collective-permute-done.23.got_ref = bf16[2,32,4096]{2,1,0:T(8,128)(2,1)S(1)} collective-permute-done((bf16[2,32,4096]{2,1,0:T(8,128)(2,1)}, bf16[2,32,4096]{2,1,0:T(8,128)(2,1)S(1)}, u32[]{:S(2)}, u32[]{:S(2)}) %collective-permute-start.23) | collective-permute-done | bytes 524320 | tf_op jit(solution)/shard_map/ppermute | solution.py:259
  244.4 2.1 halve.6
  246.5 1.4 collective-permute-start.27
  247.9 6.4 %collective-permute-done.24.got_ref = bf16[2,32,4096]{2,1,0:T(8,128)(2,1)S(1)} collective-permute-done((bf16[2,32,4096]{2,1,0:T(8,128)(2,1)}, bf16[2,32,4096]{2,1,0:T(8,128)(2,1)S(1)}, u32[]{:S(2)}, u32[]{:S(2)}) %collective-permute-start.24) | collective-permute-done | bytes 524320 | tf_op jit(solution)/shard_map/ppermute | solution.py:259
  255.2 2.2 halve.7
  258.8 14.5 %collective-permute-done.27.refs_6_ = bf16[1,32,4096]{2,1,0:T(8,128)(2,1)S(1)} collective-permute-done((bf16[1,32,4096]{2,1,0:T(8,128)(2,1)}, bf16[1,32,4096]{2,1,0:T(8,128)(2,1)S(1)}, u32[]{:S(2)}, u32[]{:S(2)}) %collective-permute-start.27) | collective-permute-done | bytes 262176 | tf_op jit(solution)/shard_map/ppermute | solution.py:259
  273.3 5.5 %collective-permute-done.28.refs_7_ = bf16[1,32,4096]{2,1,0:T(8,128)(2,1)S(1)} collective-permute-done((bf16[1,32,4096]{2,1,0:T(8,128)(2,1)}, bf16[1,32,4096]{2,1,0:T(8,128)(2,1)S(1)}, u32[]{:S(2)}, u32[]{:S(2)}) %collective-permute-start.28) | collective-permute-done | bytes 262176 | tf_op jit(solution)/shard_map/ppermute | solution.py:259
  279.5 4.0 %finish.1 = (bf16[4,32,4096]{2,1,0:T(8,128)(2,1)}, bf16[4,32,4096]{2,1,0:T(8,128)(2,1)}) custom-call(s32[1]{0:T(128)} %bitcast.me_ref.place_ref, bf16[512,4096]{1,0:T(8,128)(2,1)} %embed_ref.3, bf16[1,4096]{1,0:T(2,128)(2,1)} %broadcast_in_dim.8.mask_ref, bf16[1,4096]{1,0:T(2,128)(2,1)} %broadcast_in_dim.10.gain_ref, ...), custom_call_target="tpu_custom_call" | custom-call | tf_op jit(solution)/shard_map/finish/pallas_call | solution.py:454
  283.5 1.0 copy-done
  284.5 3.4 %shard_map.150 = bf16[128,4096]{1,0:T(8,128)(2,1)} custom-call(bf16[16,128,256]{2,1,0:T(8,128)(2,1)} %copy-done), custom_call_target="tpu_custom_call" | custom-call | bytes 2097152 | tf_op jit(solution)/shard_map/pallas_call | solution.py:475
  (109 shorter events, 14.5 us)
Async XLA Ops:
  5.8 89.7 %copy-start.10 = (bf16[4096]{0:T(1024)(128)(2,1)S(1)}, bf16[4096]{0:T(1024)(128)(2,1)}, u32[]{:S(2)}) copy-start(bf16[4096]{0:T(1024)(128)(2,1)} %param.17) | copy-start | bytes 24580
  5.8 90.3 %copy-start.11 = (bf16[4096]{0:T(1024)(128)(2,1)S(1)}, bf16[4096]{0:T(1024)(128)(2,1)}, u32[]{:S(2)}) copy-start(bf16[4096]{0:T(1024)(128)(2,1)} %param.20) | copy-start | bytes 24580
  5.8 118.1 %all-to-all-start = ((bf16[16,2,128,256]{3,2,1,0:T(8,128)(2,1)}), bf16[16,2,128,256]{3,2,1,0:T(8,128)(2,1)S(1)}, u32[]{:S(2)}, u32[]{:S(2)}) async-start(bf16[16,2,128,256]{3,2,1,0:T(8,128)(2,1)} %shard_map.148), calls=%async_computation | async-start | bytes 4194304 | tf_op jit(solution)/shard_map/all_to_all | solution.py:277
  13.4 71.2 %collective-permute-start.19 = (bf16[256,4096]{1,0:T(8,128)(2,1)}, bf16[256,4096]{1,0:T(8,128)(2,1)}, u32[]{:S(2)}, u32[]{:S(2)}) collective-permute-start(bf16[256,4096]{1,0:T(8,128)(2,1)} %refs_4_.1), channel_id=1, source_target_pairs={{0,2},{1,3},{2,0},{3,1},{4,6},{5,7},{6,4},{7,5},{8,10},{9,11},{10,... | collective-permute-start | bytes 6291464 | tf_op jit(solution)/shard_map/ppermute | solution.py:259
  18.0 89.2 %copy-start.22 = (bf16[128,256]{1,0:T(8,128)(2,1)S(1)}, bf16[128,256]{1,0:T(8,128)(2,1)}, u32[]{:S(2)}) copy-start(bf16[128,256]{1,0:T(8,128)(2,1)} %get-tuple-element.62) | copy-start | bytes 196612
  18.0 91.0 %copy-start.21 = (bf16[128,256]{1,0:T(8,128)(2,1)S(1)}, bf16[128,256]{1,0:T(8,128)(2,1)}, u32[]{:S(2)}) copy-start(bf16[128,256]{1,0:T(8,128)(2,1)} %get-tuple-element.63) | copy-start | bytes 196612
  18.0 94.5 %copy-start.19 = (bf16[128,256]{1,0:T(8,128)(2,1)S(1)}, bf16[128,256]{1,0:T(8,128)(2,1)}, u32[]{:S(2)}) copy-start(bf16[128,256]{1,0:T(8,128)(2,1)} %get-tuple-element.64) | copy-start | bytes 196612
  18.0 67.2 %collective-permute-start = (bf16[128,256]{1,0:T(8,128)(2,1)}, bf16[128,256]{1,0:T(8,128)(2,1)S(1)}, u32[]{:S(2)}, u32[]{:S(2)}) collective-permute-start(bf16[128,256]{1,0:T(8,128)(2,1)} %get-tuple-element.50), channel_id=1, source_target_pairs={{0,1},{1,0},{2,3},{3,2},{4,5},{5,4},{6,7},{7,6},{8,9},{9,8},{10,11... | collective-permute-start | bytes 196616 | tf_op jit(solution)/shard_map/ppermute | solution.py:259
  18.1 68.7 %collective-permute-start.1 = (bf16[128,256]{1,0:T(8,128)(2,1)}, bf16[128,256]{1,0:T(8,128)(2,1)S(1)}, u32[]{:S(2)}, u32[]{:S(2)}) collective-permute-start(bf16[128,256]{1,0:T(8,128)(2,1)} %get-tuple-element.51), channel_id=1, source_target_pairs={{0,2},{1,3},{2,0},{3,1},{4,6},{5,7},{6,4},{7,5},{8,10},{9,11},{10,... | collective-permute-start | bytes 196616 | tf_op jit(solution)/shard_map/ppermute | solution.py:259
  18.3 68.8 %collective-permute-start.2 = (bf16[128,256]{1,0:T(8,128)(2,1)}, bf16[128,256]{1,0:T(8,128)(2,1)S(1)}, u32[]{:S(2)}, u32[]{:S(2)}) collective-permute-start(bf16[128,256]{1,0:T(8,128)(2,1)} %get-tuple-element.52), channel_id=1, source_target_pairs={{0,3},{1,2},{2,1},{3,0},{4,7},{5,6},{6,5},{7,4},{8,11},{9,10},{10,... | collective-permute-start | bytes 196616 | tf_op jit(solution)/shard_map/ppermute | solution.py:259
  20.0 149.5 %collective-permute-start.18 = (bf16[256,4096]{1,0:T(8,128)(2,1)}, bf16[256,4096]{1,0:T(8,128)(2,1)}, u32[]{:S(2)}, u32[]{:S(2)}) collective-permute-start(bf16[256,4096]{1,0:T(8,128)(2,1)} %refs_4_.1), channel_id=1, source_target_pairs={{0,1},{1,0},{2,3},{3,2},{4,5},{5,4},{6,7},{7,6},{8,9},{9,8},{10,11... | collective-permute-start | bytes 6291464 | tf_op jit(solution)/shard_map/ppermute | solution.py:259
  84.6 84.8 %collective-permute-start.20 = (bf16[256,4096]{1,0:T(8,128)(2,1)}, bf16[256,4096]{1,0:T(8,128)(2,1)}, u32[]{:S(2)}, u32[]{:S(2)}) collective-permute-start(bf16[256,4096]{1,0:T(8,128)(2,1)} %collective-permute-done.19.refs_6_), channel_id=1, source_target_pairs={{0,1},{1,0},{2,3},{3,2},{4,5},{5,4},{6,7},{7,6},{8,9},{9,8},{10,11... | collective-permute-start | bytes 6291464 | tf_op jit(solution)/shard_map/ppermute | solution.py:259
  85.2 38.5 %copy-start.17 = (bf16[128,256]{1,0:T(8,128)(2,1)}, bf16[128,256]{1,0:T(8,128)(2,1)S(1)}, u32[]{:S(2)}) copy-start(bf16[128,256]{1,0:T(8,128)(2,1)S(1)} %collective-permute-done.refs_1_) | copy-start | bytes 196612
  85.2 4.8 %collective-permute-start.3 = (bf16[128,256]{1,0:T(8,128)(2,1)}, bf16[128,256]{1,0:T(8,128)(2,1)S(1)}, u32[]{:S(2)}, u32[]{:S(2)}) collective-permute-start(bf16[128,256]{1,0:T(8,128)(2,1)} %get-tuple-element.53), channel_id=1, source_target_pairs={{0,4},{1,5},{2,6},{3,7},{4,0},{5,1},{6,2},{7,3},{8,12},{9,13},{10,... | collective-permute-start | bytes 196616 | tf_op jit(solution)/shard_map/ppermute | solution.py:259
  86.8 36.9 %copy-start.18 = (bf16[128,256]{1,0:T(8,128)(2,1)}, bf16[128,256]{1,0:T(8,128)(2,1)S(1)}, u32[]{:S(2)}) copy-start(bf16[128,256]{1,0:T(8,128)(2,1)S(1)} %collective-permute-done.1.refs_2_) | copy-start | bytes 196612
  86.8 4.3 %collective-permute-start.4 = (bf16[128,256]{1,0:T(8,128)(2,1)}, bf16[128,256]{1,0:T(8,128)(2,1)S(1)}, u32[]{:S(2)}, u32[]{:S(2)}) collective-permute-start(bf16[128,256]{1,0:T(8,128)(2,1)} %get-tuple-element.54), channel_id=1, source_target_pairs={{0,5},{1,4},{2,7},{3,6},{4,1},{5,0},{6,3},{7,2},{8,13},{9,12},{10,... | collective-permute-start | bytes 196616 | tf_op jit(solution)/shard_map/ppermute | solution.py:259
  87.2 36.5 %copy-start.20 = (bf16[128,256]{1,0:T(8,128)(2,1)}, bf16[128,256]{1,0:T(8,128)(2,1)S(1)}, u32[]{:S(2)}) copy-start(bf16[128,256]{1,0:T(8,128)(2,1)S(1)} %collective-permute-done.2.refs_3_) | copy-start | bytes 196612
  87.2 6.3 %collective-permute-start.5 = (bf16[128,256]{1,0:T(8,128)(2,1)}, bf16[128,256]{1,0:T(8,128)(2,1)S(1)}, u32[]{:S(2)}, u32[]{:S(2)}) collective-permute-start(bf16[128,256]{1,0:T(8,128)(2,1)} %get-tuple-element.55), channel_id=1, source_target_pairs={{0,6},{1,7},{2,4},{3,5},{4,2},{5,3},{6,0},{7,1},{8,14},{9,15},{10,... | collective-permute-start | bytes 196616 | tf_op jit(solution)/shard_map/ppermute | solution.py:259
  90.1 33.7 %copy-start.23 = (bf16[128,256]{1,0:T(8,128)(2,1)}, bf16[128,256]{1,0:T(8,128)(2,1)S(1)}, u32[]{:S(2)}) copy-start(bf16[128,256]{1,0:T(8,128)(2,1)S(1)} %collective-permute-done.3.refs_4_) | copy-start | bytes 196612
  90.1 6.7 %collective-permute-start.6 = (bf16[128,256]{1,0:T(8,128)(2,1)}, bf16[128,256]{1,0:T(8,128)(2,1)S(1)}, u32[]{:S(2)}, u32[]{:S(2)}) collective-permute-start(bf16[128,256]{1,0:T(8,128)(2,1)} %get-tuple-element.56), channel_id=1, source_target_pairs={{0,7},{1,6},{2,5},{3,4},{4,3},{5,2},{6,1},{7,0},{8,15},{9,14},{10,... | collective-permute-start | bytes 196616 | tf_op jit(solution)/shard_map/ppermute | solution.py:259
  91.1 32.7 %copy-start.24 = (bf16[128,256]{1,0:T(8,128)(2,1)}, bf16[128,256]{1,0:T(8,128)(2,1)S(1)}, u32[]{:S(2)}) copy-start(bf16[128,256]{1,0:T(8,128)(2,1)S(1)} %collective-permute-done.4.refs_5_) | copy-start | bytes 196612
  91.1 8.8 %collective-permute-start.7 = (bf16[128,256]{1,0:T(8,128)(2,1)}, bf16[128,256]{1,0:T(8,128)(2,1)S(1)}, u32[]{:S(2)}, u32[]{:S(2)}) collective-permute-start(bf16[128,256]{1,0:T(8,128)(2,1)} %get-tuple-element.57), channel_id=1, source_target_pairs={{0,8},{1,9},{2,10},{3,11},{4,12},{5,13},{6,14},{7,15},{8,0},{9,1},... | collective-permute-start | bytes 196616 | tf_op jit(solution)/shard_map/ppermute | solution.py:259
  93.4 30.3 %copy-start.25 = (bf16[128,256]{1,0:T(8,128)(2,1)}, bf16[128,256]{1,0:T(8,128)(2,1)S(1)}, u32[]{:S(2)}) copy-start(bf16[128,256]{1,0:T(8,128)(2,1)S(1)} %collective-permute-done.5.refs_6_) | copy-start | bytes 196612
  93.4 7.9 %collective-permute-start.8 = (bf16[128,256]{1,0:T(8,128)(2,1)}, bf16[128,256]{1,0:T(8,128)(2,1)S(1)}, u32[]{:S(2)}, u32[]{:S(2)}) collective-permute-start(bf16[128,256]{1,0:T(8,128)(2,1)} %get-tuple-element.58), channel_id=1, source_target_pairs={{0,9},{1,8},{2,11},{3,10},{4,13},{5,12},{6,15},{7,14},{8,1},{9,0},... | collective-permute-start | bytes 196616 | tf_op jit(solution)/shard_map/ppermute | solution.py:259
  96.7 27.0 %copy-start.26 = (bf16[128,256]{1,0:T(8,128)(2,1)}, bf16[128,256]{1,0:T(8,128)(2,1)S(1)}, u32[]{:S(2)}) copy-start(bf16[128,256]{1,0:T(8,128)(2,1)S(1)} %collective-permute-done.6.refs_7_) | copy-start | bytes 196612
  96.7 10.5 %collective-permute-start.9 = (bf16[128,256]{1,0:T(8,128)(2,1)}, bf16[128,256]{1,0:T(8,128)(2,1)S(1)}, u32[]{:S(2)}, u32[]{:S(2)}) collective-permute-start(bf16[128,256]{1,0:T(8,128)(2,1)} %get-tuple-element.59), channel_id=1, source_target_pairs={{0,10},{1,11},{2,8},{3,9},{4,14},{5,15},{6,12},{7,13},{8,2},{9,3},... | collective-permute-start | bytes 196616 | tf_op jit(solution)/shard_map/ppermute | solution.py:259
  99.8 23.9 %copy-start.27 = (bf16[128,256]{1,0:T(8,128)(2,1)}, bf16[128,256]{1,0:T(8,128)(2,1)S(1)}, u32[]{:S(2)}) copy-start(bf16[128,256]{1,0:T(8,128)(2,1)S(1)} %collective-permute-done.7.refs_8_) | copy-start | bytes 196612
  99.8 9.2 %collective-permute-start.10 = (bf16[128,256]{1,0:T(8,128)(2,1)}, bf16[128,256]{1,0:T(8,128)(2,1)S(1)}, u32[]{:S(2)}, u32[]{:S(2)}) collective-permute-start(bf16[128,256]{1,0:T(8,128)(2,1)} %get-tuple-element.60), channel_id=1, source_target_pairs={{0,11},{1,10},{2,9},{3,8},{4,15},{5,14},{6,13},{7,12},{8,3},{9,2},... | collective-permute-start | bytes 196616 | tf_op jit(solution)/shard_map/ppermute | solution.py:259
  101.4 22.4 %copy-start.28 = (bf16[128,256]{1,0:T(8,128)(2,1)}, bf16[128,256]{1,0:T(8,128)(2,1)S(1)}, u32[]{:S(2)}) copy-start(bf16[128,256]{1,0:T(8,128)(2,1)S(1)} %collective-permute-done.8.refs_9_) | copy-start | bytes 196612
  101.4 11.2 %collective-permute-start.11 = (bf16[128,256]{1,0:T(8,128)(2,1)}, bf16[128,256]{1,0:T(8,128)(2,1)S(1)}, u32[]{:S(2)}, u32[]{:S(2)}) collective-permute-start(bf16[128,256]{1,0:T(8,128)(2,1)} %get-tuple-element.61), channel_id=1, source_target_pairs={{0,12},{1,13},{2,14},{3,15},{4,8},{5,9},{6,10},{7,11},{8,4},{9,5},... | collective-permute-start | bytes 196616 | tf_op jit(solution)/shard_map/ppermute | solution.py:259
  107.2 16.6 %collective-permute-start.12 = (bf16[128,256]{1,0:T(8,128)(2,1)S(1)}, bf16[128,256]{1,0:T(8,128)(2,1)S(1)}, u32[]{:S(2)}, u32[]{:S(2)}) collective-permute-start(bf16[128,256]{1,0:T(8,128)(2,1)S(1)} %copy-done.22), channel_id=1, source_target_pairs={{0,13},{1,12},{2,15},{3,14},{4,9},{5,8},{6,11},{7,10},{8,5},{9,4},... | collective-permute-start | bytes 196616 | tf_op jit(solution)/shard_map/ppermute | solution.py:259
  109.0 14.8 %collective-permute-start.13 = (bf16[128,256]{1,0:T(8,128)(2,1)S(1)}, bf16[128,256]{1,0:T(8,128)(2,1)S(1)}, u32[]{:S(2)}, u32[]{:S(2)}) collective-permute-start(bf16[128,256]{1,0:T(8,128)(2,1)S(1)} %copy-done.21), channel_id=1, source_target_pairs={{0,14},{1,15},{2,12},{3,13},{4,10},{5,11},{6,8},{7,9},{8,6},{9,7},... | collective-permute-start | bytes 196616 | tf_op jit(solution)/shard_map/ppermute | solution.py:259
  112.5 11.3 %collective-permute-start.14 = (bf16[128,256]{1,0:T(8,128)(2,1)S(1)}, bf16[128,256]{1,0:T(8,128)(2,1)S(1)}, u32[]{:S(2)}, u32[]{:S(2)}) collective-permute-start(bf16[128,256]{1,0:T(8,128)(2,1)S(1)} %copy-done.19), channel_id=1, source_target_pairs={{0,15},{1,14},{2,13},{3,12},{4,11},{5,10},{6,9},{7,8},{8,7},{9,6},... | collective-permute-start | bytes 196616 | tf_op jit(solution)/shard_map/ppermute | solution.py:259
  143.2 140.3 %all-to-all-start.1 = ((bf16[16,128,256]{2,1,0:T(8,128)(2,1)}), bf16[16,128,256]{2,1,0:T(8,128)(2,1)S(1)}, u32[]{:S(2)}, u32[]{:S(2)}) async-start(bf16[16,128,256]{2,1,0:T(8,128)(2,1)} %prompt_attention.3), calls=%async_computation.1 | async-start | bytes 2097152 | tf_op jit(solution)/shard_map/all_to_all | solution.py:449
  167.3 2.1 collective-permute-start.15
  167.8 9.7 %collective-permute-start.16 = (bf16[4,4,32,256]{3,2,1,0:T(8,128)(2,1)}, bf16[4,4,32,256]{3,2,1,0:T(8,128)(2,1)S(1)}, u32[]{:S(2)}, u32[]{:S(2)}) collective-permute-start(bf16[4,4,32,256]{3,2,1,0:T(8,128)(2,1)} %get-tuple-element.71), channel_id=1, source_target_pairs={{0,2},{1,3},{2,0},{3,1},{4,6},{5,7},{6,4},{7,5},{8,10},{9,11},{10,... | collective-permute-start | bytes 786440 | tf_op jit(solution)/shard_map/ppermute | solution.py:259
  169.4 13.5 %collective-permute-start.17 = (bf16[4,4,32,256]{3,2,1,0:T(8,128)(2,1)}, bf16[4,4,32,256]{3,2,1,0:T(8,128)(2,1)S(1)}, u32[]{:S(2)}, u32[]{:S(2)}) collective-permute-start(bf16[4,4,32,256]{3,2,1,0:T(8,128)(2,1)} %get-tuple-element.72), channel_id=1, source_target_pairs={{0,3},{1,2},{2,1},{3,0},{4,7},{5,6},{6,5},{7,4},{8,11},{9,10},{10,... | collective-permute-start | bytes 786440 | tf_op jit(solution)/shard_map/ppermute | solution.py:259
  194.8 15.1 %collective-permute-start.21 = (bf16[2,32,4096]{2,1,0:T(8,128)(2,1)}, bf16[2,32,4096]{2,1,0:T(8,128)(2,1)S(1)}, u32[]{:S(2)}, u32[]{:S(2)}) collective-permute-start(bf16[2,32,4096]{2,1,0:T(8,128)(2,1)} %get-tuple-element.74), channel_id=1, source_target_pairs={{0,4},{1,5},{2,6},{3,7},{4,0},{5,1},{6,2},{7,3},{8,12},{9,13},{10,... | collective-permute-start | bytes 1572872 | tf_op jit(solution)/shard_map/ppermute | solution.py:259
  196.7 30.0 %collective-permute-start.22 = (bf16[2,32,4096]{2,1,0:T(8,128)(2,1)}, bf16[2,32,4096]{2,1,0:T(8,128)(2,1)S(1)}, u32[]{:S(2)}, u32[]{:S(2)}) collective-permute-start(bf16[2,32,4096]{2,1,0:T(8,128)(2,1)} %get-tuple-element.77), channel_id=1, source_target_pairs={{0,4},{1,5},{2,6},{3,7},{4,0},{5,1},{6,2},{7,3},{8,12},{9,13},{10,... | collective-permute-start | bytes 1572872 | tf_op jit(solution)/shard_map/ppermute | solution.py:259
  196.9 46.7 %collective-permute-start.23 = (bf16[2,32,4096]{2,1,0:T(8,128)(2,1)}, bf16[2,32,4096]{2,1,0:T(8,128)(2,1)S(1)}, u32[]{:S(2)}, u32[]{:S(2)}) collective-permute-start(bf16[2,32,4096]{2,1,0:T(8,128)(2,1)} %get-tuple-element.80), channel_id=1, source_target_pairs={{0,4},{1,5},{2,6},{3,7},{4,0},{5,1},{6,2},{7,3},{8,12},{9,13},{10,... | collective-permute-start | bytes 1572872 | tf_op jit(solution)/shard_map/ppermute | solution.py:259
  198.7 55.6 %collective-permute-start.24 = (bf16[2,32,4096]{2,1,0:T(8,128)(2,1)}, bf16[2,32,4096]{2,1,0:T(8,128)(2,1)S(1)}, u32[]{:S(2)}, u32[]{:S(2)}) collective-permute-start(bf16[2,32,4096]{2,1,0:T(8,128)(2,1)} %get-tuple-element.83), channel_id=1, source_target_pairs={{0,4},{1,5},{2,6},{3,7},{4,0},{5,1},{6,2},{7,3},{8,12},{9,13},{10,... | collective-permute-start | bytes 1572872 | tf_op jit(solution)/shard_map/ppermute | solution.py:259
  212.9 45.9 %collective-permute-start.25 = (bf16[1,32,4096]{2,1,0:T(8,128)(2,1)}, bf16[1,32,4096]{2,1,0:T(8,128)(2,1)S(1)}, u32[]{:S(2)}, u32[]{:S(2)}) collective-permute-start(bf16[1,32,4096]{2,1,0:T(8,128)(2,1)} %get-tuple-element.85), channel_id=1, source_target_pairs={{0,8},{1,9},{2,10},{3,11},{4,12},{5,13},{6,14},{7,15},{8,0},{9,1},... | collective-permute-start | bytes 786440 | tf_op jit(solution)/shard_map/ppermute | solution.py:259
  227.5 30.6 %copy-start.12 = (bf16[4096]{0:T(1024)(128)(2,1)S(1)}, bf16[4096]{0:T(1024)(128)(2,1)}, u32[]{:S(2)}) copy-start(bf16[4096]{0:T(1024)(128)(2,1)} %param.21) | copy-start | bytes 24580
  229.7 29.1 %collective-permute-start.26 = (bf16[1,32,4096]{2,1,0:T(8,128)(2,1)}, bf16[1,32,4096]{2,1,0:T(8,128)(2,1)S(1)}, u32[]{:S(2)}, u32[]{:S(2)}) collective-permute-start(bf16[1,32,4096]{2,1,0:T(8,128)(2,1)} %get-tuple-element.86), channel_id=1, source_target_pairs={{0,8},{1,9},{2,10},{3,11},{4,12},{5,13},{6,14},{7,15},{8,0},{9,1},... | collective-permute-start | bytes 786440 | tf_op jit(solution)/shard_map/ppermute | solution.py:259
  246.5 26.8 %collective-permute-start.27 = (bf16[1,32,4096]{2,1,0:T(8,128)(2,1)}, bf16[1,32,4096]{2,1,0:T(8,128)(2,1)S(1)}, u32[]{:S(2)}, u32[]{:S(2)}) collective-permute-start(bf16[1,32,4096]{2,1,0:T(8,128)(2,1)} %get-tuple-element.87), channel_id=1, source_target_pairs={{0,8},{1,9},{2,10},{3,11},{4,12},{5,13},{6,14},{7,15},{8,0},{9,1},... | collective-permute-start | bytes 786440 | tf_op jit(solution)/shard_map/ppermute | solution.py:259
  257.3 21.5 %collective-permute-start.28 = (bf16[1,32,4096]{2,1,0:T(8,128)(2,1)}, bf16[1,32,4096]{2,1,0:T(8,128)(2,1)S(1)}, u32[]{:S(2)}, u32[]{:S(2)}) collective-permute-start(bf16[1,32,4096]{2,1,0:T(8,128)(2,1)} %get-tuple-element.88), channel_id=1, source_target_pairs={{0,8},{1,9},{2,10},{3,11},{4,12},{5,13},{6,14},{7,15},{8,0},{9,1},... | collective-permute-start | bytes 786440 | tf_op jit(solution)/shard_map/ppermute | solution.py:259
  258.8 20.1 %copy-start.6 = (bf16[1,32,4096]{2,1,0:T(8,128)(2,1)}, bf16[1,32,4096]{2,1,0:T(8,128)(2,1)S(1)}, u32[]{:S(2)}) copy-start(bf16[1,32,4096]{2,1,0:T(8,128)(2,1)S(1)} %collective-permute-done.25.refs_4_) | copy-start | bytes 786436
  258.8 20.1 %copy-start.7 = (bf16[1,32,4096]{2,1,0:T(8,128)(2,1)}, bf16[1,32,4096]{2,1,0:T(8,128)(2,1)S(1)}, u32[]{:S(2)}) copy-start(bf16[1,32,4096]{2,1,0:T(8,128)(2,1)S(1)} %collective-permute-done.26.refs_5_) | copy-start | bytes 786436
  (18 other events, 81.9 us)
where the time goes:
time: 289 us; the launch traced here: 288 us
  waiting for transfers between devices  143 us (49%)
  Pallas kernels  79.6 us (28%)
  starting transfers between devices  49.7 us (17%)
  local copies, waits for them, and re-layouts  9.74 us (3%)
  other arithmetic  3.71 us (1%)
    ppermute x29, waiting for transfers between devices, swap(): return lax.ppermute(x, 'seq', [(i, i ^ bit) for i in range(n)])  143 us
    ppermute x29, starting transfers between devices, swap(): return lax.ppermute(x, 'seq', [(i, i ^ bit) for i in range(n)])  36.9 us
    pallas_call x2, Pallas kernels, per_device(): pl.pallas_call(functools.partial(prompt_body, chunk, group), grid_spec=pl...  17.9 us
    pallas_call x1, Pallas kernels, per_device(): pl.pallas_call(functools.partial(response_body, chunk), grid_spec=pltpu.P...  17.4 us
    pallas_call x1, Pallas kernels, per_device(): pl.pallas_call(functools.partial(output_body, lows), grid_spec=pltpu.Pref...  11.2 us
    pallas_call x1, Pallas kernels, per_device(): call(project_body, (resp // block,), [pl.BlockSpec((block, model), lambda...  10.4 us
    pallas_call x4, Pallas kernels, per_device(): pl.pallas_call(halve_body, grid_spec=pltpu.PrefetchScalarGridSpec(num_sca...  8.65 us
    all_to_all x1, starting transfers between devices, per_device(): kv = lax.all_to_all(kv_send, 'seq', 0, 0, tiled=True)  7.55 us
  transfers between devices with their start and end apart: 31, of which 14 were waited for; matrix products, arithmetic and copies ran while one was open for 2% of the time, Pallas kernels for 25%

commit v1 on v0

--- a/solution.py
+++ b/solution.py
@@ -137,33 +137,44 @@
     return state
 
 
-def response_body(chunk, low_ref, kv_ref, qe_ref, qm_ref, ke_ref, km_ref, ve_ref, vm_ref, commit_ref, *refs):
+def response_body(chunk, kept, place_ref, kv_ref, qe_ref, qm_ref, ke_ref, km_ref, ve_ref, vm_ref, commit_ref, *refs):
     out_refs, scratch_ref = refs[:-1], refs[-1]
     lows = len(out_refs)
-    steps, highs, per, _ = out_refs[0].shape
-    resp = qe_ref.shape[0]
-    both = over_prompt(None, jnp.concatenate([qm_ref[...], qe_ref[...]], 0), kv_ref, chunk)
+    steps, blocks, per, _ = out_refs[0].shape
+    low, bit = place_ref[0], place_ref[1]
+    span_rows = lows * per
+    count = blocks * span_rows
+    side = bit if kept else 1 - bit
+
+    def mine(ref):
+        parts = [
+            ref[pl.ds(pl.multiple_of((2 * block + side) * span_rows, span_rows), span_rows), :]
+            for block in range(blocks)
+        ]
+        return jnp.concatenate(parts, 0) if blocks > 1 else parts[0]
+
+    by_mask, by_embed, revealed = mine(qm_ref), mine(qe_ref), mine(commit_ref)
+    both = over_prompt(None, jnp.concatenate([by_mask, by_embed], 0), kv_ref, chunk)
     mask_value = jnp.broadcast_to(vm_ref[0:1], ve_ref.shape)
-    span = min(resp, chunk * kv_ref.shape[2])
     for step in range(steps):
-        shown = commit_ref[...] <= step
-        one = commit_ref[:, 0:1] <= step
-        q = jnp.where(shown, qe_ref[...], qm_ref[...])
-        k = jnp.where(shown, ke_ref[...], km_ref[...])
-        v = jnp.where(shown, ve_ref[...], mask_value)
+        shown = revealed <= step
+        one = revealed[:, 0:1] <= step
+        shown_key = commit_ref[...] <= step
+        q = jnp.where(shown, by_embed, by_mask)
+        k = jnp.where(shown_key, ke_ref[...], km_ref[...])
+        v = jnp.where(shown_key, ve_ref[...], mask_value)
         state = (
-            jnp.where(one, both[0][resp:], both[0][:resp]),
-            jnp.where(one, both[1][resp:], both[1][:resp]),
-            jnp.where(shown, both[2][resp:], both[2][:resp]),
+            jnp.where(one, both[0][count:], both[0][:count]),
+            jnp.where(one, both[1][count:], both[1][:count]),
+            jnp.where(shown, both[2][count:], both[2][:count]),
         )
-        for first in range(0, resp, span):
-            state = merge(state, scores(q, k[first : first + span]), v[first : first + span])
-        _, total, acc = state
-        scratch_ref[...] = acc / total
-        for high in range(highs):
+        _, total, acc = merge(state, scores(q, k), v)
+        scratch_ref[step] = acc * (1.0 / total)
+    for step in range(steps):
+        for block in range(blocks):
             for k in range(lows):
-                at = (high * lows + (low_ref[0] ^ k)) * per
-                out_refs[k][step, high] = scratch_ref[pl.ds(pl.multiple_of(at, per), per), :].astype(BF16)
+                at = block * span_rows + (low ^ k) * per
+                out_refs[k][step, block] = scratch_ref[step, pl.ds(pl.multiple_of(at, per), per), :].astype(BF16)
 
 
 def prompt_body(chunk, group, me_ref, kv_ref, km_ref, vm_ref, *refs):
@@ -184,22 +195,24 @@
             out_ref[me_ref[0] ^ (turn * group + k)] = context[k * rows : (k + 1) * rows]
 
 
-def output_body(lows, place_ref, *refs):
-    x_refs, w_refs, outs = refs[:lows], refs[lows : 2 * lows], refs[2 * lows :]
-    steps, highs, per, width = x_refs[0].shape
-    sends, keeps = outs[:steps], outs[steps:]
-    bit = place_ref[1]
-    total = None
-    for x_ref, w_ref in zip(x_refs, w_refs):
-        x = x_ref[...].reshape(steps * highs * per, width)
-        term = jnp.dot(x, w_ref[...], preferred_element_type=F32)
-        total = term if total is None else total + term
-    for step in range(steps):
-        for high in range(0, highs, 2):
-            at = (step * highs + high) * per
-            first, second = total[at : at + per], total[at + per : at + 2 * per]
-            keeps[step][high // 2] = jnp.where(bit == 0, first, second)
-            sends[step][high // 2] = jnp.where(bit == 0, second, first).astype(BF16)
+def output_body(lows, split, place_ref, *refs):
+    x_refs, refs = refs[:lows], refs[lows:]
+    outs = refs[-STEPS:]
+    steps, blocks, per, width = x_refs[0].shape
+    far = lows // 2 if split else lows
+    w = jnp.concatenate([ref[...] for ref in refs[:-STEPS]], 0)
+    xs = []
+    for k, x_ref in enumerate(x_refs):
+        x = x_ref[...].reshape(steps * blocks * per, width)
+        if k >= far:
+            swapped = jnp.concatenate([x[:, width // 2 :], x[:, : width // 2]], 1)
+            x = jnp.where(place_ref[2] == 0, x, swapped)
+        xs.append(x)
+    total = jnp.dot(jnp.concatenate(xs, 1), w, preferred_element_type=F32)
+    for step, out_ref in enumerate(outs):
+        for block in range(blocks):
+            at = (step * blocks + block) * per
+            out_ref[block] = total[at : at + per].astype(out_ref.dtype)
 
 
 def halve_body(place_ref, keep_ref, got_ref, send_ref, kept_ref):
@@ -294,15 +307,19 @@
     for k in range(1, n):
         q_heads.append(swap(q_parts[k], k))
 
-    weights = [output_weight]
-    if lows == 4:
-        weights.append(swap(output_weight, 2))
-    near = swap(output_weight, 1)
-    if lows == 4:
-        last = swap(weights[1], 1)
-        weights = [output_weight, near, weights[1], last]
-    else:
-        weights = [output_weight, near]
+    groups = lax.axis_size("groups")
+    group = lax.axis_index("groups")
+    split = lows == 4 and groups % 2 == 0
+    weights = [output_weight, swap(output_weight, 1)]
+    if split:
+        half_rows = lax.dynamic_slice_in_dim(output_weight, (group & 1) * (width // 2), width // 2, 0)
+        fetched = swap(half_rows, 2)
+        given = lax.ppermute(fetched, "groups", [(i, i ^ 1) for i in range(groups)])
+        last = swap(fetched, 1)
+        weights += [fetched, given, last, swap(given, 1)]
+    elif lows == 4:
+        far = swap(output_weight, 2)
+        weights += [far, swap(far, 1)]
 
     cos_r, sin_r = tables(prompt_len + block_index[0] * resp + jnp.arange(resp, dtype=jnp.int32))
     commit = jnp.broadcast_to(commit_step[:, None], (resp, HD))
@@ -338,47 +355,47 @@
     vm_block = pl.BlockSpec((16, HD), lambda h, *_: (0, h))
     low = me & (lows - 1)
     high = me >> (lows.bit_length() - 1)
-    place = jnp.stack([low, high & 1]).astype(jnp.int32)
-    context = pl.pallas_call(
-        functools.partial(response_body, chunk),
-        grid_spec=pltpu.PrefetchScalarGridSpec(
-            num_scalar_prefetch=1,
-            grid=(heads,),
-            in_specs=[kv_block] + [key_block] * 5 + [vm_block, whole((resp, HD))],
-            out_specs=[pl.BlockSpec((STEPS, highs, per, HD), lambda h, *_: (0, 0, 0, h))] * lows,
-            scratch_shapes=[pltpu.VMEM((resp, HD), F32)],
-        ),
-        out_shape=[jax.ShapeDtypeStruct((STEPS, highs, per, width), BF16)] * lows,
-        name="response_attention",
-        cost_estimate=pl.CostEstimate(
-            flops=4 * resp * width * (2 * prompt_len + STEPS * resp),
-            bytes_accessed=4 * prompt_len * width,
-            transcendentals=heads * resp * (2 * prompt_len + STEPS * resp),
-        ),
-    )(place, kv, qe, qm, ke, km, ve, vm, commit)
-    plane_context = [context[0]]
-    for k in range(1, lows):
-        plane_context.append(swap(context[k], k))
-
-    columns = min(model, 512)
-    out_block = pl.BlockSpec((highs // 2, per, columns), lambda j, *_: (0, 0, j))
-    half = (highs // 2, per, model)
-    parts = pl.pallas_call(
-        functools.partial(output_body, lows),
-        grid_spec=pltpu.PrefetchScalarGridSpec(
-            num_scalar_prefetch=1,
-            grid=(model // columns,),
-            in_specs=[whole((STEPS, highs, per, width))] * lows
-            + [pl.BlockSpec((width, columns), lambda j, *_: (0, j))] * lows,
-            out_specs=[out_block] * (2 * STEPS),
-        ),
-        out_shape=[jax.ShapeDtypeStruct(half, BF16)] * STEPS + [jax.ShapeDtypeStruct(half, F32)] * STEPS,
-        name="output_projection",
-        cost_estimate=pl.CostEstimate(
-            flops=2 * STEPS * resp * model * width, bytes_accessed=2 * lows * width * model, transcendentals=0
-        ),
-    )(place, *plane_context, *weights)
-    sends, keeps = parts[:STEPS], parts[STEPS:]
+    blocks = highs // 2
+    place = jnp.stack([low, high & 1, group & 1]).astype(jnp.int32)
+    columns = min(model, 1024)
+    projected = {}
+    for kept in (False, True):
+        context = pl.pallas_call(
+            functools.partial(response_body, chunk, kept),
+            grid_spec=pltpu.PrefetchScalarGridSpec(
+                num_scalar_prefetch=1,
+                grid=(heads,),
+                in_specs=[kv_block] + [key_block] * 5 + [vm_block, whole((resp, HD))],
+                out_specs=[pl.BlockSpec((STEPS, blocks, per, HD), lambda h, *_: (0, 0, 0, h))] * lows,
+                scratch_shapes=[pltpu.VMEM((STEPS, resp // 2, HD), F32)],
+            ),
+            out_shape=[jax.ShapeDtypeStruct((STEPS, blocks, per, width), BF16)] * lows,
+            name="response_attention",
+            cost_estimate=pl.CostEstimate(
+                flops=2 * resp * width * (2 * prompt_len + STEPS * resp),
+                bytes_accessed=4 * prompt_len * width,
+                transcendentals=heads * resp * (2 * prompt_len + STEPS * resp) // 2,
+            ),
+        )(place, kv, qe, qm, ke, km, ve, vm, commit)
+        plane_context = [context[0]]
+        for k in range(1, lows):
+            plane_context.append(swap(context[k], k))
+        projected[kept] = pl.pallas_call(
+            functools.partial(output_body, lows, split),
+            grid_spec=pltpu.PrefetchScalarGridSpec(
+                num_scalar_prefetch=1,
+                grid=(model // columns,),
+                in_specs=[whole((STEPS, blocks, per, width))] * lows
+                + [pl.BlockSpec((w.shape[0], columns), lambda j, *_: (0, j)) for w in weights],
+                out_specs=[pl.BlockSpec((blocks, per, columns), lambda j, *_: (0, 0, j))] * STEPS,
+            ),
+            out_shape=[jax.ShapeDtypeStruct((blocks, per, model), F32 if kept else BF16)] * STEPS,
+            name="output_projection",
+            cost_estimate=pl.CostEstimate(
+                flops=STEPS * resp * model * width, bytes_accessed=2 * lows * width * model, transcendentals=0
+            ),
+        )(place, *plane_context, *weights)
+    sends, keeps = projected[False], projected[True]
 
     level = 0
     while True:
@@ -416,14 +433,14 @@
             kept.append(two)
         keeps = kept
 
-    group = max(1, min(n, 1024 // rows))
+    blocks_of_q = max(1, min(n, 1024 // rows))
     prompt_context = None
     for head in range(heads):
         of_head = functools.partial(lambda head, *_: (0, head), head)
         of_kv = functools.partial(lambda head, *_: (0, 0, 0, head), head)
         earlier = [] if prompt_context is None else [prompt_context]
         prompt_context = pl.pallas_call(
-            functools.partial(prompt_body, chunk, group),
+            functools.partial(prompt_body, chunk, blocks_of_q),
             grid_spec=pltpu.PrefetchScalarGridSpec(
                 num_scalar_prefetch=1,
                 grid=(1,),

time: 289 us -> 254 us (0.88)
  waiting for transfers between devices: 143 us -> 100 us
  Pallas kernels: 79.6 us -> 85.6 us
  starting transfers between devices: 49.7 us -> 53.1 us
    ppermute x29 -> x33, waiting for transfers between devices: 143 us -> 100 us  [swap(): return lax.ppermute(x, 'seq', [(i, i ^ bit) for i in range(n)])]
    pallas_call x4 -> x6, Pallas kernels: 46.4 us -> 52.3 us  [the longest x2 18.9 us: per_device(): pl.pallas_call(functools.partial(response_body, chunk, kept), grid_spec=p...]
    ppermute x29 -> x33, starting transfers between devices: 36.9 us -> 39.5 us  [swap(): return lax.ppermute(x, 'seq', [(i, i ^ bit) for i in range(n)])]
  transfers between devices with their start and end apart: 31 -> 36, of which waited for: 14 -> 11; matrix products, arithmetic and copies ran while one was open for 2% -> 2% of each run, Pallas kernels for 25% -> 31%
where the time goes in v1:
time: 254 us; the launch traced here: 253 us
  waiting for transfers between devices  100 us (39%)
  Pallas kernels  85.6 us (34%)
  starting transfers between devices  53.1 us (21%)
  local copies, waits for them, and re-layouts  8.69 us (3%)
  other arithmetic  3.74 us (1%)
    ppermute x33, waiting for transfers between devices, swap(): return lax.ppermute(x, 'seq', [(i, i ^ bit) for i in range(n)])  100 us
    ppermute x33, starting transfers between devices, swap(): return lax.ppermute(x, 'seq', [(i, i ^ bit) for i in range(n)])  39.5 us
    pallas_call x2, Pallas kernels, per_device(): pl.pallas_call(functools.partial(response_body, chunk, kept), grid_spec=p...  18.9 us
    pallas_call x2, Pallas kernels, per_device(): pl.pallas_call(functools.partial(prompt_body, chunk, blocks_of_q), grid_s...  17.9 us
    pallas_call x2, Pallas kernels, per_device(): pl.pallas_call(functools.partial(output_body, lows, split), grid_spec=plt...  15.5 us
    pallas_call x1, Pallas kernels, per_device(): call(project_body, (resp // block,), [pl.BlockSpec((block, model), lambda...  10.4 us
    pallas_call x4, Pallas kernels, per_device(): pl.pallas_call(halve_body, grid_spec=pltpu.PrefetchScalarGridSpec(num_sca...  8.61 us
    all_to_all x1, starting transfers between devices, per_device(): kv = lax.all_to_all(kv_send, 'seq', 0, 0, tiled=True)  7.6 us
  transfers between devices with their start and end apart: 36, of which 11 were waited for; matrix products, arithmetic and copies ran while one was open for 2% of the time, Pallas kernels for 31%

profile of v1, /device:TPU:0, one launch (start us, length us, event | category | flops | bytes accessed | tf_op | source)
XLA Modules:
  0.0 253.1 jit_solution(5059211171527421260)
XLA Ops:
  1.7 4.0 %shard_map.148 = bf16[16,2,128,256]{3,2,1,0:T(8,128)(2,1)} custom-call(bf16[128,4096]{1,0:T(8,128)(2,1)} %k_ref.1, bf16[128,4096]{1,0:T(8,128)(2,1)} %v_ref.1, f32[128,128]{1,0:T(8,128)} %get-tuple-element.105.cos_ref, f32[128,128]{1,0:T(8,128)} %get-tuple-element.106.sin_ref), custom_call_target="tpu_custom_call" | custom-call | flops 3145728 | bytes 4194304 | tf_op jit(solution)/shard_map/pallas_call | solution.py:276
  5.8 7.6 %all-to-all-start = ((bf16[16,2,128,256]{3,2,1,0:T(8,128)(2,1)}), bf16[16,2,128,256]{3,2,1,0:T(8,128)(2,1)}, u32[]{:S(2)}, u32[]{:S(2)}) async-start(bf16[16,2,128,256]{3,2,1,0:T(8,128)(2,1)} %shard_map.148), calls=%async_computation | async-start | bytes 4194304 | tf_op jit(solution)/shard_map/all_to_all | solution.py:290
  13.5 1.9 collective-permute-start.19
  15.4 45.9 %collective-permute-done.19.refs_6_ = bf16[128,4096]{1,0:T(8,128)(2,1)S(1)} collective-permute-done((bf16[128,4096]{1,0:T(8,128)(2,1)S(1)}, bf16[128,4096]{1,0:T(8,128)(2,1)S(1)}, u32[]{:S(2)}, u32[]{:S(2)}) %collective-permute-start.19) | collective-permute-done | bytes 1048608 | tf_op jit(solution)/shard_map/ppermute | solution.py:272
  61.4 1.5 collective-permute-start.20
  62.9 2.8 %pack_q.1 = (bf16[128,256]{1,0:T(8,128)(2,1)}, bf16[128,256]{1,0:T(8,128)(2,1)}, bf16[128,256]{1,0:T(8,128)(2,1)}, bf16[128,256]{1,0:T(8,128)(2,1)}, bf16[128,25...) custom-call(s32[1]{0:T(128)} %bitcast.me_ref.place_ref, ...), custom_call_target="tpu_custom_call" | custom-call | flops 3145728 | bytes 2097152 | tf_op jit(solution)/shard_map/pack_q/pallas_call | solution.py:292
  66.2 1.4 collective-permute-start.2
  67.6 1.5 collective-permute-start.3
  70.0 0.9 collective-permute-done.1.refs_2_
  72.1 2.0 collective-permute-start.6
  74.1 2.4 collective-permute-start.7
  77.1 1.0 fusion
  79.4 2.8 %collective-permute-start.9 = (bf16[128,256]{1,0:T(8,128)(2,1)}, bf16[128,256]{1,0:T(8,128)(2,1)S(1)}, u32[]{:S(2)}, u32[]{:S(2)}) collective-permute-start(bf16[128,256]{1,0:T(8,128)(2,1)} %get-tuple-element.63), channel_id=1, source_target_pairs={{0,10},{1,11},{2,8},{3,9},{4,14},{5,15},{6,12},{7,13},{8,2},{9,3},... | collective-permute-start | bytes 196616 | tf_op jit(solution)/shard_map/ppermute | solution.py:272
  82.8 1.3 collective-permute-start.10
  84.2 2.5 collective-permute-start.11
  86.8 1.0 pad_maximum_fusion
  87.8 2.0 collective-permute-start.12
  89.7 2.3 collective-permute-done.10.refs_11_
  92.8 3.3 %collective-permute-start.14 = (bf16[128,256]{1,0:T(8,128)(2,1)S(1)}, bf16[128,256]{1,0:T(8,128)(2,1)}, u32[]{:S(2)}, u32[]{:S(2)}) collective-permute-start(bf16[128,256]{1,0:T(8,128)(2,1)S(1)} %copy-done.24), channel_id=1, source_target_pairs={{0,15},{1,14},{2,13},{3,12},{4,11},{5,10},{6,9},{7,8},{8,7},{9,6},... | collective-permute-start | bytes 196616 | tf_op jit(solution)/shard_map/ppermute | solution.py:272
  96.1 10.4 %shard_map.149 = (bf16[512,256]{1,0:T(8,128)(2,1)}, bf16[512,256]{1,0:T(8,128)(2,1)}, bf16[512,256]{1,0:T(8,128)(2,1)}, bf16[512,256]{1,0:T(8,128)(2,1)}, bf16[5...) custom-call(bf16[512,4096]{1,0:T(8,128)(2,1)} %embed_ref.3, bf16[1,4096]{1,0:T(2,128)(2,1)} %broadcast_in_dim.8.mask_ref, ...), custom_call_target="tpu_custom_call" | custom-call | flops 3221225472 | bytes 10485760 | tf_op jit(solution)/shard_map/pallas_call | solution.py:329
  106.6 0.9 collective-permute-start.21
  107.6 8.9 %prompt_attention.2.refs_16_ = bf16[16,128,256]{2,1,0:T(8,128)(2,1)} custom-call(s32[1]{0:T(128)} %bitcast.me_ref.place_ref, bf16[16,2,128,256]{3,2,1,0:T(8,128)(2,1)} %all-to-all-done.kv_ref, bf16[512,256]{1,0:T(8,128)(2,1)} %get-tuple-element.51.km_ref, bf16[16,256]{1,0:T(8,128)(2,1)} %get-tuple-element.52.vm_ref, ...), custom_call_target="tpu_custom_call" | custom-call | flops 2684354560 | bytes 2097152 | tf_op jit(solution)/shard_map/prompt_attention/pallas_call | solution.py:442
  116.5 9.0 %prompt_attention.3 = bf16[16,128,256]{2,1,0:T(8,128)(2,1)} custom-call(s32[1]{0:T(128)} %bitcast.me_ref.place_ref, bf16[16,2,128,256]{3,2,1,0:T(8,128)(2,1)} %all-to-all-done.kv_ref, bf16[512,256]{1,0:T(8,128)(2,1)} %get-tuple-element.51.km_ref, bf16[16,256]{1,0:T(8,128)(2,1)} %get-tuple-element.52.vm_ref, ...), custom_call_target="tpu_custom_call", output_to_operand_aliasing={{}: (20, {})} | custom-call | flops 2684354560 | bytes 2097152 | tf_op jit(solution)/shard_map/prompt_attention/pallas_call | solution.py:442
  125.5 4.5 %all-to-all-start.1 = ((bf16[16,128,256]{2,1,0:T(8,128)(2,1)}), bf16[16,128,256]{2,1,0:T(8,128)(2,1)}, u32[]{:S(2)}, u32[]{:S(2)}) async-start(bf16[16,128,256]{2,1,0:T(8,128)(2,1)} %prompt_attention.3), calls=%async_computation.1 | async-start | bytes 2097152 | tf_op jit(solution)/shard_map/all_to_all | solution.py:466
  130.6 0.9 broadcast_in_dim.11.commit_ref
  131.5 9.5 %response_attention.3 = (bf16[4,2,32,256]{3,2,1,0:T(8,128)(2,1)}, bf16[4,2,32,256]{3,2,1,0:T(8,128)(2,1)}, bf16[4,2,32,256]{3,2,1,0:T(8,128)(2,1)}, bf16[4,2,32,256]{3,2,1,0:T(8,128)(2,1)}) custom-call(s32[3]{0:T(128)} %pad_add_fusion.place_ref, bf16[16,2,128,256]{3,2,1,0:T(8,128)(2,1)} %all-to-all-done.kv_ref, bf16[512,256]{1,0:T(8,128)(2,1)} %get-tuple-element.69.qe_ref, ...), custom_call_target="tpu_custom_call" | custom-call | flops 1610612736 | bytes 2097152 | tf_op jit(solution)/shard_map/response_attention/pallas_call | solution.py:363
  141.4 1.7 collective-permute-start.24
  143.0 9.5 %response_attention.2 = (bf16[4,2,32,256]{3,2,1,0:T(8,128)(2,1)}, bf16[4,2,32,256]{3,2,1,0:T(8,128)(2,1)}, bf16[4,2,32,256]{3,2,1,0:T(8,128)(2,1)}, bf16[4,2,32,256]{3,2,1,0:T(8,128)(2,1)}) custom-call(s32[3]{0:T(128)} %pad_add_fusion.place_ref, bf16[16,2,128,256]{3,2,1,0:T(8,128)(2,1)} %all-to-all-done.kv_ref, bf16[512,256]{1,0:T(8,128)(2,1)} %get-tuple-element.69.qe_ref, ...), custom_call_target="tpu_custom_call" | custom-call | flops 1610612736 | bytes 2097152 | tf_op jit(solution)/shard_map/response_attention/pallas_call | solution.py:363
  153.8 7.6 %output_projection.3 = (bf16[2,32,4096]{2,1,0:T(8,128)(2,1)}, bf16[2,32,4096]{2,1,0:T(8,128)(2,1)}, bf16[2,32,4096]{2,1,0:T(8,128)(2,1)}, bf16[2,32,4096]{2,1,0:T(8,128)(2,1)}) custom-call(s32[3]{0:T(128)} %pad_add_fusion.place_ref, bf16[4,2,32,256]{3,2,1,0:T(8,128)(2,1)} %get-tuple-element.78.refs_0_, bf16[4,2,32,256]{3,2,1,0:T(8,128)(2,1)} %copy-done.11, ...), custom_call_target="tpu_custom_call" | custom-call | flops 2147483648 | bytes 8388608 | tf_op jit(solution)/shard_map/output_projection/pallas_call | solution.py:383
  161.4 1.7 collective-permute-start.26
  163.5 1.7 collective-permute-start.28
  165.5 1.7 collective-permute-start.16
  167.3 3.3 %collective-permute-done.16.refs_2_ = bf16[4,2,32,256]{3,2,1,0:T(8,128)(2,1)S(1)} collective-permute-done((bf16[4,2,32,256]{3,2,1,0:T(8,128)(2,1)S(1)}, bf16[4,2,32,256]{3,2,1,0:T(8,128)(2,1)S(1)}, u32[]{:S(2)}, u32[]{:S(2)}) %collective-permute-start.16) | collective-permute-done | bytes 131104 | tf_op jit(solution)/shard_map/ppermute | solution.py:272
  170.6 5.6 %collective-permute-done.17.refs_3_ = bf16[4,2,32,256]{3,2,1,0:T(8,128)(2,1)S(1)} collective-permute-done((bf16[4,2,32,256]{3,2,1,0:T(8,128)(2,1)S(1)}, bf16[4,2,32,256]{3,2,1,0:T(8,128)(2,1)S(1)}, u32[]{:S(2)}, u32[]{:S(2)}) %collective-permute-start.17) | collective-permute-done | bytes 131104 | tf_op jit(solution)/shard_map/ppermute | solution.py:272
  176.8 7.9 %output_projection.2 = (f32[2,32,4096]{2,1,0:T(8,128)}, f32[2,32,4096]{2,1,0:T(8,128)}, f32[2,32,4096]{2,1,0:T(8,128)}, f32[2,32,4096]{2,1,0:T(8,128)}) custom-call(s32[3]{0:T(128)} %pad_add_fusion.place_ref, bf16[4,2,32,256]{3,2,1,0:T(8,128)(2,1)} %get-tuple-element.73.refs_0_, bf16[4,2,32,256]{3,2,1,0:T(8,128)(2,1)} %copy-done.10, ...), custom_call_target="tpu_custom_call" | custom-call | flops 2147483648 | bytes 8388608 | tf_op jit(solution)/shard_map/output_projection/pallas_call | solution.py:383
  185.6 2.2 halve.4
  187.7 2.6 %collective-permute-start.30 = (bf16[1,32,4096]{2,1,0:T(8,128)(2,1)}, bf16[1,32,4096]{2,1,0:T(8,128)(2,1)S(1)}, u32[]{:S(2)}, u32[]{:S(2)}) collective-permute-start(bf16[1,32,4096]{2,1,0:T(8,128)(2,1)} %get-tuple-element.93), channel_id=1, source_target_pairs={{0,8},{1,9},{2,10},{3,11},{4,12},{5,13},{6,14},{7,15},{8,0},{9,1},... | collective-permute-start | bytes 786440 | tf_op jit(solution)/shard_map/ppermute | solution.py:272
  191.1 2.2 halve.5
  193.6 16.6 %collective-permute-done.28.got_ref = bf16[2,32,4096]{2,1,0:T(8,128)(2,1)S(1)} collective-permute-done((bf16[2,32,4096]{2,1,0:T(8,128)(2,1)}, bf16[2,32,4096]{2,1,0:T(8,128)(2,1)S(1)}, u32[]{:S(2)}, u32[]{:S(2)}) %collective-permute-start.28) | collective-permute-done | bytes 524320 | tf_op jit(solution)/shard_map/ppermute | solution.py:272
  211.0 2.1 halve.6
  213.1 1.6 collective-permute-start.32
  214.8 6.3 %collective-permute-done.29.got_ref = bf16[2,32,4096]{2,1,0:T(8,128)(2,1)S(1)} collective-permute-done((bf16[2,32,4096]{2,1,0:T(8,128)(2,1)}, bf16[2,32,4096]{2,1,0:T(8,128)(2,1)S(1)}, u32[]{:S(2)}, u32[]{:S(2)}) %collective-permute-start.29) | collective-permute-done | bytes 524320 | tf_op jit(solution)/shard_map/ppermute | solution.py:272
  221.9 2.1 halve.7
  224.0 1.2 collective-permute-start.33
  225.9 13.6 %collective-permute-done.32.refs_6_ = bf16[1,32,4096]{2,1,0:T(8,128)(2,1)S(1)} collective-permute-done((bf16[1,32,4096]{2,1,0:T(8,128)(2,1)}, bf16[1,32,4096]{2,1,0:T(8,128)(2,1)S(1)}, u32[]{:S(2)}, u32[]{:S(2)}) %collective-permute-start.32) | collective-permute-done | bytes 262176 | tf_op jit(solution)/shard_map/ppermute | solution.py:272
  239.5 5.5 %collective-permute-done.33.refs_7_ = bf16[1,32,4096]{2,1,0:T(8,128)(2,1)S(1)} collective-permute-done((bf16[1,32,4096]{2,1,0:T(8,128)(2,1)}, bf16[1,32,4096]{2,1,0:T(8,128)(2,1)S(1)}, u32[]{:S(2)}, u32[]{:S(2)}) %collective-permute-start.33) | collective-permute-done | bytes 262176 | tf_op jit(solution)/shard_map/ppermute | solution.py:272
  245.8 4.0 %finish.1 = (bf16[4,32,4096]{2,1,0:T(8,128)(2,1)}, bf16[4,32,4096]{2,1,0:T(8,128)(2,1)}) custom-call(s32[1]{0:T(128)} %bitcast.me_ref.place_ref, bf16[512,4096]{1,0:T(8,128)(2,1)} %embed_ref.3, bf16[1,4096]{1,0:T(2,128)(2,1)} %broadcast_in_dim.8.mask_ref, bf16[1,4096]{1,0:T(2,128)(2,1)} %broadcast_in_dim.10.gain_ref, ...), custom_call_target="tpu_custom_call" | custom-call | tf_op jit(solution)/shard_map/finish/pallas_call | solution.py:471
  249.8 3.4 %shard_map.150 = bf16[128,4096]{1,0:T(8,128)(2,1)} custom-call(bf16[16,128,256]{2,1,0:T(8,128)(2,1)} %all-to-all-done.1.in_ref), custom_call_target="tpu_custom_call" | custom-call | bytes 2097152 | tf_op jit(solution)/shard_map/pallas_call | solution.py:492
  (122 shorter events, 15.4 us)
Async XLA Ops:
  5.8 101.8 %all-to-all-start = ((bf16[16,2,128,256]{3,2,1,0:T(8,128)(2,1)}), bf16[16,2,128,256]{3,2,1,0:T(8,128)(2,1)}, u32[]{:S(2)}, u32[]{:S(2)}) async-start(bf16[16,2,128,256]{3,2,1,0:T(8,128)(2,1)} %shard_map.148), calls=%async_computation | async-start | bytes 4194304 | tf_op jit(solution)/shard_map/all_to_all | solution.py:290
  13.4 64.7 %copy-start.16 = (bf16[4096]{0:T(1024)(128)(2,1)S(1)}, bf16[4096]{0:T(1024)(128)(2,1)}, u32[]{:S(2)}) copy-start(bf16[4096]{0:T(1024)(128)(2,1)} %param.17) | copy-start | bytes 24580
  13.4 65.4 %copy-start.17 = (bf16[4096]{0:T(1024)(128)(2,1)S(1)}, bf16[4096]{0:T(1024)(128)(2,1)}, u32[]{:S(2)}) copy-start(bf16[4096]{0:T(1024)(128)(2,1)} %param.20) | copy-start | bytes 24580
  13.5 47.9 %collective-permute-start.19 = (bf16[128,4096]{1,0:T(8,128)(2,1)S(1)}, bf16[128,4096]{1,0:T(8,128)(2,1)S(1)}, u32[]{:S(2)}, u32[]{:S(2)}) collective-permute-start(bf16[128,4096]{1,0:T(8,128)(2,1)S(1)} %constant_dynamic-slice_fusion), channel_id=1, source_target_pairs={{0,2},{1,3},{2,0},{3,1},{4,6},{5,7},{6,4},{7,5},{8,10},{9,11},{10,... | collective-permute-start | bytes 3145736 | tf_op jit(solution)/shard_map/ppermute | solution.py:272
  61.4 45.2 %copy-start.1 = (bf16[128,4096]{1,0:T(8,128)(2,1)}, bf16[128,4096]{1,0:T(8,128)(2,1)S(1)}, u32[]{:S(2)}) copy-start(bf16[128,4096]{1,0:T(8,128)(2,1)S(1)} %collective-permute-done.19.refs_6_) | copy-start | bytes 3145732
  61.4 46.1 %collective-permute-start.20 = (bf16[128,4096]{1,0:T(8,128)(2,1)S(1)}, bf16[128,4096]{1,0:T(8,128)(2,1)}, u32[]{:S(2)}, u32[]{:S(2)}) collective-permute-start(bf16[128,4096]{1,0:T(8,128)(2,1)S(1)} %collective-permute-done.19.refs_6_), channel_id=1, source_target_pairs={{0,16},{16,0},{1,17},{17,1},{2,18},{18,2},{3,19},{19,3},{4,20},{20... | collective-permute-start | bytes 3145736 | tf_op jit(solution)/shard_map/ppermute | solution.py:317
  65.6 26.4 %copy-start.26 = (bf16[128,256]{1,0:T(8,128)(2,1)S(1)}, bf16[128,256]{1,0:T(8,128)(2,1)}, u32[]{:S(2)}) copy-start(bf16[128,256]{1,0:T(8,128)(2,1)} %get-tuple-element.67) | copy-start | bytes 196612
  65.6 27.2 %copy-start.24 = (bf16[128,256]{1,0:T(8,128)(2,1)S(1)}, bf16[128,256]{1,0:T(8,128)(2,1)}, u32[]{:S(2)}) copy-start(bf16[128,256]{1,0:T(8,128)(2,1)} %get-tuple-element.68) | copy-start | bytes 196612
  65.6 4.0 %collective-permute-start = (bf16[128,256]{1,0:T(8,128)(2,1)}, bf16[128,256]{1,0:T(8,128)(2,1)S(1)}, u32[]{:S(2)}, u32[]{:S(2)}) collective-permute-start(bf16[128,256]{1,0:T(8,128)(2,1)} %get-tuple-element.54), channel_id=1, source_target_pairs={{0,1},{1,0},{2,3},{3,2},{4,5},{5,4},{6,7},{7,6},{8,9},{9,8},{10,11... | collective-permute-start | bytes 196616 | tf_op jit(solution)/shard_map/ppermute | solution.py:272
  65.7 5.2 %collective-permute-start.1 = (bf16[128,256]{1,0:T(8,128)(2,1)}, bf16[128,256]{1,0:T(8,128)(2,1)S(1)}, u32[]{:S(2)}, u32[]{:S(2)}) collective-permute-start(bf16[128,256]{1,0:T(8,128)(2,1)} %get-tuple-element.55), channel_id=1, source_target_pairs={{0,2},{1,3},{2,0},{3,1},{4,6},{5,7},{6,4},{7,5},{8,10},{9,11},{10,... | collective-permute-start | bytes 196616 | tf_op jit(solution)/shard_map/ppermute | solution.py:272
  66.2 5.4 %collective-permute-start.2 = (bf16[128,256]{1,0:T(8,128)(2,1)}, bf16[128,256]{1,0:T(8,128)(2,1)S(1)}, u32[]{:S(2)}, u32[]{:S(2)}) collective-permute-start(bf16[128,256]{1,0:T(8,128)(2,1)} %get-tuple-element.56), channel_id=1, source_target_pairs={{0,3},{1,2},{2,1},{3,0},{4,7},{5,6},{6,5},{7,4},{8,11},{9,10},{10,... | collective-permute-start | bytes 196616 | tf_op jit(solution)/shard_map/ppermute | solution.py:272
  67.6 4.6 %collective-permute-start.3 = (bf16[128,256]{1,0:T(8,128)(2,1)}, bf16[128,256]{1,0:T(8,128)(2,1)S(1)}, u32[]{:S(2)}, u32[]{:S(2)}) collective-permute-start(bf16[128,256]{1,0:T(8,128)(2,1)} %get-tuple-element.57), channel_id=1, source_target_pairs={{0,4},{1,5},{2,6},{3,7},{4,0},{5,1},{6,2},{7,3},{8,12},{9,13},{10,... | collective-permute-start | bytes 196616 | tf_op jit(solution)/shard_map/ppermute | solution.py:272
  69.7 36.8 %copy-start.22 = (bf16[128,256]{1,0:T(8,128)(2,1)}, bf16[128,256]{1,0:T(8,128)(2,1)S(1)}, u32[]{:S(2)}) copy-start(bf16[128,256]{1,0:T(8,128)(2,1)S(1)} %collective-permute-done.refs_1_) | copy-start | bytes 196612
  69.7 4.4 %collective-permute-start.4 = (bf16[128,256]{1,0:T(8,128)(2,1)}, bf16[128,256]{1,0:T(8,128)(2,1)S(1)}, u32[]{:S(2)}, u32[]{:S(2)}) collective-permute-start(bf16[128,256]{1,0:T(8,128)(2,1)} %get-tuple-element.58), channel_id=1, source_target_pairs={{0,5},{1,4},{2,7},{3,6},{4,1},{5,0},{6,3},{7,2},{8,13},{9,12},{10,... | collective-permute-start | bytes 196616 | tf_op jit(solution)/shard_map/ppermute | solution.py:272
  71.0 35.6 %copy-start.23 = (bf16[128,256]{1,0:T(8,128)(2,1)}, bf16[128,256]{1,0:T(8,128)(2,1)S(1)}, u32[]{:S(2)}) copy-start(bf16[128,256]{1,0:T(8,128)(2,1)S(1)} %collective-permute-done.1.refs_2_) | copy-start | bytes 196612
  71.0 5.5 %collective-permute-start.5 = (bf16[128,256]{1,0:T(8,128)(2,1)}, bf16[128,256]{1,0:T(8,128)(2,1)S(1)}, u32[]{:S(2)}, u32[]{:S(2)}) collective-permute-start(bf16[128,256]{1,0:T(8,128)(2,1)} %get-tuple-element.59), channel_id=1, source_target_pairs={{0,6},{1,7},{2,4},{3,5},{4,2},{5,3},{6,0},{7,1},{8,14},{9,15},{10,... | collective-permute-start | bytes 196616 | tf_op jit(solution)/shard_map/ppermute | solution.py:272
  71.6 34.9 %copy-start.25 = (bf16[128,256]{1,0:T(8,128)(2,1)}, bf16[128,256]{1,0:T(8,128)(2,1)S(1)}, u32[]{:S(2)}) copy-start(bf16[128,256]{1,0:T(8,128)(2,1)S(1)} %collective-permute-done.2.refs_3_) | copy-start | bytes 196612
  71.6 80.9 %collective-permute-start.18 = (bf16[256,4096]{1,0:T(8,128)(2,1)S(1)}, bf16[256,4096]{1,0:T(8,128)(2,1)}, u32[]{:S(2)}, u32[]{:S(2)}) collective-permute-start(bf16[256,4096]{1,0:T(8,128)(2,1)S(1)} %copy-done), channel_id=1, source_target_pairs={{0,1},{1,0},{2,3},{3,2},{4,5},{5,4},{6,7},{7,6},{8,9},{9,8},{10,11... | collective-permute-start | bytes 6291464 | tf_op jit(solution)/shard_map/ppermute | solution.py:272
  72.1 7.2 %collective-permute-start.6 = (bf16[128,256]{1,0:T(8,128)(2,1)}, bf16[128,256]{1,0:T(8,128)(2,1)S(1)}, u32[]{:S(2)}, u32[]{:S(2)}) collective-permute-start(bf16[128,256]{1,0:T(8,128)(2,1)} %get-tuple-element.60), channel_id=1, source_target_pairs={{0,7},{1,6},{2,5},{3,4},{4,3},{5,2},{6,1},{7,0},{8,15},{9,14},{10,... | collective-permute-start | bytes 196616 | tf_op jit(solution)/shard_map/ppermute | solution.py:272
  74.1 8.1 %collective-permute-start.7 = (bf16[128,256]{1,0:T(8,128)(2,1)}, bf16[128,256]{1,0:T(8,128)(2,1)S(1)}, u32[]{:S(2)}, u32[]{:S(2)}) collective-permute-start(bf16[128,256]{1,0:T(8,128)(2,1)} %get-tuple-element.61), channel_id=1, source_target_pairs={{0,8},{1,9},{2,10},{3,11},{4,12},{5,13},{6,14},{7,15},{8,0},{9,1},... | collective-permute-start | bytes 196616 | tf_op jit(solution)/shard_map/ppermute | solution.py:272
  76.5 7.7 %collective-permute-start.8 = (bf16[128,256]{1,0:T(8,128)(2,1)}, bf16[128,256]{1,0:T(8,128)(2,1)}, u32[]{:S(2)}, u32[]{:S(2)}) collective-permute-start(bf16[128,256]{1,0:T(8,128)(2,1)} %get-tuple-element.62), channel_id=1, source_target_pairs={{0,9},{1,8},{2,11},{3,10},{4,13},{5,12},{6,15},{7,14},{8,1},{9,0},... | collective-permute-start | bytes 196616 | tf_op jit(solution)/shard_map/ppermute | solution.py:272
  79.4 8.4 %collective-permute-start.9 = (bf16[128,256]{1,0:T(8,128)(2,1)}, bf16[128,256]{1,0:T(8,128)(2,1)S(1)}, u32[]{:S(2)}, u32[]{:S(2)}) collective-permute-start(bf16[128,256]{1,0:T(8,128)(2,1)} %get-tuple-element.63), channel_id=1, source_target_pairs={{0,10},{1,11},{2,8},{3,9},{4,14},{5,15},{6,12},{7,13},{8,2},{9,3},... | collective-permute-start | bytes 196616 | tf_op jit(solution)/shard_map/ppermute | solution.py:272
  82.8 9.2 %collective-permute-start.10 = (bf16[128,256]{1,0:T(8,128)(2,1)}, bf16[128,256]{1,0:T(8,128)(2,1)S(1)}, u32[]{:S(2)}, u32[]{:S(2)}) collective-permute-start(bf16[128,256]{1,0:T(8,128)(2,1)} %get-tuple-element.64), channel_id=1, source_target_pairs={{0,11},{1,10},{2,9},{3,8},{4,15},{5,14},{6,13},{7,12},{8,3},{9,2},... | collective-permute-start | bytes 196616 | tf_op jit(solution)/shard_map/ppermute | solution.py:272
  84.2 8.6 %collective-permute-start.11 = (bf16[128,256]{1,0:T(8,128)(2,1)}, bf16[128,256]{1,0:T(8,128)(2,1)S(1)}, u32[]{:S(2)}, u32[]{:S(2)}) collective-permute-start(bf16[128,256]{1,0:T(8,128)(2,1)} %get-tuple-element.65), channel_id=1, source_target_pairs={{0,12},{1,13},{2,14},{3,15},{4,8},{5,9},{6,10},{7,11},{8,4},{9,5},... | collective-permute-start | bytes 196616 | tf_op jit(solution)/shard_map/ppermute | solution.py:272
  87.8 18.8 %copy-start.32 = (bf16[128,256]{1,0:T(8,128)(2,1)}, bf16[128,256]{1,0:T(8,128)(2,1)S(1)}, u32[]{:S(2)}) copy-start(bf16[128,256]{1,0:T(8,128)(2,1)S(1)} %collective-permute-done.9.refs_10_) | copy-start | bytes 196612
  87.8 18.8 %collective-permute-start.12 = (bf16[128,256]{1,0:T(8,128)(2,1)}, bf16[128,256]{1,0:T(8,128)(2,1)}, u32[]{:S(2)}, u32[]{:S(2)}) collective-permute-start(bf16[128,256]{1,0:T(8,128)(2,1)} %get-tuple-element.66), channel_id=1, source_target_pairs={{0,13},{1,12},{2,15},{3,14},{4,9},{5,8},{6,11},{7,10},{8,5},{9,4},... | collective-permute-start | bytes 196616 | tf_op jit(solution)/shard_map/ppermute | solution.py:272
  92.0 15.6 %collective-permute-start.13 = (bf16[128,256]{1,0:T(8,128)(2,1)S(1)}, bf16[128,256]{1,0:T(8,128)(2,1)}, u32[]{:S(2)}, u32[]{:S(2)}) collective-permute-start(bf16[128,256]{1,0:T(8,128)(2,1)S(1)} %copy-done.26), channel_id=1, source_target_pairs={{0,14},{1,15},{2,12},{3,13},{4,10},{5,11},{6,8},{7,9},{8,6},{9,7},... | collective-permute-start | bytes 196616 | tf_op jit(solution)/shard_map/ppermute | solution.py:272
  92.8 14.8 %collective-permute-start.14 = (bf16[128,256]{1,0:T(8,128)(2,1)S(1)}, bf16[128,256]{1,0:T(8,128)(2,1)}, u32[]{:S(2)}, u32[]{:S(2)}) collective-permute-start(bf16[128,256]{1,0:T(8,128)(2,1)S(1)} %copy-done.24), channel_id=1, source_target_pairs={{0,15},{1,14},{2,13},{3,12},{4,11},{5,10},{6,9},{7,8},{8,7},{9,6},... | collective-permute-start | bytes 196616 | tf_op jit(solution)/shard_map/ppermute | solution.py:272
  106.6 36.4 %collective-permute-start.21 = (bf16[128,4096]{1,0:T(8,128)(2,1)S(1)}, bf16[128,4096]{1,0:T(8,128)(2,1)}, u32[]{:S(2)}, u32[]{:S(2)}) collective-permute-start(bf16[128,4096]{1,0:T(8,128)(2,1)S(1)} %collective-permute-done.19.refs_6_), channel_id=1, source_target_pairs={{0,1},{1,0},{2,3},{3,2},{4,5},{5,4},{6,7},{7,6},{8,9},{9,8},{10,11... | collective-permute-start | bytes 3145736 | tf_op jit(solution)/shard_map/ppermute | solution.py:272
  107.5 45.5 %collective-permute-start.22 = (bf16[128,4096]{1,0:T(8,128)(2,1)}, bf16[128,4096]{1,0:T(8,128)(2,1)}, u32[]{:S(2)}, u32[]{:S(2)}) collective-permute-start(bf16[128,4096]{1,0:T(8,128)(2,1)} %collective-permute-done.20.refs_7_), channel_id=1, source_target_pairs={{0,1},{1,0},{2,3},{3,2},{4,5},{5,4},{6,7},{7,6},{8,9},{9,8},{10,11... | collective-permute-start | bytes 3145736 | tf_op jit(solution)/shard_map/ppermute | solution.py:272
  125.5 124.3 %all-to-all-start.1 = ((bf16[16,128,256]{2,1,0:T(8,128)(2,1)}), bf16[16,128,256]{2,1,0:T(8,128)(2,1)}, u32[]{:S(2)}, u32[]{:S(2)}) async-start(bf16[16,128,256]{2,1,0:T(8,128)(2,1)} %prompt_attention.3), calls=%async_computation.1 | async-start | bytes 2097152 | tf_op jit(solution)/shard_map/all_to_all | solution.py:466
  141.0 12.1 %collective-permute-start.23 = (bf16[4,2,32,256]{3,2,1,0:T(8,128)(2,1)}, bf16[4,2,32,256]{3,2,1,0:T(8,128)(2,1)S(1)}, u32[]{:S(2)}, u32[]{:S(2)}) collective-permute-start(bf16[4,2,32,256]{3,2,1,0:T(8,128)(2,1)} %get-tuple-element.79), channel_id=1, source_target_pairs={{0,1},{1,0},{2,3},{3,2},{4,5},{5,4},{6,7},{7,6},{8,9},{9,8},{10,11... | collective-permute-start | bytes 393224 | tf_op jit(solution)/shard_map/ppermute | solution.py:272
  141.4 11.7 %collective-permute-start.24 = (bf16[4,2,32,256]{3,2,1,0:T(8,128)(2,1)}, bf16[4,2,32,256]{3,2,1,0:T(8,128)(2,1)S(1)}, u32[]{:S(2)}, u32[]{:S(2)}) collective-permute-start(bf16[4,2,32,256]{3,2,1,0:T(8,128)(2,1)} %get-tuple-element.80), channel_id=1, source_target_pairs={{0,2},{1,3},{2,0},{3,1},{4,6},{5,7},{6,4},{7,5},{8,10},{9,11},{10,... | collective-permute-start | bytes 393224 | tf_op jit(solution)/shard_map/ppermute | solution.py:272
  143.0 10.1 %collective-permute-start.25 = (bf16[4,2,32,256]{3,2,1,0:T(8,128)(2,1)}, bf16[4,2,32,256]{3,2,1,0:T(8,128)(2,1)S(1)}, u32[]{:S(2)}, u32[]{:S(2)}) collective-permute-start(bf16[4,2,32,256]{3,2,1,0:T(8,128)(2,1)} %get-tuple-element.81), channel_id=1, source_target_pairs={{0,3},{1,2},{2,1},{3,0},{4,7},{5,6},{6,5},{7,4},{8,11},{9,10},{10,... | collective-permute-start | bytes 393224 | tf_op jit(solution)/shard_map/ppermute | solution.py:272
  152.5 13.0 %collective-permute-start.15 = (bf16[4,2,32,256]{3,2,1,0:T(8,128)(2,1)}, bf16[4,2,32,256]{3,2,1,0:T(8,128)(2,1)S(1)}, u32[]{:S(2)}, u32[]{:S(2)}) collective-permute-start(bf16[4,2,32,256]{3,2,1,0:T(8,128)(2,1)} %get-tuple-element.74), channel_id=1, source_target_pairs={{0,1},{1,0},{2,3},{3,2},{4,5},{5,4},{6,7},{7,6},{8,9},{9,8},{10,11... | collective-permute-start | bytes 393224 | tf_op jit(solution)/shard_map/ppermute | solution.py:272
  161.4 23.3 %collective-permute-start.26 = (bf16[2,32,4096]{2,1,0:T(8,128)(2,1)}, bf16[2,32,4096]{2,1,0:T(8,128)(2,1)S(1)}, u32[]{:S(2)}, u32[]{:S(2)}) collective-permute-start(bf16[2,32,4096]{2,1,0:T(8,128)(2,1)} %get-tuple-element.82), channel_id=1, source_target_pairs={{0,4},{1,5},{2,6},{3,7},{4,0},{5,1},{6,2},{7,3},{8,12},{9,13},{10,... | collective-permute-start | bytes 1572872 | tf_op jit(solution)/shard_map/ppermute | solution.py:272
  163.1 27.1 %collective-permute-start.27 = (bf16[2,32,4096]{2,1,0:T(8,128)(2,1)}, bf16[2,32,4096]{2,1,0:T(8,128)(2,1)S(1)}, u32[]{:S(2)}, u32[]{:S(2)}) collective-permute-start(bf16[2,32,4096]{2,1,0:T(8,128)(2,1)} %get-tuple-element.85), channel_id=1, source_target_pairs={{0,4},{1,5},{2,6},{3,7},{4,0},{5,1},{6,2},{7,3},{8,12},{9,13},{10,... | collective-permute-start | bytes 1572872 | tf_op jit(solution)/shard_map/ppermute | solution.py:272
  163.5 46.7 %collective-permute-start.28 = (bf16[2,32,4096]{2,1,0:T(8,128)(2,1)}, bf16[2,32,4096]{2,1,0:T(8,128)(2,1)S(1)}, u32[]{:S(2)}, u32[]{:S(2)}) collective-permute-start(bf16[2,32,4096]{2,1,0:T(8,128)(2,1)} %get-tuple-element.88), channel_id=1, source_target_pairs={{0,4},{1,5},{2,6},{3,7},{4,0},{5,1},{6,2},{7,3},{8,12},{9,13},{10,... | collective-permute-start | bytes 1572872 | tf_op jit(solution)/shard_map/ppermute | solution.py:272
  165.2 55.9 %collective-permute-start.29 = (bf16[2,32,4096]{2,1,0:T(8,128)(2,1)}, bf16[2,32,4096]{2,1,0:T(8,128)(2,1)S(1)}, u32[]{:S(2)}, u32[]{:S(2)}) collective-permute-start(bf16[2,32,4096]{2,1,0:T(8,128)(2,1)} %get-tuple-element.91), channel_id=1, source_target_pairs={{0,4},{1,5},{2,6},{3,7},{4,0},{5,1},{6,2},{7,3},{8,12},{9,13},{10,... | collective-permute-start | bytes 1572872 | tf_op jit(solution)/shard_map/ppermute | solution.py:272
  165.5 5.0 %collective-permute-start.16 = (bf16[4,2,32,256]{3,2,1,0:T(8,128)(2,1)S(1)}, bf16[4,2,32,256]{3,2,1,0:T(8,128)(2,1)S(1)}, u32[]{:S(2)}, u32[]{:S(2)}) collective-permute-start(bf16[4,2,32,256]{3,2,1,0:T(8,128)(2,1)S(1)} %copy-done.21), channel_id=1, source_target_pairs={{0,2},{1,3},{2,0},{3,1},{4,6},{5,7},{6,4},{7,5},{8,10},{9,11},{10,... | collective-permute-start | bytes 393224 | tf_op jit(solution)/shard_map/ppermute | solution.py:272
  170.6 5.6 %collective-permute-start.17 = (bf16[4,2,32,256]{3,2,1,0:T(8,128)(2,1)S(1)}, bf16[4,2,32,256]{3,2,1,0:T(8,128)(2,1)S(1)}, u32[]{:S(2)}, u32[]{:S(2)}) collective-permute-start(bf16[4,2,32,256]{3,2,1,0:T(8,128)(2,1)S(1)} %copy-done.20), channel_id=1, source_target_pairs={{0,3},{1,2},{2,1},{3,0},{4,7},{5,6},{6,5},{7,4},{8,11},{9,10},{10,... | collective-permute-start | bytes 393224 | tf_op jit(solution)/shard_map/ppermute | solution.py:272
  187.7 38.1 %collective-permute-start.30 = (bf16[1,32,4096]{2,1,0:T(8,128)(2,1)}, bf16[1,32,4096]{2,1,0:T(8,128)(2,1)S(1)}, u32[]{:S(2)}, u32[]{:S(2)}) collective-permute-start(bf16[1,32,4096]{2,1,0:T(8,128)(2,1)} %get-tuple-element.93), channel_id=1, source_target_pairs={{0,8},{1,9},{2,10},{3,11},{4,12},{5,13},{6,14},{7,15},{8,0},{9,1},... | collective-permute-start | bytes 786440 | tf_op jit(solution)/shard_map/ppermute | solution.py:272
  191.1 34.2 %copy-start.18 = (bf16[4096]{0:T(1024)(128)(2,1)S(1)}, bf16[4096]{0:T(1024)(128)(2,1)}, u32[]{:S(2)}) copy-start(bf16[4096]{0:T(1024)(128)(2,1)} %param.21) | copy-start | bytes 24580
  193.2 32.6 %collective-permute-start.31 = (bf16[1,32,4096]{2,1,0:T(8,128)(2,1)}, bf16[1,32,4096]{2,1,0:T(8,128)(2,1)S(1)}, u32[]{:S(2)}, u32[]{:S(2)}) collective-permute-start(bf16[1,32,4096]{2,1,0:T(8,128)(2,1)} %get-tuple-element.94), channel_id=1, source_target_pairs={{0,8},{1,9},{2,10},{3,11},{4,12},{5,13},{6,14},{7,15},{8,0},{9,1},... | collective-permute-start | bytes 786440 | tf_op jit(solution)/shard_map/ppermute | solution.py:272
  213.1 26.4 %collective-permute-start.32 = (bf16[1,32,4096]{2,1,0:T(8,128)(2,1)}, bf16[1,32,4096]{2,1,0:T(8,128)(2,1)S(1)}, u32[]{:S(2)}, u32[]{:S(2)}) collective-permute-start(bf16[1,32,4096]{2,1,0:T(8,128)(2,1)} %get-tuple-element.95), channel_id=1, source_target_pairs={{0,8},{1,9},{2,10},{3,11},{4,12},{5,13},{6,14},{7,15},{8,0},{9,1},... | collective-permute-start | bytes 786440 | tf_op jit(solution)/shard_map/ppermute | solution.py:272
  224.0 21.0 %collective-permute-start.33 = (bf16[1,32,4096]{2,1,0:T(8,128)(2,1)}, bf16[1,32,4096]{2,1,0:T(8,128)(2,1)S(1)}, u32[]{:S(2)}, u32[]{:S(2)}) collective-permute-start(bf16[1,32,4096]{2,1,0:T(8,128)(2,1)} %get-tuple-element.96), channel_id=1, source_target_pairs={{0,8},{1,9},{2,10},{3,11},{4,12},{5,13},{6,14},{7,15},{8,0},{9,1},... | collective-permute-start | bytes 786440 | tf_op jit(solution)/shard_map/ppermute | solution.py:272
  225.9 19.2 %copy-start.6 = (bf16[1,32,4096]{2,1,0:T(8,128)(2,1)}, bf16[1,32,4096]{2,1,0:T(8,128)(2,1)S(1)}, u32[]{:S(2)}) copy-start(bf16[1,32,4096]{2,1,0:T(8,128)(2,1)S(1)} %collective-permute-done.30.refs_4_) | copy-start | bytes 786436
  225.9 19.2 %copy-start.7 = (bf16[1,32,4096]{2,1,0:T(8,128)(2,1)}, bf16[1,32,4096]{2,1,0:T(8,128)(2,1)S(1)}, u32[]{:S(2)}) copy-start(bf16[1,32,4096]{2,1,0:T(8,128)(2,1)S(1)} %collective-permute-done.31.refs_5_) | copy-start | bytes 786436
  (23 other events, 95.8 us)

commit v2 on v1

--- a/solution.py
+++ b/solution.py
@@ -60,14 +60,15 @@
         out_ref[dest, 1] = v_ref[:, dest * width : (dest + 1) * width]
 
 
-def pack_q_body(me_ref, q_ref, cos_ref, sin_ref, *out_refs):
+def pack_q_body(q_ref, cos_ref, sin_ref, out_ref):
     cosine, sine = cos_ref[...] * SCORE_SCALE, sin_ref[...] * SCORE_SCALE
-    width = out_refs[0].shape[1]
-    for k, out_ref in enumerate(out_refs):
-        start = (me_ref[0] ^ k) * width
+    width = out_ref.shape[2]
+    for dest in range(out_ref.shape[0]):
         for lane in range(0, width, HD):
-            u = q_ref[:, pl.ds(pl.multiple_of(start + lane, HD), HD)].astype(F32)
-            out_ref[:, lane : lane + HD] = rope(u, cosine, sine).astype(BF16)
+            column = dest * width + lane
+            out_ref[dest, :, lane : lane + HD] = rope(
+                q_ref[:, column : column + HD].astype(F32), cosine, sine
+            ).astype(BF16)
 
 
 def normed(rows, gain):
@@ -177,22 +178,19 @@
                 out_refs[k][step, block] = scratch_ref[step, pl.ds(pl.multiple_of(at, per), per), :].astype(BF16)
 
 
-def prompt_body(chunk, group, me_ref, kv_ref, km_ref, vm_ref, *refs):
-    q_refs, out_ref, queries = refs[: kv_ref.shape[0]], refs[-2], refs[-1]
-    rows = out_ref.shape[1]
-    for k, ref in enumerate(q_refs):
-        queries[k * rows : (k + 1) * rows] = ref[...]
-
-    @pl.loop(0, len(q_refs) // group)
+def prompt_body(chunk, group, q_ref, kv_ref, km_ref, vm_ref, *refs):
+    out_ref = refs[-1]
+    sources, rows, width = q_ref.shape
+
+    @pl.loop(0, sources // group)
     def _(turn):
-        q = queries[pl.ds(pl.multiple_of(turn * (group * rows), group * rows), group * rows), :]
+        at = pl.ds(turn * group, group)
+        q = q_ref[at].reshape(group * rows, width)
         s = scores(q, km_ref[...])
         top = jnp.max(s, axis=-1, keepdims=True)
         total = jnp.sum(jnp.exp2(s - top), axis=-1, keepdims=True)
         state = over_prompt((top, total, total * vm_ref[0:1].astype(F32)), q, kv_ref, chunk)
-        context = (state[2] / state[1]).astype(BF16)
-        for k in range(group):
-            out_ref[me_ref[0] ^ (turn * group + k)] = context[k * rows : (k + 1) * rows]
+        out_ref[at] = (state[2] / state[1]).astype(BF16).reshape(group, rows, width)
 
 
 def output_body(lows, split, place_ref, *refs):
@@ -224,16 +222,14 @@
         send_ref[pair] = jnp.where(bit == 0, second, first).astype(BF16)
 
 
-def finish_body(steps, place_ref, embed_ref, mask_ref, gain_ref, commit_ref, *refs):
-    keeps, gots, (residual_ref, normed_ref) = refs[:steps], refs[steps : 2 * steps], refs[2 * steps :]
-    gain = gain_ref[...].astype(F32)
-    for step in range(steps):
-        shown = commit_ref[:, 0:1] <= step
-        rows = jnp.where(shown, embed_ref[...].astype(F32), mask_ref[...].astype(F32))
-        hidden = rows + (keeps[step][0] + gots[step][0].astype(F32))
-        residual_ref[step] = hidden.astype(BF16)
-        scale = lax.rsqrt(jnp.mean(hidden * hidden, axis=-1, keepdims=True) + NORM_EPS)
-        normed_ref[step] = (hidden * scale * gain).astype(BF16)
+def finish_body(step, place_ref, embed_ref, mask_ref, gain_ref, commit_ref, keep_ref, got_ref, *refs):
+    residual_ref, normed_ref = refs[-2:]
+    shown = commit_ref[:, 0:1] <= step
+    rows = jnp.where(shown, embed_ref[...].astype(F32), mask_ref[...].astype(F32))
+    hidden = rows + (keep_ref[0] + got_ref[0].astype(F32))
+    residual_ref[0] = hidden.astype(BF16)
+    scale = lax.rsqrt(jnp.mean(hidden * hidden, axis=-1, keepdims=True) + NORM_EPS)
+    normed_ref[0] = (hidden * scale * gain_ref[...].astype(F32)).astype(BF16)
 
 
 def unpack_body(in_ref, out_ref):
@@ -288,24 +284,20 @@
         moved=8 * rows * head_cols,
     )(prompt_key, prompt_value, cos_p, sin_p)
     kv = lax.all_to_all(kv_send, "seq", 0, 0, tiled=True)
-    where = me.astype(jnp.int32).reshape(1)
-    q_parts = pl.pallas_call(
+    q_send = call(
         pack_q_body,
-        grid_spec=pltpu.PrefetchScalarGridSpec(
-            num_scalar_prefetch=1,
-            grid=(1,),
-            in_specs=[whole((rows, head_cols)), whole((rows, HD)), whole((rows, HD))],
-            out_specs=[whole((rows, width))] * n,
-        ),
-        out_shape=[jax.ShapeDtypeStruct((rows, width), BF16)] * n,
-        name="pack_q",
-        cost_estimate=pl.CostEstimate(
-            flops=6 * rows * head_cols, bytes_accessed=4 * rows * head_cols, transcendentals=0
-        ),
-    )(where, prompt_query, cos_p, sin_p)
-    q_heads = [q_parts[0]]
-    for k in range(1, n):
-        q_heads.append(swap(q_parts[k], k))
+        (n // dests,),
+        [
+            pl.BlockSpec((rows, dests * width), lambda j: (0, j)),
+            whole((rows, HD)),
+            whole((rows, HD)),
+        ],
+        pl.BlockSpec((dests, rows, width), lambda j: (j, 0, 0)),
+        jax.ShapeDtypeStruct((n, rows, width), BF16),
+        flops=6 * rows * head_cols,
+        moved=4 * rows * head_cols,
+    )(prompt_query, cos_p, sin_p)
+    q_heads = lax.all_to_all(q_send, "seq", 0, 0, tiled=True)
 
     groups = lax.axis_size("groups")
     group = lax.axis_index("groups")
@@ -437,57 +429,58 @@
     prompt_context = None
     for head in range(heads):
         of_head = functools.partial(lambda head, *_: (0, head), head)
+        of_block = functools.partial(lambda head, *_: (0, 0, head), head)
         of_kv = functools.partial(lambda head, *_: (0, 0, 0, head), head)
         earlier = [] if prompt_context is None else [prompt_context]
         prompt_context = pl.pallas_call(
             functools.partial(prompt_body, chunk, blocks_of_q),
-            grid_spec=pltpu.PrefetchScalarGridSpec(
-                num_scalar_prefetch=1,
-                grid=(1,),
-                in_specs=[
-                    pl.BlockSpec((n, 2, rows, HD), of_kv),
-                    pl.BlockSpec((resp, HD), of_head),
-                    pl.BlockSpec((16, HD), of_head),
-                ]
-                + [pl.BlockSpec((rows, HD), of_head)] * n
-                + [pl.BlockSpec(memory_space=pl.ANY)] * len(earlier),
-                out_specs=pl.BlockSpec((n, rows, HD), functools.partial(lambda head, *_: (0, 0, head), head)),
-                scratch_shapes=[pltpu.VMEM((n * rows, HD), BF16)],
-            ),
+            grid=(1,),
+            in_specs=[
+                pl.BlockSpec((n, rows, HD), of_block),
+                pl.BlockSpec((n, 2, rows, HD), of_kv),
+                pl.BlockSpec((resp, HD), of_head),
+                pl.BlockSpec((16, HD), of_head),
+            ]
+            + [pl.BlockSpec(memory_space=pl.ANY)] * len(earlier),
+            out_specs=pl.BlockSpec((n, rows, HD), of_block),
             out_shape=jax.ShapeDtypeStruct((n, rows, width), BF16),
             name="prompt_attention",
-            input_output_aliases={n + 4: 0} if earlier else {},
+            input_output_aliases={4: 0} if earlier else {},
             cost_estimate=pl.CostEstimate(
                 flops=4 * prompt_len * HD * (prompt_len + resp),
                 bytes_accessed=8 * prompt_len * HD,
                 transcendentals=prompt_len * (prompt_len + resp),
             ),
-        )(where, kv, km, vm, *q_heads, *earlier)
+        )(q_heads, kv, km, vm, *earlier)
     back = lax.all_to_all(prompt_context, "seq", 0, 0, tiled=True)
 
-    row_block = pl.BlockSpec((per, model), lambda i, at: (at[0], 0))
-    sums = pl.BlockSpec((1, per, model), lambda i, at: (0, 0, 0))
-    result = pl.BlockSpec((STEPS, per, model), lambda i, at: (0, 0, 0))
-    residual, normed_rows = pl.pallas_call(
-        functools.partial(finish_body, STEPS),
-        grid_spec=pltpu.PrefetchScalarGridSpec(
-            num_scalar_prefetch=1,
-            grid=(1,),
-            in_specs=[
-                row_block,
-                pl.BlockSpec((1, model), lambda i, at: (0, 0)),
-                pl.BlockSpec((1, model), lambda i, at: (0, 0)),
-                pl.BlockSpec((per, HD), lambda i, at: (at[0], 0)),
-            ]
-            + [sums] * (2 * STEPS),
-            out_specs=[result, result],
-        ),
-        out_shape=[jax.ShapeDtypeStruct((STEPS, per, model), BF16)] * 2,
-        name="finish",
-    )(
-        where, response_embed, mask_embed[None, :], residual_gain[None, :],
-        commit, *keeps, *gots,
-    )
+    results = []
+    for step in range(STEPS):
+        at_row = lambda i, at: (at[0], 0)
+        at_step = functools.partial(lambda step, i, at: (step, 0, 0), step)
+        one_row = pl.BlockSpec((1, model), lambda i, at: (0, 0))
+        one_sum = pl.BlockSpec((1, per, model), lambda i, at: (0, 0, 0))
+        results = pl.pallas_call(
+            functools.partial(finish_body, step),
+            grid_spec=pltpu.PrefetchScalarGridSpec(
+                num_scalar_prefetch=1,
+                grid=(1,),
+                in_specs=[
+                    pl.BlockSpec((per, model), at_row), one_row, one_row,
+                    pl.BlockSpec((per, HD), at_row), one_sum, one_sum,
+                ]
+                + [pl.BlockSpec(memory_space=pl.ANY)] * len(results),
+                out_specs=[pl.BlockSpec((1, per, model), at_step)] * 2,
+            ),
+            out_shape=[jax.ShapeDtypeStruct((STEPS, per, model), BF16)] * 2,
+            name="finish",
+            input_output_aliases={7: 0, 8: 1} if results else {},
+            cost_estimate=pl.CostEstimate(flops=8 * per * model, bytes_accessed=12 * per * model, transcendentals=0),
+        )(
+            me.astype(jnp.int32).reshape(1), response_embed, mask_embed[None, :], residual_gain[None, :],
+            commit, keeps[step], gots[step], *results,
+        )
+    residual, normed_rows = results
     columns = max(1, n // 4)
     prompt_out = call(
         unpack_body,

time: 254 us -> 260 us (1.024)
  starting transfers between devices: 53.1 us -> 37.4 us
  waiting for transfers between devices: 100 us -> 115 us
  Pallas kernels: 85.6 us -> 91.2 us
    ppermute x33 -> x18, starting transfers between devices: 39.5 us -> 16.7 us  [swap(): return lax.ppermute(x, 'seq', [(i, i ^ bit) for i in range(n)])]
    all_to_all x0 -> x1, waiting for transfers between devices: none -> 18.8 us  [per_device(): q_heads = lax.all_to_all(q_send, 'seq', 0, 0, tiled=True)]
    ppermute x33 -> x18, waiting for transfers between devices: 100 us -> 87.9 us  [swap(): return lax.ppermute(x, 'seq', [(i, i ^ bit) for i in range(n)])]
    ppermute x1, waiting for transfers between devices: 0.01 us -> 8.27 us  [per_device(): given = lax.ppermute(fetched, 'groups', [(i, i ^ 1) for i in range(groups)])]
    all_to_all x0 -> x1, starting transfers between devices: none -> 7.41 us  [per_device(): q_heads = lax.all_to_all(q_send, 'seq', 0, 0, tiled=True)]
    pallas_call x4 -> x7, Pallas kernels: 24.6 us -> 30.1 us  [the longest x2 17.4 us: per_device(): pl.pallas_call(functools.partial(prompt_body, chunk, blocks_of_q), grid=(...]
    unnamed x70 -> x46, local copies, waits for them, and re-layouts: 5.94 us -> 7.47 us
  transfers between devices with their start and end apart: 36 -> 22, of which waited for: 11 -> 9; matrix products, arithmetic and copies ran while one was open for 2% -> 2% of each run, Pallas kernels for 31% -> 32%
where the time goes in v2:
time: 260 us; the launch traced here: 259 us
  waiting for transfers between devices  115 us (44%)
  Pallas kernels  91.2 us (35%)
  starting transfers between devices  37.4 us (14%)
  local copies, waits for them, and re-layouts  10.2 us (4%)
  other arithmetic  3.75 us (1%)
    ppermute x18, waiting for transfers between devices, swap(): return lax.ppermute(x, 'seq', [(i, i ^ bit) for i in range(n)])  87.9 us
    pallas_call x2, Pallas kernels, per_device(): pl.pallas_call(functools.partial(response_body, chunk, kept), grid_spec=p...  18.9 us
    all_to_all x1, waiting for transfers between devices, per_device(): q_heads = lax.all_to_all(q_send, 'seq', 0, 0, tiled=True)  18.8 us
    pallas_call x2, Pallas kernels, per_device(): pl.pallas_call(functools.partial(prompt_body, chunk, blocks_of_q), grid=(...  17.4 us
    ppermute x18, starting transfers between devices, swap(): return lax.ppermute(x, 'seq', [(i, i ^ bit) for i in range(n)])  16.7 us
    pallas_call x2, Pallas kernels, per_device(): pl.pallas_call(functools.partial(output_body, lows, split), grid_spec=plt...  15.6 us
    pallas_call x1, Pallas kernels, per_device(): call(project_body, (resp // block,), [pl.BlockSpec((block, model), lambda...  10.5 us
    pallas_call x4, Pallas kernels, per_device(): pl.pallas_call(functools.partial(finish_body, step), grid_spec=pltpu.Pref...  8.98 us
  transfers between devices with their start and end apart: 22, of which 9 were waited for; matrix products, arithmetic and copies ran while one was open for 2% of the time, Pallas kernels for 32%

profile of v2, /device:TPU:0, one launch (start us, length us, event | category | flops | bytes accessed | tf_op | source)
XLA Modules:
  0.0 259.1 jit_solution(6174607052320568568)
XLA Ops:
  1.0 0.8 pad_maximum_fusion.2
  1.7 3.7 %shard_map.148 = bf16[16,128,256]{2,1,0:T(8,128)(2,1)} custom-call(bf16[128,4096]{1,0:T(8,128)(2,1)} %q_ref.1, f32[128,128]{1,0:T(8,128)} %get-tuple-element.85.cos_ref, f32[128,128]{1,0:T(8,128)} %get-tuple-element.86.sin_ref), custom_call_target="tpu_custom_call" | custom-call | flops 3145728 | bytes 2097152 | tf_op jit(solution)/shard_map/pallas_call | solution.py:287
  5.5 7.4 %all-to-all-start = ((bf16[16,128,256]{2,1,0:T(8,128)(2,1)}), bf16[16,128,256]{2,1,0:T(8,128)(2,1)S(1)}, u32[]{:S(2)}, u32[]{:S(2)}) async-start(bf16[16,128,256]{2,1,0:T(8,128)(2,1)} %shard_map.148), calls=%async_computation | async-start | bytes 2097152 | tf_op jit(solution)/shard_map/all_to_all | solution.py:300
  12.9 4.1 %shard_map.149 = bf16[16,2,128,256]{3,2,1,0:T(8,128)(2,1)} custom-call(bf16[128,4096]{1,0:T(8,128)(2,1)} %k_ref.1, bf16[128,4096]{1,0:T(8,128)(2,1)} %v_ref.1, f32[128,128]{1,0:T(8,128)} %get-tuple-element.85.cos_ref, f32[128,128]{1,0:T(8,128)} %get-tuple-element.86.sin_ref), custom_call_target="tpu_custom_call" | custom-call | flops 3145728 | bytes 4194304 | tf_op jit(solution)/shard_map/pallas_call | solution.py:272
  17.0 18.8 %all-to-all-done.q_ref = bf16[16,128,256]{2,1,0:T(8,128)(2,1)S(1)} async-done(((bf16[16,128,256]{2,1,0:T(8,128)(2,1)}), bf16[16,128,256]{2,1,0:T(8,128)(2,1)S(1)}, u32[]{:S(2)}, u32[]{:S(2)}) %all-to-all-start) | async-done | bytes 1048608 | tf_op jit(solution)/shard_map/all_to_all | solution.py:300
  35.8 6.8 %all-to-all-start.1 = ((bf16[16,2,128,256]{3,2,1,0:T(8,128)(2,1)}), bf16[16,2,128,256]{3,2,1,0:T(8,128)(2,1)}, u32[]{:S(2)}, u32[]{:S(2)}) async-start(bf16[16,2,128,256]{3,2,1,0:T(8,128)(2,1)} %shard_map.149), calls=%async_computation.1 | async-start | bytes 4194304 | tf_op jit(solution)/shard_map/all_to_all | solution.py:286
  42.8 1.9 collective-permute-start.4
  44.7 45.9 %collective-permute-done.4.refs_6_ = bf16[128,4096]{1,0:T(8,128)(2,1)S(1)} collective-permute-done((bf16[128,4096]{1,0:T(8,128)(2,1)S(1)}, bf16[128,4096]{1,0:T(8,128)(2,1)S(1)}, u32[]{:S(2)}, u32[]{:S(2)}) %collective-permute-start.4) | collective-permute-done | bytes 1048608 | tf_op jit(solution)/shard_map/ppermute | solution.py:268
  90.6 1.5 collective-permute-start.5
  94.0 1.0 fusion
  95.0 1.0 pad_maximum_fusion
  96.0 10.5 %shard_map.150 = (bf16[512,256]{1,0:T(8,128)(2,1)}, bf16[512,256]{1,0:T(8,128)(2,1)}, bf16[512,256]{1,0:T(8,128)(2,1)}, bf16[512,256]{1,0:T(8,128)(2,1)}, bf16[5...) custom-call(bf16[512,4096]{1,0:T(8,128)(2,1)} %embed_ref.9, bf16[1,4096]{1,0:T(2,128)(2,1)} %broadcast_in_dim.8.mask_ref, ...), custom_call_target="tpu_custom_call" | custom-call | flops 3221225472 | bytes 10485760 | tf_op jit(solution)/shard_map/pallas_call | solution.py:321
  107.0 8.3 %collective-permute-done.5.refs_7_ = bf16[128,4096]{1,0:T(8,128)(2,1)} collective-permute-done((bf16[128,4096]{1,0:T(8,128)(2,1)S(1)}, bf16[128,4096]{1,0:T(8,128)(2,1)}, u32[]{:S(2)}, u32[]{:S(2)}) %collective-permute-start.5) | collective-permute-done | bytes 1048608 | tf_op jit(solution)/shard_map/ppermute | solution.py:309
  115.3 8.7 %prompt_attention.2.refs_0_ = bf16[16,128,256]{2,1,0:T(8,128)(2,1)} custom-call(bf16[16,128,256]{2,1,0:T(8,128)(2,1)} %copy-done.2, bf16[16,2,128,256]{3,2,1,0:T(8,128)(2,1)} %all-to-all-done.1.kv_ref, bf16[512,256]{1,0:T(8,128)(2,1)} %get-tuple-element.41.km_ref, bf16[16,256]{1,0:T(8,128)(2,1)} %get-tuple-element.42.vm_ref), custom_call_target="tpu_custom_call" | custom-call | flops 2684354560 | bytes 2097152 | tf_op jit(solution)/shard_map/prompt_attention/pallas_call | solution.py:435
  124.0 8.7 %prompt_attention.3 = bf16[16,128,256]{2,1,0:T(8,128)(2,1)} custom-call(bf16[16,128,256]{2,1,0:T(8,128)(2,1)} %copy-done.2, bf16[16,2,128,256]{3,2,1,0:T(8,128)(2,1)} %all-to-all-done.1.kv_ref, bf16[512,256]{1,0:T(8,128)(2,1)} %get-tuple-element.41.km_ref, bf16[16,256]{1,0:T(8,128)(2,1)} %get-tuple-element.42.vm_ref, ...), custom_call_target="tpu_custom_call", output_to_operand_aliasing={{}: (4, {})} | custom-call | flops 2684354560 | bytes 2097152 | tf_op jit(solution)/shard_map/prompt_attention/pallas_call | solution.py:435
  132.7 4.9 %all-to-all-start.2 = ((bf16[16,128,256]{2,1,0:T(8,128)(2,1)}), bf16[16,128,256]{2,1,0:T(8,128)(2,1)}, u32[]{:S(2)}, u32[]{:S(2)}) async-start(bf16[16,128,256]{2,1,0:T(8,128)(2,1)} %prompt_attention.3), calls=%async_computation.2 | async-start | bytes 2097152 | tf_op jit(solution)/shard_map/all_to_all | solution.py:455
  138.3 0.8 broadcast_in_dim.11.commit_ref
  139.2 9.5 %response_attention.3 = (bf16[4,2,32,256]{3,2,1,0:T(8,128)(2,1)}, bf16[4,2,32,256]{3,2,1,0:T(8,128)(2,1)}, bf16[4,2,32,256]{3,2,1,0:T(8,128)(2,1)}, bf16[4,2,32,256]{3,2,1,0:T(8,128)(2,1)}) custom-call(s32[3]{0:T(128)} %pad_add_fusion.place_ref, bf16[16,2,128,256]{3,2,1,0:T(8,128)(2,1)} %all-to-all-done.1.kv_ref, bf16[512,256]{1,0:T(8,128)(2,1)} %get-tuple-element.43.qe_ref, ...), custom_call_target="tpu_custom_call" | custom-call | flops 1610612736 | bytes 2097152 | tf_op jit(solution)/shard_map/response_attention/pallas_call | solution.py:355
  149.1 1.6 collective-permute-start.9
  150.7 9.5 %response_attention.2 = (bf16[4,2,32,256]{3,2,1,0:T(8,128)(2,1)}, bf16[4,2,32,256]{3,2,1,0:T(8,128)(2,1)}, bf16[4,2,32,256]{3,2,1,0:T(8,128)(2,1)}, bf16[4,2,32,256]{3,2,1,0:T(8,128)(2,1)}) custom-call(s32[3]{0:T(128)} %pad_add_fusion.place_ref, bf16[16,2,128,256]{3,2,1,0:T(8,128)(2,1)} %all-to-all-done.1.kv_ref, bf16[512,256]{1,0:T(8,128)(2,1)} %get-tuple-element.43.qe_ref, ...), custom_call_target="tpu_custom_call" | custom-call | flops 1610612736 | bytes 2097152 | tf_op jit(solution)/shard_map/response_attention/pallas_call | solution.py:355
  161.5 7.6 %output_projection.3 = (bf16[2,32,4096]{2,1,0:T(8,128)(2,1)}, bf16[2,32,4096]{2,1,0:T(8,128)(2,1)}, bf16[2,32,4096]{2,1,0:T(8,128)(2,1)}, bf16[2,32,4096]{2,1,0:T(8,128)(2,1)}) custom-call(s32[3]{0:T(128)} %pad_add_fusion.place_ref, bf16[4,2,32,256]{3,2,1,0:T(8,128)(2,1)} %get-tuple-element.52.refs_0_, bf16[4,2,32,256]{3,2,1,0:T(8,128)(2,1)} %copy-done.12, ...), custom_call_target="tpu_custom_call" | custom-call | flops 2147483648 | bytes 8388608 | tf_op jit(solution)/shard_map/output_projection/pallas_call | solution.py:375
  169.1 1.7 collective-permute-start.17
  171.2 1.7 collective-permute-start.13
  173.2 1.7 collective-permute-start.1
  174.9 3.3 %collective-permute-done.1.refs_2_ = bf16[4,2,32,256]{3,2,1,0:T(8,128)(2,1)S(1)} collective-permute-done((bf16[4,2,32,256]{3,2,1,0:T(8,128)(2,1)S(1)}, bf16[4,2,32,256]{3,2,1,0:T(8,128)(2,1)S(1)}, u32[]{:S(2)}, u32[]{:S(2)}) %collective-permute-start.1) | collective-permute-done | bytes 131104 | tf_op jit(solution)/shard_map/ppermute | solution.py:268
  178.3 5.6 %collective-permute-done.2.refs_3_ = bf16[4,2,32,256]{3,2,1,0:T(8,128)(2,1)S(1)} collective-permute-done((bf16[4,2,32,256]{3,2,1,0:T(8,128)(2,1)S(1)}, bf16[4,2,32,256]{3,2,1,0:T(8,128)(2,1)S(1)}, u32[]{:S(2)}, u32[]{:S(2)}) %collective-permute-start.2) | collective-permute-done | bytes 131104 | tf_op jit(solution)/shard_map/ppermute | solution.py:268
  184.5 8.0 %output_projection.2 = (f32[2,32,4096]{2,1,0:T(8,128)}, f32[2,32,4096]{2,1,0:T(8,128)}, f32[2,32,4096]{2,1,0:T(8,128)}, f32[2,32,4096]{2,1,0:T(8,128)}) custom-call(s32[3]{0:T(128)} %pad_add_fusion.place_ref, bf16[4,2,32,256]{3,2,1,0:T(8,128)(2,1)} %get-tuple-element.47.refs_0_, bf16[4,2,32,256]{3,2,1,0:T(8,128)(2,1)} %copy-done.11, ...), custom_call_target="tpu_custom_call" | custom-call | flops 2147483648 | bytes 8388608 | tf_op jit(solution)/shard_map/output_projection/pallas_call | solution.py:375
  192.5 0.8 copy-done.6
  193.3 2.2 halve.7
  195.5 2.6 collective-permute-start.18
  198.1 0.8 copy-done.5
  198.9 2.2 halve.6
  201.4 16.5 %collective-permute-done.13.got_ref = bf16[2,32,4096]{2,1,0:T(8,128)(2,1)S(1)} collective-permute-done((bf16[2,32,4096]{2,1,0:T(8,128)(2,1)}, bf16[2,32,4096]{2,1,0:T(8,128)(2,1)S(1)}, u32[]{:S(2)}, u32[]{:S(2)}) %collective-permute-start.13) | collective-permute-done | bytes 524320 | tf_op jit(solution)/shard_map/ppermute | solution.py:268
  217.9 0.8 copy-done.4
  218.7 2.2 halve.5
  220.8 1.6 collective-permute-start.14
  222.5 6.3 %collective-permute-done.11.got_ref = bf16[2,32,4096]{2,1,0:T(8,128)(2,1)S(1)} collective-permute-done((bf16[2,32,4096]{2,1,0:T(8,128)(2,1)}, bf16[2,32,4096]{2,1,0:T(8,128)(2,1)S(1)}, u32[]{:S(2)}, u32[]{:S(2)}) %collective-permute-start.11) | collective-permute-done | bytes 524320 | tf_op jit(solution)/shard_map/ppermute | solution.py:268
  228.8 0.8 copy-done.3
  229.6 2.2 halve.4
  231.8 1.2 collective-permute-start.12
  234.3 2.2 finish.4
  236.6 0.7 copy-done.9
  237.3 2.2 finish.5
  239.6 7.7 %collective-permute-done.14.got_ref = bf16[1,32,4096]{2,1,0:T(8,128)(2,1)S(1)} collective-permute-done((bf16[1,32,4096]{2,1,0:T(8,128)(2,1)}, bf16[1,32,4096]{2,1,0:T(8,128)(2,1)S(1)}, u32[]{:S(2)}, u32[]{:S(2)}) %collective-permute-start.14) | collective-permute-done | bytes 262176 | tf_op jit(solution)/shard_map/ppermute | solution.py:268
  247.9 2.2 finish.6
  250.2 2.6 collective-permute-done.12.got_ref
  253.5 2.2 finish.7
  255.7 3.4 %shard_map.151 = bf16[128,4096]{1,0:T(8,128)(2,1)} custom-call(bf16[16,128,256]{2,1,0:T(8,128)(2,1)} %all-to-all-done.2.in_ref), custom_call_target="tpu_custom_call" | custom-call | bytes 2097152 | tf_op jit(solution)/shard_map/pallas_call | solution.py:485
  (73 shorter events, 9.1 us)
Async XLA Ops:
  5.5 30.3 %all-to-all-start = ((bf16[16,128,256]{2,1,0:T(8,128)(2,1)}), bf16[16,128,256]{2,1,0:T(8,128)(2,1)S(1)}, u32[]{:S(2)}, u32[]{:S(2)}) async-start(bf16[16,128,256]{2,1,0:T(8,128)(2,1)} %shard_map.148), calls=%async_computation | async-start | bytes 2097152 | tf_op jit(solution)/shard_map/all_to_all | solution.py:300
  17.0 25.7 %copy-start = (bf16[256,4096]{1,0:T(8,128)(2,1)S(1)}, bf16[256,4096]{1,0:T(8,128)(2,1)}, u32[]{:S(2)}) copy-start(bf16[256,4096]{1,0:T(8,128)(2,1)} %refs_4_.3) | copy-start | bytes 6291460
  35.8 6.9 %copy-start.2 = (bf16[16,128,256]{2,1,0:T(8,128)(2,1)}, bf16[16,128,256]{2,1,0:T(8,128)(2,1)S(1)}, u32[]{:S(2)}) copy-start(bf16[16,128,256]{2,1,0:T(8,128)(2,1)S(1)} %all-to-all-done.q_ref) | copy-start | bytes 3145732
  35.8 79.5 %all-to-all-start.1 = ((bf16[16,2,128,256]{3,2,1,0:T(8,128)(2,1)}), bf16[16,2,128,256]{3,2,1,0:T(8,128)(2,1)}, u32[]{:S(2)}, u32[]{:S(2)}) async-start(bf16[16,2,128,256]{3,2,1,0:T(8,128)(2,1)} %shard_map.149), calls=%async_computation.1 | async-start | bytes 4194304 | tf_op jit(solution)/shard_map/all_to_all | solution.py:286
  42.6 50.1 %copy-start.17 = (bf16[4096]{0:T(1024)(128)(2,1)S(1)}, bf16[4096]{0:T(1024)(128)(2,1)}, u32[]{:S(2)}) copy-start(bf16[4096]{0:T(1024)(128)(2,1)} %param.17) | copy-start | bytes 24580
  42.6 50.7 %copy-start.18 = (bf16[4096]{0:T(1024)(128)(2,1)S(1)}, bf16[4096]{0:T(1024)(128)(2,1)}, u32[]{:S(2)}) copy-start(bf16[4096]{0:T(1024)(128)(2,1)} %param.20) | copy-start | bytes 24580
  42.8 47.8 %collective-permute-start.4 = (bf16[128,4096]{1,0:T(8,128)(2,1)S(1)}, bf16[128,4096]{1,0:T(8,128)(2,1)S(1)}, u32[]{:S(2)}, u32[]{:S(2)}) collective-permute-start(bf16[128,4096]{1,0:T(8,128)(2,1)S(1)} %constant_dynamic-slice_fusion), channel_id=1, source_target_pairs={{0,2},{1,3},{2,0},{3,1},{4,6},{5,7},{6,4},{7,5},{8,10},{9,11},{10,... | collective-permute-start | bytes 3145736 | tf_op jit(solution)/shard_map/ppermute | solution.py:268
  90.6 15.9 %copy-start.1 = (bf16[128,4096]{1,0:T(8,128)(2,1)}, bf16[128,4096]{1,0:T(8,128)(2,1)S(1)}, u32[]{:S(2)}) copy-start(bf16[128,4096]{1,0:T(8,128)(2,1)S(1)} %collective-permute-done.4.refs_6_) | copy-start | bytes 3145732
  90.6 24.7 %collective-permute-start.5 = (bf16[128,4096]{1,0:T(8,128)(2,1)S(1)}, bf16[128,4096]{1,0:T(8,128)(2,1)}, u32[]{:S(2)}, u32[]{:S(2)}) collective-permute-start(bf16[128,4096]{1,0:T(8,128)(2,1)S(1)} %collective-permute-done.4.refs_6_), channel_id=1, source_target_pairs={{0,16},{16,0},{1,17},{17,1},{2,18},{18,2},{3,19},{19,3},{4,20},{20... | collective-permute-start | bytes 3145736 | tf_op jit(solution)/shard_map/ppermute | solution.py:309
  92.1 68.1 %collective-permute-start.3 = (bf16[256,4096]{1,0:T(8,128)(2,1)S(1)}, bf16[256,4096]{1,0:T(8,128)(2,1)}, u32[]{:S(2)}, u32[]{:S(2)}) collective-permute-start(bf16[256,4096]{1,0:T(8,128)(2,1)S(1)} %copy-done), channel_id=1, source_target_pairs={{0,1},{1,0},{2,3},{3,2},{4,5},{5,4},{6,7},{7,6},{8,9},{9,8},{10,11... | collective-permute-start | bytes 6291464 | tf_op jit(solution)/shard_map/ppermute | solution.py:268
  106.5 44.2 %collective-permute-start.6 = (bf16[128,4096]{1,0:T(8,128)(2,1)S(1)}, bf16[128,4096]{1,0:T(8,128)(2,1)}, u32[]{:S(2)}, u32[]{:S(2)}) collective-permute-start(bf16[128,4096]{1,0:T(8,128)(2,1)S(1)} %collective-permute-done.4.refs_6_), channel_id=1, source_target_pairs={{0,1},{1,0},{2,3},{3,2},{4,5},{5,4},{6,7},{7,6},{8,9},{9,8},{10,11... | collective-permute-start | bytes 3145736 | tf_op jit(solution)/shard_map/ppermute | solution.py:268
  115.3 45.4 %collective-permute-start.7 = (bf16[128,4096]{1,0:T(8,128)(2,1)}, bf16[128,4096]{1,0:T(8,128)(2,1)}, u32[]{:S(2)}, u32[]{:S(2)}) collective-permute-start(bf16[128,4096]{1,0:T(8,128)(2,1)} %collective-permute-done.5.refs_7_), channel_id=1, source_target_pairs={{0,1},{1,0},{2,3},{3,2},{4,5},{5,4},{6,7},{7,6},{8,9},{9,8},{10,11... | collective-permute-start | bytes 3145736 | tf_op jit(solution)/shard_map/ppermute | solution.py:268
  132.7 5.6 %copy-start.20 = (s32[512]{0:T(512)S(1)}, s32[512]{0:T(512)}, u32[]{:S(2)}) copy-start(s32[512]{0:T(512)} %param.18) | copy-start | bytes 6148
  132.7 123.0 %all-to-all-start.2 = ((bf16[16,128,256]{2,1,0:T(8,128)(2,1)}), bf16[16,128,256]{2,1,0:T(8,128)(2,1)}, u32[]{:S(2)}, u32[]{:S(2)}) async-start(bf16[16,128,256]{2,1,0:T(8,128)(2,1)} %prompt_attention.3), calls=%async_computation.2 | async-start | bytes 2097152 | tf_op jit(solution)/shard_map/all_to_all | solution.py:455
  148.7 12.1 %collective-permute-start.8 = (bf16[4,2,32,256]{3,2,1,0:T(8,128)(2,1)}, bf16[4,2,32,256]{3,2,1,0:T(8,128)(2,1)S(1)}, u32[]{:S(2)}, u32[]{:S(2)}) collective-permute-start(bf16[4,2,32,256]{3,2,1,0:T(8,128)(2,1)} %get-tuple-element.53), channel_id=1, source_target_pairs={{0,1},{1,0},{2,3},{3,2},{4,5},{5,4},{6,7},{7,6},{8,9},{9,8},{10,11... | collective-permute-start | bytes 393224 | tf_op jit(solution)/shard_map/ppermute | solution.py:268
  149.1 11.7 %collective-permute-start.9 = (bf16[4,2,32,256]{3,2,1,0:T(8,128)(2,1)}, bf16[4,2,32,256]{3,2,1,0:T(8,128)(2,1)S(1)}, u32[]{:S(2)}, u32[]{:S(2)}) collective-permute-start(bf16[4,2,32,256]{3,2,1,0:T(8,128)(2,1)} %get-tuple-element.54), channel_id=1, source_target_pairs={{0,2},{1,3},{2,0},{3,1},{4,6},{5,7},{6,4},{7,5},{8,10},{9,11},{10,... | collective-permute-start | bytes 393224 | tf_op jit(solution)/shard_map/ppermute | solution.py:268
  150.7 10.1 %collective-permute-start.10 = (bf16[4,2,32,256]{3,2,1,0:T(8,128)(2,1)}, bf16[4,2,32,256]{3,2,1,0:T(8,128)(2,1)S(1)}, u32[]{:S(2)}, u32[]{:S(2)}) collective-permute-start(bf16[4,2,32,256]{3,2,1,0:T(8,128)(2,1)} %get-tuple-element.55), channel_id=1, source_target_pairs={{0,3},{1,2},{2,1},{3,0},{4,7},{5,6},{6,5},{7,4},{8,11},{9,10},{10,... | collective-permute-start | bytes 393224 | tf_op jit(solution)/shard_map/ppermute | solution.py:268
  160.2 13.0 %collective-permute-start = (bf16[4,2,32,256]{3,2,1,0:T(8,128)(2,1)}, bf16[4,2,32,256]{3,2,1,0:T(8,128)(2,1)S(1)}, u32[]{:S(2)}, u32[]{:S(2)}) collective-permute-start(bf16[4,2,32,256]{3,2,1,0:T(8,128)(2,1)} %get-tuple-element.48), channel_id=1, source_target_pairs={{0,1},{1,0},{2,3},{3,2},{4,5},{5,4},{6,7},{7,6},{8,9},{9,8},{10,11... | collective-permute-start | bytes 393224 | tf_op jit(solution)/shard_map/ppermute | solution.py:268
  160.7 0.7 copy-start.12
  160.8 0.7 copy-start.13
  160.8 0.7 copy-start.14
  161.5 11.7 %copy-start.22 = (bf16[4,2,32,256]{3,2,1,0:T(8,128)(2,1)S(1)}, bf16[4,2,32,256]{3,2,1,0:T(8,128)(2,1)}, u32[]{:S(2)}) copy-start(bf16[4,2,32,256]{3,2,1,0:T(8,128)(2,1)} %get-tuple-element.49) | copy-start | bytes 393220
  161.5 16.8 %copy-start.21 = (bf16[4,2,32,256]{3,2,1,0:T(8,128)(2,1)S(1)}, bf16[4,2,32,256]{3,2,1,0:T(8,128)(2,1)}, u32[]{:S(2)}) copy-start(bf16[4,2,32,256]{3,2,1,0:T(8,128)(2,1)} %get-tuple-element.50) | copy-start | bytes 393220
  169.1 23.4 %collective-permute-start.17 = (bf16[2,32,4096]{2,1,0:T(8,128)(2,1)}, bf16[2,32,4096]{2,1,0:T(8,128)(2,1)S(1)}, u32[]{:S(2)}, u32[]{:S(2)}) collective-permute-start(bf16[2,32,4096]{2,1,0:T(8,128)(2,1)} %get-tuple-element.68), channel_id=1, source_target_pairs={{0,4},{1,5},{2,6},{3,7},{4,0},{5,1},{6,2},{7,3},{8,12},{9,13},{10,... | collective-permute-start | bytes 1572872 | tf_op jit(solution)/shard_map/ppermute | solution.py:268
  170.8 27.2 %collective-permute-start.15 = (bf16[2,32,4096]{2,1,0:T(8,128)(2,1)}, bf16[2,32,4096]{2,1,0:T(8,128)(2,1)S(1)}, u32[]{:S(2)}, u32[]{:S(2)}) collective-permute-start(bf16[2,32,4096]{2,1,0:T(8,128)(2,1)} %get-tuple-element.64), channel_id=1, source_target_pairs={{0,4},{1,5},{2,6},{3,7},{4,0},{5,1},{6,2},{7,3},{8,12},{9,13},{10,... | collective-permute-start | bytes 1572872 | tf_op jit(solution)/shard_map/ppermute | solution.py:268
  171.2 46.7 %collective-permute-start.13 = (bf16[2,32,4096]{2,1,0:T(8,128)(2,1)}, bf16[2,32,4096]{2,1,0:T(8,128)(2,1)S(1)}, u32[]{:S(2)}, u32[]{:S(2)}) collective-permute-start(bf16[2,32,4096]{2,1,0:T(8,128)(2,1)} %get-tuple-element.60), channel_id=1, source_target_pairs={{0,4},{1,5},{2,6},{3,7},{4,0},{5,1},{6,2},{7,3},{8,12},{9,13},{10,... | collective-permute-start | bytes 1572872 | tf_op jit(solution)/shard_map/ppermute | solution.py:268
  172.8 55.9 %collective-permute-start.11 = (bf16[2,32,4096]{2,1,0:T(8,128)(2,1)}, bf16[2,32,4096]{2,1,0:T(8,128)(2,1)S(1)}, u32[]{:S(2)}, u32[]{:S(2)}) collective-permute-start(bf16[2,32,4096]{2,1,0:T(8,128)(2,1)} %get-tuple-element.56), channel_id=1, source_target_pairs={{0,4},{1,5},{2,6},{3,7},{4,0},{5,1},{6,2},{7,3},{8,12},{9,13},{10,... | collective-permute-start | bytes 1572872 | tf_op jit(solution)/shard_map/ppermute | solution.py:268
  173.2 10.6 %copy-start.11 = (bf16[4,2,32,256]{3,2,1,0:T(8,128)(2,1)}, bf16[4,2,32,256]{3,2,1,0:T(8,128)(2,1)S(1)}, u32[]{:S(2)}) copy-start(bf16[4,2,32,256]{3,2,1,0:T(8,128)(2,1)S(1)} %collective-permute-done.refs_1_) | copy-start | bytes 393220
  173.2 5.0 %collective-permute-start.1 = (bf16[4,2,32,256]{3,2,1,0:T(8,128)(2,1)S(1)}, bf16[4,2,32,256]{3,2,1,0:T(8,128)(2,1)S(1)}, u32[]{:S(2)}, u32[]{:S(2)}) collective-permute-start(bf16[4,2,32,256]{3,2,1,0:T(8,128)(2,1)S(1)} %copy-done.22), channel_id=1, source_target_pairs={{0,2},{1,3},{2,0},{3,1},{4,6},{5,7},{6,4},{7,5},{8,10},{9,11},{10,... | collective-permute-start | bytes 393224 | tf_op jit(solution)/shard_map/ppermute | solution.py:268
  178.3 5.6 %copy-start.15 = (bf16[4,2,32,256]{3,2,1,0:T(8,128)(2,1)}, bf16[4,2,32,256]{3,2,1,0:T(8,128)(2,1)S(1)}, u32[]{:S(2)}) copy-start(bf16[4,2,32,256]{3,2,1,0:T(8,128)(2,1)S(1)} %collective-permute-done.1.refs_2_) | copy-start | bytes 393220
  178.3 5.6 %collective-permute-start.2 = (bf16[4,2,32,256]{3,2,1,0:T(8,128)(2,1)S(1)}, bf16[4,2,32,256]{3,2,1,0:T(8,128)(2,1)S(1)}, u32[]{:S(2)}, u32[]{:S(2)}) collective-permute-start(bf16[4,2,32,256]{3,2,1,0:T(8,128)(2,1)S(1)} %copy-done.21), channel_id=1, source_target_pairs={{0,3},{1,2},{2,1},{3,0},{4,7},{5,6},{6,5},{7,4},{8,11},{9,10},{10,... | collective-permute-start | bytes 393224 | tf_op jit(solution)/shard_map/ppermute | solution.py:268
  183.9 0.7 copy-start.16
  192.5 0.8 copy-start.6
  195.5 38.1 %collective-permute-start.18 = (bf16[1,32,4096]{2,1,0:T(8,128)(2,1)}, bf16[1,32,4096]{2,1,0:T(8,128)(2,1)S(1)}, u32[]{:S(2)}, u32[]{:S(2)}) collective-permute-start(bf16[1,32,4096]{2,1,0:T(8,128)(2,1)} %get-tuple-element.70), channel_id=1, source_target_pairs={{0,8},{1,9},{2,10},{3,11},{4,12},{5,13},{6,14},{7,15},{8,0},{9,1},... | collective-permute-start | bytes 786440 | tf_op jit(solution)/shard_map/ppermute | solution.py:268
  198.1 0.8 copy-start.5
  198.9 34.1 %copy-start.19 = (bf16[4096]{0:T(1024)(128)(2,1)S(1)}, bf16[4096]{0:T(1024)(128)(2,1)}, u32[]{:S(2)}) copy-start(bf16[4096]{0:T(1024)(128)(2,1)} %param.21) | copy-start | bytes 24580
  201.0 35.5 %collective-permute-start.16 = (bf16[1,32,4096]{2,1,0:T(8,128)(2,1)}, bf16[1,32,4096]{2,1,0:T(8,128)(2,1)S(1)}, u32[]{:S(2)}, u32[]{:S(2)}) collective-permute-start(bf16[1,32,4096]{2,1,0:T(8,128)(2,1)} %get-tuple-element.66), channel_id=1, source_target_pairs={{0,8},{1,9},{2,10},{3,11},{4,12},{5,13},{6,14},{7,15},{8,0},{9,1},... | collective-permute-start | bytes 786440 | tf_op jit(solution)/shard_map/ppermute | solution.py:268
  217.9 0.8 copy-start.4
  220.8 26.4 %collective-permute-start.14 = (bf16[1,32,4096]{2,1,0:T(8,128)(2,1)}, bf16[1,32,4096]{2,1,0:T(8,128)(2,1)S(1)}, u32[]{:S(2)}, u32[]{:S(2)}) collective-permute-start(bf16[1,32,4096]{2,1,0:T(8,128)(2,1)} %get-tuple-element.62), channel_id=1, source_target_pairs={{0,8},{1,9},{2,10},{3,11},{4,12},{5,13},{6,14},{7,15},{8,0},{9,1},... | collective-permute-start | bytes 786440 | tf_op jit(solution)/shard_map/ppermute | solution.py:268
  228.8 0.8 copy-start.3
  231.8 21.0 %collective-permute-start.12 = (bf16[1,32,4096]{2,1,0:T(8,128)(2,1)}, bf16[1,32,4096]{2,1,0:T(8,128)(2,1)S(1)}, u32[]{:S(2)}, u32[]{:S(2)}) collective-permute-start(bf16[1,32,4096]{2,1,0:T(8,128)(2,1)} %get-tuple-element.58), channel_id=1, source_target_pairs={{0,8},{1,9},{2,10},{3,11},{4,12},{5,13},{6,14},{7,15},{8,0},{9,1},... | collective-permute-start | bytes 786440 | tf_op jit(solution)/shard_map/ppermute | solution.py:268
  233.6 0.7 copy-start.7
  236.6 0.7 copy-start.9
  247.2 0.7 copy-start.10
  252.8 0.7 copy-start.8

commit v3 on v2

--- a/solution.py
+++ b/solution.py
@@ -178,19 +178,14 @@
                 out_refs[k][step, block] = scratch_ref[step, pl.ds(pl.multiple_of(at, per), per), :].astype(BF16)
 
 
-def prompt_body(chunk, group, q_ref, kv_ref, km_ref, vm_ref, *refs):
-    out_ref = refs[-1]
+def prompt_body(chunk, q_ref, kv_ref, km_ref, vm_ref, *refs):
     sources, rows, width = q_ref.shape
-
-    @pl.loop(0, sources // group)
-    def _(turn):
-        at = pl.ds(turn * group, group)
-        q = q_ref[at].reshape(group * rows, width)
-        s = scores(q, km_ref[...])
-        top = jnp.max(s, axis=-1, keepdims=True)
-        total = jnp.sum(jnp.exp2(s - top), axis=-1, keepdims=True)
-        state = over_prompt((top, total, total * vm_ref[0:1].astype(F32)), q, kv_ref, chunk)
-        out_ref[at] = (state[2] / state[1]).astype(BF16).reshape(group, rows, width)
+    q = q_ref[...].reshape(sources * rows, width)
+    s = scores(q, km_ref[...])
+    top = jnp.max(s, axis=-1, keepdims=True)
+    total = jnp.sum(jnp.exp2(s - top), axis=-1, keepdims=True)
+    state = over_prompt((top, total, total * vm_ref[0:1].astype(F32)), q, kv_ref, chunk)
+    refs[-1][...] = (state[2] / state[1]).astype(BF16).reshape(sources, rows, width)
 
 
 def output_body(lows, split, place_ref, *refs):
@@ -429,29 +424,30 @@
     prompt_context = None
     for head in range(heads):
         of_head = functools.partial(lambda head, *_: (0, head), head)
-        of_block = functools.partial(lambda head, *_: (0, 0, head), head)
         of_kv = functools.partial(lambda head, *_: (0, 0, 0, head), head)
-        earlier = [] if prompt_context is None else [prompt_context]
-        prompt_context = pl.pallas_call(
-            functools.partial(prompt_body, chunk, blocks_of_q),
-            grid=(1,),
-            in_specs=[
-                pl.BlockSpec((n, rows, HD), of_block),
-                pl.BlockSpec((n, 2, rows, HD), of_kv),
-                pl.BlockSpec((resp, HD), of_head),
-                pl.BlockSpec((16, HD), of_head),
-            ]
-            + [pl.BlockSpec(memory_space=pl.ANY)] * len(earlier),
-            out_specs=pl.BlockSpec((n, rows, HD), of_block),
-            out_shape=jax.ShapeDtypeStruct((n, rows, width), BF16),
-            name="prompt_attention",
-            input_output_aliases={4: 0} if earlier else {},
-            cost_estimate=pl.CostEstimate(
-                flops=4 * prompt_len * HD * (prompt_len + resp),
-                bytes_accessed=8 * prompt_len * HD,
-                transcendentals=prompt_len * (prompt_len + resp),
-            ),
-        )(q_heads, kv, km, vm, *earlier)
+        for turn in range(n // blocks_of_q):
+            of_block = functools.partial(lambda head, turn, *_: (turn, 0, head), head, turn)
+            earlier = [] if prompt_context is None else [prompt_context]
+            prompt_context = pl.pallas_call(
+                functools.partial(prompt_body, chunk),
+                grid=(1,),
+                in_specs=[
+                    pl.BlockSpec((blocks_of_q, rows, HD), of_block),
+                    pl.BlockSpec((n, 2, rows, HD), of_kv),
+                    pl.BlockSpec((resp, HD), of_head),
+                    pl.BlockSpec((16, HD), of_head),
+                ]
+                + [pl.BlockSpec(memory_space=pl.ANY)] * len(earlier),
+                out_specs=pl.BlockSpec((blocks_of_q, rows, HD), of_block),
+                out_shape=jax.ShapeDtypeStruct((n, rows, width), BF16),
+                name="prompt_attention",
+                input_output_aliases={4: 0} if earlier else {},
+                cost_estimate=pl.CostEstimate(
+                    flops=4 * blocks_of_q * rows * HD * (prompt_len + resp),
+                    bytes_accessed=4 * prompt_len * HD + 4 * blocks_of_q * rows * HD,
+                    transcendentals=blocks_of_q * rows * (prompt_len + resp),
+                ),
+            )(q_heads, kv, km, vm, *earlier)
     back = lax.all_to_all(prompt_context, "seq", 0, 0, tiled=True)
 
     results = []

time: 260 us -> 266 us (1.023)
  Pallas kernels: 91.2 us -> 95.2 us
  local copies, waits for them, and re-layouts: 10.2 us -> 13.8 us
    pallas_call x2 -> x4, Pallas kernels: 17.4 us -> 21.3 us  [per_device(): pl.pallas_call(functools.partial(prompt_body, chunk), grid=(1,), in_specs...]
  transfers between devices with their start and end apart: 22 -> 22, of which waited for: 9 -> 9; matrix products, arithmetic and copies ran while one was open for 2% -> 2% of each run, Pallas kernels for 32% -> 33%
where the time goes in v3:
time: 266 us; the launch traced here: 265 us
  waiting for transfers between devices  114 us (43%)
  Pallas kernels  95.2 us (36%)
  starting transfers between devices  37.6 us (14%)
  local copies, waits for them, and re-layouts  13.8 us (5%)
  other arithmetic  3.69 us (1%)
    ppermute x18, waiting for transfers between devices, swap(): return lax.ppermute(x, 'seq', [(i, i ^ bit) for i in range(n)])  86.5 us
    pallas_call x4, Pallas kernels, per_device(): pl.pallas_call(functools.partial(prompt_body, chunk), grid=(1,), in_specs...  21.3 us
    pallas_call x2, Pallas kernels, per_device(): pl.pallas_call(functools.partial(response_body, chunk, kept), grid_spec=p...  19 us
    all_to_all x1, waiting for transfers between devices, per_device(): q_heads = lax.all_to_all(q_send, 'seq', 0, 0, tiled=True)  18.8 us
    ppermute x18, starting transfers between devices, swap(): return lax.ppermute(x, 'seq', [(i, i ^ bit) for i in range(n)])  17 us
    pallas_call x2, Pallas kernels, per_device(): pl.pallas_call(functools.partial(output_body, lows, split), grid_spec=plt...  15.6 us
    pallas_call x1, Pallas kernels, per_device(): call(project_body, (resp // block,), [pl.BlockSpec((block, model), lambda...  10.5 us
    unnamed x46, local copies, waits for them, and re-layouts  9.86 us
  transfers between devices with their start and end apart: 22, of which 9 were waited for; matrix products, arithmetic and copies ran while one was open for 2% of the time, Pallas kernels for 33%

profile of v3, /device:TPU:0, one launch (start us, length us, event | category | flops | bytes accessed | tf_op | source)
XLA Modules:
  0.0 265.3 jit_solution(7464901255040425272)
XLA Ops:
  1.7 3.7 %shard_map.148 = bf16[16,128,256]{2,1,0:T(8,128)(2,1)} custom-call(bf16[128,4096]{1,0:T(8,128)(2,1)} %q_ref.1, f32[128,128]{1,0:T(8,128)} %get-tuple-element.85.cos_ref, f32[128,128]{1,0:T(8,128)} %get-tuple-element.86.sin_ref), custom_call_target="tpu_custom_call" | custom-call | flops 3145728 | bytes 2097152 | tf_op jit(solution)/shard_map/pallas_call | solution.py:282
  5.5 7.4 %all-to-all-start = ((bf16[16,128,256]{2,1,0:T(8,128)(2,1)}), bf16[16,128,256]{2,1,0:T(8,128)(2,1)S(1)}, u32[]{:S(2)}, u32[]{:S(2)}) async-start(bf16[16,128,256]{2,1,0:T(8,128)(2,1)} %shard_map.148), calls=%async_computation | async-start | bytes 2097152 | tf_op jit(solution)/shard_map/all_to_all | solution.py:295
  12.9 4.1 %shard_map.149 = bf16[16,2,128,256]{3,2,1,0:T(8,128)(2,1)} custom-call(bf16[128,4096]{1,0:T(8,128)(2,1)} %k_ref.1, bf16[128,4096]{1,0:T(8,128)(2,1)} %v_ref.1, f32[128,128]{1,0:T(8,128)} %get-tuple-element.85.cos_ref, f32[128,128]{1,0:T(8,128)} %get-tuple-element.86.sin_ref), custom_call_target="tpu_custom_call" | custom-call | flops 3145728 | bytes 4194304 | tf_op jit(solution)/shard_map/pallas_call | solution.py:267
  17.0 18.8 %all-to-all-done.q_ref = bf16[16,128,256]{2,1,0:T(8,128)(2,1)S(1)} async-done(((bf16[16,128,256]{2,1,0:T(8,128)(2,1)}), bf16[16,128,256]{2,1,0:T(8,128)(2,1)S(1)}, u32[]{:S(2)}, u32[]{:S(2)}) %all-to-all-start) | async-done | bytes 1048608 | tf_op jit(solution)/shard_map/all_to_all | solution.py:295
  35.8 6.8 %all-to-all-start.1 = ((bf16[16,2,128,256]{3,2,1,0:T(8,128)(2,1)}), bf16[16,2,128,256]{3,2,1,0:T(8,128)(2,1)S(1)}, u32[]{:S(2)}, u32[]{:S(2)}) async-start(bf16[16,2,128,256]{3,2,1,0:T(8,128)(2,1)} %shard_map.149), calls=%async_computation.1 | async-start | bytes 4194304 | tf_op jit(solution)/shard_map/all_to_all | solution.py:281
  42.6 1.3 constant_dynamic-slice_fusion
  43.9 2.0 collective-permute-start.4
  45.9 44.7 %collective-permute-done.4.refs_6_ = bf16[128,4096]{1,0:T(8,128)(2,1)S(1)} collective-permute-done((bf16[128,4096]{1,0:T(8,128)(2,1)S(1)}, bf16[128,4096]{1,0:T(8,128)(2,1)S(1)}, u32[]{:S(2)}, u32[]{:S(2)}) %collective-permute-start.4) | collective-permute-done | bytes 1048608 | tf_op jit(solution)/shard_map/ppermute | solution.py:263
  90.6 1.5 collective-permute-start.5
  94.0 1.0 fusion
  95.0 1.0 pad_maximum_fusion
  96.0 10.5 %shard_map.150 = (bf16[512,256]{1,0:T(8,128)(2,1)}, bf16[512,256]{1,0:T(8,128)(2,1)}, bf16[512,256]{1,0:T(8,128)(2,1)}, bf16[512,256]{1,0:T(8,128)(2,1)}, bf16[5...) custom-call(bf16[512,4096]{1,0:T(8,128)(2,1)} %embed_ref.9, bf16[1,4096]{1,0:T(2,128)(2,1)} %broadcast_in_dim.8.mask_ref, ...), custom_call_target="tpu_custom_call" | custom-call | flops 3221225472 | bytes 10485760 | tf_op jit(solution)/shard_map/pallas_call | solution.py:316
  107.0 8.3 %collective-permute-done.5.refs_7_ = bf16[128,4096]{1,0:T(8,128)(2,1)} collective-permute-done((bf16[128,4096]{1,0:T(8,128)(2,1)S(1)}, bf16[128,4096]{1,0:T(8,128)(2,1)}, u32[]{:S(2)}, u32[]{:S(2)}) %collective-permute-start.5) | collective-permute-done | bytes 1048608 | tf_op jit(solution)/shard_map/ppermute | solution.py:304
  115.3 1.4 copy-done
  116.7 5.3 %prompt_attention.4.refs_0_ = bf16[16,128,256]{2,1,0:T(8,128)(2,1)} custom-call(bf16[16,128,256]{2,1,0:T(8,128)(2,1)} %copy-done.1, bf16[16,2,128,256]{3,2,1,0:T(8,128)(2,1)} %copy-done, bf16[512,256]{1,0:T(8,128)(2,1)} %get-tuple-element.41.km_ref, bf16[16,256]{1,0:T(8,128)(2,1)} %get-tuple-element.42.vm_ref), custom_call_target="tpu_custom_call" | custom-call | flops 1342177280 | bytes 1572864 | tf_op jit(solution)/shard_map/prompt_attention/pallas_call | solution.py:431
  122.0 5.3 %prompt_attention.5.refs_0_ = bf16[16,128,256]{2,1,0:T(8,128)(2,1)} custom-call(bf16[16,128,256]{2,1,0:T(8,128)(2,1)} %copy-done.1, bf16[16,2,128,256]{3,2,1,0:T(8,128)(2,1)} %copy-done, bf16[512,256]{1,0:T(8,128)(2,1)} %get-tuple-element.41.km_ref, bf16[16,256]{1,0:T(8,128)(2,1)} %get-tuple-element.42.vm_ref, ...), custom_call_target="tpu_custom_call", output_to_operand_aliasing={{}: (4, {})} | custom-call | flops 1342177280 | bytes 1572864 | tf_op jit(solution)/shard_map/prompt_attention/pallas_call | solution.py:431
  127.2 5.3 %prompt_attention.6.refs_0_ = bf16[16,128,256]{2,1,0:T(8,128)(2,1)} custom-call(bf16[16,128,256]{2,1,0:T(8,128)(2,1)} %copy-done.1, bf16[16,2,128,256]{3,2,1,0:T(8,128)(2,1)} %copy-done, bf16[512,256]{1,0:T(8,128)(2,1)} %get-tuple-element.41.km_ref, bf16[16,256]{1,0:T(8,128)(2,1)} %get-tuple-element.42.vm_ref, ...), custom_call_target="tpu_custom_call", output_to_operand_aliasing={{}: (4, {})} | custom-call | flops 1342177280 | bytes 1572864 | tf_op jit(solution)/shard_map/prompt_attention/pallas_call | solution.py:431
  132.5 5.5 %prompt_attention.7 = bf16[16,128,256]{2,1,0:T(8,128)(2,1)} custom-call(bf16[16,128,256]{2,1,0:T(8,128)(2,1)} %copy-done.1, bf16[16,2,128,256]{3,2,1,0:T(8,128)(2,1)} %copy-done, bf16[512,256]{1,0:T(8,128)(2,1)} %get-tuple-element.41.km_ref, bf16[16,256]{1,0:T(8,128)(2,1)} %get-tuple-element.42.vm_ref, ...), custom_call_target="tpu_custom_call", output_to_operand_aliasing={{}: (4, {})} | custom-call | flops 1342177280 | bytes 1572864 | tf_op jit(solution)/shard_map/prompt_attention/pallas_call | solution.py:431
  138.0 4.9 %all-to-all-start.2 = ((bf16[16,128,256]{2,1,0:T(8,128)(2,1)}), bf16[16,128,256]{2,1,0:T(8,128)(2,1)S(1)}, u32[]{:S(2)}, u32[]{:S(2)}) async-start(bf16[16,128,256]{2,1,0:T(8,128)(2,1)} %prompt_attention.7), calls=%async_computation.2 | async-start | bytes 2097152 | tf_op jit(solution)/shard_map/all_to_all | solution.py:451
  143.5 0.8 broadcast_in_dim.11.commit_ref
  144.4 9.5 %response_attention.3 = (bf16[4,2,32,256]{3,2,1,0:T(8,128)(2,1)}, bf16[4,2,32,256]{3,2,1,0:T(8,128)(2,1)}, bf16[4,2,32,256]{3,2,1,0:T(8,128)(2,1)}, bf16[4,2,32,256]{3,2,1,0:T(8,128)(2,1)}) custom-call(s32[3]{0:T(128)} %pad_add_fusion.place_ref, bf16[16,2,128,256]{3,2,1,0:T(8,128)(2,1)} %copy-done, bf16[512,256]{1,0:T(8,128)(2,1)} %get-tuple-element.43.qe_ref, ...), custom_call_target="tpu_custom_call" | custom-call | flops 1610612736 | bytes 2097152 | tf_op jit(solution)/shard_map/response_attention/pallas_call | solution.py:350
  154.3 1.6 collective-permute-start.9
  156.0 9.5 %response_attention.2 = (bf16[4,2,32,256]{3,2,1,0:T(8,128)(2,1)}, bf16[4,2,32,256]{3,2,1,0:T(8,128)(2,1)}, bf16[4,2,32,256]{3,2,1,0:T(8,128)(2,1)}, bf16[4,2,32,256]{3,2,1,0:T(8,128)(2,1)}) custom-call(s32[3]{0:T(128)} %pad_add_fusion.place_ref, bf16[16,2,128,256]{3,2,1,0:T(8,128)(2,1)} %copy-done, bf16[512,256]{1,0:T(8,128)(2,1)} %get-tuple-element.43.qe_ref, ...), custom_call_target="tpu_custom_call" | custom-call | flops 1610612736 | bytes 2097152 | tf_op jit(solution)/shard_map/response_attention/pallas_call | solution.py:350
  166.8 7.6 %output_projection.3 = (bf16[2,32,4096]{2,1,0:T(8,128)(2,1)}, bf16[2,32,4096]{2,1,0:T(8,128)(2,1)}, bf16[2,32,4096]{2,1,0:T(8,128)(2,1)}, bf16[2,32,4096]{2,1,0:T(8,128)(2,1)}) custom-call(s32[3]{0:T(128)} %pad_add_fusion.place_ref, bf16[4,2,32,256]{3,2,1,0:T(8,128)(2,1)} %get-tuple-element.52.refs_0_, bf16[4,2,32,256]{3,2,1,0:T(8,128)(2,1)} %copy-done.13, ...), custom_call_target="tpu_custom_call" | custom-call | flops 2147483648 | bytes 8388608 | tf_op jit(solution)/shard_map/output_projection/pallas_call | solution.py:370
  174.4 1.7 collective-permute-start.17
  176.5 1.6 collective-permute-start.13
  178.5 1.7 collective-permute-start.1
  180.2 3.3 %collective-permute-done.1.refs_2_ = bf16[4,2,32,256]{3,2,1,0:T(8,128)(2,1)S(1)} collective-permute-done((bf16[4,2,32,256]{3,2,1,0:T(8,128)(2,1)S(1)}, bf16[4,2,32,256]{3,2,1,0:T(8,128)(2,1)S(1)}, u32[]{:S(2)}, u32[]{:S(2)}) %collective-permute-start.1) | collective-permute-done | bytes 131104 | tf_op jit(solution)/shard_map/ppermute | solution.py:263
  183.5 5.8 %collective-permute-done.2.refs_3_ = bf16[4,2,32,256]{3,2,1,0:T(8,128)(2,1)S(1)} collective-permute-done((bf16[4,2,32,256]{3,2,1,0:T(8,128)(2,1)}, bf16[4,2,32,256]{3,2,1,0:T(8,128)(2,1)S(1)}, u32[]{:S(2)}, u32[]{:S(2)}) %collective-permute-start.2) | collective-permute-done | bytes 131104 | tf_op jit(solution)/shard_map/ppermute | solution.py:263
  190.0 8.0 %output_projection.2 = (f32[2,32,4096]{2,1,0:T(8,128)}, f32[2,32,4096]{2,1,0:T(8,128)}, f32[2,32,4096]{2,1,0:T(8,128)}, f32[2,32,4096]{2,1,0:T(8,128)}) custom-call(s32[3]{0:T(128)} %pad_add_fusion.place_ref, bf16[4,2,32,256]{3,2,1,0:T(8,128)(2,1)} %get-tuple-element.47.refs_0_, bf16[4,2,32,256]{3,2,1,0:T(8,128)(2,1)} %copy-done.12, ...), custom_call_target="tpu_custom_call" | custom-call | flops 2147483648 | bytes 8388608 | tf_op jit(solution)/shard_map/output_projection/pallas_call | solution.py:370
  198.8 2.2 halve.7
  201.0 2.5 collective-permute-start.18
  203.5 0.8 copy-done.6
  204.3 2.2 halve.6
  206.9 16.2 %collective-permute-done.13.got_ref = bf16[2,32,4096]{2,1,0:T(8,128)(2,1)S(1)} collective-permute-done((bf16[2,32,4096]{2,1,0:T(8,128)(2,1)}, bf16[2,32,4096]{2,1,0:T(8,128)(2,1)S(1)}, u32[]{:S(2)}, u32[]{:S(2)}) %collective-permute-start.13) | collective-permute-done | bytes 524320 | tf_op jit(solution)/shard_map/ppermute | solution.py:263
  223.9 2.2 halve.5
  226.1 1.6 collective-permute-start.14
  227.8 6.1 %collective-permute-done.11.got_ref = bf16[2,32,4096]{2,1,0:T(8,128)(2,1)S(1)} collective-permute-done((bf16[2,32,4096]{2,1,0:T(8,128)(2,1)}, bf16[2,32,4096]{2,1,0:T(8,128)(2,1)S(1)}, u32[]{:S(2)}, u32[]{:S(2)}) %collective-permute-start.11) | collective-permute-done | bytes 524320 | tf_op jit(solution)/shard_map/ppermute | solution.py:263
  234.7 2.1 halve.4
  236.9 1.4 collective-permute-start.12
  239.5 2.2 finish.4
  242.5 2.2 finish.5
  244.7 7.7 %collective-permute-done.14.got_ref = bf16[1,32,4096]{2,1,0:T(8,128)(2,1)S(1)} collective-permute-done((bf16[1,32,4096]{2,1,0:T(8,128)(2,1)}, bf16[1,32,4096]{2,1,0:T(8,128)(2,1)S(1)}, u32[]{:S(2)}, u32[]{:S(2)}) %collective-permute-start.14) | collective-permute-done | bytes 262176 | tf_op jit(solution)/shard_map/ppermute | solution.py:263
  253.2 2.2 finish.6
  255.5 2.5 collective-permute-done.12.got_ref
  258.7 2.2 finish.7
  260.9 1.0 copy-done.3
  262.0 3.4 %shard_map.151 = bf16[128,4096]{1,0:T(8,128)(2,1)} custom-call(bf16[16,128,256]{2,1,0:T(8,128)(2,1)} %copy-done.3), custom_call_target="tpu_custom_call" | custom-call | bytes 2097152 | tf_op jit(solution)/shard_map/pallas_call | solution.py:481
  (75 shorter events, 13.0 us)
Async XLA Ops:
  5.5 30.3 %all-to-all-start = ((bf16[16,128,256]{2,1,0:T(8,128)(2,1)}), bf16[16,128,256]{2,1,0:T(8,128)(2,1)S(1)}, u32[]{:S(2)}, u32[]{:S(2)}) async-start(bf16[16,128,256]{2,1,0:T(8,128)(2,1)} %shard_map.148), calls=%async_computation | async-start | bytes 2097152 | tf_op jit(solution)/shard_map/all_to_all | solution.py:295
  35.8 6.8 %copy-start.1 = (bf16[16,128,256]{2,1,0:T(8,128)(2,1)}, bf16[16,128,256]{2,1,0:T(8,128)(2,1)S(1)}, u32[]{:S(2)}) copy-start(bf16[16,128,256]{2,1,0:T(8,128)(2,1)S(1)} %all-to-all-done.q_ref) | copy-start | bytes 3145732
  35.8 79.5 %all-to-all-start.1 = ((bf16[16,2,128,256]{3,2,1,0:T(8,128)(2,1)}), bf16[16,2,128,256]{3,2,1,0:T(8,128)(2,1)S(1)}, u32[]{:S(2)}, u32[]{:S(2)}) async-start(bf16[16,2,128,256]{3,2,1,0:T(8,128)(2,1)} %shard_map.149), calls=%async_computation.1 | async-start | bytes 4194304 | tf_op jit(solution)/shard_map/all_to_all | solution.py:281
  42.6 50.2 %copy-start.18 = (bf16[4096]{0:T(1024)(128)(2,1)S(1)}, bf16[4096]{0:T(1024)(128)(2,1)}, u32[]{:S(2)}) copy-start(bf16[4096]{0:T(1024)(128)(2,1)} %param.17) | copy-start | bytes 24580
  42.6 50.8 %copy-start.19 = (bf16[4096]{0:T(1024)(128)(2,1)S(1)}, bf16[4096]{0:T(1024)(128)(2,1)}, u32[]{:S(2)}) copy-start(bf16[4096]{0:T(1024)(128)(2,1)} %param.20) | copy-start | bytes 24580
  43.9 46.7 %collective-permute-start.4 = (bf16[128,4096]{1,0:T(8,128)(2,1)S(1)}, bf16[128,4096]{1,0:T(8,128)(2,1)S(1)}, u32[]{:S(2)}, u32[]{:S(2)}) collective-permute-start(bf16[128,4096]{1,0:T(8,128)(2,1)S(1)} %constant_dynamic-slice_fusion), channel_id=1, source_target_pairs={{0,2},{1,3},{2,0},{3,1},{4,6},{5,7},{6,4},{7,5},{8,10},{9,11},{10,... | collective-permute-start | bytes 3145736 | tf_op jit(solution)/shard_map/ppermute | solution.py:263
  90.6 15.9 %copy-start.2 = (bf16[128,4096]{1,0:T(8,128)(2,1)}, bf16[128,4096]{1,0:T(8,128)(2,1)S(1)}, u32[]{:S(2)}) copy-start(bf16[128,4096]{1,0:T(8,128)(2,1)S(1)} %collective-permute-done.4.refs_6_) | copy-start | bytes 3145732
  90.6 24.7 %collective-permute-start.5 = (bf16[128,4096]{1,0:T(8,128)(2,1)S(1)}, bf16[128,4096]{1,0:T(8,128)(2,1)}, u32[]{:S(2)}, u32[]{:S(2)}) collective-permute-start(bf16[128,4096]{1,0:T(8,128)(2,1)S(1)} %collective-permute-done.4.refs_6_), channel_id=1, source_target_pairs={{0,16},{16,0},{1,17},{17,1},{2,18},{18,2},{3,19},{19,3},{4,20},{20... | collective-permute-start | bytes 3145736 | tf_op jit(solution)/shard_map/ppermute | solution.py:304
  92.1 73.3 %collective-permute-start.3 = (bf16[256,4096]{1,0:T(8,128)(2,1)}, bf16[256,4096]{1,0:T(8,128)(2,1)}, u32[]{:S(2)}, u32[]{:S(2)}) collective-permute-start(bf16[256,4096]{1,0:T(8,128)(2,1)} %refs_4_.3), channel_id=1, source_target_pairs={{0,1},{1,0},{2,3},{3,2},{4,5},{5,4},{6,7},{7,6},{8,9},{9,8},{10,11... | collective-permute-start | bytes 6291464 | tf_op jit(solution)/shard_map/ppermute | solution.py:263
  106.5 49.5 %collective-permute-start.6 = (bf16[128,4096]{1,0:T(8,128)(2,1)S(1)}, bf16[128,4096]{1,0:T(8,128)(2,1)}, u32[]{:S(2)}, u32[]{:S(2)}) collective-permute-start(bf16[128,4096]{1,0:T(8,128)(2,1)S(1)} %collective-permute-done.4.refs_6_), channel_id=1, source_target_pairs={{0,1},{1,0},{2,3},{3,2},{4,5},{5,4},{6,7},{7,6},{8,9},{9,8},{10,11... | collective-permute-start | bytes 3145736 | tf_op jit(solution)/shard_map/ppermute | solution.py:263
  115.3 50.7 %collective-permute-start.7 = (bf16[128,4096]{1,0:T(8,128)(2,1)}, bf16[128,4096]{1,0:T(8,128)(2,1)}, u32[]{:S(2)}, u32[]{:S(2)}) collective-permute-start(bf16[128,4096]{1,0:T(8,128)(2,1)} %collective-permute-done.5.refs_7_), channel_id=1, source_target_pairs={{0,1},{1,0},{2,3},{3,2},{4,5},{5,4},{6,7},{7,6},{8,9},{9,8},{10,11... | collective-permute-start | bytes 3145736 | tf_op jit(solution)/shard_map/ppermute | solution.py:263
  115.3 1.4 copy-start
  138.0 5.5 %copy-start.21 = (s32[512]{0:T(512)S(1)}, s32[512]{0:T(512)}, u32[]{:S(2)}) copy-start(s32[512]{0:T(512)} %param.18) | copy-start | bytes 6148
  138.0 122.9 %all-to-all-start.2 = ((bf16[16,128,256]{2,1,0:T(8,128)(2,1)}), bf16[16,128,256]{2,1,0:T(8,128)(2,1)S(1)}, u32[]{:S(2)}, u32[]{:S(2)}) async-start(bf16[16,128,256]{2,1,0:T(8,128)(2,1)} %prompt_attention.7), calls=%async_computation.2 | async-start | bytes 2097152 | tf_op jit(solution)/shard_map/all_to_all | solution.py:451
  153.9 12.2 %collective-permute-start.8 = (bf16[4,2,32,256]{3,2,1,0:T(8,128)(2,1)}, bf16[4,2,32,256]{3,2,1,0:T(8,128)(2,1)S(1)}, u32[]{:S(2)}, u32[]{:S(2)}) collective-permute-start(bf16[4,2,32,256]{3,2,1,0:T(8,128)(2,1)} %get-tuple-element.53), channel_id=1, source_target_pairs={{0,1},{1,0},{2,3},{3,2},{4,5},{5,4},{6,7},{7,6},{8,9},{9,8},{10,11... | collective-permute-start | bytes 393224 | tf_op jit(solution)/shard_map/ppermute | solution.py:263
  154.3 11.7 %collective-permute-start.9 = (bf16[4,2,32,256]{3,2,1,0:T(8,128)(2,1)}, bf16[4,2,32,256]{3,2,1,0:T(8,128)(2,1)S(1)}, u32[]{:S(2)}, u32[]{:S(2)}) collective-permute-start(bf16[4,2,32,256]{3,2,1,0:T(8,128)(2,1)} %get-tuple-element.54), channel_id=1, source_target_pairs={{0,2},{1,3},{2,0},{3,1},{4,6},{5,7},{6,4},{7,5},{8,10},{9,11},{10,... | collective-permute-start | bytes 393224 | tf_op jit(solution)/shard_map/ppermute | solution.py:263
  156.0 10.1 %collective-permute-start.10 = (bf16[4,2,32,256]{3,2,1,0:T(8,128)(2,1)}, bf16[4,2,32,256]{3,2,1,0:T(8,128)(2,1)S(1)}, u32[]{:S(2)}, u32[]{:S(2)}) collective-permute-start(bf16[4,2,32,256]{3,2,1,0:T(8,128)(2,1)} %get-tuple-element.55), channel_id=1, source_target_pairs={{0,3},{1,2},{2,1},{3,0},{4,7},{5,6},{6,5},{7,4},{8,11},{9,10},{10,... | collective-permute-start | bytes 393224 | tf_op jit(solution)/shard_map/ppermute | solution.py:263
  165.4 13.1 %collective-permute-start = (bf16[4,2,32,256]{3,2,1,0:T(8,128)(2,1)}, bf16[4,2,32,256]{3,2,1,0:T(8,128)(2,1)S(1)}, u32[]{:S(2)}, u32[]{:S(2)}) collective-permute-start(bf16[4,2,32,256]{3,2,1,0:T(8,128)(2,1)} %get-tuple-element.48), channel_id=1, source_target_pairs={{0,1},{1,0},{2,3},{3,2},{4,5},{5,4},{6,7},{7,6},{8,9},{9,8},{10,11... | collective-permute-start | bytes 393224 | tf_op jit(solution)/shard_map/ppermute | solution.py:263
  166.0 0.7 copy-start.13
  166.0 0.7 copy-start.14
  166.1 0.8 copy-start.15
  166.8 11.7 %copy-start.22 = (bf16[4,2,32,256]{3,2,1,0:T(8,128)(2,1)S(1)}, bf16[4,2,32,256]{3,2,1,0:T(8,128)(2,1)}, u32[]{:S(2)}) copy-start(bf16[4,2,32,256]{3,2,1,0:T(8,128)(2,1)} %get-tuple-element.49) | copy-start | bytes 393220
  174.4 23.6 %collective-permute-start.17 = (bf16[2,32,4096]{2,1,0:T(8,128)(2,1)}, bf16[2,32,4096]{2,1,0:T(8,128)(2,1)S(1)}, u32[]{:S(2)}, u32[]{:S(2)}) collective-permute-start(bf16[2,32,4096]{2,1,0:T(8,128)(2,1)} %get-tuple-element.68), channel_id=1, source_target_pairs={{0,4},{1,5},{2,6},{3,7},{4,0},{5,1},{6,2},{7,3},{8,12},{9,13},{10,... | collective-permute-start | bytes 1572872 | tf_op jit(solution)/shard_map/ppermute | solution.py:263
  176.1 27.4 %collective-permute-start.15 = (bf16[2,32,4096]{2,1,0:T(8,128)(2,1)}, bf16[2,32,4096]{2,1,0:T(8,128)(2,1)S(1)}, u32[]{:S(2)}, u32[]{:S(2)}) collective-permute-start(bf16[2,32,4096]{2,1,0:T(8,128)(2,1)} %get-tuple-element.64), channel_id=1, source_target_pairs={{0,4},{1,5},{2,6},{3,7},{4,0},{5,1},{6,2},{7,3},{8,12},{9,13},{10,... | collective-permute-start | bytes 1572872 | tf_op jit(solution)/shard_map/ppermute | solution.py:263
  176.5 46.7 %collective-permute-start.13 = (bf16[2,32,4096]{2,1,0:T(8,128)(2,1)}, bf16[2,32,4096]{2,1,0:T(8,128)(2,1)S(1)}, u32[]{:S(2)}, u32[]{:S(2)}) collective-permute-start(bf16[2,32,4096]{2,1,0:T(8,128)(2,1)} %get-tuple-element.60), channel_id=1, source_target_pairs={{0,4},{1,5},{2,6},{3,7},{4,0},{5,1},{6,2},{7,3},{8,12},{9,13},{10,... | collective-permute-start | bytes 1572872 | tf_op jit(solution)/shard_map/ppermute | solution.py:263
  178.1 55.8 %collective-permute-start.11 = (bf16[2,32,4096]{2,1,0:T(8,128)(2,1)}, bf16[2,32,4096]{2,1,0:T(8,128)(2,1)S(1)}, u32[]{:S(2)}, u32[]{:S(2)}) collective-permute-start(bf16[2,32,4096]{2,1,0:T(8,128)(2,1)} %get-tuple-element.56), channel_id=1, source_target_pairs={{0,4},{1,5},{2,6},{3,7},{4,0},{5,1},{6,2},{7,3},{8,12},{9,13},{10,... | collective-permute-start | bytes 1572872 | tf_op jit(solution)/shard_map/ppermute | solution.py:263
  178.5 10.9 %copy-start.12 = (bf16[4,2,32,256]{3,2,1,0:T(8,128)(2,1)}, bf16[4,2,32,256]{3,2,1,0:T(8,128)(2,1)S(1)}, u32[]{:S(2)}) copy-start(bf16[4,2,32,256]{3,2,1,0:T(8,128)(2,1)S(1)} %collective-permute-done.refs_1_) | copy-start | bytes 393220
  178.5 5.0 %collective-permute-start.1 = (bf16[4,2,32,256]{3,2,1,0:T(8,128)(2,1)S(1)}, bf16[4,2,32,256]{3,2,1,0:T(8,128)(2,1)S(1)}, u32[]{:S(2)}, u32[]{:S(2)}) collective-permute-start(bf16[4,2,32,256]{3,2,1,0:T(8,128)(2,1)S(1)} %copy-done.22), channel_id=1, source_target_pairs={{0,2},{1,3},{2,0},{3,1},{4,6},{5,7},{6,4},{7,5},{8,10},{9,11},{10,... | collective-permute-start | bytes 393224 | tf_op jit(solution)/shard_map/ppermute | solution.py:263
  183.5 5.8 %copy-start.16 = (bf16[4,2,32,256]{3,2,1,0:T(8,128)(2,1)}, bf16[4,2,32,256]{3,2,1,0:T(8,128)(2,1)S(1)}, u32[]{:S(2)}) copy-start(bf16[4,2,32,256]{3,2,1,0:T(8,128)(2,1)S(1)} %collective-permute-done.1.refs_2_) | copy-start | bytes 393220
  183.5 5.8 %collective-permute-start.2 = (bf16[4,2,32,256]{3,2,1,0:T(8,128)(2,1)}, bf16[4,2,32,256]{3,2,1,0:T(8,128)(2,1)S(1)}, u32[]{:S(2)}, u32[]{:S(2)}) collective-permute-start(bf16[4,2,32,256]{3,2,1,0:T(8,128)(2,1)} %get-tuple-element.50), channel_id=1, source_target_pairs={{0,3},{1,2},{2,1},{3,0},{4,7},{5,6},{6,5},{7,4},{8,11},{9,10},{10,... | collective-permute-start | bytes 393224 | tf_op jit(solution)/shard_map/ppermute | solution.py:263
  189.4 0.7 copy-start.17
  198.0 0.8 copy-start.7
  201.0 37.8 %collective-permute-start.18 = (bf16[1,32,4096]{2,1,0:T(8,128)(2,1)}, bf16[1,32,4096]{2,1,0:T(8,128)(2,1)S(1)}, u32[]{:S(2)}, u32[]{:S(2)}) collective-permute-start(bf16[1,32,4096]{2,1,0:T(8,128)(2,1)} %get-tuple-element.70), channel_id=1, source_target_pairs={{0,8},{1,9},{2,10},{3,11},{4,12},{5,13},{6,14},{7,15},{8,0},{9,1},... | collective-permute-start | bytes 786440 | tf_op jit(solution)/shard_map/ppermute | solution.py:263
  203.5 0.8 copy-start.6
  204.3 33.9 %copy-start.20 = (bf16[4096]{0:T(1024)(128)(2,1)S(1)}, bf16[4096]{0:T(1024)(128)(2,1)}, u32[]{:S(2)}) copy-start(bf16[4096]{0:T(1024)(128)(2,1)} %param.21) | copy-start | bytes 24580
  206.5 35.3 %collective-permute-start.16 = (bf16[1,32,4096]{2,1,0:T(8,128)(2,1)}, bf16[1,32,4096]{2,1,0:T(8,128)(2,1)S(1)}, u32[]{:S(2)}, u32[]{:S(2)}) collective-permute-start(bf16[1,32,4096]{2,1,0:T(8,128)(2,1)} %get-tuple-element.66), channel_id=1, source_target_pairs={{0,8},{1,9},{2,10},{3,11},{4,12},{5,13},{6,14},{7,15},{8,0},{9,1},... | collective-permute-start | bytes 786440 | tf_op jit(solution)/shard_map/ppermute | solution.py:263
  223.2 0.8 copy-start.5
  226.1 26.3 %collective-permute-start.14 = (bf16[1,32,4096]{2,1,0:T(8,128)(2,1)}, bf16[1,32,4096]{2,1,0:T(8,128)(2,1)S(1)}, u32[]{:S(2)}, u32[]{:S(2)}) collective-permute-start(bf16[1,32,4096]{2,1,0:T(8,128)(2,1)} %get-tuple-element.62), channel_id=1, source_target_pairs={{0,8},{1,9},{2,10},{3,11},{4,12},{5,13},{6,14},{7,15},{8,0},{9,1},... | collective-permute-start | bytes 786440 | tf_op jit(solution)/shard_map/ppermute | solution.py:263
  233.9 0.8 copy-start.4
  236.9 21.1 %collective-permute-start.12 = (bf16[1,32,4096]{2,1,0:T(8,128)(2,1)}, bf16[1,32,4096]{2,1,0:T(8,128)(2,1)S(1)}, u32[]{:S(2)}, u32[]{:S(2)}) collective-permute-start(bf16[1,32,4096]{2,1,0:T(8,128)(2,1)} %get-tuple-element.58), channel_id=1, source_target_pairs={{0,8},{1,9},{2,10},{3,11},{4,12},{5,13},{6,14},{7,15},{8,0},{9,1},... | collective-permute-start | bytes 786440 | tf_op jit(solution)/shard_map/ppermute | solution.py:263
  238.8 0.7 copy-start.8
  241.8 0.7 copy-start.10
  252.5 0.7 copy-start.11
  258.0 0.7 copy-start.9
  260.9 1.0 copy-start.3

commit v4 on v3

--- a/solution.py
+++ b/solution.py
@@ -17,6 +17,9 @@
 
 F32 = jnp.float32
 BF16 = jnp.bfloat16
+
+
+GRANT = pltpu.CompilerParams(vmem_limit_bytes=28 << 20)
 
 
 def call(body, grid, in_specs, out_specs, out_shape, scratch=(), flops=0, moved=0, exps=0):
@@ -27,6 +30,7 @@
         out_specs=out_specs,
         out_shape=out_shape,
         scratch_shapes=list(scratch),
+        compiler_params=GRANT,
         cost_estimate=pl.CostEstimate(flops=flops, bytes_accessed=moved, transcendentals=exps),
     )
 
@@ -193,7 +197,9 @@
     outs = refs[-STEPS:]
     steps, blocks, per, width = x_refs[0].shape
     far = lows // 2 if split else lows
-    w = jnp.concatenate([ref[...] for ref in refs[:-STEPS]], 0)
+    columns = outs[0].shape[2]
+    here = pl.ds(pl.multiple_of(pl.program_id(0) * columns, columns), columns)
+    w = jnp.concatenate([ref[:, here] for ref in refs[:-STEPS]], 0)
     xs = []
     for k, x_ref in enumerate(x_refs):
         x = x_ref[...].reshape(steps * blocks * per, width)
@@ -358,6 +364,7 @@
             ),
             out_shape=[jax.ShapeDtypeStruct((STEPS, blocks, per, width), BF16)] * lows,
             name="response_attention",
+            compiler_params=GRANT,
             cost_estimate=pl.CostEstimate(
                 flops=2 * resp * width * (2 * prompt_len + STEPS * resp),
                 bytes_accessed=4 * prompt_len * width,
@@ -373,11 +380,12 @@
                 num_scalar_prefetch=1,
                 grid=(model // columns,),
                 in_specs=[whole((STEPS, blocks, per, width))] * lows
-                + [pl.BlockSpec((w.shape[0], columns), lambda j, *_: (0, j)) for w in weights],
+                + [pl.BlockSpec(memory_space=pltpu.VMEM)] * len(weights),
                 out_specs=[pl.BlockSpec((blocks, per, columns), lambda j, *_: (0, 0, j))] * STEPS,
             ),
             out_shape=[jax.ShapeDtypeStruct((blocks, per, model), F32 if kept else BF16)] * STEPS,
             name="output_projection",
+            compiler_params=GRANT,
             cost_estimate=pl.CostEstimate(
                 flops=STEPS * resp * model * width, bytes_accessed=2 * lows * width * model, transcendentals=0
             ),
@@ -396,7 +404,7 @@
         bit = ((high >> level) & 1).astype(jnp.int32).reshape(1)
         sends, kept = [], []
         for step in range(STEPS):
-            columns = min(model, 2048)
+            columns = model
             get = pl.BlockSpec((count, per, columns), lambda j, *_: (0, 0, j))
             put = pl.BlockSpec((count // 2, per, columns), lambda j, *_: (0, 0, j))
             one, two = pl.pallas_call(
@@ -412,6 +420,7 @@
                     jax.ShapeDtypeStruct((count // 2, per, model), F32),
                 ],
                 name="halve",
+                compiler_params=GRANT,
                 cost_estimate=pl.CostEstimate(
                     flops=count * per * model, bytes_accessed=9 * count * per * model, transcendentals=0
                 ),
@@ -441,6 +450,7 @@
                 out_specs=pl.BlockSpec((blocks_of_q, rows, HD), of_block),
                 out_shape=jax.ShapeDtypeStruct((n, rows, width), BF16),
                 name="prompt_attention",
+                compiler_params=GRANT,
                 input_output_aliases={4: 0} if earlier else {},
                 cost_estimate=pl.CostEstimate(
                     flops=4 * blocks_of_q * rows * HD * (prompt_len + resp),
@@ -470,6 +480,7 @@
             ),
             out_shape=[jax.ShapeDtypeStruct((STEPS, per, model), BF16)] * 2,
             name="finish",
+            compiler_params=GRANT,
             input_output_aliases={7: 0, 8: 1} if results else {},
             cost_estimate=pl.CostEstimate(flops=8 * per * model, bytes_accessed=12 * per * model, transcendentals=0),
         )(

time: 266 us -> 255 us (0.959)
  Pallas kernels: 95.2 us -> 64.5 us
  waiting for transfers between devices: 114 us -> 126 us
  local copies, waits for them, and re-layouts: 13.8 us -> 22.2 us
    ppermute x18, waiting for transfers between devices: 86.5 us -> 98.4 us  [swap(): return lax.ppermute(x, 'seq', [(i, i ^ bit) for i in range(n)])]
    unnamed x46 -> x76, local copies, waits for them, and re-layouts: 9.86 us -> 20.6 us
    pallas_call x4, Pallas kernels: 21.3 us -> 14.7 us  [per_device(): pl.pallas_call(functools.partial(prompt_body, chunk), grid=(1,), in_specs...]
    pallas_call x4, Pallas kernels: 8.98 us -> 4.03 us  [per_device(): pl.pallas_call(functools.partial(finish_body, step), grid_spec=pltpu.Pref...]
    pallas_call x1, Pallas kernels: 10.5 us -> 6.59 us  [per_device(): call(project_body, (resp // block,), [pl.BlockSpec((block, model), lambda...]
    pallas_call x4, Pallas kernels: 8.72 us -> 4.87 us  [per_device(): pl.pallas_call(halve_body, grid_spec=pltpu.PrefetchScalarGridSpec(num_sca...]
    pallas_call x1, Pallas kernels: 4.08 us -> 0.94 us  [per_device(): call(pack_kv_body, (n // dests,), [pl.BlockSpec((rows, dests * width), la...]
    pallas_call x2, Pallas kernels: 19 us -> 16 us  [per_device(): pl.pallas_call(functools.partial(response_body, chunk, kept), grid_spec=p...]
  transfers between devices with their start and end apart: 22 -> 22, of which waited for: 9 -> 9; matrix products, arithmetic and copies ran while one was open for 2% -> 1% of each run, Pallas kernels for 33% -> 24%
where the time goes in v4:
time: 255 us; the launch traced here: 254 us
  waiting for transfers between devices  126 us (49%)
  Pallas kernels  64.5 us (25%)
  starting transfers between devices  37.9 us (15%)
  local copies, waits for them, and re-layouts  22.2 us (9%)
    ppermute x18, waiting for transfers between devices, swap(): return lax.ppermute(x, 'seq', [(i, i ^ bit) for i in range(n)])  98.4 us
    unnamed x76, local copies, waits for them, and re-layouts  20.6 us
    all_to_all x1, waiting for transfers between devices, per_device(): q_heads = lax.all_to_all(q_send, 'seq', 0, 0, tiled=True)  20.6 us
    ppermute x18, starting transfers between devices, swap(): return lax.ppermute(x, 'seq', [(i, i ^ bit) for i in range(n)])  17.3 us
    pallas_call x2, Pallas kernels, per_device(): pl.pallas_call(functools.partial(response_body, chunk, kept), grid_spec=p...  16 us
    pallas_call x4, Pallas kernels, per_device(): pl.pallas_call(functools.partial(prompt_body, chunk), grid=(1,), in_specs...  14.7 us
    pallas_call x2, Pallas kernels, per_device(): pl.pallas_call(functools.partial(output_body, lows, split), grid_spec=plt...  13.7 us
    all_to_all x1, starting transfers between devices, per_device(): q_heads = lax.all_to_all(q_send, 'seq', 0, 0, tiled=True)  7.41 us
  transfers between devices with their start and end apart: 22, of which 9 were waited for; matrix products, arithmetic and copies ran while one was open for 1% of the time, Pallas kernels for 24%

profile of v4, /device:TPU:0, one launch (start us, length us, event | category | flops | bytes accessed | tf_op | source)
XLA Modules:
  0.0 253.7 jit_solution(6480510377159532443)
XLA Ops:
  1.1 1.2 copy-done.9
  2.3 2.1 shard_map.148
  4.4 7.4 %all-to-all-start = ((bf16[16,128,256]{2,1,0:T(8,128)(2,1)}), bf16[16,128,256]{2,1,0:T(8,128)(2,1)S(1)}, u32[]{:S(2)}, u32[]{:S(2)}) async-start(bf16[16,128,256]{2,1,0:T(8,128)(2,1)} %shard_map.148), calls=%async_computation | async-start | bytes 2097152 | tf_op jit(solution)/shard_map/all_to_all | solution.py:301
  12.8 1.4 copy-done.5
  14.2 20.6 %all-to-all-done.q_ref = bf16[16,128,256]{2,1,0:T(8,128)(2,1)S(1)} async-done(((bf16[16,128,256]{2,1,0:T(8,128)(2,1)}), bf16[16,128,256]{2,1,0:T(8,128)(2,1)S(1)}, u32[]{:S(2)}, u32[]{:S(2)}) %all-to-all-start) | async-done | bytes 1048608 | tf_op jit(solution)/shard_map/all_to_all | solution.py:301
  34.7 6.8 %all-to-all-start.1 = ((bf16[16,2,128,256]{3,2,1,0:T(8,128)(2,1)}), bf16[16,2,128,256]{3,2,1,0:T(8,128)(2,1)S(1)}, u32[]{:S(2)}, u32[]{:S(2)}) async-start(bf16[16,2,128,256]{3,2,1,0:T(8,128)(2,1)} %copy-done.5), calls=%async_computation.1 | async-start | bytes 4194304 | tf_op jit(solution)/shard_map/all_to_all | solution.py:287
  41.6 1.4 constant_dynamic-slice_fusion
  43.0 2.0 collective-permute-start.4
  45.0 44.7 %collective-permute-done.4.refs_6_ = bf16[128,4096]{1,0:T(8,128)(2,1)} collective-permute-done((bf16[128,4096]{1,0:T(8,128)(2,1)S(1)}, bf16[128,4096]{1,0:T(8,128)(2,1)}, u32[]{:S(2)}, u32[]{:S(2)}) %collective-permute-start.4) | collective-permute-done | bytes 1048608 | tf_op jit(solution)/shard_map/ppermute | solution.py:269
  89.7 1.5 collective-permute-start.5
  91.9 1.0 fusion
  93.1 1.6 copy-done.20
  94.7 1.6 copy-done.21
  96.3 1.6 copy-done.22
  97.9 6.6 %shard_map.150 = (bf16[512,256]{1,0:T(8,128)(2,1)S(1)}, bf16[512,256]{1,0:T(8,128)(2,1)S(1)}, bf16[512,256]{1,0:T(8,128)(2,1)S(1)}, bf16[512,256]{1,0:T(8,128)(2...) custom-call(bf16[512,4096]{1,0:T(8,128)(2,1)S(1)} %copy-done, ...), custom_call_target="tpu_custom_call" | custom-call | flops 3221225472 | bytes 10485760 | tf_op jit(solution)/shard_map/pallas_call | solution.py:322
  107.8 6.7 %collective-permute-done.5.refs_7_ = bf16[128,4096]{1,0:T(8,128)(2,1)} collective-permute-done((bf16[128,4096]{1,0:T(8,128)(2,1)}, bf16[128,4096]{1,0:T(8,128)(2,1)}, u32[]{:S(2)}, u32[]{:S(2)}) %collective-permute-start.5) | collective-permute-done | bytes 1048608 | tf_op jit(solution)/shard_map/ppermute | solution.py:310
  114.6 3.6 %prompt_attention.4.refs_0_ = bf16[16,128,256]{2,1,0:T(8,128)(2,1)S(1)} custom-call(bf16[16,128,256]{2,1,0:T(8,128)(2,1)S(1)} %all-to-all-done.q_ref, bf16[16,2,128,256]{3,2,1,0:T(8,128)(2,1)S(1)} %all-to-all-done.1.kv_ref, bf16[512,256]{1,0:T(8,128)(2,1)S(1)} %get-tuple-element.41.km_ref, bf16[16,256]{1,0:T(8,128)(2,1)S(1)} %get-tuple-element.42.vm_ref), custom_call_target="tpu_custom_call" | custom-call | flops 1342177280 | bytes 1572864 | tf_op jit(solution)/shard_map/prompt_attention/pallas_call | solution.py:440
  118.2 3.6 %prompt_attention.5.refs_0_ = bf16[16,128,256]{2,1,0:T(8,128)(2,1)S(1)} custom-call(bf16[16,128,256]{2,1,0:T(8,128)(2,1)S(1)} %all-to-all-done.q_ref, bf16[16,2,128,256]{3,2,1,0:T(8,128)(2,1)S(1)} %all-to-all-done.1.kv_ref, bf16[512,256]{1,0:T(8,128)(2,1)S(1)} %get-tuple-element.41.km_ref, ...), custom_call_target="tpu_custom_call", output_to_operand_aliasing={{}: (4, {})} | custom-call | flops 1342177280 | bytes 1572864 | tf_op jit(solution)/shard_map/prompt_attention/pallas_call | solution.py:440
  121.8 3.6 %prompt_attention.6.refs_0_ = bf16[16,128,256]{2,1,0:T(8,128)(2,1)S(1)} custom-call(bf16[16,128,256]{2,1,0:T(8,128)(2,1)S(1)} %all-to-all-done.q_ref, bf16[16,2,128,256]{3,2,1,0:T(8,128)(2,1)S(1)} %all-to-all-done.1.kv_ref, bf16[512,256]{1,0:T(8,128)(2,1)S(1)} %get-tuple-element.41.km_ref, ...), custom_call_target="tpu_custom_call", output_to_operand_aliasing={{}: (4, {})} | custom-call | flops 1342177280 | bytes 1572864 | tf_op jit(solution)/shard_map/prompt_attention/pallas_call | solution.py:440
  125.4 3.8 %prompt_attention.7 = bf16[16,128,256]{2,1,0:T(8,128)(2,1)S(1)} custom-call(bf16[16,128,256]{2,1,0:T(8,128)(2,1)S(1)} %all-to-all-done.q_ref, bf16[16,2,128,256]{3,2,1,0:T(8,128)(2,1)S(1)} %all-to-all-done.1.kv_ref, bf16[512,256]{1,0:T(8,128)(2,1)S(1)} %get-tuple-element.41.km_ref, ...), custom_call_target="tpu_custom_call", output_to_operand_aliasing={{}: (4, {})} | custom-call | flops 1342177280 | bytes 1572864 | tf_op jit(solution)/shard_map/prompt_attention/pallas_call | solution.py:440
  129.3 1.0 copy-done.2
  130.3 4.9 %all-to-all-start.2 = ((bf16[16,128,256]{2,1,0:T(8,128)(2,1)}), bf16[16,128,256]{2,1,0:T(8,128)(2,1)S(1)}, u32[]{:S(2)}, u32[]{:S(2)}) async-start(bf16[16,128,256]{2,1,0:T(8,128)(2,1)} %copy-done.2), calls=%async_computation.2 | async-start | bytes 2097152 | tf_op jit(solution)/shard_map/all_to_all | solution.py:461
  140.2 7.7 %response_attention.3 = (bf16[4,2,32,256]{3,2,1,0:T(8,128)(2,1)S(1)}, bf16[4,2,32,256]{3,2,1,0:T(8,128)(2,1)S(1)}, bf16[4,2,32,256]{3,2,1,0:T(8,128)(2,1)S(1)}, bf16[4,2,32,256]{3,2,1,0:T(8,128)(2,1)S(1)}) custom-call(s32[3]{0:T(128)S(1)} %pad_add_fusion.place_ref, bf16[16,2,128,256]{3,2,1,0:T(8,128)(2,1)S(1)} %all-to-all-done.1.kv_ref, ...), custom_call_target="tpu_custom_call" | custom-call | flops 1610612736 | bytes 2097152 | tf_op jit(solution)/shard_map/response_attention/pallas_call | solution.py:356
  148.3 1.6 collective-permute-start.9
  150.9 8.3 %response_attention.2 = (bf16[4,2,32,256]{3,2,1,0:T(8,128)(2,1)S(1)}, bf16[4,2,32,256]{3,2,1,0:T(8,128)(2,1)S(1)}, bf16[4,2,32,256]{3,2,1,0:T(8,128)(2,1)S(1)}, bf16[4,2,32,256]{3,2,1,0:T(8,128)(2,1)}) custom-call(s32[3]{0:T(128)S(1)} %pad_add_fusion.place_ref, bf16[16,2,128,256]{3,2,1,0:T(8,128)(2,1)S(1)} %all-to-all-done.1.kv_ref, ...), custom_call_target="tpu_custom_call" | custom-call | flops 1610612736 | bytes 2097152 | tf_op jit(solution)/shard_map/response_attention/pallas_call | solution.py:356
  159.8 7.1 %output_projection.3 = (bf16[2,32,4096]{2,1,0:T(8,128)(2,1)}, bf16[2,32,4096]{2,1,0:T(8,128)(2,1)}, bf16[2,32,4096]{2,1,0:T(8,128)(2,1)}, bf16[2,32,4096]{2,1,0:T(8,128)(2,1)}) custom-call(s32[3]{0:T(128)S(1)} %pad_add_fusion.place_ref, bf16[4,2,32,256]{3,2,1,0:T(8,128)(2,1)S(1)} %get-tuple-element.52.refs_0_, ...), custom_call_target="tpu_custom_call" | custom-call | flops 2147483648 | bytes 8388608 | tf_op jit(solution)/shard_map/output_projection/pallas_call | solution.py:377
  166.9 1.9 collective-permute-start.17
  168.9 1.9 collective-permute-start.13
  171.6 2.1 collective-permute-start.1
  173.7 2.9 %collective-permute-done.1.refs_2_ = bf16[4,2,32,256]{3,2,1,0:T(8,128)(2,1)S(1)} collective-permute-done((bf16[4,2,32,256]{3,2,1,0:T(8,128)(2,1)S(1)}, bf16[4,2,32,256]{3,2,1,0:T(8,128)(2,1)S(1)}, u32[]{:S(2)}, u32[]{:S(2)}) %collective-permute-start.1) | collective-permute-done | bytes 131104 | tf_op jit(solution)/shard_map/ppermute | solution.py:269
  177.4 5.4 %collective-permute-done.2.refs_3_ = bf16[4,2,32,256]{3,2,1,0:T(8,128)(2,1)} collective-permute-done((bf16[4,2,32,256]{3,2,1,0:T(8,128)(2,1)}, bf16[4,2,32,256]{3,2,1,0:T(8,128)(2,1)}, u32[]{:S(2)}, u32[]{:S(2)}) %collective-permute-start.2) | collective-permute-done | bytes 131104 | tf_op jit(solution)/shard_map/ppermute | solution.py:269
  185.3 6.6 %output_projection.2 = (f32[2,32,4096]{2,1,0:T(8,128)S(1)}, f32[2,32,4096]{2,1,0:T(8,128)S(1)}, f32[2,32,4096]{2,1,0:T(8,128)S(1)}, f32[2,32,4096]{2,1,0:T(8,128)S(1)}) custom-call(s32[3]{0:T(128)S(1)} %copy-done.19, bf16[4,2,32,256]{3,2,1,0:T(8,128)(2,1)S(1)} %get-tuple-element.47.refs_0_, bf16[4,2,32,256]{3,2,1,0:T(8,128)(2,1)S(1)} %copy-done.13, ...), custom_call_target="tpu_custom_call" | custom-call | flops 2147483648 | bytes 8388608 | tf_op jit(solution)/shard_map/output_projection/pallas_call | solution.py:377
  191.9 1.2 halve.7
  193.1 2.9 %collective-permute-start.18 = (bf16[1,32,4096]{2,1,0:T(8,128)(2,1)S(1)}, bf16[1,32,4096]{2,1,0:T(8,128)(2,1)S(1)}, u32[]{:S(2)}, u32[]{:S(2)}) collective-permute-start(bf16[1,32,4096]{2,1,0:T(8,128)(2,1)S(1)} %get-tuple-element.70), channel_id=1, source_target_pairs={{0,8},{1,9},{2,10},{3,11},{4,12},{5,13},{6,14},{7,15},{8,0},{9,1},... | collective-permute-start | bytes 786440 | tf_op jit(solution)/shard_map/ppermute | solution.py:269
  196.1 1.3 halve.6
  197.5 18.2 %collective-permute-done.13.got_ref = bf16[2,32,4096]{2,1,0:T(8,128)(2,1)} collective-permute-done((bf16[2,32,4096]{2,1,0:T(8,128)(2,1)}, bf16[2,32,4096]{2,1,0:T(8,128)(2,1)}, u32[]{:S(2)}, u32[]{:S(2)}) %collective-permute-start.13) | collective-permute-done | bytes 524320 | tf_op jit(solution)/shard_map/ppermute | solution.py:269
  215.7 1.2 halve.5
  216.9 1.4 collective-permute-start.14
  218.3 8.0 %collective-permute-done.11.got_ref = bf16[2,32,4096]{2,1,0:T(8,128)(2,1)} collective-permute-done((bf16[2,32,4096]{2,1,0:T(8,128)(2,1)}, bf16[2,32,4096]{2,1,0:T(8,128)(2,1)}, u32[]{:S(2)}, u32[]{:S(2)}) %collective-permute-start.11) | collective-permute-done | bytes 524320 | tf_op jit(solution)/shard_map/ppermute | solution.py:269
  226.3 1.2 halve.4
  227.5 1.4 collective-permute-start.12
  228.9 1.0 finish.4
  229.9 1.0 finish.5
  230.9 14.7 %collective-permute-done.14.got_ref = bf16[1,32,4096]{2,1,0:T(8,128)(2,1)S(1)} collective-permute-done((bf16[1,32,4096]{2,1,0:T(8,128)(2,1)S(1)}, bf16[1,32,4096]{2,1,0:T(8,128)(2,1)S(1)}, u32[]{:S(2)}, u32[]{:S(2)}) %collective-permute-start.14) | collective-permute-done | bytes 262176 | tf_op jit(solution)/shard_map/ppermute | solution.py:269
  245.6 1.0 finish.6
  246.6 4.5 %collective-permute-done.12.got_ref = bf16[1,32,4096]{2,1,0:T(8,128)(2,1)S(1)} collective-permute-done((bf16[1,32,4096]{2,1,0:T(8,128)(2,1)S(1)}, bf16[1,32,4096]{2,1,0:T(8,128)(2,1)S(1)}, u32[]{:S(2)}, u32[]{:S(2)}) %collective-permute-start.12) | collective-permute-done | bytes 262176 | tf_op jit(solution)/shard_map/ppermute | solution.py:269
  251.1 1.0 finish.7
  252.1 1.5 shard_map.151
  (105 shorter events, 16.3 us)
Async XLA Ops:
  1.1 1.2 copy-start.9
  2.3 9.5 %copy-start.10 = (bf16[128,4096]{1,0:T(8,128)(2,1)S(1)}, bf16[128,4096]{1,0:T(8,128)(2,1)}, u32[]{:S(2)}) copy-start(bf16[128,4096]{1,0:T(8,128)(2,1)} %k_ref.1) | copy-start | bytes 3145732
  2.3 9.5 %copy-start.11 = (bf16[128,4096]{1,0:T(8,128)(2,1)S(1)}, bf16[128,4096]{1,0:T(8,128)(2,1)}, u32[]{:S(2)}) copy-start(bf16[128,4096]{1,0:T(8,128)(2,1)} %v_ref.1) | copy-start | bytes 3145732
  4.4 30.3 %all-to-all-start = ((bf16[16,128,256]{2,1,0:T(8,128)(2,1)}), bf16[16,128,256]{2,1,0:T(8,128)(2,1)S(1)}, u32[]{:S(2)}, u32[]{:S(2)}) async-start(bf16[16,128,256]{2,1,0:T(8,128)(2,1)} %shard_map.148), calls=%async_computation | async-start | bytes 2097152 | tf_op jit(solution)/shard_map/all_to_all | solution.py:301
  12.8 1.4 copy-start.5
  34.7 79.9 %all-to-all-start.1 = ((bf16[16,2,128,256]{3,2,1,0:T(8,128)(2,1)}), bf16[16,2,128,256]{3,2,1,0:T(8,128)(2,1)S(1)}, u32[]{:S(2)}, u32[]{:S(2)}) async-start(bf16[16,2,128,256]{3,2,1,0:T(8,128)(2,1)} %copy-done.5), calls=%async_computation.1 | async-start | bytes 4194304 | tf_op jit(solution)/shard_map/all_to_all | solution.py:287
  41.5 50.3 %copy-start.34 = (bf16[4096]{0:T(1024)(128)(2,1)S(1)}, bf16[4096]{0:T(1024)(128)(2,1)}, u32[]{:S(2)}) copy-start(bf16[4096]{0:T(1024)(128)(2,1)} %param.17) | copy-start | bytes 24580
  41.5 50.3 %copy-start.35 = (bf16[4096]{0:T(1024)(128)(2,1)S(1)}, bf16[4096]{0:T(1024)(128)(2,1)}, u32[]{:S(2)}) copy-start(bf16[4096]{0:T(1024)(128)(2,1)} %param.20) | copy-start | bytes 24580
  41.5 51.5 %copy-start = (bf16[512,4096]{1,0:T(8,128)(2,1)S(1)}, bf16[512,4096]{1,0:T(8,128)(2,1)}, u32[]{:S(2)}) copy-start(bf16[512,4096]{1,0:T(8,128)(2,1)} %embed_ref.9) | copy-start | bytes 12582916
  43.0 46.6 %collective-permute-start.4 = (bf16[128,4096]{1,0:T(8,128)(2,1)S(1)}, bf16[128,4096]{1,0:T(8,128)(2,1)}, u32[]{:S(2)}, u32[]{:S(2)}) collective-permute-start(bf16[128,4096]{1,0:T(8,128)(2,1)S(1)} %constant_dynamic-slice_fusion), channel_id=1, source_target_pairs={{0,2},{1,3},{2,0},{3,1},{4,6},{5,7},{6,4},{7,5},{8,10},{9,11},{10,... | collective-permute-start | bytes 3145736 | tf_op jit(solution)/shard_map/ppermute | solution.py:269
  89.7 24.9 %collective-permute-start.5 = (bf16[128,4096]{1,0:T(8,128)(2,1)}, bf16[128,4096]{1,0:T(8,128)(2,1)}, u32[]{:S(2)}, u32[]{:S(2)}) collective-permute-start(bf16[128,4096]{1,0:T(8,128)(2,1)} %collective-permute-done.4.refs_6_), channel_id=1, source_target_pairs={{0,16},{16,0},{1,17},{17,1},{2,18},{18,2},{3,19},{19,3},{4,20},{20... | collective-permute-start | bytes 3145736 | tf_op jit(solution)/shard_map/ppermute | solution.py:310
  91.1 68.1 %collective-permute-start.3 = (bf16[256,4096]{1,0:T(8,128)(2,1)}, bf16[256,4096]{1,0:T(8,128)(2,1)}, u32[]{:S(2)}, u32[]{:S(2)}) collective-permute-start(bf16[256,4096]{1,0:T(8,128)(2,1)} %refs_4_.3), channel_id=1, source_target_pairs={{0,1},{1,0},{2,3},{3,2},{4,5},{5,4},{6,7},{7,6},{8,9},{9,8},{10,11... | collective-permute-start | bytes 6291464 | tf_op jit(solution)/shard_map/ppermute | solution.py:269
  93.1 1.6 copy-start.20
  94.7 1.6 copy-start.21
  96.3 1.6 copy-start.22
  107.3 18.1 %copy-start.6 = (bf16[512,256]{1,0:T(8,128)(2,1)}, bf16[512,256]{1,0:T(8,128)(2,1)S(1)}, u32[]{:S(2)}) copy-start(bf16[512,256]{1,0:T(8,128)(2,1)S(1)} %get-tuple-element.41.km_ref) | copy-start | bytes 786436
  107.3 28.1 %copy-start.16 = (bf16[16,256]{1,0:T(8,128)(2,1)}, bf16[16,256]{1,0:T(8,128)(2,1)S(1)}, u32[]{:S(2)}) copy-start(bf16[16,256]{1,0:T(8,128)(2,1)S(1)} %get-tuple-element.42.vm_ref) | copy-start | bytes 24580
  107.3 42.6 %collective-permute-start.6 = (bf16[128,4096]{1,0:T(8,128)(2,1)}, bf16[128,4096]{1,0:T(8,128)(2,1)}, u32[]{:S(2)}, u32[]{:S(2)}) collective-permute-start(bf16[128,4096]{1,0:T(8,128)(2,1)} %collective-permute-done.4.refs_6_), channel_id=1, source_target_pairs={{0,1},{1,0},{2,3},{3,2},{4,5},{5,4},{6,7},{7,6},{8,9},{9,8},{10,11... | collective-permute-start | bytes 3145736 | tf_op jit(solution)/shard_map/ppermute | solution.py:269
  114.6 45.2 %collective-permute-start.7 = (bf16[128,4096]{1,0:T(8,128)(2,1)}, bf16[128,4096]{1,0:T(8,128)(2,1)}, u32[]{:S(2)}, u32[]{:S(2)}) collective-permute-start(bf16[128,4096]{1,0:T(8,128)(2,1)} %collective-permute-done.5.refs_7_), channel_id=1, source_target_pairs={{0,1},{1,0},{2,3},{3,2},{4,5},{5,4},{6,7},{7,6},{8,9},{9,8},{10,11... | collective-permute-start | bytes 3145736 | tf_op jit(solution)/shard_map/ppermute | solution.py:269
  129.3 1.0 copy-start.2
  130.3 5.0 %copy-start.37 = (s32[512]{0:T(512)S(1)}, s32[512]{0:T(512)}, u32[]{:S(2)}) copy-start(s32[512]{0:T(512)} %param.18) | copy-start | bytes 6148
  130.3 121.9 %all-to-all-start.2 = ((bf16[16,128,256]{2,1,0:T(8,128)(2,1)}), bf16[16,128,256]{2,1,0:T(8,128)(2,1)S(1)}, u32[]{:S(2)}, u32[]{:S(2)}) async-start(bf16[16,128,256]{2,1,0:T(8,128)(2,1)} %copy-done.2), calls=%async_computation.2 | async-start | bytes 2097152 | tf_op jit(solution)/shard_map/all_to_all | solution.py:461
  135.2 24.5 %copy-start.18 = (s32[3]{0:T(128)}, s32[3]{0:T(128)S(1)}, u32[]{:S(2)}) copy-start(s32[3]{0:T(128)S(1)} %pad_add_fusion.place_ref) | copy-start | bytes 40
  135.4 1.0 copy-start.7
  136.3 0.9 copy-start.24
  137.3 0.9 copy-start.27
  140.1 9.9 %copy-start.8 = (bf16[512,256]{1,0:T(8,128)(2,1)S(1)}, bf16[512,256]{1,0:T(8,128)(2,1)}, u32[]{:S(2)}) copy-start(bf16[512,256]{1,0:T(8,128)(2,1)} %copy-done.6) | copy-start | bytes 786436
  140.1 9.9 %copy-start.25 = (bf16[512,256]{1,0:T(8,128)(2,1)S(1)}, bf16[512,256]{1,0:T(8,128)(2,1)}, u32[]{:S(2)}) copy-start(bf16[512,256]{1,0:T(8,128)(2,1)} %copy-done.23) | copy-start | bytes 786436
  140.1 9.9 %copy-start.28 = (bf16[512,256]{1,0:T(8,128)(2,1)S(1)}, bf16[512,256]{1,0:T(8,128)(2,1)}, u32[]{:S(2)}) copy-start(bf16[512,256]{1,0:T(8,128)(2,1)} %copy-done.26) | copy-start | bytes 786436
  140.1 9.9 %copy-start.31 = (bf16[512,256]{1,0:T(8,128)(2,1)S(1)}, bf16[512,256]{1,0:T(8,128)(2,1)}, u32[]{:S(2)}) copy-start(bf16[512,256]{1,0:T(8,128)(2,1)} %copy-done.29) | copy-start | bytes 786436
  147.9 11.9 %collective-permute-start.8 = (bf16[4,2,32,256]{3,2,1,0:T(8,128)(2,1)S(1)}, bf16[4,2,32,256]{3,2,1,0:T(8,128)(2,1)S(1)}, u32[]{:S(2)}, u32[]{:S(2)}) collective-permute-start(bf16[4,2,32,256]{3,2,1,0:T(8,128)(2,1)S(1)} %get-tuple-element.53), channel_id=1, source_target_pairs={{0,1},{1,0},{2,3},{3,2},{4,5},{5,4},{6,7},{7,6},{8,9},{9,8},{10,11... | collective-permute-start | bytes 393224 | tf_op jit(solution)/shard_map/ppermute | solution.py:269
  148.3 11.4 %collective-permute-start.9 = (bf16[4,2,32,256]{3,2,1,0:T(8,128)(2,1)S(1)}, bf16[4,2,32,256]{3,2,1,0:T(8,128)(2,1)S(1)}, u32[]{:S(2)}, u32[]{:S(2)}) collective-permute-start(bf16[4,2,32,256]{3,2,1,0:T(8,128)(2,1)S(1)} %get-tuple-element.54), channel_id=1, source_target_pairs={{0,2},{1,3},{2,0},{3,1},{4,6},{5,7},{6,4},{7,5},{8,10},{9,11},{10,... | collective-permute-start | bytes 393224 | tf_op jit(solution)/shard_map/ppermute | solution.py:269
  150.0 9.8 %copy-start.3 = (bf16[256,4096]{1,0:T(8,128)(2,1)S(1)}, bf16[256,4096]{1,0:T(8,128)(2,1)}, u32[]{:S(2)}) copy-start(bf16[256,4096]{1,0:T(8,128)(2,1)} %refs_4_.3) | copy-start | bytes 6291460
  150.0 9.8 %collective-permute-start.10 = (bf16[4,2,32,256]{3,2,1,0:T(8,128)(2,1)S(1)}, bf16[4,2,32,256]{3,2,1,0:T(8,128)(2,1)S(1)}, u32[]{:S(2)}, u32[]{:S(2)}) collective-permute-start(bf16[4,2,32,256]{3,2,1,0:T(8,128)(2,1)S(1)} %get-tuple-element.55), channel_id=1, source_target_pairs={{0,3},{1,2},{2,1},{3,0},{4,7},{5,6},{6,5},{7,4},{8,11},{9,10},{10,... | collective-permute-start | bytes 393224 | tf_op jit(solution)/shard_map/ppermute | solution.py:269
  159.2 11.7 %collective-permute-start = (bf16[4,2,32,256]{3,2,1,0:T(8,128)(2,1)S(1)}, bf16[4,2,32,256]{3,2,1,0:T(8,128)(2,1)S(1)}, u32[]{:S(2)}, u32[]{:S(2)}) collective-permute-start(bf16[4,2,32,256]{3,2,1,0:T(8,128)(2,1)S(1)} %get-tuple-element.48), channel_id=1, source_target_pairs={{0,1},{1,0},{2,3},{3,2},{4,5},{5,4},{6,7},{7,6},{8,9},{9,8},{10,11... | collective-permute-start | bytes 393224 | tf_op jit(solution)/shard_map/ppermute | solution.py:269
  159.8 23.1 %copy-start.4 = (bf16[256,4096]{1,0:T(8,128)(2,1)S(1)}, bf16[256,4096]{1,0:T(8,128)(2,1)}, u32[]{:S(2)}) copy-start(bf16[256,4096]{1,0:T(8,128)(2,1)} %refs_4_.3) | copy-start | bytes 6291460
  166.9 25.0 %collective-permute-start.17 = (bf16[2,32,4096]{2,1,0:T(8,128)(2,1)}, bf16[2,32,4096]{2,1,0:T(8,128)(2,1)}, u32[]{:S(2)}, u32[]{:S(2)}) collective-permute-start(bf16[2,32,4096]{2,1,0:T(8,128)(2,1)} %get-tuple-element.68), channel_id=1, source_target_pairs={{0,4},{1,5},{2,6},{3,7},{4,0},{5,1},{6,2},{7,3},{8,12},{9,13},{10,... | collective-permute-start | bytes 1572872 | tf_op jit(solution)/shard_map/ppermute | solution.py:269
  168.8 27.3 %collective-permute-start.15 = (bf16[2,32,4096]{2,1,0:T(8,128)(2,1)}, bf16[2,32,4096]{2,1,0:T(8,128)(2,1)}, u32[]{:S(2)}, u32[]{:S(2)}) collective-permute-start(bf16[2,32,4096]{2,1,0:T(8,128)(2,1)} %get-tuple-element.64), channel_id=1, source_target_pairs={{0,4},{1,5},{2,6},{3,7},{4,0},{5,1},{6,2},{7,3},{8,12},{9,13},{10,... | collective-permute-start | bytes 1572872 | tf_op jit(solution)/shard_map/ppermute | solution.py:269
  168.9 46.8 %collective-permute-start.13 = (bf16[2,32,4096]{2,1,0:T(8,128)(2,1)}, bf16[2,32,4096]{2,1,0:T(8,128)(2,1)}, u32[]{:S(2)}, u32[]{:S(2)}) collective-permute-start(bf16[2,32,4096]{2,1,0:T(8,128)(2,1)} %get-tuple-element.60), channel_id=1, source_target_pairs={{0,4},{1,5},{2,6},{3,7},{4,0},{5,1},{6,2},{7,3},{8,12},{9,13},{10,... | collective-permute-start | bytes 1572872 | tf_op jit(solution)/shard_map/ppermute | solution.py:269
  170.8 55.5 %collective-permute-start.11 = (bf16[2,32,4096]{2,1,0:T(8,128)(2,1)}, bf16[2,32,4096]{2,1,0:T(8,128)(2,1)}, u32[]{:S(2)}, u32[]{:S(2)}) collective-permute-start(bf16[2,32,4096]{2,1,0:T(8,128)(2,1)} %get-tuple-element.56), channel_id=1, source_target_pairs={{0,4},{1,5},{2,6},{3,7},{4,0},{5,1},{6,2},{7,3},{8,12},{9,13},{10,... | collective-permute-start | bytes 1572872 | tf_op jit(solution)/shard_map/ppermute | solution.py:269
  171.6 5.0 %collective-permute-start.1 = (bf16[4,2,32,256]{3,2,1,0:T(8,128)(2,1)S(1)}, bf16[4,2,32,256]{3,2,1,0:T(8,128)(2,1)S(1)}, u32[]{:S(2)}, u32[]{:S(2)}) collective-permute-start(bf16[4,2,32,256]{3,2,1,0:T(8,128)(2,1)S(1)} %get-tuple-element.49), channel_id=1, source_target_pairs={{0,2},{1,3},{2,0},{3,1},{4,6},{5,7},{6,4},{7,5},{8,10},{9,11},{10,... | collective-permute-start | bytes 393224 | tf_op jit(solution)/shard_map/ppermute | solution.py:269
  177.3 5.5 %collective-permute-start.2 = (bf16[4,2,32,256]{3,2,1,0:T(8,128)(2,1)}, bf16[4,2,32,256]{3,2,1,0:T(8,128)(2,1)}, u32[]{:S(2)}, u32[]{:S(2)}) collective-permute-start(bf16[4,2,32,256]{3,2,1,0:T(8,128)(2,1)} %get-tuple-element.50), channel_id=1, source_target_pairs={{0,3},{1,2},{2,1},{3,0},{4,7},{5,6},{6,5},{7,4},{8,11},{9,10},{10,... | collective-permute-start | bytes 393224 | tf_op jit(solution)/shard_map/ppermute | solution.py:269
  193.1 35.8 %collective-permute-start.18 = (bf16[1,32,4096]{2,1,0:T(8,128)(2,1)S(1)}, bf16[1,32,4096]{2,1,0:T(8,128)(2,1)S(1)}, u32[]{:S(2)}, u32[]{:S(2)}) collective-permute-start(bf16[1,32,4096]{2,1,0:T(8,128)(2,1)S(1)} %get-tuple-element.70), channel_id=1, source_target_pairs={{0,8},{1,9},{2,10},{3,11},{4,12},{5,13},{6,14},{7,15},{8,0},{9,1},... | collective-permute-start | bytes 786440 | tf_op jit(solution)/shard_map/ppermute | solution.py:269
  196.1 32.8 %copy-start.36 = (bf16[4096]{0:T(1024)(128)(2,1)S(1)}, bf16[4096]{0:T(1024)(128)(2,1)}, u32[]{:S(2)}) copy-start(bf16[4096]{0:T(1024)(128)(2,1)} %param.21) | copy-start | bytes 24580
  196.1 32.8 %copy-start.1 = (bf16[512,4096]{1,0:T(8,128)(2,1)S(1)}, bf16[512,4096]{1,0:T(8,128)(2,1)}, u32[]{:S(2)}) copy-start(bf16[512,4096]{1,0:T(8,128)(2,1)} %embed_ref.9) | copy-start | bytes 12582916
  197.4 32.5 %collective-permute-start.16 = (bf16[1,32,4096]{2,1,0:T(8,128)(2,1)S(1)}, bf16[1,32,4096]{2,1,0:T(8,128)(2,1)S(1)}, u32[]{:S(2)}, u32[]{:S(2)}) collective-permute-start(bf16[1,32,4096]{2,1,0:T(8,128)(2,1)S(1)} %get-tuple-element.66), channel_id=1, source_target_pairs={{0,8},{1,9},{2,10},{3,11},{4,12},{5,13},{6,14},{7,15},{8,0},{9,1},... | collective-permute-start | bytes 786440 | tf_op jit(solution)/shard_map/ppermute | solution.py:269
  216.9 28.7 %collective-permute-start.14 = (bf16[1,32,4096]{2,1,0:T(8,128)(2,1)S(1)}, bf16[1,32,4096]{2,1,0:T(8,128)(2,1)S(1)}, u32[]{:S(2)}, u32[]{:S(2)}) collective-permute-start(bf16[1,32,4096]{2,1,0:T(8,128)(2,1)S(1)} %get-tuple-element.62), channel_id=1, source_target_pairs={{0,8},{1,9},{2,10},{3,11},{4,12},{5,13},{6,14},{7,15},{8,0},{9,1},... | collective-permute-start | bytes 786440 | tf_op jit(solution)/shard_map/ppermute | solution.py:269
  227.5 23.6 %collective-permute-start.12 = (bf16[1,32,4096]{2,1,0:T(8,128)(2,1)S(1)}, bf16[1,32,4096]{2,1,0:T(8,128)(2,1)S(1)}, u32[]{:S(2)}, u32[]{:S(2)}) collective-permute-start(bf16[1,32,4096]{2,1,0:T(8,128)(2,1)S(1)} %get-tuple-element.58), channel_id=1, source_target_pairs={{0,8},{1,9},{2,10},{3,11},{4,12},{5,13},{6,14},{7,15},{8,0},{9,1},... | collective-permute-start | bytes 786440 | tf_op jit(solution)/shard_map/ppermute | solution.py:269
  (12 other events, 9.4 us)

commit v5 on v3

--- a/solution.py
+++ b/solution.py
@@ -17,6 +17,9 @@
 
 F32 = jnp.float32
 BF16 = jnp.bfloat16
+
+
+GRANT = pltpu.CompilerParams(vmem_limit_bytes=28 << 20)
 
 
 def call(body, grid, in_specs, out_specs, out_shape, scratch=(), flops=0, moved=0, exps=0):
@@ -138,7 +141,23 @@
     return state
 
 
-def response_body(chunk, kept, place_ref, kv_ref, qe_ref, qm_ref, ke_ref, km_ref, ve_ref, vm_ref, commit_ref, *refs):
+def early_body(qe_ref, qm_ref, ke_ref, km_ref, ve_ref, vm_ref, commit_ref, acc_ref, stats_ref):
+    mask_value = jnp.broadcast_to(vm_ref[0:1], ve_ref.shape)
+    lane = lax.broadcasted_iota(jnp.int32, stats_ref.shape, 1)
+    stats = jnp.zeros(stats_ref.shape, F32)
+    for step in range(acc_ref.shape[0]):
+        shown = commit_ref[...] <= step
+        q = jnp.where(shown, qe_ref[...], qm_ref[...])
+        k = jnp.where(shown, ke_ref[...], km_ref[...])
+        v = jnp.where(shown, ve_ref[...], mask_value)
+        top, total, acc = merge(None, scores(q, k), v)
+        acc_ref[step] = acc
+        stats = jnp.where(lane == step, top, stats)
+        stats = jnp.where(lane == STEPS + step, total, stats)
+    stats_ref[...] = stats
+
+
+def response_body(chunk, kept, place_ref, kv_ref, qe_ref, qm_ref, acc_ref, stats_ref, commit_ref, *refs):
     out_refs, scratch_ref = refs[:-1], refs[-1]
     lows = len(out_refs)
     steps, blocks, per, _ = out_refs[0].shape
@@ -147,30 +166,26 @@
     count = blocks * span_rows
     side = bit if kept else 1 - bit
 
-    def mine(ref):
+    def mine(ref, *lead):
         parts = [
-            ref[pl.ds(pl.multiple_of((2 * block + side) * span_rows, span_rows), span_rows), :]
+            ref[(*lead, pl.ds(pl.multiple_of((2 * block + side) * span_rows, span_rows), span_rows), slice(None))]
             for block in range(blocks)
         ]
         return jnp.concatenate(parts, 0) if blocks > 1 else parts[0]
 
-    by_mask, by_embed, revealed = mine(qm_ref), mine(qe_ref), mine(commit_ref)
-    both = over_prompt(None, jnp.concatenate([by_mask, by_embed], 0), kv_ref, chunk)
-    mask_value = jnp.broadcast_to(vm_ref[0:1], ve_ref.shape)
+    revealed, stats = mine(commit_ref), mine(stats_ref)
+    both = over_prompt(None, jnp.concatenate([mine(qm_ref), mine(qe_ref)], 0), kv_ref, chunk)
     for step in range(steps):
         shown = revealed <= step
         one = revealed[:, 0:1] <= step
-        shown_key = commit_ref[...] <= step
-        q = jnp.where(shown, by_embed, by_mask)
-        k = jnp.where(shown_key, ke_ref[...], km_ref[...])
-        v = jnp.where(shown_key, ve_ref[...], mask_value)
-        state = (
-            jnp.where(one, both[0][count:], both[0][:count]),
-            jnp.where(one, both[1][count:], both[1][:count]),
-            jnp.where(shown, both[2][count:], both[2][:count]),
-        )
-        _, total, acc = merge(state, scores(q, k), v)
-        scratch_ref[step] = acc * (1.0 / total)
+        top_p = jnp.where(one, both[0][count:], both[0][:count])
+        total_p = jnp.where(one, both[1][count:], both[1][:count])
+        acc_p = jnp.where(shown, both[2][count:], both[2][:count])
+        top_r, total_r = stats[:, step : step + 1], stats[:, STEPS + step : STEPS + step + 1]
+        top = jnp.maximum(top_p, top_r)
+        keep_p, keep_r = jnp.exp2(top_p - top), jnp.exp2(top_r - top)
+        scale = 1.0 / (total_p * keep_p + total_r * keep_r)
+        scratch_ref[step] = acc_p * (keep_p * scale) + mine(acc_ref, step) * (keep_r * scale)
     for step in range(steps):
         for block in range(blocks):
             for k in range(lows):
@@ -217,7 +232,7 @@
         send_ref[pair] = jnp.where(bit == 0, second, first).astype(BF16)
 
 
-def finish_body(step, place_ref, embed_ref, mask_ref, gain_ref, commit_ref, keep_ref, got_ref, *refs):
+def finish_body(step, embed_ref, mask_ref, gain_ref, commit_ref, keep_ref, got_ref, *refs):
     residual_ref, normed_ref = refs[-2:]
     shown = commit_ref[:, 0:1] <= step
     rows = jnp.where(shown, embed_ref[...].astype(F32), mask_ref[...].astype(F32))
@@ -344,6 +359,16 @@
     high = me >> (lows.bit_length() - 1)
     blocks = highs // 2
     place = jnp.stack([low, high & 1, group & 1]).astype(jnp.int32)
+    early_acc, early_stats = call(
+        early_body,
+        (heads,),
+        [key_block] * 5 + [vm_block, whole((resp, HD))],
+        [pl.BlockSpec((STEPS, resp, HD), lambda h: (0, 0, h)), pl.BlockSpec((resp, HD), lambda h: (0, h))],
+        [jax.ShapeDtypeStruct((STEPS, resp, width), F32), jax.ShapeDtypeStruct((resp, width), F32)],
+        flops=4 * STEPS * resp * resp * width,
+        moved=20 * resp * width,
+        exps=heads * STEPS * resp * resp,
+    )(qe, qm, ke, km, ve, vm, commit)
     columns = min(model, 1024)
     projected = {}
     for kept in (False, True):
@@ -352,18 +377,21 @@
             grid_spec=pltpu.PrefetchScalarGridSpec(
                 num_scalar_prefetch=1,
                 grid=(heads,),
-                in_specs=[kv_block] + [key_block] * 5 + [vm_block, whole((resp, HD))],
+                in_specs=[
+                    kv_block, key_block, key_block,
+                    pl.BlockSpec((STEPS, resp, HD), lambda h, *_: (0, 0, h)), key_block, whole((resp, HD)),
+                ],
                 out_specs=[pl.BlockSpec((STEPS, blocks, per, HD), lambda h, *_: (0, 0, 0, h))] * lows,
                 scratch_shapes=[pltpu.VMEM((STEPS, resp // 2, HD), F32)],
             ),
             out_shape=[jax.ShapeDtypeStruct((STEPS, blocks, per, width), BF16)] * lows,
             name="response_attention",
             cost_estimate=pl.CostEstimate(
-                flops=2 * resp * width * (2 * prompt_len + STEPS * resp),
+                flops=4 * resp * width * prompt_len,
                 bytes_accessed=4 * prompt_len * width,
-                transcendentals=heads * resp * (2 * prompt_len + STEPS * resp) // 2,
+                transcendentals=heads * resp * prompt_len,
             ),
-        )(place, kv, qe, qm, ke, km, ve, vm, commit)
+        )(place, kv, qe, qm, early_acc, early_stats, commit)
         plane_context = [context[0]]
         for k in range(1, lows):
             plane_context.append(swap(context[k], k))
@@ -396,7 +424,7 @@
         bit = ((high >> level) & 1).astype(jnp.int32).reshape(1)
         sends, kept = [], []
         for step in range(STEPS):
-            columns = min(model, 2048)
+            columns = model
             get = pl.BlockSpec((count, per, columns), lambda j, *_: (0, 0, j))
             put = pl.BlockSpec((count // 2, per, columns), lambda j, *_: (0, 0, j))
             one, two = pl.pallas_call(
@@ -441,6 +469,7 @@
                 out_specs=pl.BlockSpec((blocks_of_q, rows, HD), of_block),
                 out_shape=jax.ShapeDtypeStruct((n, rows, width), BF16),
                 name="prompt_attention",
+                compiler_params=GRANT,
                 input_output_aliases={4: 0} if earlier else {},
                 cost_estimate=pl.CostEstimate(
                     flops=4 * blocks_of_q * rows * HD * (prompt_len + resp),
@@ -450,31 +479,27 @@
             )(q_heads, kv, km, vm, *earlier)
     back = lax.all_to_all(prompt_context, "seq", 0, 0, tiled=True)
 
+    my_embed = lax.dynamic_slice_in_dim(response_embed, me * per, per, 0)
+    my_commit = jnp.broadcast_to(lax.dynamic_slice_in_dim(commit_step, me * per, per, 0)[:, None], (per, HD))
     results = []
     for step in range(STEPS):
-        at_row = lambda i, at: (at[0], 0)
-        at_step = functools.partial(lambda step, i, at: (step, 0, 0), step)
-        one_row = pl.BlockSpec((1, model), lambda i, at: (0, 0))
-        one_sum = pl.BlockSpec((1, per, model), lambda i, at: (0, 0, 0))
+        at_step = functools.partial(lambda step, i: (step, 0, 0), step)
         results = pl.pallas_call(
             functools.partial(finish_body, step),
-            grid_spec=pltpu.PrefetchScalarGridSpec(
-                num_scalar_prefetch=1,
-                grid=(1,),
-                in_specs=[
-                    pl.BlockSpec((per, model), at_row), one_row, one_row,
-                    pl.BlockSpec((per, HD), at_row), one_sum, one_sum,
-                ]
-                + [pl.BlockSpec(memory_space=pl.ANY)] * len(results),
-                out_specs=[pl.BlockSpec((1, per, model), at_step)] * 2,
-            ),
+            grid=(1,),
+            in_specs=[
+                whole((per, model)), whole((1, model)), whole((1, model)), whole((per, HD)),
+                whole((1, per, model)), whole((1, per, model)),
+            ]
+            + [pl.BlockSpec(memory_space=pl.ANY)] * len(results),
+            out_specs=[pl.BlockSpec((1, per, model), at_step)] * 2,
             out_shape=[jax.ShapeDtypeStruct((STEPS, per, model), BF16)] * 2,
             name="finish",
-            input_output_aliases={7: 0, 8: 1} if results else {},
+            input_output_aliases={6: 0, 7: 1} if results else {},
             cost_estimate=pl.CostEstimate(flops=8 * per * model, bytes_accessed=12 * per * model, transcendentals=0),
         )(
-            me.astype(jnp.int32).reshape(1), response_embed, mask_embed[None, :], residual_gain[None, :],
-            commit, keeps[step], gots[step], *results,
+            my_embed, mask_embed[None, :], residual_gain[None, :], my_commit,
+            keeps[step], gots[step], *results,
         )
     residual, normed_rows = results
     columns = max(1, n // 4)

time: 266 us -> 277 us (1.041)
  waiting for transfers between devices: 114 us -> 120 us
  local copies, waits for them, and re-layouts: 13.8 us -> 16.9 us
    pallas_call x4, Pallas kernels: 21.3 us -> 14.7 us  [per_device(): pl.pallas_call(functools.partial(prompt_body, chunk), grid=(1,), in_specs...]
    ppermute x18, waiting for transfers between devices: 86.5 us -> 92.7 us  [swap(): return lax.ppermute(x, 'seq', [(i, i ^ bit) for i in range(n)])]
    pallas_call x4 -> x5, Pallas kernels: 8.98 us -> 14.8 us  [the longest x4 8.98 us: per_device(): pl.pallas_call(functools.partial(finish_body, step), grid=(1,), in_specs=...]
    unnamed x46 -> x48, local copies, waits for them, and re-layouts: 9.86 us -> 10.5 us
  transfers between devices with their start and end apart: 22 -> 22, of which waited for: 9 -> 8; matrix products, arithmetic and copies ran while one was open for 2% -> 3% of each run, Pallas kernels for 33% -> 32%
where the time goes in v5:
time: 277 us; the launch traced here: 276 us
  waiting for transfers between devices  120 us (43%)
  Pallas kernels  96.3 us (35%)
  starting transfers between devices  37.8 us (14%)
  local copies, waits for them, and re-layouts  16.9 us (6%)
  other arithmetic  3.74 us (1%)
    ppermute x18, waiting for transfers between devices, swap(): return lax.ppermute(x, 'seq', [(i, i ^ bit) for i in range(n)])  92.7 us
    pallas_call x2, Pallas kernels, per_device(): pl.pallas_call(functools.partial(response_body, chunk, kept), grid_spec=p...  20.2 us
    all_to_all x1, waiting for transfers between devices, per_device(): q_heads = lax.all_to_all(q_send, 'seq', 0, 0, tiled=True)  18.8 us
    ppermute x18, starting transfers between devices, swap(): return lax.ppermute(x, 'seq', [(i, i ^ bit) for i in range(n)])  17.3 us
    pallas_call x2, Pallas kernels, per_device(): pl.pallas_call(functools.partial(output_body, lows, split), grid_spec=plt...  15.5 us
    pallas_call x4, Pallas kernels, per_device(): pl.pallas_call(functools.partial(prompt_body, chunk), grid=(1,), in_specs...  14.7 us
    unnamed x48, local copies, waits for them, and re-layouts  10.5 us
    pallas_call x1, Pallas kernels, per_device(): call(project_body, (resp // block,), [pl.BlockSpec((block, model), lambda...  10.5 us
  transfers between devices with their start and end apart: 22, of which 8 were waited for; matrix products, arithmetic and copies ran while one was open for 3% of the time, Pallas kernels for 32%

profile of v5, /device:TPU:0, one launch (start us, length us, event | category | flops | bytes accessed | tf_op | source)
XLA Modules:
  0.0 276.3 jit_solution(1979256237139248925)
XLA Ops:
  1.7 3.7 %shard_map.148 = bf16[16,128,256]{2,1,0:T(8,128)(2,1)} custom-call(bf16[128,4096]{1,0:T(8,128)(2,1)} %q_ref.1, f32[128,128]{1,0:T(8,128)} %get-tuple-element.89.cos_ref, f32[128,128]{1,0:T(8,128)} %get-tuple-element.90.sin_ref), custom_call_target="tpu_custom_call" | custom-call | flops 3145728 | bytes 2097152 | tf_op jit(solution)/shard_map/pallas_call | solution.py:297
  5.5 7.4 %all-to-all-start = ((bf16[16,128,256]{2,1,0:T(8,128)(2,1)}), bf16[16,128,256]{2,1,0:T(8,128)(2,1)S(1)}, u32[]{:S(2)}, u32[]{:S(2)}) async-start(bf16[16,128,256]{2,1,0:T(8,128)(2,1)} %shard_map.148), calls=%async_computation | async-start | bytes 2097152 | tf_op jit(solution)/shard_map/all_to_all | solution.py:310
  12.9 4.1 %shard_map.149 = bf16[16,2,128,256]{3,2,1,0:T(8,128)(2,1)} custom-call(bf16[128,4096]{1,0:T(8,128)(2,1)} %k_ref.1, bf16[128,4096]{1,0:T(8,128)(2,1)} %v_ref.1, f32[128,128]{1,0:T(8,128)} %get-tuple-element.89.cos_ref, f32[128,128]{1,0:T(8,128)} %get-tuple-element.90.sin_ref), custom_call_target="tpu_custom_call" | custom-call | flops 3145728 | bytes 4194304 | tf_op jit(solution)/shard_map/pallas_call | solution.py:282
  17.0 18.8 %all-to-all-done.q_ref = bf16[16,128,256]{2,1,0:T(8,128)(2,1)S(1)} async-done(((bf16[16,128,256]{2,1,0:T(8,128)(2,1)}), bf16[16,128,256]{2,1,0:T(8,128)(2,1)S(1)}, u32[]{:S(2)}, u32[]{:S(2)}) %all-to-all-start) | async-done | bytes 1048608 | tf_op jit(solution)/shard_map/all_to_all | solution.py:310
  35.8 6.8 %all-to-all-start.1 = ((bf16[16,2,128,256]{3,2,1,0:T(8,128)(2,1)}), bf16[16,2,128,256]{3,2,1,0:T(8,128)(2,1)S(1)}, u32[]{:S(2)}, u32[]{:S(2)}) async-start(bf16[16,2,128,256]{3,2,1,0:T(8,128)(2,1)} %shard_map.149), calls=%async_computation.1 | async-start | bytes 4194304 | tf_op jit(solution)/shard_map/all_to_all | solution.py:296
  42.6 1.3 constant_dynamic-slice_fusion
  43.9 2.0 collective-permute-start.4
  45.9 44.8 %collective-permute-done.4.refs_6_ = bf16[128,4096]{1,0:T(8,128)(2,1)} collective-permute-done((bf16[128,4096]{1,0:T(8,128)(2,1)S(1)}, bf16[128,4096]{1,0:T(8,128)(2,1)}, u32[]{:S(2)}, u32[]{:S(2)}) %collective-permute-start.4) | collective-permute-done | bytes 1048608 | tf_op jit(solution)/shard_map/ppermute | solution.py:278
  90.7 1.5 collective-permute-start.5
  94.1 1.0 fusion
  95.1 1.0 pad_maximum_fusion
  96.1 10.5 %shard_map.150 = (bf16[512,256]{1,0:T(8,128)(2,1)}, bf16[512,256]{1,0:T(8,128)(2,1)}, bf16[512,256]{1,0:T(8,128)(2,1)}, bf16[512,256]{1,0:T(8,128)(2,1)}, bf16[5...) custom-call(bf16[512,4096]{1,0:T(8,128)(2,1)} %embed_ref.1, bf16[1,4096]{1,0:T(2,128)(2,1)} %broadcast_in_dim.10.mask_ref, ...), custom_call_target="tpu_custom_call" | custom-call | flops 3221225472 | bytes 10485760 | tf_op jit(solution)/shard_map/pallas_call | solution.py:331
  107.1 8.5 %collective-permute-done.5.refs_7_ = bf16[128,4096]{1,0:T(8,128)(2,1)} collective-permute-done((bf16[128,4096]{1,0:T(8,128)(2,1)}, bf16[128,4096]{1,0:T(8,128)(2,1)}, u32[]{:S(2)}, u32[]{:S(2)}) %collective-permute-start.5) | collective-permute-done | bytes 1048608 | tf_op jit(solution)/shard_map/ppermute | solution.py:319
  115.6 1.1 copy-done.2
  117.4 3.6 %prompt_attention.4.refs_0_ = bf16[16,128,256]{2,1,0:T(8,128)(2,1)S(1)} custom-call(bf16[16,128,256]{2,1,0:T(8,128)(2,1)S(1)} %all-to-all-done.q_ref, bf16[16,2,128,256]{3,2,1,0:T(8,128)(2,1)S(1)} %all-to-all-done.1.kv_ref, bf16[512,256]{1,0:T(8,128)(2,1)S(1)} %copy-done.2, bf16[16,256]{1,0:T(8,128)(2,1)S(1)} %copy-done.3), custom_call_target="tpu_custom_call" | custom-call | flops 1342177280 | bytes 1572864 | tf_op jit(solution)/shard_map/prompt_attention/pallas_call | solution.py:459
  121.1 3.6 %prompt_attention.5.refs_0_ = bf16[16,128,256]{2,1,0:T(8,128)(2,1)S(1)} custom-call(bf16[16,128,256]{2,1,0:T(8,128)(2,1)S(1)} %all-to-all-done.q_ref, bf16[16,2,128,256]{3,2,1,0:T(8,128)(2,1)S(1)} %all-to-all-done.1.kv_ref, bf16[512,256]{1,0:T(8,128)(2,1)S(1)} %copy-done.2, bf16[16,256]{1,0:T(8,128)(2,1)S(1)} %copy-done.3, ...), custom_call_target="tpu_custom_call", output_to_operand_aliasing={{}: (4, {})} | custom-call | flops 1342177280 | bytes 1572864 | tf_op jit(solution)/shard_map/prompt_attention/pallas_call | solution.py:459
  124.7 3.6 %prompt_attention.6.refs_0_ = bf16[16,128,256]{2,1,0:T(8,128)(2,1)S(1)} custom-call(bf16[16,128,256]{2,1,0:T(8,128)(2,1)S(1)} %all-to-all-done.q_ref, bf16[16,2,128,256]{3,2,1,0:T(8,128)(2,1)S(1)} %all-to-all-done.1.kv_ref, bf16[512,256]{1,0:T(8,128)(2,1)S(1)} %copy-done.2, bf16[16,256]{1,0:T(8,128)(2,1)S(1)} %copy-done.3, ...), custom_call_target="tpu_custom_call", output_to_operand_aliasing={{}: (4, {})} | custom-call | flops 1342177280 | bytes 1572864 | tf_op jit(solution)/shard_map/prompt_attention/pallas_call | solution.py:459
  128.3 3.8 %prompt_attention.7 = bf16[16,128,256]{2,1,0:T(8,128)(2,1)S(1)} custom-call(bf16[16,128,256]{2,1,0:T(8,128)(2,1)S(1)} %all-to-all-done.q_ref, bf16[16,2,128,256]{3,2,1,0:T(8,128)(2,1)S(1)} %all-to-all-done.1.kv_ref, bf16[512,256]{1,0:T(8,128)(2,1)S(1)} %copy-done.2, bf16[16,256]{1,0:T(8,128)(2,1)S(1)} %copy-done.3, ...), custom_call_target="tpu_custom_call", output_to_operand_aliasing={{}: (4, {})} | custom-call | flops 1342177280 | bytes 1572864 | tf_op jit(solution)/shard_map/prompt_attention/pallas_call | solution.py:459
  132.2 1.0 copy-done.1
  133.1 4.9 %all-to-all-start.2 = ((bf16[16,128,256]{2,1,0:T(8,128)(2,1)}), bf16[16,128,256]{2,1,0:T(8,128)(2,1)S(1)}, u32[]{:S(2)}, u32[]{:S(2)}) async-start(bf16[16,128,256]{2,1,0:T(8,128)(2,1)} %copy-done.1), calls=%async_computation.2 | async-start | bytes 2097152 | tf_op jit(solution)/shard_map/all_to_all | solution.py:480
  138.9 5.8 %shard_map.152 = (f32[4,512,256]{2,1,0:T(8,128)}, f32[512,256]{1,0:T(8,128)}) custom-call(bf16[512,256]{1,0:T(8,128)(2,1)} %get-tuple-element.45.qe_ref, bf16[512,256]{1,0:T(8,128)(2,1)} %get-tuple-element.46.qm_ref, bf16[512,256]{1,0:T(8,128)(2,1)} %get-tuple-element.47.ke_ref, bf16[512,256]{1,0:T(8,128)(2,1)} %get-tuple-element.43.km_ref, ...), custom_call_target="tpu_custom_call" | custom-call | flops 1073741824 | bytes 2621440 | tf_op jit(solution)/shard_map/pallas_call | solution.py:362
  145.4 10.1 %response_attention.3 = (bf16[4,2,32,256]{3,2,1,0:T(8,128)(2,1)}, bf16[4,2,32,256]{3,2,1,0:T(8,128)(2,1)}, bf16[4,2,32,256]{3,2,1,0:T(8,128)(2,1)}, bf16[4,2,32,256]{3,2,1,0:T(8,128)(2,1)}) custom-call(s32[3]{0:T(128)} %pad_add_fusion.place_ref, bf16[16,2,128,256]{3,2,1,0:T(8,128)(2,1)} %copy-done, bf16[512,256]{1,0:T(8,128)(2,1)} %get-tuple-element.45.qe_ref, ...), custom_call_target="tpu_custom_call" | custom-call | flops 1073741824 | bytes 2097152 | tf_op jit(solution)/shard_map/response_attention/pallas_call | solution.py:375
  155.9 1.6 collective-permute-start.9
  157.5 10.1 %response_attention.2 = (bf16[4,2,32,256]{3,2,1,0:T(8,128)(2,1)}, bf16[4,2,32,256]{3,2,1,0:T(8,128)(2,1)}, bf16[4,2,32,256]{3,2,1,0:T(8,128)(2,1)}, bf16[4,2,32,256]{3,2,1,0:T(8,128)(2,1)}) custom-call(s32[3]{0:T(128)} %pad_add_fusion.place_ref, bf16[16,2,128,256]{3,2,1,0:T(8,128)(2,1)} %copy-done, bf16[512,256]{1,0:T(8,128)(2,1)} %get-tuple-element.45.qe_ref, ...), custom_call_target="tpu_custom_call" | custom-call | flops 1073741824 | bytes 2097152 | tf_op jit(solution)/shard_map/response_attention/pallas_call | solution.py:375
  168.9 7.6 %output_projection.3 = (bf16[2,32,4096]{2,1,0:T(8,128)(2,1)}, bf16[2,32,4096]{2,1,0:T(8,128)(2,1)}, bf16[2,32,4096]{2,1,0:T(8,128)(2,1)}, bf16[2,32,4096]{2,1,0:T(8,128)(2,1)}) custom-call(s32[3]{0:T(128)} %pad_add_fusion.place_ref, bf16[4,2,32,256]{3,2,1,0:T(8,128)(2,1)} %get-tuple-element.56.refs_0_, bf16[4,2,32,256]{3,2,1,0:T(8,128)(2,1)} %copy-done.14, ...), custom_call_target="tpu_custom_call" | custom-call | flops 2147483648 | bytes 8388608 | tf_op jit(solution)/shard_map/output_projection/pallas_call | solution.py:398
  176.5 1.7 collective-permute-start.11
  178.6 1.6 collective-permute-start.15
  180.6 1.7 collective-permute-start.1
  182.3 3.3 %collective-permute-done.1.refs_2_ = bf16[4,2,32,256]{3,2,1,0:T(8,128)(2,1)S(1)} collective-permute-done((bf16[4,2,32,256]{3,2,1,0:T(8,128)(2,1)S(1)}, bf16[4,2,32,256]{3,2,1,0:T(8,128)(2,1)S(1)}, u32[]{:S(2)}, u32[]{:S(2)}) %collective-permute-start.1) | collective-permute-done | bytes 131104 | tf_op jit(solution)/shard_map/ppermute | solution.py:278
  186.3 5.1 %collective-permute-done.2.refs_3_ = bf16[4,2,32,256]{3,2,1,0:T(8,128)(2,1)S(1)} collective-permute-done((bf16[4,2,32,256]{3,2,1,0:T(8,128)(2,1)}, bf16[4,2,32,256]{3,2,1,0:T(8,128)(2,1)S(1)}, u32[]{:S(2)}, u32[]{:S(2)}) %collective-permute-start.2) | collective-permute-done | bytes 131104 | tf_op jit(solution)/shard_map/ppermute | solution.py:278
  192.1 7.9 %output_projection.2 = (f32[2,32,4096]{2,1,0:T(8,128)}, f32[2,32,4096]{2,1,0:T(8,128)}, f32[2,32,4096]{2,1,0:T(8,128)}, f32[2,32,4096]{2,1,0:T(8,128)}) custom-call(s32[3]{0:T(128)} %pad_add_fusion.place_ref, bf16[4,2,32,256]{3,2,1,0:T(8,128)(2,1)} %get-tuple-element.51.refs_0_, bf16[4,2,32,256]{3,2,1,0:T(8,128)(2,1)} %copy-done.13, ...), custom_call_target="tpu_custom_call" | custom-call | flops 2147483648 | bytes 8388608 | tf_op jit(solution)/shard_map/output_projection/pallas_call | solution.py:398
  200.9 2.4 halve.4
  203.2 2.7 collective-permute-start.12
  206.8 2.4 halve.5
  209.3 15.9 %collective-permute-done.15.got_ref = bf16[2,32,4096]{2,1,0:T(8,128)(2,1)S(1)} collective-permute-done((bf16[2,32,4096]{2,1,0:T(8,128)(2,1)}, bf16[2,32,4096]{2,1,0:T(8,128)(2,1)S(1)}, u32[]{:S(2)}, u32[]{:S(2)}) %collective-permute-start.15) | collective-permute-done | bytes 524320 | tf_op jit(solution)/shard_map/ppermute | solution.py:278
  226.1 2.4 halve.6
  228.5 1.6 collective-permute-start.16
  230.1 5.5 %collective-permute-done.17.got_ref = bf16[2,32,4096]{2,1,0:T(8,128)(2,1)S(1)} collective-permute-done((bf16[2,32,4096]{2,1,0:T(8,128)(2,1)}, bf16[2,32,4096]{2,1,0:T(8,128)(2,1)S(1)}, u32[]{:S(2)}, u32[]{:S(2)}) %collective-permute-start.17) | collective-permute-done | bytes 524320 | tf_op jit(solution)/shard_map/ppermute | solution.py:278
  236.5 2.3 halve.7
  238.8 1.7 collective-permute-start.18
  240.5 1.7 constant_dynamic-slice_fusion.1.embed_ref
  242.2 17.9 %collective-permute-done.18.got_ref = bf16[1,32,4096]{2,1,0:T(8,128)(2,1)S(1)} collective-permute-done((bf16[1,32,4096]{2,1,0:T(8,128)(2,1)}, bf16[1,32,4096]{2,1,0:T(8,128)(2,1)S(1)}, u32[]{:S(2)}, u32[]{:S(2)}) %collective-permute-start.18) | collective-permute-done | bytes 262176 | tf_op jit(solution)/shard_map/ppermute | solution.py:278
  260.8 2.2 finish.4
  263.7 2.2 finish.5
  266.7 2.2 finish.6
  269.6 2.2 finish.7
  271.9 1.0 copy-done.4
  272.9 3.4 %shard_map.151 = bf16[128,4096]{1,0:T(8,128)(2,1)} custom-call(bf16[16,128,256]{2,1,0:T(8,128)(2,1)} %copy-done.4), custom_call_target="tpu_custom_call" | custom-call | bytes 2097152 | tf_op jit(solution)/shard_map/pallas_call | solution.py:506
  (81 shorter events, 15.2 us)
Async XLA Ops:
  5.5 30.3 %all-to-all-start = ((bf16[16,128,256]{2,1,0:T(8,128)(2,1)}), bf16[16,128,256]{2,1,0:T(8,128)(2,1)S(1)}, u32[]{:S(2)}, u32[]{:S(2)}) async-start(bf16[16,128,256]{2,1,0:T(8,128)(2,1)} %shard_map.148), calls=%async_computation | async-start | bytes 2097152 | tf_op jit(solution)/shard_map/all_to_all | solution.py:310
  35.8 79.9 %all-to-all-start.1 = ((bf16[16,2,128,256]{3,2,1,0:T(8,128)(2,1)}), bf16[16,2,128,256]{3,2,1,0:T(8,128)(2,1)S(1)}, u32[]{:S(2)}, u32[]{:S(2)}) async-start(bf16[16,2,128,256]{3,2,1,0:T(8,128)(2,1)} %shard_map.149), calls=%async_computation.1 | async-start | bytes 4194304 | tf_op jit(solution)/shard_map/all_to_all | solution.py:296
  42.6 50.3 %copy-start.19 = (bf16[4096]{0:T(1024)(128)(2,1)S(1)}, bf16[4096]{0:T(1024)(128)(2,1)}, u32[]{:S(2)}) copy-start(bf16[4096]{0:T(1024)(128)(2,1)} %param.17) | copy-start | bytes 24580
  42.6 50.9 %copy-start.20 = (bf16[4096]{0:T(1024)(128)(2,1)S(1)}, bf16[4096]{0:T(1024)(128)(2,1)}, u32[]{:S(2)}) copy-start(bf16[4096]{0:T(1024)(128)(2,1)} %param.20) | copy-start | bytes 24580
  43.9 46.8 %collective-permute-start.4 = (bf16[128,4096]{1,0:T(8,128)(2,1)S(1)}, bf16[128,4096]{1,0:T(8,128)(2,1)}, u32[]{:S(2)}, u32[]{:S(2)}) collective-permute-start(bf16[128,4096]{1,0:T(8,128)(2,1)S(1)} %constant_dynamic-slice_fusion), channel_id=1, source_target_pairs={{0,2},{1,3},{2,0},{3,1},{4,6},{5,7},{6,4},{7,5},{8,10},{9,11},{10,... | collective-permute-start | bytes 3145736 | tf_op jit(solution)/shard_map/ppermute | solution.py:278
  90.7 24.9 %collective-permute-start.5 = (bf16[128,4096]{1,0:T(8,128)(2,1)}, bf16[128,4096]{1,0:T(8,128)(2,1)}, u32[]{:S(2)}, u32[]{:S(2)}) collective-permute-start(bf16[128,4096]{1,0:T(8,128)(2,1)} %collective-permute-done.4.refs_6_), channel_id=1, source_target_pairs={{0,16},{16,0},{1,17},{17,1},{2,18},{18,2},{3,19},{19,3},{4,20},{20... | collective-permute-start | bytes 3145736 | tf_op jit(solution)/shard_map/ppermute | solution.py:319
  92.2 75.4 %collective-permute-start.3 = (bf16[256,4096]{1,0:T(8,128)(2,1)}, bf16[256,4096]{1,0:T(8,128)(2,1)}, u32[]{:S(2)}, u32[]{:S(2)}) collective-permute-start(bf16[256,4096]{1,0:T(8,128)(2,1)} %refs_4_.3), channel_id=1, source_target_pairs={{0,1},{1,0},{2,3},{3,2},{4,5},{5,4},{6,7},{7,6},{8,9},{9,8},{10,11... | collective-permute-start | bytes 6291464 | tf_op jit(solution)/shard_map/ppermute | solution.py:278
  106.6 51.0 %collective-permute-start.6 = (bf16[128,4096]{1,0:T(8,128)(2,1)}, bf16[128,4096]{1,0:T(8,128)(2,1)}, u32[]{:S(2)}, u32[]{:S(2)}) collective-permute-start(bf16[128,4096]{1,0:T(8,128)(2,1)} %collective-permute-done.4.refs_6_), channel_id=1, source_target_pairs={{0,1},{1,0},{2,3},{3,2},{4,5},{5,4},{6,7},{7,6},{8,9},{9,8},{10,11... | collective-permute-start | bytes 3145736 | tf_op jit(solution)/shard_map/ppermute | solution.py:278
  115.6 52.6 %collective-permute-start.7 = (bf16[128,4096]{1,0:T(8,128)(2,1)}, bf16[128,4096]{1,0:T(8,128)(2,1)}, u32[]{:S(2)}, u32[]{:S(2)}) collective-permute-start(bf16[128,4096]{1,0:T(8,128)(2,1)} %collective-permute-done.5.refs_7_), channel_id=1, source_target_pairs={{0,1},{1,0},{2,3},{3,2},{4,5},{5,4},{6,7},{7,6},{8,9},{9,8},{10,11... | collective-permute-start | bytes 3145736 | tf_op jit(solution)/shard_map/ppermute | solution.py:278
  115.6 12.7 %copy-start = (bf16[16,2,128,256]{3,2,1,0:T(8,128)(2,1)}, bf16[16,2,128,256]{3,2,1,0:T(8,128)(2,1)S(1)}, u32[]{:S(2)}) copy-start(bf16[16,2,128,256]{3,2,1,0:T(8,128)(2,1)S(1)} %all-to-all-done.1.kv_ref) | copy-start | bytes 6291460
  115.6 1.1 copy-start.2
  116.8 0.7 copy-start.3
  132.1 1.0 copy-start.1
  133.1 4.9 %copy-start.22 = (s32[512]{0:T(512)S(1)}, s32[512]{0:T(512)}, u32[]{:S(2)}) copy-start(s32[512]{0:T(512)} %param.18) | copy-start | bytes 6148
  133.1 138.8 %all-to-all-start.2 = ((bf16[16,128,256]{2,1,0:T(8,128)(2,1)}), bf16[16,128,256]{2,1,0:T(8,128)(2,1)S(1)}, u32[]{:S(2)}, u32[]{:S(2)}) async-start(bf16[16,128,256]{2,1,0:T(8,128)(2,1)} %copy-done.1), calls=%async_computation.2 | async-start | bytes 2097152 | tf_op jit(solution)/shard_map/all_to_all | solution.py:480
  155.5 12.7 %collective-permute-start.8 = (bf16[4,2,32,256]{3,2,1,0:T(8,128)(2,1)}, bf16[4,2,32,256]{3,2,1,0:T(8,128)(2,1)S(1)}, u32[]{:S(2)}, u32[]{:S(2)}) collective-permute-start(bf16[4,2,32,256]{3,2,1,0:T(8,128)(2,1)} %get-tuple-element.57), channel_id=1, source_target_pairs={{0,1},{1,0},{2,3},{3,2},{4,5},{5,4},{6,7},{7,6},{8,9},{9,8},{10,11... | collective-permute-start | bytes 393224 | tf_op jit(solution)/shard_map/ppermute | solution.py:278
  155.9 12.3 %collective-permute-start.9 = (bf16[4,2,32,256]{3,2,1,0:T(8,128)(2,1)}, bf16[4,2,32,256]{3,2,1,0:T(8,128)(2,1)S(1)}, u32[]{:S(2)}, u32[]{:S(2)}) collective-permute-start(bf16[4,2,32,256]{3,2,1,0:T(8,128)(2,1)} %get-tuple-element.58), channel_id=1, source_target_pairs={{0,2},{1,3},{2,0},{3,1},{4,6},{5,7},{6,4},{7,5},{8,10},{9,11},{10,... | collective-permute-start | bytes 393224 | tf_op jit(solution)/shard_map/ppermute | solution.py:278
  157.5 10.7 %collective-permute-start.10 = (bf16[4,2,32,256]{3,2,1,0:T(8,128)(2,1)}, bf16[4,2,32,256]{3,2,1,0:T(8,128)(2,1)S(1)}, u32[]{:S(2)}, u32[]{:S(2)}) collective-permute-start(bf16[4,2,32,256]{3,2,1,0:T(8,128)(2,1)} %get-tuple-element.59), channel_id=1, source_target_pairs={{0,3},{1,2},{2,1},{3,0},{4,7},{5,6},{6,5},{7,4},{8,11},{9,10},{10,... | collective-permute-start | bytes 393224 | tf_op jit(solution)/shard_map/ppermute | solution.py:278
  167.6 13.0 %collective-permute-start = (bf16[4,2,32,256]{3,2,1,0:T(8,128)(2,1)}, bf16[4,2,32,256]{3,2,1,0:T(8,128)(2,1)S(1)}, u32[]{:S(2)}, u32[]{:S(2)}) collective-permute-start(bf16[4,2,32,256]{3,2,1,0:T(8,128)(2,1)} %get-tuple-element.52), channel_id=1, source_target_pairs={{0,1},{1,0},{2,3},{3,2},{4,5},{5,4},{6,7},{7,6},{8,9},{9,8},{10,11... | collective-permute-start | bytes 393224 | tf_op jit(solution)/shard_map/ppermute | solution.py:278
  168.2 0.7 copy-start.14
  168.2 0.7 copy-start.15
  168.2 0.7 copy-start.17
  168.9 11.7 %copy-start.23 = (bf16[4,2,32,256]{3,2,1,0:T(8,128)(2,1)S(1)}, bf16[4,2,32,256]{3,2,1,0:T(8,128)(2,1)}, u32[]{:S(2)}) copy-start(bf16[4,2,32,256]{3,2,1,0:T(8,128)(2,1)} %get-tuple-element.53) | copy-start | bytes 393220
  168.9 16.8 %copy-start.21 = (bf16[4096]{0:T(1024)(128)(2,1)S(1)}, bf16[4096]{0:T(1024)(128)(2,1)}, u32[]{:S(2)}) copy-start(bf16[4096]{0:T(1024)(128)(2,1)} %param.21) | copy-start | bytes 24580
  176.5 23.6 %collective-permute-start.11 = (bf16[2,32,4096]{2,1,0:T(8,128)(2,1)}, bf16[2,32,4096]{2,1,0:T(8,128)(2,1)S(1)}, u32[]{:S(2)}, u32[]{:S(2)}) collective-permute-start(bf16[2,32,4096]{2,1,0:T(8,128)(2,1)} %get-tuple-element.60), channel_id=1, source_target_pairs={{0,4},{1,5},{2,6},{3,7},{4,0},{5,1},{6,2},{7,3},{8,12},{9,13},{10,... | collective-permute-start | bytes 1572872 | tf_op jit(solution)/shard_map/ppermute | solution.py:278
  178.2 27.8 %collective-permute-start.13 = (bf16[2,32,4096]{2,1,0:T(8,128)(2,1)}, bf16[2,32,4096]{2,1,0:T(8,128)(2,1)S(1)}, u32[]{:S(2)}, u32[]{:S(2)}) collective-permute-start(bf16[2,32,4096]{2,1,0:T(8,128)(2,1)} %get-tuple-element.64), channel_id=1, source_target_pairs={{0,4},{1,5},{2,6},{3,7},{4,0},{5,1},{6,2},{7,3},{8,12},{9,13},{10,... | collective-permute-start | bytes 1572872 | tf_op jit(solution)/shard_map/ppermute | solution.py:278
  178.6 46.7 %collective-permute-start.15 = (bf16[2,32,4096]{2,1,0:T(8,128)(2,1)}, bf16[2,32,4096]{2,1,0:T(8,128)(2,1)S(1)}, u32[]{:S(2)}, u32[]{:S(2)}) collective-permute-start(bf16[2,32,4096]{2,1,0:T(8,128)(2,1)} %get-tuple-element.68), channel_id=1, source_target_pairs={{0,4},{1,5},{2,6},{3,7},{4,0},{5,1},{6,2},{7,3},{8,12},{9,13},{10,... | collective-permute-start | bytes 1572872 | tf_op jit(solution)/shard_map/ppermute | solution.py:278
  180.2 55.4 %collective-permute-start.17 = (bf16[2,32,4096]{2,1,0:T(8,128)(2,1)}, bf16[2,32,4096]{2,1,0:T(8,128)(2,1)S(1)}, u32[]{:S(2)}, u32[]{:S(2)}) collective-permute-start(bf16[2,32,4096]{2,1,0:T(8,128)(2,1)} %get-tuple-element.72), channel_id=1, source_target_pairs={{0,4},{1,5},{2,6},{3,7},{4,0},{5,1},{6,2},{7,3},{8,12},{9,13},{10,... | collective-permute-start | bytes 1572872 | tf_op jit(solution)/shard_map/ppermute | solution.py:278
  180.6 10.9 %copy-start.13 = (bf16[4,2,32,256]{3,2,1,0:T(8,128)(2,1)}, bf16[4,2,32,256]{3,2,1,0:T(8,128)(2,1)S(1)}, u32[]{:S(2)}) copy-start(bf16[4,2,32,256]{3,2,1,0:T(8,128)(2,1)S(1)} %collective-permute-done.refs_1_) | copy-start | bytes 393220
  180.6 5.0 %collective-permute-start.1 = (bf16[4,2,32,256]{3,2,1,0:T(8,128)(2,1)S(1)}, bf16[4,2,32,256]{3,2,1,0:T(8,128)(2,1)S(1)}, u32[]{:S(2)}, u32[]{:S(2)}) collective-permute-start(bf16[4,2,32,256]{3,2,1,0:T(8,128)(2,1)S(1)} %copy-done.23), channel_id=1, source_target_pairs={{0,2},{1,3},{2,0},{3,1},{4,6},{5,7},{6,4},{7,5},{8,10},{9,11},{10,... | collective-permute-start | bytes 393224 | tf_op jit(solution)/shard_map/ppermute | solution.py:278
  185.7 5.8 %copy-start.16 = (bf16[4,2,32,256]{3,2,1,0:T(8,128)(2,1)}, bf16[4,2,32,256]{3,2,1,0:T(8,128)(2,1)S(1)}, u32[]{:S(2)}) copy-start(bf16[4,2,32,256]{3,2,1,0:T(8,128)(2,1)S(1)} %collective-permute-done.1.refs_2_) | copy-start | bytes 393220
  185.7 5.8 %collective-permute-start.2 = (bf16[4,2,32,256]{3,2,1,0:T(8,128)(2,1)}, bf16[4,2,32,256]{3,2,1,0:T(8,128)(2,1)S(1)}, u32[]{:S(2)}, u32[]{:S(2)}) collective-permute-start(bf16[4,2,32,256]{3,2,1,0:T(8,128)(2,1)} %get-tuple-element.54), channel_id=1, source_target_pairs={{0,3},{1,2},{2,1},{3,0},{4,7},{5,6},{6,5},{7,4},{8,11},{9,10},{10,... | collective-permute-start | bytes 393224 | tf_op jit(solution)/shard_map/ppermute | solution.py:278
  191.5 0.7 copy-start.18
  200.1 0.8 copy-start.8
  203.2 65.7 %collective-permute-start.12 = (bf16[1,32,4096]{2,1,0:T(8,128)(2,1)}, bf16[1,32,4096]{2,1,0:T(8,128)(2,1)S(1)}, u32[]{:S(2)}, u32[]{:S(2)}) collective-permute-start(bf16[1,32,4096]{2,1,0:T(8,128)(2,1)} %get-tuple-element.62), channel_id=1, source_target_pairs={{0,8},{1,9},{2,10},{3,11},{4,12},{5,13},{6,14},{7,15},{8,0},{9,1},... | collective-permute-start | bytes 786440 | tf_op jit(solution)/shard_map/ppermute | solution.py:278
  205.9 0.8 copy-start.7
  209.1 56.9 %collective-permute-start.14 = (bf16[1,32,4096]{2,1,0:T(8,128)(2,1)}, bf16[1,32,4096]{2,1,0:T(8,128)(2,1)S(1)}, u32[]{:S(2)}, u32[]{:S(2)}) collective-permute-start(bf16[1,32,4096]{2,1,0:T(8,128)(2,1)} %get-tuple-element.66), channel_id=1, source_target_pairs={{0,8},{1,9},{2,10},{3,11},{4,12},{5,13},{6,14},{7,15},{8,0},{9,1},... | collective-permute-start | bytes 786440 | tf_op jit(solution)/shard_map/ppermute | solution.py:278
  225.3 0.8 copy-start.6
  228.5 34.5 %collective-permute-start.16 = (bf16[1,32,4096]{2,1,0:T(8,128)(2,1)}, bf16[1,32,4096]{2,1,0:T(8,128)(2,1)S(1)}, u32[]{:S(2)}, u32[]{:S(2)}) collective-permute-start(bf16[1,32,4096]{2,1,0:T(8,128)(2,1)} %get-tuple-element.70), channel_id=1, source_target_pairs={{0,8},{1,9},{2,10},{3,11},{4,12},{5,13},{6,14},{7,15},{8,0},{9,1},... | collective-permute-start | bytes 786440 | tf_op jit(solution)/shard_map/ppermute | solution.py:278
  235.7 0.8 copy-start.5
  238.8 21.3 %collective-permute-start.18 = (bf16[1,32,4096]{2,1,0:T(8,128)(2,1)}, bf16[1,32,4096]{2,1,0:T(8,128)(2,1)S(1)}, u32[]{:S(2)}, u32[]{:S(2)}) collective-permute-start(bf16[1,32,4096]{2,1,0:T(8,128)(2,1)} %get-tuple-element.74), channel_id=1, source_target_pairs={{0,8},{1,9},{2,10},{3,11},{4,12},{5,13},{6,14},{7,15},{8,0},{9,1},... | collective-permute-start | bytes 786440 | tf_op jit(solution)/shard_map/ppermute | solution.py:278
  260.1 0.7 copy-start.12
  263.0 0.7 copy-start.11
  266.0 0.7 copy-start.10
  269.0 0.7 copy-start.9
  271.9 1.0 copy-start.4

commit v6 on v5

--- a/solution.py
+++ b/solution.py
@@ -157,24 +157,19 @@
     stats_ref[...] = stats
 
 
-def response_body(chunk, kept, place_ref, kv_ref, qe_ref, qm_ref, acc_ref, stats_ref, commit_ref, *refs):
+def response_body(chunk, place_ref, kv_ref, qe_ref, qm_ref, acc_ref, stats_ref, commit_ref, *refs):
     out_refs, scratch_ref = refs[:-1], refs[-1]
     lows = len(out_refs)
     steps, blocks, per, _ = out_refs[0].shape
-    low, bit = place_ref[0], place_ref[1]
+    low = place_ref[0]
     span_rows = lows * per
     count = blocks * span_rows
-    side = bit if kept else 1 - bit
-
-    def mine(ref, *lead):
-        parts = [
-            ref[(*lead, pl.ds(pl.multiple_of((2 * block + side) * span_rows, span_rows), span_rows), slice(None))]
-            for block in range(blocks)
-        ]
-        return jnp.concatenate(parts, 0) if blocks > 1 else parts[0]
-
-    revealed, stats = mine(commit_ref), mine(stats_ref)
-    both = over_prompt(None, jnp.concatenate([mine(qm_ref), mine(qe_ref)], 0), kv_ref, chunk)
+
+    def flat(value):
+        return value.reshape(count, HD)
+
+    revealed, stats = flat(commit_ref[...]), flat(stats_ref[...])
+    both = over_prompt(None, jnp.concatenate([flat(qm_ref[...]), flat(qe_ref[...])], 0), kv_ref, chunk)
     for step in range(steps):
         shown = revealed <= step
         one = revealed[:, 0:1] <= step
@@ -185,7 +180,7 @@
         top = jnp.maximum(top_p, top_r)
         keep_p, keep_r = jnp.exp2(top_p - top), jnp.exp2(top_r - top)
         scale = 1.0 / (total_p * keep_p + total_r * keep_r)
-        scratch_ref[step] = acc_p * (keep_p * scale) + mine(acc_ref, step) * (keep_r * scale)
+        scratch_ref[step] = acc_p * (keep_p * scale) + flat(acc_ref[step]) * (keep_r * scale)
     for step in range(steps):
         for block in range(blocks):
             for k in range(lows):
@@ -369,17 +364,27 @@
         moved=20 * resp * width,
         exps=heads * STEPS * resp * resp,
     )(qe, qm, ke, km, ve, vm, commit)
+
+    def paired(array, *lead):
+        return array.reshape(*lead, blocks, 2, lows * per, array.shape[-1])
+
     columns = min(model, 1024)
     projected = {}
     for kept in (False, True):
+        side = (lambda at: at[1]) if kept else (lambda at: 1 - at[1])
+        half_rows_of = pl.BlockSpec((blocks, None, lows * per, HD), lambda h, at, side=side: (0, side(at), 0, h))
         context = pl.pallas_call(
-            functools.partial(response_body, chunk, kept),
+            functools.partial(response_body, 2 * chunk),
             grid_spec=pltpu.PrefetchScalarGridSpec(
                 num_scalar_prefetch=1,
                 grid=(heads,),
                 in_specs=[
-                    kv_block, key_block, key_block,
-                    pl.BlockSpec((STEPS, resp, HD), lambda h, *_: (0, 0, h)), key_block, whole((resp, HD)),
+                    kv_block, half_rows_of, half_rows_of,
+                    pl.BlockSpec(
+                        (STEPS, blocks, None, lows * per, HD), lambda h, at, side=side: (0, 0, side(at), 0, h)
+                    ),
+                    half_rows_of,
+                    pl.BlockSpec((blocks, None, lows * per, HD), lambda h, at, side=side: (0, side(at), 0, 0)),
                 ],
                 out_specs=[pl.BlockSpec((STEPS, blocks, per, HD), lambda h, *_: (0, 0, 0, h))] * lows,
                 scratch_shapes=[pltpu.VMEM((STEPS, resp // 2, HD), F32)],
@@ -391,7 +396,9 @@
                 bytes_accessed=4 * prompt_len * width,
                 transcendentals=heads * resp * prompt_len,
             ),
-        )(place, kv, qe, qm, early_acc, early_stats, commit)
+        )(
+            place, kv, paired(qe), paired(qm), paired(early_acc, STEPS), paired(early_stats), paired(commit)
+        )
         plane_context = [context[0]]
         for k in range(1, lows):
             plane_context.append(swap(context[k], k))

time: 277 us -> 275 us (level)
  Pallas kernels: 96.3 us -> 93.1 us
    pallas_call x2, Pallas kernels: 20.2 us -> 17 us  [per_device(): pl.pallas_call(functools.partial(response_body, 2 * chunk), grid_spec=plt...]
  transfers between devices with their start and end apart: 22 -> 22, of which waited for: 8 -> 9; matrix products, arithmetic and copies ran while one was open for 3% -> 4% of each run, Pallas kernels for 32% -> 31%
where the time goes in v6:
time: 275 us; the launch traced here: 274 us
  waiting for transfers between devices  121 us (44%)
  Pallas kernels  93.1 us (34%)
  starting transfers between devices  37.2 us (14%)
  local copies, waits for them, and re-layouts  17.7 us (6%)
  other arithmetic  3.74 us (1%)
    ppermute x18, waiting for transfers between devices, swap(): return lax.ppermute(x, 'seq', [(i, i ^ bit) for i in range(n)])  93.4 us
    all_to_all x1, waiting for transfers between devices, per_device(): q_heads = lax.all_to_all(q_send, 'seq', 0, 0, tiled=True)  18.8 us
    pallas_call x2, Pallas kernels, per_device(): pl.pallas_call(functools.partial(response_body, 2 * chunk), grid_spec=plt...  17 us
    ppermute x18, starting transfers between devices, swap(): return lax.ppermute(x, 'seq', [(i, i ^ bit) for i in range(n)])  16.6 us
    pallas_call x2, Pallas kernels, per_device(): pl.pallas_call(functools.partial(output_body, lows, split), grid_spec=plt...  15.5 us
    pallas_call x4, Pallas kernels, per_device(): pl.pallas_call(functools.partial(prompt_body, chunk), grid=(1,), in_specs...  14.7 us
    pallas_call x1, Pallas kernels, per_device(): call(project_body, (resp // block,), [pl.BlockSpec((block, model), lambda...  10.5 us
    unnamed x48, local copies, waits for them, and re-layouts  10.4 us
  transfers between devices with their start and end apart: 22, of which 9 were waited for; matrix products, arithmetic and copies ran while one was open for 4% of the time, Pallas kernels for 31%

profile of v6, /device:TPU:0, one launch (start us, length us, event | category | flops | bytes accessed | tf_op | source)
XLA Modules:
  0.0 273.9 jit_solution(11497756162528751534)
XLA Ops:
  1.7 3.7 %shard_map.148 = bf16[16,128,256]{2,1,0:T(8,128)(2,1)} custom-call(bf16[128,4096]{1,0:T(8,128)(2,1)} %q_ref.1, f32[128,128]{1,0:T(8,128)} %get-tuple-element.89.cos_ref, f32[128,128]{1,0:T(8,128)} %get-tuple-element.90.sin_ref), custom_call_target="tpu_custom_call" | custom-call | flops 3145728 | bytes 2097152 | tf_op jit(solution)/shard_map/pallas_call | solution.py:292
  5.5 7.4 %all-to-all-start = ((bf16[16,128,256]{2,1,0:T(8,128)(2,1)}), bf16[16,128,256]{2,1,0:T(8,128)(2,1)S(1)}, u32[]{:S(2)}, u32[]{:S(2)}) async-start(bf16[16,128,256]{2,1,0:T(8,128)(2,1)} %shard_map.148), calls=%async_computation | async-start | bytes 2097152 | tf_op jit(solution)/shard_map/all_to_all | solution.py:305
  12.9 4.1 %shard_map.149 = bf16[16,2,128,256]{3,2,1,0:T(8,128)(2,1)} custom-call(bf16[128,4096]{1,0:T(8,128)(2,1)} %k_ref.1, bf16[128,4096]{1,0:T(8,128)(2,1)} %v_ref.1, f32[128,128]{1,0:T(8,128)} %get-tuple-element.89.cos_ref, f32[128,128]{1,0:T(8,128)} %get-tuple-element.90.sin_ref), custom_call_target="tpu_custom_call" | custom-call | flops 3145728 | bytes 4194304 | tf_op jit(solution)/shard_map/pallas_call | solution.py:277
  17.0 18.8 %all-to-all-done.q_ref = bf16[16,128,256]{2,1,0:T(8,128)(2,1)S(1)} async-done(((bf16[16,128,256]{2,1,0:T(8,128)(2,1)}), bf16[16,128,256]{2,1,0:T(8,128)(2,1)S(1)}, u32[]{:S(2)}, u32[]{:S(2)}) %all-to-all-start) | async-done | bytes 1048608 | tf_op jit(solution)/shard_map/all_to_all | solution.py:305
  35.8 6.8 %all-to-all-start.1 = ((bf16[16,2,128,256]{3,2,1,0:T(8,128)(2,1)}), bf16[16,2,128,256]{3,2,1,0:T(8,128)(2,1)S(1)}, u32[]{:S(2)}, u32[]{:S(2)}) async-start(bf16[16,2,128,256]{3,2,1,0:T(8,128)(2,1)} %shard_map.149), calls=%async_computation.1 | async-start | bytes 4194304 | tf_op jit(solution)/shard_map/all_to_all | solution.py:291
  42.6 1.3 constant_dynamic-slice_fusion
  43.9 2.0 collective-permute-start.4
  45.9 44.8 %collective-permute-done.4.refs_6_ = bf16[128,4096]{1,0:T(8,128)(2,1)} collective-permute-done((bf16[128,4096]{1,0:T(8,128)(2,1)S(1)}, bf16[128,4096]{1,0:T(8,128)(2,1)}, u32[]{:S(2)}, u32[]{:S(2)}) %collective-permute-start.4) | collective-permute-done | bytes 1048608 | tf_op jit(solution)/shard_map/ppermute | solution.py:273
  90.7 1.5 collective-permute-start.5
  94.1 1.0 fusion
  95.1 1.0 pad_maximum_fusion
  96.1 10.5 %shard_map.150 = (bf16[512,256]{1,0:T(8,128)(2,1)}, bf16[512,256]{1,0:T(8,128)(2,1)}, bf16[512,256]{1,0:T(8,128)(2,1)}, bf16[512,256]{1,0:T(8,128)(2,1)}, bf16[5...) custom-call(bf16[512,4096]{1,0:T(8,128)(2,1)} %embed_ref.1, bf16[1,4096]{1,0:T(2,128)(2,1)} %broadcast_in_dim.14.mask_ref, ...), custom_call_target="tpu_custom_call" | custom-call | flops 3221225472 | bytes 10485760 | tf_op jit(solution)/shard_map/pallas_call | solution.py:326
  107.1 8.5 %collective-permute-done.5.refs_7_ = bf16[128,4096]{1,0:T(8,128)(2,1)} collective-permute-done((bf16[128,4096]{1,0:T(8,128)(2,1)}, bf16[128,4096]{1,0:T(8,128)(2,1)}, u32[]{:S(2)}, u32[]{:S(2)}) %collective-permute-start.5) | collective-permute-done | bytes 1048608 | tf_op jit(solution)/shard_map/ppermute | solution.py:314
  115.6 1.1 copy-done.2
  117.4 3.6 %prompt_attention.4.refs_0_ = bf16[16,128,256]{2,1,0:T(8,128)(2,1)S(1)} custom-call(bf16[16,128,256]{2,1,0:T(8,128)(2,1)S(1)} %all-to-all-done.q_ref, bf16[16,2,128,256]{3,2,1,0:T(8,128)(2,1)S(1)} %all-to-all-done.1.kv_ref, bf16[512,256]{1,0:T(8,128)(2,1)S(1)} %copy-done.2, bf16[16,256]{1,0:T(8,128)(2,1)S(1)} %copy-done.3), custom_call_target="tpu_custom_call" | custom-call | flops 1342177280 | bytes 1572864 | tf_op jit(solution)/shard_map/prompt_attention/pallas_call | solution.py:466
  121.1 3.6 %prompt_attention.5.refs_0_ = bf16[16,128,256]{2,1,0:T(8,128)(2,1)S(1)} custom-call(bf16[16,128,256]{2,1,0:T(8,128)(2,1)S(1)} %all-to-all-done.q_ref, bf16[16,2,128,256]{3,2,1,0:T(8,128)(2,1)S(1)} %all-to-all-done.1.kv_ref, bf16[512,256]{1,0:T(8,128)(2,1)S(1)} %copy-done.2, bf16[16,256]{1,0:T(8,128)(2,1)S(1)} %copy-done.3, ...), custom_call_target="tpu_custom_call", output_to_operand_aliasing={{}: (4, {})} | custom-call | flops 1342177280 | bytes 1572864 | tf_op jit(solution)/shard_map/prompt_attention/pallas_call | solution.py:466
  124.7 3.6 %prompt_attention.6.refs_0_ = bf16[16,128,256]{2,1,0:T(8,128)(2,1)S(1)} custom-call(bf16[16,128,256]{2,1,0:T(8,128)(2,1)S(1)} %all-to-all-done.q_ref, bf16[16,2,128,256]{3,2,1,0:T(8,128)(2,1)S(1)} %all-to-all-done.1.kv_ref, bf16[512,256]{1,0:T(8,128)(2,1)S(1)} %copy-done.2, bf16[16,256]{1,0:T(8,128)(2,1)S(1)} %copy-done.3, ...), custom_call_target="tpu_custom_call", output_to_operand_aliasing={{}: (4, {})} | custom-call | flops 1342177280 | bytes 1572864 | tf_op jit(solution)/shard_map/prompt_attention/pallas_call | solution.py:466
  128.3 3.8 %prompt_attention.7 = bf16[16,128,256]{2,1,0:T(8,128)(2,1)S(1)} custom-call(bf16[16,128,256]{2,1,0:T(8,128)(2,1)S(1)} %all-to-all-done.q_ref, bf16[16,2,128,256]{3,2,1,0:T(8,128)(2,1)S(1)} %all-to-all-done.1.kv_ref, bf16[512,256]{1,0:T(8,128)(2,1)S(1)} %copy-done.2, bf16[16,256]{1,0:T(8,128)(2,1)S(1)} %copy-done.3, ...), custom_call_target="tpu_custom_call", output_to_operand_aliasing={{}: (4, {})} | custom-call | flops 1342177280 | bytes 1572864 | tf_op jit(solution)/shard_map/prompt_attention/pallas_call | solution.py:466
  132.2 1.0 copy-done.1
  133.1 4.9 %all-to-all-start.2 = ((bf16[16,128,256]{2,1,0:T(8,128)(2,1)}), bf16[16,128,256]{2,1,0:T(8,128)(2,1)S(1)}, u32[]{:S(2)}, u32[]{:S(2)}) async-start(bf16[16,128,256]{2,1,0:T(8,128)(2,1)} %copy-done.1), calls=%async_computation.2 | async-start | bytes 2097152 | tf_op jit(solution)/shard_map/all_to_all | solution.py:487
  138.9 5.8 %shard_map.152 = (f32[4,512,256]{2,1,0:T(8,128)}, f32[512,256]{1,0:T(8,128)}) custom-call(bf16[512,256]{1,0:T(8,128)(2,1)} %get-tuple-element.45.qe_ref, bf16[512,256]{1,0:T(8,128)(2,1)} %get-tuple-element.46.qm_ref, bf16[512,256]{1,0:T(8,128)(2,1)} %get-tuple-element.47.ke_ref, bf16[512,256]{1,0:T(8,128)(2,1)} %get-tuple-element.43.km_ref, ...), custom_call_target="tpu_custom_call" | custom-call | flops 1073741824 | bytes 2621440 | tf_op jit(solution)/shard_map/pallas_call | solution.py:357
  146.2 8.5 %response_attention.3 = (bf16[4,2,32,256]{3,2,1,0:T(8,128)(2,1)}, bf16[4,2,32,256]{3,2,1,0:T(8,128)(2,1)}, bf16[4,2,32,256]{3,2,1,0:T(8,128)(2,1)}, bf16[4,2,32,256]{3,2,1,0:T(8,128)(2,1)}) custom-call(s32[3]{0:T(128)} %pad_add_fusion.place_ref, bf16[16,2,128,256]{3,2,1,0:T(8,128)(2,1)} %copy-done, bf16[2,2,128,256]{3,2,1,0:T(8,128)(2,1)} %bitcast.14, ...), custom_call_target="tpu_custom_call" | custom-call | flops 1073741824 | bytes 2097152 | tf_op jit(solution)/shard_map/response_attention/pallas_call | solution.py:376
  155.1 1.6 collective-permute-start.9
  156.8 8.5 %response_attention.2 = (bf16[4,2,32,256]{3,2,1,0:T(8,128)(2,1)}, bf16[4,2,32,256]{3,2,1,0:T(8,128)(2,1)}, bf16[4,2,32,256]{3,2,1,0:T(8,128)(2,1)}, bf16[4,2,32,256]{3,2,1,0:T(8,128)(2,1)}) custom-call(s32[3]{0:T(128)} %pad_add_fusion.place_ref, bf16[16,2,128,256]{3,2,1,0:T(8,128)(2,1)} %copy-done, bf16[2,2,128,256]{3,2,1,0:T(8,128)(2,1)} %bitcast.15, ...), custom_call_target="tpu_custom_call" | custom-call | flops 1073741824 | bytes 2097152 | tf_op jit(solution)/shard_map/response_attention/pallas_call | solution.py:376
  166.7 7.6 %output_projection.3 = (bf16[2,32,4096]{2,1,0:T(8,128)(2,1)}, bf16[2,32,4096]{2,1,0:T(8,128)(2,1)}, bf16[2,32,4096]{2,1,0:T(8,128)(2,1)}, bf16[2,32,4096]{2,1,0:T(8,128)(2,1)}) custom-call(s32[3]{0:T(128)} %pad_add_fusion.place_ref, bf16[4,2,32,256]{3,2,1,0:T(8,128)(2,1)} %get-tuple-element.56.refs_0_, bf16[4,2,32,256]{3,2,1,0:T(8,128)(2,1)} %copy-done.14, ...), custom_call_target="tpu_custom_call" | custom-call | flops 2147483648 | bytes 8388608 | tf_op jit(solution)/shard_map/output_projection/pallas_call | solution.py:405
  174.3 1.5 collective-permute-start.11
  176.4 1.5 collective-permute-start.15
  178.4 1.5 collective-permute-start.1
  179.9 3.5 %collective-permute-done.1.refs_2_ = bf16[4,2,32,256]{3,2,1,0:T(8,128)(2,1)S(1)} collective-permute-done((bf16[4,2,32,256]{3,2,1,0:T(8,128)(2,1)S(1)}, bf16[4,2,32,256]{3,2,1,0:T(8,128)(2,1)S(1)}, u32[]{:S(2)}, u32[]{:S(2)}) %collective-permute-start.1) | collective-permute-done | bytes 131104 | tf_op jit(solution)/shard_map/ppermute | solution.py:273
  184.1 5.3 %collective-permute-done.2.refs_3_ = bf16[4,2,32,256]{3,2,1,0:T(8,128)(2,1)S(1)} collective-permute-done((bf16[4,2,32,256]{3,2,1,0:T(8,128)(2,1)}, bf16[4,2,32,256]{3,2,1,0:T(8,128)(2,1)S(1)}, u32[]{:S(2)}, u32[]{:S(2)}) %collective-permute-start.2) | collective-permute-done | bytes 131104 | tf_op jit(solution)/shard_map/ppermute | solution.py:273
  190.1 7.9 %output_projection.2 = (f32[2,32,4096]{2,1,0:T(8,128)}, f32[2,32,4096]{2,1,0:T(8,128)}, f32[2,32,4096]{2,1,0:T(8,128)}, f32[2,32,4096]{2,1,0:T(8,128)}) custom-call(s32[3]{0:T(128)} %pad_add_fusion.place_ref, bf16[4,2,32,256]{3,2,1,0:T(8,128)(2,1)} %get-tuple-element.51.refs_0_, bf16[4,2,32,256]{3,2,1,0:T(8,128)(2,1)} %copy-done.13, ...), custom_call_target="tpu_custom_call" | custom-call | flops 2147483648 | bytes 8388608 | tf_op jit(solution)/shard_map/output_projection/pallas_call | solution.py:405
  198.8 2.4 halve.4
  201.2 2.4 collective-permute-start.12
  204.4 2.4 halve.5
  207.3 15.8 %collective-permute-done.15.got_ref = bf16[2,32,4096]{2,1,0:T(8,128)(2,1)S(1)} collective-permute-done((bf16[2,32,4096]{2,1,0:T(8,128)(2,1)}, bf16[2,32,4096]{2,1,0:T(8,128)(2,1)S(1)}, u32[]{:S(2)}, u32[]{:S(2)}) %collective-permute-start.15) | collective-permute-done | bytes 524320 | tf_op jit(solution)/shard_map/ppermute | solution.py:273
  223.9 2.4 halve.6
  226.3 1.5 collective-permute-start.16
  227.8 5.9 %collective-permute-done.17.got_ref = bf16[2,32,4096]{2,1,0:T(8,128)(2,1)S(1)} collective-permute-done((bf16[2,32,4096]{2,1,0:T(8,128)(2,1)}, bf16[2,32,4096]{2,1,0:T(8,128)(2,1)S(1)}, u32[]{:S(2)}, u32[]{:S(2)}) %collective-permute-start.17) | collective-permute-done | bytes 524320 | tf_op jit(solution)/shard_map/ppermute | solution.py:273
  234.4 2.3 halve.7
  236.8 1.4 collective-permute-start.18
  238.1 1.7 constant_dynamic-slice_fusion.1.embed_ref
  239.8 17.9 %collective-permute-done.18.got_ref = bf16[1,32,4096]{2,1,0:T(8,128)(2,1)S(1)} collective-permute-done((bf16[1,32,4096]{2,1,0:T(8,128)(2,1)}, bf16[1,32,4096]{2,1,0:T(8,128)(2,1)S(1)}, u32[]{:S(2)}, u32[]{:S(2)}) %collective-permute-start.18) | collective-permute-done | bytes 262176 | tf_op jit(solution)/shard_map/ppermute | solution.py:273
  258.4 2.2 finish.4
  261.4 2.2 finish.5
  264.3 2.2 finish.6
  267.3 2.2 finish.7
  269.5 1.0 copy-done.4
  270.6 3.4 %shard_map.151 = bf16[128,4096]{1,0:T(8,128)(2,1)} custom-call(bf16[16,128,256]{2,1,0:T(8,128)(2,1)} %copy-done.4), custom_call_target="tpu_custom_call" | custom-call | bytes 2097152 | tf_op jit(solution)/shard_map/pallas_call | solution.py:513
  (82 shorter events, 16.8 us)
Async XLA Ops:
  5.5 30.3 %all-to-all-start = ((bf16[16,128,256]{2,1,0:T(8,128)(2,1)}), bf16[16,128,256]{2,1,0:T(8,128)(2,1)S(1)}, u32[]{:S(2)}, u32[]{:S(2)}) async-start(bf16[16,128,256]{2,1,0:T(8,128)(2,1)} %shard_map.148), calls=%async_computation | async-start | bytes 2097152 | tf_op jit(solution)/shard_map/all_to_all | solution.py:305
  35.8 79.9 %all-to-all-start.1 = ((bf16[16,2,128,256]{3,2,1,0:T(8,128)(2,1)}), bf16[16,2,128,256]{3,2,1,0:T(8,128)(2,1)S(1)}, u32[]{:S(2)}, u32[]{:S(2)}) async-start(bf16[16,2,128,256]{3,2,1,0:T(8,128)(2,1)} %shard_map.149), calls=%async_computation.1 | async-start | bytes 4194304 | tf_op jit(solution)/shard_map/all_to_all | solution.py:291
  42.6 50.3 %copy-start.20 = (bf16[4096]{0:T(1024)(128)(2,1)S(1)}, bf16[4096]{0:T(1024)(128)(2,1)}, u32[]{:S(2)}) copy-start(bf16[4096]{0:T(1024)(128)(2,1)} %param.17) | copy-start | bytes 24580
  42.6 50.9 %copy-start.21 = (bf16[4096]{0:T(1024)(128)(2,1)S(1)}, bf16[4096]{0:T(1024)(128)(2,1)}, u32[]{:S(2)}) copy-start(bf16[4096]{0:T(1024)(128)(2,1)} %param.20) | copy-start | bytes 24580
  43.9 46.8 %collective-permute-start.4 = (bf16[128,4096]{1,0:T(8,128)(2,1)S(1)}, bf16[128,4096]{1,0:T(8,128)(2,1)}, u32[]{:S(2)}, u32[]{:S(2)}) collective-permute-start(bf16[128,4096]{1,0:T(8,128)(2,1)S(1)} %constant_dynamic-slice_fusion), channel_id=1, source_target_pairs={{0,2},{1,3},{2,0},{3,1},{4,6},{5,7},{6,4},{7,5},{8,10},{9,11},{10,... | collective-permute-start | bytes 3145736 | tf_op jit(solution)/shard_map/ppermute | solution.py:273
  90.7 24.9 %collective-permute-start.5 = (bf16[128,4096]{1,0:T(8,128)(2,1)}, bf16[128,4096]{1,0:T(8,128)(2,1)}, u32[]{:S(2)}, u32[]{:S(2)}) collective-permute-start(bf16[128,4096]{1,0:T(8,128)(2,1)} %collective-permute-done.4.refs_6_), channel_id=1, source_target_pairs={{0,16},{16,0},{1,17},{17,1},{2,18},{18,2},{3,19},{19,3},{4,20},{20... | collective-permute-start | bytes 3145736 | tf_op jit(solution)/shard_map/ppermute | solution.py:314
  92.2 73.1 %collective-permute-start.3 = (bf16[256,4096]{1,0:T(8,128)(2,1)}, bf16[256,4096]{1,0:T(8,128)(2,1)}, u32[]{:S(2)}, u32[]{:S(2)}) collective-permute-start(bf16[256,4096]{1,0:T(8,128)(2,1)} %refs_4_.3), channel_id=1, source_target_pairs={{0,1},{1,0},{2,3},{3,2},{4,5},{5,4},{6,7},{7,6},{8,9},{9,8},{10,11... | collective-permute-start | bytes 6291464 | tf_op jit(solution)/shard_map/ppermute | solution.py:273
  106.6 50.2 %collective-permute-start.6 = (bf16[128,4096]{1,0:T(8,128)(2,1)}, bf16[128,4096]{1,0:T(8,128)(2,1)}, u32[]{:S(2)}, u32[]{:S(2)}) collective-permute-start(bf16[128,4096]{1,0:T(8,128)(2,1)} %collective-permute-done.4.refs_6_), channel_id=1, source_target_pairs={{0,1},{1,0},{2,3},{3,2},{4,5},{5,4},{6,7},{7,6},{8,9},{9,8},{10,11... | collective-permute-start | bytes 3145736 | tf_op jit(solution)/shard_map/ppermute | solution.py:273
  115.6 50.2 %collective-permute-start.7 = (bf16[128,4096]{1,0:T(8,128)(2,1)}, bf16[128,4096]{1,0:T(8,128)(2,1)}, u32[]{:S(2)}, u32[]{:S(2)}) collective-permute-start(bf16[128,4096]{1,0:T(8,128)(2,1)} %collective-permute-done.5.refs_7_), channel_id=1, source_target_pairs={{0,1},{1,0},{2,3},{3,2},{4,5},{5,4},{6,7},{7,6},{8,9},{9,8},{10,11... | collective-permute-start | bytes 3145736 | tf_op jit(solution)/shard_map/ppermute | solution.py:273
  115.6 12.7 %copy-start = (bf16[16,2,128,256]{3,2,1,0:T(8,128)(2,1)}, bf16[16,2,128,256]{3,2,1,0:T(8,128)(2,1)S(1)}, u32[]{:S(2)}) copy-start(bf16[16,2,128,256]{3,2,1,0:T(8,128)(2,1)S(1)} %all-to-all-done.1.kv_ref) | copy-start | bytes 6291460
  115.6 1.1 copy-start.2
  116.8 0.7 copy-start.3
  132.1 1.0 copy-start.1
  133.1 4.9 %copy-start.19 = (s32[512]{0:T(512)S(1)}, s32[512]{0:T(512)}, u32[]{:S(2)}) copy-start(s32[512]{0:T(512)} %param.18) | copy-start | bytes 6148
  133.1 136.4 %all-to-all-start.2 = ((bf16[16,128,256]{2,1,0:T(8,128)(2,1)}), bf16[16,128,256]{2,1,0:T(8,128)(2,1)S(1)}, u32[]{:S(2)}, u32[]{:S(2)}) async-start(bf16[16,128,256]{2,1,0:T(8,128)(2,1)} %copy-done.1), calls=%async_computation.2 | async-start | bytes 2097152 | tf_op jit(solution)/shard_map/all_to_all | solution.py:487
  154.7 11.1 %collective-permute-start.8 = (bf16[4,2,32,256]{3,2,1,0:T(8,128)(2,1)}, bf16[4,2,32,256]{3,2,1,0:T(8,128)(2,1)S(1)}, u32[]{:S(2)}, u32[]{:S(2)}) collective-permute-start(bf16[4,2,32,256]{3,2,1,0:T(8,128)(2,1)} %get-tuple-element.57), channel_id=1, source_target_pairs={{0,1},{1,0},{2,3},{3,2},{4,5},{5,4},{6,7},{7,6},{8,9},{9,8},{10,11... | collective-permute-start | bytes 393224 | tf_op jit(solution)/shard_map/ppermute | solution.py:273
  155.1 10.7 %collective-permute-start.9 = (bf16[4,2,32,256]{3,2,1,0:T(8,128)(2,1)}, bf16[4,2,32,256]{3,2,1,0:T(8,128)(2,1)S(1)}, u32[]{:S(2)}, u32[]{:S(2)}) collective-permute-start(bf16[4,2,32,256]{3,2,1,0:T(8,128)(2,1)} %get-tuple-element.58), channel_id=1, source_target_pairs={{0,2},{1,3},{2,0},{3,1},{4,6},{5,7},{6,4},{7,5},{8,10},{9,11},{10,... | collective-permute-start | bytes 393224 | tf_op jit(solution)/shard_map/ppermute | solution.py:273
  156.8 9.3 %collective-permute-start.10 = (bf16[4,2,32,256]{3,2,1,0:T(8,128)(2,1)}, bf16[4,2,32,256]{3,2,1,0:T(8,128)(2,1)S(1)}, u32[]{:S(2)}, u32[]{:S(2)}) collective-permute-start(bf16[4,2,32,256]{3,2,1,0:T(8,128)(2,1)} %get-tuple-element.59), channel_id=1, source_target_pairs={{0,3},{1,2},{2,1},{3,0},{4,7},{5,6},{6,5},{7,4},{8,11},{9,10},{10,... | collective-permute-start | bytes 393224 | tf_op jit(solution)/shard_map/ppermute | solution.py:273
  165.3 13.1 %collective-permute-start = (bf16[4,2,32,256]{3,2,1,0:T(8,128)(2,1)}, bf16[4,2,32,256]{3,2,1,0:T(8,128)(2,1)S(1)}, u32[]{:S(2)}, u32[]{:S(2)}) collective-permute-start(bf16[4,2,32,256]{3,2,1,0:T(8,128)(2,1)} %get-tuple-element.52), channel_id=1, source_target_pairs={{0,1},{1,0},{2,3},{3,2},{4,5},{5,4},{6,7},{7,6},{8,9},{9,8},{10,11... | collective-permute-start | bytes 393224 | tf_op jit(solution)/shard_map/ppermute | solution.py:273
  165.8 0.7 copy-start.14
  165.9 0.7 copy-start.15
  166.1 0.6 copy-start.17
  166.7 11.7 %copy-start.23 = (bf16[4,2,32,256]{3,2,1,0:T(8,128)(2,1)S(1)}, bf16[4,2,32,256]{3,2,1,0:T(8,128)(2,1)}, u32[]{:S(2)}) copy-start(bf16[4,2,32,256]{3,2,1,0:T(8,128)(2,1)} %get-tuple-element.53) | copy-start | bytes 393220
  166.7 16.8 %copy-start.22 = (bf16[4096]{0:T(1024)(128)(2,1)S(1)}, bf16[4096]{0:T(1024)(128)(2,1)}, u32[]{:S(2)}) copy-start(bf16[4096]{0:T(1024)(128)(2,1)} %param.21) | copy-start | bytes 24580
  174.3 23.7 %collective-permute-start.11 = (bf16[2,32,4096]{2,1,0:T(8,128)(2,1)}, bf16[2,32,4096]{2,1,0:T(8,128)(2,1)S(1)}, u32[]{:S(2)}, u32[]{:S(2)}) collective-permute-start(bf16[2,32,4096]{2,1,0:T(8,128)(2,1)} %get-tuple-element.60), channel_id=1, source_target_pairs={{0,4},{1,5},{2,6},{3,7},{4,0},{5,1},{6,2},{7,3},{8,12},{9,13},{10,... | collective-permute-start | bytes 1572872 | tf_op jit(solution)/shard_map/ppermute | solution.py:273
  175.8 27.8 %collective-permute-start.13 = (bf16[2,32,4096]{2,1,0:T(8,128)(2,1)}, bf16[2,32,4096]{2,1,0:T(8,128)(2,1)S(1)}, u32[]{:S(2)}, u32[]{:S(2)}) collective-permute-start(bf16[2,32,4096]{2,1,0:T(8,128)(2,1)} %get-tuple-element.64), channel_id=1, source_target_pairs={{0,4},{1,5},{2,6},{3,7},{4,0},{5,1},{6,2},{7,3},{8,12},{9,13},{10,... | collective-permute-start | bytes 1572872 | tf_op jit(solution)/shard_map/ppermute | solution.py:273
  176.4 46.7 %collective-permute-start.15 = (bf16[2,32,4096]{2,1,0:T(8,128)(2,1)}, bf16[2,32,4096]{2,1,0:T(8,128)(2,1)S(1)}, u32[]{:S(2)}, u32[]{:S(2)}) collective-permute-start(bf16[2,32,4096]{2,1,0:T(8,128)(2,1)} %get-tuple-element.68), channel_id=1, source_target_pairs={{0,4},{1,5},{2,6},{3,7},{4,0},{5,1},{6,2},{7,3},{8,12},{9,13},{10,... | collective-permute-start | bytes 1572872 | tf_op jit(solution)/shard_map/ppermute | solution.py:273
  177.9 55.8 %collective-permute-start.17 = (bf16[2,32,4096]{2,1,0:T(8,128)(2,1)}, bf16[2,32,4096]{2,1,0:T(8,128)(2,1)S(1)}, u32[]{:S(2)}, u32[]{:S(2)}) collective-permute-start(bf16[2,32,4096]{2,1,0:T(8,128)(2,1)} %get-tuple-element.72), channel_id=1, source_target_pairs={{0,4},{1,5},{2,6},{3,7},{4,0},{5,1},{6,2},{7,3},{8,12},{9,13},{10,... | collective-permute-start | bytes 1572872 | tf_op jit(solution)/shard_map/ppermute | solution.py:273
  178.4 11.0 %copy-start.13 = (bf16[4,2,32,256]{3,2,1,0:T(8,128)(2,1)}, bf16[4,2,32,256]{3,2,1,0:T(8,128)(2,1)S(1)}, u32[]{:S(2)}) copy-start(bf16[4,2,32,256]{3,2,1,0:T(8,128)(2,1)S(1)} %collective-permute-done.refs_1_) | copy-start | bytes 393220
  178.4 5.0 %collective-permute-start.1 = (bf16[4,2,32,256]{3,2,1,0:T(8,128)(2,1)S(1)}, bf16[4,2,32,256]{3,2,1,0:T(8,128)(2,1)S(1)}, u32[]{:S(2)}, u32[]{:S(2)}) collective-permute-start(bf16[4,2,32,256]{3,2,1,0:T(8,128)(2,1)S(1)} %copy-done.23), channel_id=1, source_target_pairs={{0,2},{1,3},{2,0},{3,1},{4,6},{5,7},{6,4},{7,5},{8,10},{9,11},{10,... | collective-permute-start | bytes 393224 | tf_op jit(solution)/shard_map/ppermute | solution.py:273
  183.4 6.0 %copy-start.16 = (bf16[4,2,32,256]{3,2,1,0:T(8,128)(2,1)}, bf16[4,2,32,256]{3,2,1,0:T(8,128)(2,1)S(1)}, u32[]{:S(2)}) copy-start(bf16[4,2,32,256]{3,2,1,0:T(8,128)(2,1)S(1)} %collective-permute-done.1.refs_2_) | copy-start | bytes 393220
  183.4 6.0 %collective-permute-start.2 = (bf16[4,2,32,256]{3,2,1,0:T(8,128)(2,1)}, bf16[4,2,32,256]{3,2,1,0:T(8,128)(2,1)S(1)}, u32[]{:S(2)}, u32[]{:S(2)}) collective-permute-start(bf16[4,2,32,256]{3,2,1,0:T(8,128)(2,1)} %get-tuple-element.54), channel_id=1, source_target_pairs={{0,3},{1,2},{2,1},{3,0},{4,7},{5,6},{6,5},{7,4},{8,11},{9,10},{10,... | collective-permute-start | bytes 393224 | tf_op jit(solution)/shard_map/ppermute | solution.py:273
  189.4 0.7 copy-start.18
  198.0 0.8 copy-start.8
  201.2 65.4 %collective-permute-start.12 = (bf16[1,32,4096]{2,1,0:T(8,128)(2,1)}, bf16[1,32,4096]{2,1,0:T(8,128)(2,1)S(1)}, u32[]{:S(2)}, u32[]{:S(2)}) collective-permute-start(bf16[1,32,4096]{2,1,0:T(8,128)(2,1)} %get-tuple-element.62), channel_id=1, source_target_pairs={{0,8},{1,9},{2,10},{3,11},{4,12},{5,13},{6,14},{7,15},{8,0},{9,1},... | collective-permute-start | bytes 786440 | tf_op jit(solution)/shard_map/ppermute | solution.py:273
  203.6 0.8 copy-start.7
  206.8 56.9 %collective-permute-start.14 = (bf16[1,32,4096]{2,1,0:T(8,128)(2,1)}, bf16[1,32,4096]{2,1,0:T(8,128)(2,1)S(1)}, u32[]{:S(2)}, u32[]{:S(2)}) collective-permute-start(bf16[1,32,4096]{2,1,0:T(8,128)(2,1)} %get-tuple-element.66), channel_id=1, source_target_pairs={{0,8},{1,9},{2,10},{3,11},{4,12},{5,13},{6,14},{7,15},{8,0},{9,1},... | collective-permute-start | bytes 786440 | tf_op jit(solution)/shard_map/ppermute | solution.py:273
  223.1 0.8 copy-start.6
  226.3 34.4 %collective-permute-start.16 = (bf16[1,32,4096]{2,1,0:T(8,128)(2,1)}, bf16[1,32,4096]{2,1,0:T(8,128)(2,1)S(1)}, u32[]{:S(2)}, u32[]{:S(2)}) collective-permute-start(bf16[1,32,4096]{2,1,0:T(8,128)(2,1)} %get-tuple-element.70), channel_id=1, source_target_pairs={{0,8},{1,9},{2,10},{3,11},{4,12},{5,13},{6,14},{7,15},{8,0},{9,1},... | collective-permute-start | bytes 786440 | tf_op jit(solution)/shard_map/ppermute | solution.py:273
  233.6 0.8 copy-start.5
  236.8 21.0 %collective-permute-start.18 = (bf16[1,32,4096]{2,1,0:T(8,128)(2,1)}, bf16[1,32,4096]{2,1,0:T(8,128)(2,1)S(1)}, u32[]{:S(2)}, u32[]{:S(2)}) collective-permute-start(bf16[1,32,4096]{2,1,0:T(8,128)(2,1)} %get-tuple-element.74), channel_id=1, source_target_pairs={{0,8},{1,9},{2,10},{3,11},{4,12},{5,13},{6,14},{7,15},{8,0},{9,1},... | collective-permute-start | bytes 786440 | tf_op jit(solution)/shard_map/ppermute | solution.py:273
  257.7 0.7 copy-start.12
  260.7 0.7 copy-start.11
  263.6 0.7 copy-start.10
  266.6 0.7 copy-start.9
  269.5 1.0 copy-start.4

commit v7 on v6

--- a/solution.py
+++ b/solution.py
@@ -17,9 +17,6 @@
 
 F32 = jnp.float32
 BF16 = jnp.bfloat16
-
-
-GRANT = pltpu.CompilerParams(vmem_limit_bytes=28 << 20)
 
 
 def call(body, grid, in_specs, out_specs, out_shape, scratch=(), flops=0, moved=0, exps=0):
@@ -221,8 +218,8 @@
 def halve_body(place_ref, keep_ref, got_ref, send_ref, kept_ref):
     bit = place_ref[0]
     for pair in range(send_ref.shape[0]):
-        first = keep_ref[2 * pair] + got_ref[2 * pair].astype(F32)
-        second = keep_ref[2 * pair + 1] + got_ref[2 * pair + 1].astype(F32)
+        first = keep_ref[2 * pair].astype(F32) + got_ref[2 * pair].astype(F32)
+        second = keep_ref[2 * pair + 1].astype(F32) + got_ref[2 * pair + 1].astype(F32)
         kept_ref[pair] = jnp.where(bit == 0, first, second)
         send_ref[pair] = jnp.where(bit == 0, second, first).astype(BF16)
 
@@ -320,6 +317,7 @@
 
     cos_r, sin_r = tables(prompt_len + block_index[0] * resp + jnp.arange(resp, dtype=jnp.int32))
     commit = jnp.broadcast_to(commit_step[:, None], (resp, HD))
+    commit = lax.optimization_barrier(commit)
     block = min(resp, 128)
     row_block = pl.BlockSpec((block, width), lambda i: (i, 0))
     wide = jax.ShapeDtypeStruct((resp, width), BF16)
@@ -411,7 +409,7 @@
                 + [pl.BlockSpec((w.shape[0], columns), lambda j, *_: (0, j)) for w in weights],
                 out_specs=[pl.BlockSpec((blocks, per, columns), lambda j, *_: (0, 0, j))] * STEPS,
             ),
-            out_shape=[jax.ShapeDtypeStruct((blocks, per, model), F32 if kept else BF16)] * STEPS,
+            out_shape=[jax.ShapeDtypeStruct((blocks, per, model), BF16)] * STEPS,
             name="output_projection",
             cost_estimate=pl.CostEstimate(
                 flops=STEPS * resp * model * width, bytes_accessed=2 * lows * width * model, transcendentals=0
@@ -460,12 +458,14 @@
     for head in range(heads):
         of_head = functools.partial(lambda head, *_: (0, head), head)
         of_kv = functools.partial(lambda head, *_: (0, 0, 0, head), head)
-        for turn in range(n // blocks_of_q):
-            of_block = functools.partial(lambda head, turn, *_: (turn, 0, head), head, turn)
+        turns = n // blocks_of_q
+        for turn in range(turns if head == 0 else 1):
+            count = 1 if head == 0 else turns
+            of_block = functools.partial(lambda head, turn, i: (turn + i, 0, head), head, turn)
             earlier = [] if prompt_context is None else [prompt_context]
             prompt_context = pl.pallas_call(
                 functools.partial(prompt_body, chunk),
-                grid=(1,),
+                grid=(count,),
                 in_specs=[
                     pl.BlockSpec((blocks_of_q, rows, HD), of_block),
                     pl.BlockSpec((n, 2, rows, HD), of_kv),
@@ -476,12 +476,11 @@
                 out_specs=pl.BlockSpec((blocks_of_q, rows, HD), of_block),
                 out_shape=jax.ShapeDtypeStruct((n, rows, width), BF16),
                 name="prompt_attention",
-                compiler_params=GRANT,
                 input_output_aliases={4: 0} if earlier else {},
                 cost_estimate=pl.CostEstimate(
-                    flops=4 * blocks_of_q * rows * HD * (prompt_len + resp),
-                    bytes_accessed=4 * prompt_len * HD + 4 * blocks_of_q * rows * HD,
-                    transcendentals=blocks_of_q * rows * (prompt_len + resp),
+                    flops=4 * count * blocks_of_q * rows * HD * (prompt_len + resp),
+                    bytes_accessed=4 * prompt_len * HD + 4 * count * blocks_of_q * rows * HD,
+                    transcendentals=count * blocks_of_q * rows * (prompt_len + resp),
                 ),
             )(q_heads, kv, km, vm, *earlier)
     back = lax.all_to_all(prompt_context, "seq", 0, 0, tiled=True)

time: 275 us -> 278 us (1.011)
  Pallas kernels: 93.1 us -> 96.4 us
    pallas_call x4 -> x3, Pallas kernels: 14.7 us -> 19.2 us  [per_device(): pl.pallas_call(functools.partial(prompt_body, chunk), grid=(count,), in_s...]
    unnamed x48 -> x46, local copies, waits for them, and re-layouts: 10.4 us -> 10 us
  transfers between devices with their start and end apart: 22 -> 22, of which waited for: 9 -> 9; matrix products, arithmetic and copies ran while one was open for 4% -> 3% of each run, Pallas kernels for 31% -> 32%
where the time goes in v7:
time: 278 us; the launch traced here: 277 us
  waiting for transfers between devices  122 us (44%)
  Pallas kernels  96.4 us (35%)
  starting transfers between devices  37.1 us (13%)
  local copies, waits for them, and re-layouts  16.4 us (6%)
  other arithmetic  3.69 us (1%)
    ppermute x18, waiting for transfers between devices, swap(): return lax.ppermute(x, 'seq', [(i, i ^ bit) for i in range(n)])  94.6 us
    pallas_call x3, Pallas kernels, per_device(): pl.pallas_call(functools.partial(prompt_body, chunk), grid=(count,), in_s...  19.2 us
    all_to_all x1, waiting for transfers between devices, per_device(): q_heads = lax.all_to_all(q_send, 'seq', 0, 0, tiled=True)  18.8 us
    pallas_call x2, Pallas kernels, per_device(): pl.pallas_call(functools.partial(response_body, 2 * chunk), grid_spec=plt...  17 us
    ppermute x18, starting transfers between devices, swap(): return lax.ppermute(x, 'seq', [(i, i ^ bit) for i in range(n)])  16.5 us
    pallas_call x2, Pallas kernels, per_device(): pl.pallas_call(functools.partial(output_body, lows, split), grid_spec=plt...  15 us
    pallas_call x1, Pallas kernels, per_device(): call(project_body, (resp // block,), [pl.BlockSpec((block, model), lambda...  10.4 us
    unnamed x46, local copies, waits for them, and re-layouts  10 us
  transfers between devices with their start and end apart: 22, of which 9 were waited for; matrix products, arithmetic and copies ran while one was open for 3% of the time, Pallas kernels for 32%

profile of v7, /device:TPU:0, one launch (start us, length us, event | category | flops | bytes accessed | tf_op | source)
XLA Modules:
  0.0 276.8 jit_solution(17836342941601133922)
XLA Ops:
  1.7 3.7 %shard_map.148 = bf16[16,128,256]{2,1,0:T(8,128)(2,1)} custom-call(bf16[128,4096]{1,0:T(8,128)(2,1)} %q_ref.1, f32[128,128]{1,0:T(8,128)} %get-tuple-element.89.cos_ref, f32[128,128]{1,0:T(8,128)} %get-tuple-element.90.sin_ref), custom_call_target="tpu_custom_call" | custom-call | flops 3145728 | bytes 2097152 | tf_op jit(solution)/shard_map/pallas_call | solution.py:289
  5.5 7.4 %all-to-all-start = ((bf16[16,128,256]{2,1,0:T(8,128)(2,1)}), bf16[16,128,256]{2,1,0:T(8,128)(2,1)S(1)}, u32[]{:S(2)}, u32[]{:S(2)}) async-start(bf16[16,128,256]{2,1,0:T(8,128)(2,1)} %shard_map.148), calls=%async_computation | async-start | bytes 2097152 | tf_op jit(solution)/shard_map/all_to_all | solution.py:302
  12.9 4.1 %shard_map.149 = bf16[16,2,128,256]{3,2,1,0:T(8,128)(2,1)} custom-call(bf16[128,4096]{1,0:T(8,128)(2,1)} %k_ref.1, bf16[128,4096]{1,0:T(8,128)(2,1)} %v_ref.1, f32[128,128]{1,0:T(8,128)} %get-tuple-element.89.cos_ref, f32[128,128]{1,0:T(8,128)} %get-tuple-element.90.sin_ref), custom_call_target="tpu_custom_call" | custom-call | flops 3145728 | bytes 4194304 | tf_op jit(solution)/shard_map/pallas_call | solution.py:274
  17.0 18.8 %all-to-all-done.q_ref = bf16[16,128,256]{2,1,0:T(8,128)(2,1)S(1)} async-done(((bf16[16,128,256]{2,1,0:T(8,128)(2,1)}), bf16[16,128,256]{2,1,0:T(8,128)(2,1)S(1)}, u32[]{:S(2)}, u32[]{:S(2)}) %all-to-all-start) | async-done | bytes 1048608 | tf_op jit(solution)/shard_map/all_to_all | solution.py:302
  35.8 1.0 copy-done.3
  36.7 6.8 %all-to-all-start.1 = ((bf16[16,2,128,256]{3,2,1,0:T(8,128)(2,1)}), bf16[16,2,128,256]{3,2,1,0:T(8,128)(2,1)S(1)}, u32[]{:S(2)}, u32[]{:S(2)}) async-start(bf16[16,2,128,256]{3,2,1,0:T(8,128)(2,1)} %shard_map.149), calls=%async_computation.1 | async-start | bytes 4194304 | tf_op jit(solution)/shard_map/all_to_all | solution.py:288
  43.6 1.3 constant_dynamic-slice_fusion
  44.9 2.0 collective-permute-start.4
  46.9 44.7 %collective-permute-done.4.refs_6_ = bf16[128,4096]{1,0:T(8,128)(2,1)S(1)} collective-permute-done((bf16[128,4096]{1,0:T(8,128)(2,1)S(1)}, bf16[128,4096]{1,0:T(8,128)(2,1)S(1)}, u32[]{:S(2)}, u32[]{:S(2)}) %collective-permute-start.4) | collective-permute-done | bytes 1048608 | tf_op jit(solution)/shard_map/ppermute | solution.py:270
  91.6 1.5 collective-permute-start.5
  95.0 1.0 fusion
  96.0 1.0 pad_maximum_fusion
  97.0 10.4 %shard_map.150 = (bf16[512,256]{1,0:T(8,128)(2,1)}, bf16[512,256]{1,0:T(8,128)(2,1)}, bf16[512,256]{1,0:T(8,128)(2,1)}, bf16[512,256]{1,0:T(8,128)(2,1)}, bf16[5...) custom-call(bf16[512,4096]{1,0:T(8,128)(2,1)} %embed_ref.1, bf16[1,4096]{1,0:T(2,128)(2,1)} %broadcast_in_dim.10.mask_ref, ...), custom_call_target="tpu_custom_call" | custom-call | flops 3221225472 | bytes 10485760 | tf_op jit(solution)/shard_map/pallas_call | solution.py:324
  108.0 8.3 %collective-permute-done.5.refs_7_ = bf16[128,4096]{1,0:T(8,128)(2,1)} collective-permute-done((bf16[128,4096]{1,0:T(8,128)(2,1)S(1)}, bf16[128,4096]{1,0:T(8,128)(2,1)}, u32[]{:S(2)}, u32[]{:S(2)}) %collective-permute-start.5) | collective-permute-done | bytes 1048608 | tf_op jit(solution)/shard_map/ppermute | solution.py:311
  116.3 1.4 copy-done
  117.6 5.3 %prompt_attention.3.refs_0_ = bf16[16,128,256]{2,1,0:T(8,128)(2,1)} custom-call(bf16[16,128,256]{2,1,0:T(8,128)(2,1)} %copy-done.3, bf16[16,2,128,256]{3,2,1,0:T(8,128)(2,1)} %copy-done, bf16[512,256]{1,0:T(8,128)(2,1)} %get-tuple-element.43.km_ref, bf16[16,256]{1,0:T(8,128)(2,1)} %get-tuple-element.44.vm_ref), custom_call_target="tpu_custom_call" | custom-call | flops 1342177280 | bytes 1572864 | tf_op jit(solution)/shard_map/prompt_attention/pallas_call | solution.py:466
  122.9 5.3 %prompt_attention.4.refs_0_ = bf16[16,128,256]{2,1,0:T(8,128)(2,1)} custom-call(bf16[16,128,256]{2,1,0:T(8,128)(2,1)} %copy-done.3, bf16[16,2,128,256]{3,2,1,0:T(8,128)(2,1)} %copy-done, bf16[512,256]{1,0:T(8,128)(2,1)} %get-tuple-element.43.km_ref, bf16[16,256]{1,0:T(8,128)(2,1)} %get-tuple-element.44.vm_ref, ...), custom_call_target="tpu_custom_call", output_to_operand_aliasing={{}: (4, {})} | custom-call | flops 1342177280 | bytes 1572864 | tf_op jit(solution)/shard_map/prompt_attention/pallas_call | solution.py:466
  128.2 8.6 %prompt_attention.5 = bf16[16,128,256]{2,1,0:T(8,128)(2,1)} custom-call(bf16[16,128,256]{2,1,0:T(8,128)(2,1)} %copy-done.3, bf16[16,2,128,256]{3,2,1,0:T(8,128)(2,1)} %copy-done, bf16[512,256]{1,0:T(8,128)(2,1)} %get-tuple-element.43.km_ref, bf16[16,256]{1,0:T(8,128)(2,1)} %get-tuple-element.44.vm_ref, ...), custom_call_target="tpu_custom_call", output_to_operand_aliasing={{}: (4, {})} | custom-call | flops 2684354560 | bytes 2097152 | tf_op jit(solution)/shard_map/prompt_attention/pallas_call | solution.py:466
  136.8 4.9 %all-to-all-start.2 = ((bf16[16,128,256]{2,1,0:T(8,128)(2,1)}), bf16[16,128,256]{2,1,0:T(8,128)(2,1)S(1)}, u32[]{:S(2)}, u32[]{:S(2)}) async-start(bf16[16,128,256]{2,1,0:T(8,128)(2,1)} %prompt_attention.5), calls=%async_computation.2 | async-start | bytes 2097152 | tf_op jit(solution)/shard_map/all_to_all | solution.py:486
  141.7 0.9 broadcast_in_dim.14.commit_ref
  142.6 5.8 %shard_map.152 = (f32[4,512,256]{2,1,0:T(8,128)}, f32[512,256]{1,0:T(8,128)}) custom-call(bf16[512,256]{1,0:T(8,128)(2,1)} %get-tuple-element.45.qe_ref, bf16[512,256]{1,0:T(8,128)(2,1)} %get-tuple-element.46.qm_ref, bf16[512,256]{1,0:T(8,128)(2,1)} %get-tuple-element.47.ke_ref, bf16[512,256]{1,0:T(8,128)(2,1)} %get-tuple-element.43.km_ref, ...), custom_call_target="tpu_custom_call" | custom-call | flops 1073741824 | bytes 2621440 | tf_op jit(solution)/shard_map/pallas_call | solution.py:355
  149.0 8.5 %response_attention.3 = (bf16[4,2,32,256]{3,2,1,0:T(8,128)(2,1)}, bf16[4,2,32,256]{3,2,1,0:T(8,128)(2,1)}, bf16[4,2,32,256]{3,2,1,0:T(8,128)(2,1)}, bf16[4,2,32,256]{3,2,1,0:T(8,128)(2,1)}) custom-call(s32[3]{0:T(128)} %pad_add_fusion.place_ref, bf16[16,2,128,256]{3,2,1,0:T(8,128)(2,1)} %copy-done, bf16[2,2,128,256]{3,2,1,0:T(8,128)(2,1)} %bitcast.16, ...), custom_call_target="tpu_custom_call" | custom-call | flops 1073741824 | bytes 2097152 | tf_op jit(solution)/shard_map/response_attention/pallas_call | solution.py:374
  158.0 1.6 collective-permute-start.9
  159.6 8.5 %response_attention.2 = (bf16[4,2,32,256]{3,2,1,0:T(8,128)(2,1)}, bf16[4,2,32,256]{3,2,1,0:T(8,128)(2,1)}, bf16[4,2,32,256]{3,2,1,0:T(8,128)(2,1)}, bf16[4,2,32,256]{3,2,1,0:T(8,128)(2,1)}) custom-call(s32[3]{0:T(128)} %pad_add_fusion.place_ref, bf16[16,2,128,256]{3,2,1,0:T(8,128)(2,1)} %copy-done, bf16[2,2,128,256]{3,2,1,0:T(8,128)(2,1)} %bitcast.17, ...), custom_call_target="tpu_custom_call" | custom-call | flops 1073741824 | bytes 2097152 | tf_op jit(solution)/shard_map/response_attention/pallas_call | solution.py:374
  169.6 7.6 %output_projection.3 = (bf16[2,32,4096]{2,1,0:T(8,128)(2,1)}, bf16[2,32,4096]{2,1,0:T(8,128)(2,1)}, bf16[2,32,4096]{2,1,0:T(8,128)(2,1)}, bf16[2,32,4096]{2,1,0:T(8,128)(2,1)}) custom-call(s32[3]{0:T(128)} %pad_add_fusion.place_ref, bf16[4,2,32,256]{3,2,1,0:T(8,128)(2,1)} %get-tuple-element.56.refs_0_, bf16[4,2,32,256]{3,2,1,0:T(8,128)(2,1)} %copy-done.13, ...), custom_call_target="tpu_custom_call" | custom-call | flops 2147483648 | bytes 8388608 | tf_op jit(solution)/shard_map/output_projection/pallas_call | solution.py:403
  177.1 1.6 collective-permute-start.11
  179.2 1.5 collective-permute-start.15
  181.3 1.6 collective-permute-start.1
  182.8 3.5 %collective-permute-done.1.refs_2_ = bf16[4,2,32,256]{3,2,1,0:T(8,128)(2,1)S(1)} collective-permute-done((bf16[4,2,32,256]{3,2,1,0:T(8,128)(2,1)S(1)}, bf16[4,2,32,256]{3,2,1,0:T(8,128)(2,1)S(1)}, u32[]{:S(2)}, u32[]{:S(2)}) %collective-permute-start.1) | collective-permute-done | bytes 131104 | tf_op jit(solution)/shard_map/ppermute | solution.py:270
  187.0 5.3 %collective-permute-done.2.refs_3_ = bf16[4,2,32,256]{3,2,1,0:T(8,128)(2,1)S(1)} collective-permute-done((bf16[4,2,32,256]{3,2,1,0:T(8,128)(2,1)}, bf16[4,2,32,256]{3,2,1,0:T(8,128)(2,1)S(1)}, u32[]{:S(2)}, u32[]{:S(2)}) %collective-permute-start.2) | collective-permute-done | bytes 131104 | tf_op jit(solution)/shard_map/ppermute | solution.py:270
  192.9 7.4 %output_projection.2 = (bf16[2,32,4096]{2,1,0:T(8,128)(2,1)}, bf16[2,32,4096]{2,1,0:T(8,128)(2,1)}, bf16[2,32,4096]{2,1,0:T(8,128)(2,1)}, bf16[2,32,4096]{2,1,0:T(8,128)(2,1)}) custom-call(s32[3]{0:T(128)} %pad_add_fusion.place_ref, bf16[4,2,32,256]{3,2,1,0:T(8,128)(2,1)} %get-tuple-element.51.refs_0_, bf16[4,2,32,256]{3,2,1,0:T(8,128)(2,1)} %copy-done.12, ...), custom_call_target="tpu_custom_call" | custom-call | flops 2147483648 | bytes 8388608 | tf_op jit(solution)/shard_map/output_projection/pallas_call | solution.py:403
  201.1 2.2 halve.4
  203.3 2.4 collective-permute-start.12
  206.6 2.2 halve.5
  209.3 16.6 %collective-permute-done.15.got_ref = bf16[2,32,4096]{2,1,0:T(8,128)(2,1)S(1)} collective-permute-done((bf16[2,32,4096]{2,1,0:T(8,128)(2,1)}, bf16[2,32,4096]{2,1,0:T(8,128)(2,1)S(1)}, u32[]{:S(2)}, u32[]{:S(2)}) %collective-permute-start.15) | collective-permute-done | bytes 524320 | tf_op jit(solution)/shard_map/ppermute | solution.py:270
  226.7 2.2 halve.6
  228.9 1.5 collective-permute-start.16
  230.4 6.3 %collective-permute-done.17.got_ref = bf16[2,32,4096]{2,1,0:T(8,128)(2,1)S(1)} collective-permute-done((bf16[2,32,4096]{2,1,0:T(8,128)(2,1)}, bf16[2,32,4096]{2,1,0:T(8,128)(2,1)S(1)}, u32[]{:S(2)}, u32[]{:S(2)}) %collective-permute-start.17) | collective-permute-done | bytes 524320 | tf_op jit(solution)/shard_map/ppermute | solution.py:270
  237.5 2.2 halve.7
  239.7 1.2 collective-permute-start.18
  240.9 1.7 constant_dynamic-slice_fusion.1.embed_ref
  242.6 18.0 %collective-permute-done.18.got_ref = bf16[1,32,4096]{2,1,0:T(8,128)(2,1)S(1)} collective-permute-done((bf16[1,32,4096]{2,1,0:T(8,128)(2,1)}, bf16[1,32,4096]{2,1,0:T(8,128)(2,1)S(1)}, u32[]{:S(2)}, u32[]{:S(2)}) %collective-permute-start.18) | collective-permute-done | bytes 262176 | tf_op jit(solution)/shard_map/ppermute | solution.py:270
  261.3 2.2 finish.4
  264.3 2.2 finish.5
  267.2 2.2 finish.6
  270.2 2.2 finish.7
  272.4 1.0 copy-done.2
  273.5 3.4 %shard_map.151 = bf16[128,4096]{1,0:T(8,128)(2,1)} custom-call(bf16[16,128,256]{2,1,0:T(8,128)(2,1)} %copy-done.2), custom_call_target="tpu_custom_call" | custom-call | bytes 2097152 | tf_op jit(solution)/shard_map/pallas_call | solution.py:512
  (78 shorter events, 14.3 us)
Async XLA Ops:
  5.5 30.3 %all-to-all-start = ((bf16[16,128,256]{2,1,0:T(8,128)(2,1)}), bf16[16,128,256]{2,1,0:T(8,128)(2,1)S(1)}, u32[]{:S(2)}, u32[]{:S(2)}) async-start(bf16[16,128,256]{2,1,0:T(8,128)(2,1)} %shard_map.148), calls=%async_computation | async-start | bytes 2097152 | tf_op jit(solution)/shard_map/all_to_all | solution.py:302
  35.8 1.0 copy-start.3
  36.7 79.5 %all-to-all-start.1 = ((bf16[16,2,128,256]{3,2,1,0:T(8,128)(2,1)}), bf16[16,2,128,256]{3,2,1,0:T(8,128)(2,1)S(1)}, u32[]{:S(2)}, u32[]{:S(2)}) async-start(bf16[16,2,128,256]{3,2,1,0:T(8,128)(2,1)} %shard_map.149), calls=%async_computation.1 | async-start | bytes 4194304 | tf_op jit(solution)/shard_map/all_to_all | solution.py:288
  43.5 50.2 %copy-start.18 = (bf16[4096]{0:T(1024)(128)(2,1)S(1)}, bf16[4096]{0:T(1024)(128)(2,1)}, u32[]{:S(2)}) copy-start(bf16[4096]{0:T(1024)(128)(2,1)} %param.17) | copy-start | bytes 24580
  43.5 50.8 %copy-start.19 = (bf16[4096]{0:T(1024)(128)(2,1)S(1)}, bf16[4096]{0:T(1024)(128)(2,1)}, u32[]{:S(2)}) copy-start(bf16[4096]{0:T(1024)(128)(2,1)} %param.20) | copy-start | bytes 24580
  44.9 46.7 %collective-permute-start.4 = (bf16[128,4096]{1,0:T(8,128)(2,1)S(1)}, bf16[128,4096]{1,0:T(8,128)(2,1)S(1)}, u32[]{:S(2)}, u32[]{:S(2)}) collective-permute-start(bf16[128,4096]{1,0:T(8,128)(2,1)S(1)} %constant_dynamic-slice_fusion), channel_id=1, source_target_pairs={{0,2},{1,3},{2,0},{3,1},{4,6},{5,7},{6,4},{7,5},{8,10},{9,11},{10,... | collective-permute-start | bytes 3145736 | tf_op jit(solution)/shard_map/ppermute | solution.py:270
  91.6 15.9 %copy-start.1 = (bf16[128,4096]{1,0:T(8,128)(2,1)}, bf16[128,4096]{1,0:T(8,128)(2,1)S(1)}, u32[]{:S(2)}) copy-start(bf16[128,4096]{1,0:T(8,128)(2,1)S(1)} %collective-permute-done.4.refs_6_) | copy-start | bytes 3145732
  91.6 24.7 %collective-permute-start.5 = (bf16[128,4096]{1,0:T(8,128)(2,1)S(1)}, bf16[128,4096]{1,0:T(8,128)(2,1)}, u32[]{:S(2)}, u32[]{:S(2)}) collective-permute-start(bf16[128,4096]{1,0:T(8,128)(2,1)S(1)} %collective-permute-done.4.refs_6_), channel_id=1, source_target_pairs={{0,16},{16,0},{1,17},{17,1},{2,18},{18,2},{3,19},{19,3},{4,20},{20... | collective-permute-start | bytes 3145736 | tf_op jit(solution)/shard_map/ppermute | solution.py:311
  93.1 75.0 %collective-permute-start.3 = (bf16[256,4096]{1,0:T(8,128)(2,1)}, bf16[256,4096]{1,0:T(8,128)(2,1)}, u32[]{:S(2)}, u32[]{:S(2)}) collective-permute-start(bf16[256,4096]{1,0:T(8,128)(2,1)} %refs_4_.3), channel_id=1, source_target_pairs={{0,1},{1,0},{2,3},{3,2},{4,5},{5,4},{6,7},{7,6},{8,9},{9,8},{10,11... | collective-permute-start | bytes 6291464 | tf_op jit(solution)/shard_map/ppermute | solution.py:270
  107.4 52.2 %collective-permute-start.6 = (bf16[128,4096]{1,0:T(8,128)(2,1)S(1)}, bf16[128,4096]{1,0:T(8,128)(2,1)}, u32[]{:S(2)}, u32[]{:S(2)}) collective-permute-start(bf16[128,4096]{1,0:T(8,128)(2,1)S(1)} %collective-permute-done.4.refs_6_), channel_id=1, source_target_pairs={{0,1},{1,0},{2,3},{3,2},{4,5},{5,4},{6,7},{7,6},{8,9},{9,8},{10,11... | collective-permute-start | bytes 3145736 | tf_op jit(solution)/shard_map/ppermute | solution.py:270
  116.3 52.4 %collective-permute-start.7 = (bf16[128,4096]{1,0:T(8,128)(2,1)}, bf16[128,4096]{1,0:T(8,128)(2,1)}, u32[]{:S(2)}, u32[]{:S(2)}) collective-permute-start(bf16[128,4096]{1,0:T(8,128)(2,1)} %collective-permute-done.5.refs_7_), channel_id=1, source_target_pairs={{0,1},{1,0},{2,3},{3,2},{4,5},{5,4},{6,7},{7,6},{8,9},{9,8},{10,11... | collective-permute-start | bytes 3145736 | tf_op jit(solution)/shard_map/ppermute | solution.py:270
  116.3 1.4 copy-start
  136.8 4.9 %copy-start.21 = (s32[512]{0:T(512)S(1)}, s32[512]{0:T(512)}, u32[]{:S(2)}) copy-start(s32[512]{0:T(512)} %param.18) | copy-start | bytes 6148
  136.8 135.6 %all-to-all-start.2 = ((bf16[16,128,256]{2,1,0:T(8,128)(2,1)}), bf16[16,128,256]{2,1,0:T(8,128)(2,1)S(1)}, u32[]{:S(2)}, u32[]{:S(2)}) async-start(bf16[16,128,256]{2,1,0:T(8,128)(2,1)} %prompt_attention.5), calls=%async_computation.2 | async-start | bytes 2097152 | tf_op jit(solution)/shard_map/all_to_all | solution.py:486
  157.5 11.1 %collective-permute-start.8 = (bf16[4,2,32,256]{3,2,1,0:T(8,128)(2,1)}, bf16[4,2,32,256]{3,2,1,0:T(8,128)(2,1)S(1)}, u32[]{:S(2)}, u32[]{:S(2)}) collective-permute-start(bf16[4,2,32,256]{3,2,1,0:T(8,128)(2,1)} %get-tuple-element.57), channel_id=1, source_target_pairs={{0,1},{1,0},{2,3},{3,2},{4,5},{5,4},{6,7},{7,6},{8,9},{9,8},{10,11... | collective-permute-start | bytes 393224 | tf_op jit(solution)/shard_map/ppermute | solution.py:270
  158.0 10.7 %collective-permute-start.9 = (bf16[4,2,32,256]{3,2,1,0:T(8,128)(2,1)}, bf16[4,2,32,256]{3,2,1,0:T(8,128)(2,1)S(1)}, u32[]{:S(2)}, u32[]{:S(2)}) collective-permute-start(bf16[4,2,32,256]{3,2,1,0:T(8,128)(2,1)} %get-tuple-element.58), channel_id=1, source_target_pairs={{0,2},{1,3},{2,0},{3,1},{4,6},{5,7},{6,4},{7,5},{8,10},{9,11},{10,... | collective-permute-start | bytes 393224 | tf_op jit(solution)/shard_map/ppermute | solution.py:270
  159.6 9.3 %collective-permute-start.10 = (bf16[4,2,32,256]{3,2,1,0:T(8,128)(2,1)}, bf16[4,2,32,256]{3,2,1,0:T(8,128)(2,1)S(1)}, u32[]{:S(2)}, u32[]{:S(2)}) collective-permute-start(bf16[4,2,32,256]{3,2,1,0:T(8,128)(2,1)} %get-tuple-element.59), channel_id=1, source_target_pairs={{0,3},{1,2},{2,1},{3,0},{4,7},{5,6},{6,5},{7,4},{8,11},{9,10},{10,... | collective-permute-start | bytes 393224 | tf_op jit(solution)/shard_map/ppermute | solution.py:270
  168.1 13.1 %collective-permute-start = (bf16[4,2,32,256]{3,2,1,0:T(8,128)(2,1)}, bf16[4,2,32,256]{3,2,1,0:T(8,128)(2,1)S(1)}, u32[]{:S(2)}, u32[]{:S(2)}) collective-permute-start(bf16[4,2,32,256]{3,2,1,0:T(8,128)(2,1)} %get-tuple-element.52), channel_id=1, source_target_pairs={{0,1},{1,0},{2,3},{3,2},{4,5},{5,4},{6,7},{7,6},{8,9},{9,8},{10,11... | collective-permute-start | bytes 393224 | tf_op jit(solution)/shard_map/ppermute | solution.py:270
  168.7 0.7 copy-start.13
  168.7 0.7 copy-start.14
  168.9 0.7 copy-start.16
  169.6 11.7 %copy-start.22 = (bf16[4,2,32,256]{3,2,1,0:T(8,128)(2,1)S(1)}, bf16[4,2,32,256]{3,2,1,0:T(8,128)(2,1)}, u32[]{:S(2)}) copy-start(bf16[4,2,32,256]{3,2,1,0:T(8,128)(2,1)} %get-tuple-element.53) | copy-start | bytes 393220
  169.6 16.8 %copy-start.20 = (bf16[4096]{0:T(1024)(128)(2,1)S(1)}, bf16[4096]{0:T(1024)(128)(2,1)}, u32[]{:S(2)}) copy-start(bf16[4096]{0:T(1024)(128)(2,1)} %param.21) | copy-start | bytes 24580
  177.1 23.2 %collective-permute-start.11 = (bf16[2,32,4096]{2,1,0:T(8,128)(2,1)}, bf16[2,32,4096]{2,1,0:T(8,128)(2,1)S(1)}, u32[]{:S(2)}, u32[]{:S(2)}) collective-permute-start(bf16[2,32,4096]{2,1,0:T(8,128)(2,1)} %get-tuple-element.60), channel_id=1, source_target_pairs={{0,4},{1,5},{2,6},{3,7},{4,0},{5,1},{6,2},{7,3},{8,12},{9,13},{10,... | collective-permute-start | bytes 1572872 | tf_op jit(solution)/shard_map/ppermute | solution.py:270
  178.7 27.1 %collective-permute-start.13 = (bf16[2,32,4096]{2,1,0:T(8,128)(2,1)}, bf16[2,32,4096]{2,1,0:T(8,128)(2,1)S(1)}, u32[]{:S(2)}, u32[]{:S(2)}) collective-permute-start(bf16[2,32,4096]{2,1,0:T(8,128)(2,1)} %get-tuple-element.64), channel_id=1, source_target_pairs={{0,4},{1,5},{2,6},{3,7},{4,0},{5,1},{6,2},{7,3},{8,12},{9,13},{10,... | collective-permute-start | bytes 1572872 | tf_op jit(solution)/shard_map/ppermute | solution.py:270
  179.2 46.7 %collective-permute-start.15 = (bf16[2,32,4096]{2,1,0:T(8,128)(2,1)}, bf16[2,32,4096]{2,1,0:T(8,128)(2,1)S(1)}, u32[]{:S(2)}, u32[]{:S(2)}) collective-permute-start(bf16[2,32,4096]{2,1,0:T(8,128)(2,1)} %get-tuple-element.68), channel_id=1, source_target_pairs={{0,4},{1,5},{2,6},{3,7},{4,0},{5,1},{6,2},{7,3},{8,12},{9,13},{10,... | collective-permute-start | bytes 1572872 | tf_op jit(solution)/shard_map/ppermute | solution.py:270
  180.7 56.0 %collective-permute-start.17 = (bf16[2,32,4096]{2,1,0:T(8,128)(2,1)}, bf16[2,32,4096]{2,1,0:T(8,128)(2,1)S(1)}, u32[]{:S(2)}, u32[]{:S(2)}) collective-permute-start(bf16[2,32,4096]{2,1,0:T(8,128)(2,1)} %get-tuple-element.72), channel_id=1, source_target_pairs={{0,4},{1,5},{2,6},{3,7},{4,0},{5,1},{6,2},{7,3},{8,12},{9,13},{10,... | collective-permute-start | bytes 1572872 | tf_op jit(solution)/shard_map/ppermute | solution.py:270
  181.3 11.0 %copy-start.12 = (bf16[4,2,32,256]{3,2,1,0:T(8,128)(2,1)}, bf16[4,2,32,256]{3,2,1,0:T(8,128)(2,1)S(1)}, u32[]{:S(2)}) copy-start(bf16[4,2,32,256]{3,2,1,0:T(8,128)(2,1)S(1)} %collective-permute-done.refs_1_) | copy-start | bytes 393220
  181.3 5.0 %collective-permute-start.1 = (bf16[4,2,32,256]{3,2,1,0:T(8,128)(2,1)S(1)}, bf16[4,2,32,256]{3,2,1,0:T(8,128)(2,1)S(1)}, u32[]{:S(2)}, u32[]{:S(2)}) collective-permute-start(bf16[4,2,32,256]{3,2,1,0:T(8,128)(2,1)S(1)} %copy-done.22), channel_id=1, source_target_pairs={{0,2},{1,3},{2,0},{3,1},{4,6},{5,7},{6,4},{7,5},{8,10},{9,11},{10,... | collective-permute-start | bytes 393224 | tf_op jit(solution)/shard_map/ppermute | solution.py:270
  186.3 6.0 %copy-start.15 = (bf16[4,2,32,256]{3,2,1,0:T(8,128)(2,1)}, bf16[4,2,32,256]{3,2,1,0:T(8,128)(2,1)S(1)}, u32[]{:S(2)}) copy-start(bf16[4,2,32,256]{3,2,1,0:T(8,128)(2,1)S(1)} %collective-permute-done.1.refs_2_) | copy-start | bytes 393220
  186.3 6.0 %collective-permute-start.2 = (bf16[4,2,32,256]{3,2,1,0:T(8,128)(2,1)}, bf16[4,2,32,256]{3,2,1,0:T(8,128)(2,1)S(1)}, u32[]{:S(2)}, u32[]{:S(2)}) collective-permute-start(bf16[4,2,32,256]{3,2,1,0:T(8,128)(2,1)} %get-tuple-element.54), channel_id=1, source_target_pairs={{0,3},{1,2},{2,1},{3,0},{4,7},{5,6},{6,5},{7,4},{8,11},{9,10},{10,... | collective-permute-start | bytes 393224 | tf_op jit(solution)/shard_map/ppermute | solution.py:270
  192.2 0.7 copy-start.17
  200.3 0.8 copy-start.7
  203.3 66.2 %collective-permute-start.12 = (bf16[1,32,4096]{2,1,0:T(8,128)(2,1)}, bf16[1,32,4096]{2,1,0:T(8,128)(2,1)S(1)}, u32[]{:S(2)}, u32[]{:S(2)}) collective-permute-start(bf16[1,32,4096]{2,1,0:T(8,128)(2,1)} %get-tuple-element.62), channel_id=1, source_target_pairs={{0,8},{1,9},{2,10},{3,11},{4,12},{5,13},{6,14},{7,15},{8,0},{9,1},... | collective-permute-start | bytes 786440 | tf_op jit(solution)/shard_map/ppermute | solution.py:270
  205.8 0.8 copy-start.6
  208.8 57.7 %collective-permute-start.14 = (bf16[1,32,4096]{2,1,0:T(8,128)(2,1)}, bf16[1,32,4096]{2,1,0:T(8,128)(2,1)S(1)}, u32[]{:S(2)}, u32[]{:S(2)}) collective-permute-start(bf16[1,32,4096]{2,1,0:T(8,128)(2,1)} %get-tuple-element.66), channel_id=1, source_target_pairs={{0,8},{1,9},{2,10},{3,11},{4,12},{5,13},{6,14},{7,15},{8,0},{9,1},... | collective-permute-start | bytes 786440 | tf_op jit(solution)/shard_map/ppermute | solution.py:270
  225.9 0.8 copy-start.5
  228.9 34.6 %collective-permute-start.16 = (bf16[1,32,4096]{2,1,0:T(8,128)(2,1)}, bf16[1,32,4096]{2,1,0:T(8,128)(2,1)S(1)}, u32[]{:S(2)}, u32[]{:S(2)}) collective-permute-start(bf16[1,32,4096]{2,1,0:T(8,128)(2,1)} %get-tuple-element.70), channel_id=1, source_target_pairs={{0,8},{1,9},{2,10},{3,11},{4,12},{5,13},{6,14},{7,15},{8,0},{9,1},... | collective-permute-start | bytes 786440 | tf_op jit(solution)/shard_map/ppermute | solution.py:270
  236.7 0.8 copy-start.4
  239.7 20.9 %collective-permute-start.18 = (bf16[1,32,4096]{2,1,0:T(8,128)(2,1)}, bf16[1,32,4096]{2,1,0:T(8,128)(2,1)S(1)}, u32[]{:S(2)}, u32[]{:S(2)}) collective-permute-start(bf16[1,32,4096]{2,1,0:T(8,128)(2,1)} %get-tuple-element.74), channel_id=1, source_target_pairs={{0,8},{1,9},{2,10},{3,11},{4,12},{5,13},{6,14},{7,15},{8,0},{9,1},... | collective-permute-start | bytes 786440 | tf_op jit(solution)/shard_map/ppermute | solution.py:270
  260.6 0.7 copy-start.11
  263.6 0.7 copy-start.10
  266.5 0.7 copy-start.9
  269.5 0.7 copy-start.8
  272.4 1.0 copy-start.2

commit v8 on v7

--- a/solution.py
+++ b/solution.py
@@ -148,9 +148,8 @@
         k = jnp.where(shown, ke_ref[...], km_ref[...])
         v = jnp.where(shown, ve_ref[...], mask_value)
         top, total, acc = merge(None, scores(q, k), v)
-        acc_ref[step] = acc
-        stats = jnp.where(lane == step, top, stats)
-        stats = jnp.where(lane == STEPS + step, total, stats)
+        acc_ref[step] = acc * (1.0 / total)
+        stats = jnp.where(lane == step, top + jnp.log2(total), stats)
     stats_ref[...] = stats
 
 
@@ -167,17 +166,14 @@
 
     revealed, stats = flat(commit_ref[...]), flat(stats_ref[...])
     both = over_prompt(None, jnp.concatenate([flat(qm_ref[...]), flat(qe_ref[...])], 0), kv_ref, chunk)
+    log_p = both[0] + jnp.log2(both[1])
+    mean_p = both[2] * (1.0 / both[1])
     for step in range(steps):
-        shown = revealed <= step
         one = revealed[:, 0:1] <= step
-        top_p = jnp.where(one, both[0][count:], both[0][:count])
-        total_p = jnp.where(one, both[1][count:], both[1][:count])
-        acc_p = jnp.where(shown, both[2][count:], both[2][:count])
-        top_r, total_r = stats[:, step : step + 1], stats[:, STEPS + step : STEPS + step + 1]
-        top = jnp.maximum(top_p, top_r)
-        keep_p, keep_r = jnp.exp2(top_p - top), jnp.exp2(top_r - top)
-        scale = 1.0 / (total_p * keep_p + total_r * keep_r)
-        scratch_ref[step] = acc_p * (keep_p * scale) + flat(acc_ref[step]) * (keep_r * scale)
+        from_prompt = jnp.where(revealed <= step, mean_p[count:], mean_p[:count])
+        gap = jnp.where(one, log_p[count:], log_p[:count]) - stats[:, step : step + 1]
+        share = 1.0 / (1.0 + jnp.exp2(gap))
+        scratch_ref[step] = from_prompt + share * (flat(acc_ref[step]) - from_prompt)
     for step in range(steps):
         for block in range(blocks):
             for k in range(lows):

time: 278 us -> 277 us (level)
  Pallas kernels: 96.4 us -> 93.4 us
  waiting for transfers between devices: 122 us -> 125 us
    ppermute x18, waiting for transfers between devices: 94.6 us -> 97.7 us  [swap(): return lax.ppermute(x, 'seq', [(i, i ^ bit) for i in range(n)])]
    pallas_call x2, Pallas kernels: 17 us -> 13.9 us  [per_device(): pl.pallas_call(functools.partial(response_body, 2 * chunk), grid_spec=plt...]
  transfers between devices with their start and end apart: 22 -> 22, of which waited for: 9 -> 10; matrix products, arithmetic and copies ran while one was open for 3% -> 3% of each run, Pallas kernels for 32% -> 31%
where the time goes in v8:
time: 277 us; the launch traced here: 276 us
  waiting for transfers between devices  125 us (45%)
  Pallas kernels  93.4 us (34%)
  starting transfers between devices  36.2 us (13%)
  local copies, waits for them, and re-layouts  16.4 us (6%)
  other arithmetic  3.69 us (1%)
    ppermute x18, waiting for transfers between devices, swap(): return lax.ppermute(x, 'seq', [(i, i ^ bit) for i in range(n)])  97.7 us
    pallas_call x3, Pallas kernels, per_device(): pl.pallas_call(functools.partial(prompt_body, chunk), grid=(count,), in_s...  19.2 us
    all_to_all x1, waiting for transfers between devices, per_device(): q_heads = lax.all_to_all(q_send, 'seq', 0, 0, tiled=True)  18.8 us
    ppermute x18, starting transfers between devices, swap(): return lax.ppermute(x, 'seq', [(i, i ^ bit) for i in range(n)])  15.6 us
    pallas_call x2, Pallas kernels, per_device(): pl.pallas_call(functools.partial(output_body, lows, split), grid_spec=plt...  15 us
    pallas_call x2, Pallas kernels, per_device(): pl.pallas_call(functools.partial(response_body, 2 * chunk), grid_spec=plt...  13.9 us
    pallas_call x1, Pallas kernels, per_device(): call(project_body, (resp // block,), [pl.BlockSpec((block, model), lambda...  10.4 us
    unnamed x46, local copies, waits for them, and re-layouts  10 us
  transfers between devices with their start and end apart: 22, of which 10 were waited for; matrix products, arithmetic and copies ran while one was open for 3% of the time, Pallas kernels for 31%

profile of v8, /device:TPU:0, one launch (start us, length us, event | category | flops | bytes accessed | tf_op | source)
XLA Modules:
  0.0 276.0 jit_solution(5880628125947301939)
XLA Ops:
  1.7 3.7 %shard_map.148 = bf16[16,128,256]{2,1,0:T(8,128)(2,1)} custom-call(bf16[128,4096]{1,0:T(8,128)(2,1)} %q_ref.1, f32[128,128]{1,0:T(8,128)} %get-tuple-element.89.cos_ref, f32[128,128]{1,0:T(8,128)} %get-tuple-element.90.sin_ref), custom_call_target="tpu_custom_call" | custom-call | flops 3145728 | bytes 2097152 | tf_op jit(solution)/shard_map/pallas_call | solution.py:285
  5.5 7.4 %all-to-all-start = ((bf16[16,128,256]{2,1,0:T(8,128)(2,1)}), bf16[16,128,256]{2,1,0:T(8,128)(2,1)S(1)}, u32[]{:S(2)}, u32[]{:S(2)}) async-start(bf16[16,128,256]{2,1,0:T(8,128)(2,1)} %shard_map.148), calls=%async_computation | async-start | bytes 2097152 | tf_op jit(solution)/shard_map/all_to_all | solution.py:298
  12.9 4.1 %shard_map.149 = bf16[16,2,128,256]{3,2,1,0:T(8,128)(2,1)} custom-call(bf16[128,4096]{1,0:T(8,128)(2,1)} %k_ref.1, bf16[128,4096]{1,0:T(8,128)(2,1)} %v_ref.1, f32[128,128]{1,0:T(8,128)} %get-tuple-element.89.cos_ref, f32[128,128]{1,0:T(8,128)} %get-tuple-element.90.sin_ref), custom_call_target="tpu_custom_call" | custom-call | flops 3145728 | bytes 4194304 | tf_op jit(solution)/shard_map/pallas_call | solution.py:270
  17.0 18.8 %all-to-all-done.q_ref = bf16[16,128,256]{2,1,0:T(8,128)(2,1)S(1)} async-done(((bf16[16,128,256]{2,1,0:T(8,128)(2,1)}), bf16[16,128,256]{2,1,0:T(8,128)(2,1)S(1)}, u32[]{:S(2)}, u32[]{:S(2)}) %all-to-all-start) | async-done | bytes 1048608 | tf_op jit(solution)/shard_map/all_to_all | solution.py:298
  35.8 1.0 copy-done.3
  36.7 6.8 %all-to-all-start.1 = ((bf16[16,2,128,256]{3,2,1,0:T(8,128)(2,1)}), bf16[16,2,128,256]{3,2,1,0:T(8,128)(2,1)S(1)}, u32[]{:S(2)}, u32[]{:S(2)}) async-start(bf16[16,2,128,256]{3,2,1,0:T(8,128)(2,1)} %shard_map.149), calls=%async_computation.1 | async-start | bytes 4194304 | tf_op jit(solution)/shard_map/all_to_all | solution.py:284
  43.6 1.3 constant_dynamic-slice_fusion
  44.9 2.0 collective-permute-start.4
  46.9 44.7 %collective-permute-done.4.refs_6_ = bf16[128,4096]{1,0:T(8,128)(2,1)S(1)} collective-permute-done((bf16[128,4096]{1,0:T(8,128)(2,1)S(1)}, bf16[128,4096]{1,0:T(8,128)(2,1)S(1)}, u32[]{:S(2)}, u32[]{:S(2)}) %collective-permute-start.4) | collective-permute-done | bytes 1048608 | tf_op jit(solution)/shard_map/ppermute | solution.py:266
  91.6 1.5 collective-permute-start.5
  95.0 1.0 fusion
  96.0 1.0 pad_maximum_fusion
  97.0 10.4 %shard_map.150 = (bf16[512,256]{1,0:T(8,128)(2,1)}, bf16[512,256]{1,0:T(8,128)(2,1)}, bf16[512,256]{1,0:T(8,128)(2,1)}, bf16[512,256]{1,0:T(8,128)(2,1)}, bf16[5...) custom-call(bf16[512,4096]{1,0:T(8,128)(2,1)} %embed_ref.1, bf16[1,4096]{1,0:T(2,128)(2,1)} %broadcast_in_dim.10.mask_ref, ...), custom_call_target="tpu_custom_call" | custom-call | flops 3221225472 | bytes 10485760 | tf_op jit(solution)/shard_map/pallas_call | solution.py:320
  108.0 8.3 %collective-permute-done.5.refs_7_ = bf16[128,4096]{1,0:T(8,128)(2,1)} collective-permute-done((bf16[128,4096]{1,0:T(8,128)(2,1)S(1)}, bf16[128,4096]{1,0:T(8,128)(2,1)}, u32[]{:S(2)}, u32[]{:S(2)}) %collective-permute-start.5) | collective-permute-done | bytes 1048608 | tf_op jit(solution)/shard_map/ppermute | solution.py:307
  116.3 1.4 copy-done
  117.6 5.3 %prompt_attention.3.refs_0_ = bf16[16,128,256]{2,1,0:T(8,128)(2,1)} custom-call(bf16[16,128,256]{2,1,0:T(8,128)(2,1)} %copy-done.3, bf16[16,2,128,256]{3,2,1,0:T(8,128)(2,1)} %copy-done, bf16[512,256]{1,0:T(8,128)(2,1)} %get-tuple-element.43.km_ref, bf16[16,256]{1,0:T(8,128)(2,1)} %get-tuple-element.44.vm_ref), custom_call_target="tpu_custom_call" | custom-call | flops 1342177280 | bytes 1572864 | tf_op jit(solution)/shard_map/prompt_attention/pallas_call | solution.py:462
  122.9 5.3 %prompt_attention.4.refs_0_ = bf16[16,128,256]{2,1,0:T(8,128)(2,1)} custom-call(bf16[16,128,256]{2,1,0:T(8,128)(2,1)} %copy-done.3, bf16[16,2,128,256]{3,2,1,0:T(8,128)(2,1)} %copy-done, bf16[512,256]{1,0:T(8,128)(2,1)} %get-tuple-element.43.km_ref, bf16[16,256]{1,0:T(8,128)(2,1)} %get-tuple-element.44.vm_ref, ...), custom_call_target="tpu_custom_call", output_to_operand_aliasing={{}: (4, {})} | custom-call | flops 1342177280 | bytes 1572864 | tf_op jit(solution)/shard_map/prompt_attention/pallas_call | solution.py:462
  128.2 8.6 %prompt_attention.5 = bf16[16,128,256]{2,1,0:T(8,128)(2,1)} custom-call(bf16[16,128,256]{2,1,0:T(8,128)(2,1)} %copy-done.3, bf16[16,2,128,256]{3,2,1,0:T(8,128)(2,1)} %copy-done, bf16[512,256]{1,0:T(8,128)(2,1)} %get-tuple-element.43.km_ref, bf16[16,256]{1,0:T(8,128)(2,1)} %get-tuple-element.44.vm_ref, ...), custom_call_target="tpu_custom_call", output_to_operand_aliasing={{}: (4, {})} | custom-call | flops 2684354560 | bytes 2097152 | tf_op jit(solution)/shard_map/prompt_attention/pallas_call | solution.py:462
  136.8 4.9 %all-to-all-start.2 = ((bf16[16,128,256]{2,1,0:T(8,128)(2,1)}), bf16[16,128,256]{2,1,0:T(8,128)(2,1)S(1)}, u32[]{:S(2)}, u32[]{:S(2)}) async-start(bf16[16,128,256]{2,1,0:T(8,128)(2,1)} %prompt_attention.5), calls=%async_computation.2 | async-start | bytes 2097152 | tf_op jit(solution)/shard_map/all_to_all | solution.py:482
  141.7 0.9 broadcast_in_dim.14.commit_ref
  142.6 5.9 %shard_map.152 = (f32[4,512,256]{2,1,0:T(8,128)}, f32[512,256]{1,0:T(8,128)}) custom-call(bf16[512,256]{1,0:T(8,128)(2,1)} %get-tuple-element.45.qe_ref, bf16[512,256]{1,0:T(8,128)(2,1)} %get-tuple-element.46.qm_ref, bf16[512,256]{1,0:T(8,128)(2,1)} %get-tuple-element.47.ke_ref, bf16[512,256]{1,0:T(8,128)(2,1)} %get-tuple-element.43.km_ref, ...), custom_call_target="tpu_custom_call" | custom-call | flops 1073741824 | bytes 2621440 | tf_op jit(solution)/shard_map/pallas_call | solution.py:351
  149.1 7.0 %response_attention.3 = (bf16[4,2,32,256]{3,2,1,0:T(8,128)(2,1)}, bf16[4,2,32,256]{3,2,1,0:T(8,128)(2,1)}, bf16[4,2,32,256]{3,2,1,0:T(8,128)(2,1)}, bf16[4,2,32,256]{3,2,1,0:T(8,128)(2,1)}) custom-call(s32[3]{0:T(128)} %pad_add_fusion.place_ref, bf16[16,2,128,256]{3,2,1,0:T(8,128)(2,1)} %copy-done, bf16[2,2,128,256]{3,2,1,0:T(8,128)(2,1)} %bitcast.16, ...), custom_call_target="tpu_custom_call" | custom-call | flops 1073741824 | bytes 2097152 | tf_op jit(solution)/shard_map/response_attention/pallas_call | solution.py:370
  156.5 1.6 collective-permute-start.9
  158.1 7.0 %response_attention.2 = (bf16[4,2,32,256]{3,2,1,0:T(8,128)(2,1)}, bf16[4,2,32,256]{3,2,1,0:T(8,128)(2,1)}, bf16[4,2,32,256]{3,2,1,0:T(8,128)(2,1)}, bf16[4,2,32,256]{3,2,1,0:T(8,128)(2,1)}) custom-call(s32[3]{0:T(128)} %pad_add_fusion.place_ref, bf16[16,2,128,256]{3,2,1,0:T(8,128)(2,1)} %copy-done, bf16[2,2,128,256]{3,2,1,0:T(8,128)(2,1)} %bitcast.17, ...), custom_call_target="tpu_custom_call" | custom-call | flops 1073741824 | bytes 2097152 | tf_op jit(solution)/shard_map/response_attention/pallas_call | solution.py:370
  165.9 1.4 collective-permute-done.10.refs_3_
  168.0 7.6 %output_projection.3 = (bf16[2,32,4096]{2,1,0:T(8,128)(2,1)}, bf16[2,32,4096]{2,1,0:T(8,128)(2,1)}, bf16[2,32,4096]{2,1,0:T(8,128)(2,1)}, bf16[2,32,4096]{2,1,0:T(8,128)(2,1)}) custom-call(s32[3]{0:T(128)} %pad_add_fusion.place_ref, bf16[4,2,32,256]{3,2,1,0:T(8,128)(2,1)} %get-tuple-element.56.refs_0_, bf16[4,2,32,256]{3,2,1,0:T(8,128)(2,1)} %copy-done.13, ...), custom_call_target="tpu_custom_call" | custom-call | flops 2147483648 | bytes 8388608 | tf_op jit(solution)/shard_map/output_projection/pallas_call | solution.py:399
  175.5 2.6 collective-permute-start.11
  178.2 1.9 collective-permute-start.15
  180.3 1.4 collective-permute-start.1
  181.6 3.7 %collective-permute-done.1.refs_2_ = bf16[4,2,32,256]{3,2,1,0:T(8,128)(2,1)S(1)} collective-permute-done((bf16[4,2,32,256]{3,2,1,0:T(8,128)(2,1)S(1)}, bf16[4,2,32,256]{3,2,1,0:T(8,128)(2,1)S(1)}, u32[]{:S(2)}, u32[]{:S(2)}) %collective-permute-start.1) | collective-permute-done | bytes 131104 | tf_op jit(solution)/shard_map/ppermute | solution.py:266
  186.0 5.2 %collective-permute-done.2.refs_3_ = bf16[4,2,32,256]{3,2,1,0:T(8,128)(2,1)S(1)} collective-permute-done((bf16[4,2,32,256]{3,2,1,0:T(8,128)(2,1)}, bf16[4,2,32,256]{3,2,1,0:T(8,128)(2,1)S(1)}, u32[]{:S(2)}, u32[]{:S(2)}) %collective-permute-start.2) | collective-permute-done | bytes 131104 | tf_op jit(solution)/shard_map/ppermute | solution.py:266
  191.8 7.4 %output_projection.2 = (bf16[2,32,4096]{2,1,0:T(8,128)(2,1)}, bf16[2,32,4096]{2,1,0:T(8,128)(2,1)}, bf16[2,32,4096]{2,1,0:T(8,128)(2,1)}, bf16[2,32,4096]{2,1,0:T(8,128)(2,1)}) custom-call(s32[3]{0:T(128)} %pad_add_fusion.place_ref, bf16[4,2,32,256]{3,2,1,0:T(8,128)(2,1)} %get-tuple-element.51.refs_0_, bf16[4,2,32,256]{3,2,1,0:T(8,128)(2,1)} %copy-done.12, ...), custom_call_target="tpu_custom_call" | custom-call | flops 2147483648 | bytes 8388608 | tf_op jit(solution)/shard_map/output_projection/pallas_call | solution.py:399
  200.0 2.2 halve.4
  202.2 2.6 collective-permute-start.12
  205.6 2.2 halve.5
  208.2 16.6 %collective-permute-done.15.got_ref = bf16[2,32,4096]{2,1,0:T(8,128)(2,1)S(1)} collective-permute-done((bf16[2,32,4096]{2,1,0:T(8,128)(2,1)}, bf16[2,32,4096]{2,1,0:T(8,128)(2,1)S(1)}, u32[]{:S(2)}, u32[]{:S(2)}) %collective-permute-start.15) | collective-permute-done | bytes 524320 | tf_op jit(solution)/shard_map/ppermute | solution.py:266
  225.6 2.2 halve.6
  227.8 0.9 collective-permute-start.16
  228.7 6.9 %collective-permute-done.17.got_ref = bf16[2,32,4096]{2,1,0:T(8,128)(2,1)S(1)} collective-permute-done((bf16[2,32,4096]{2,1,0:T(8,128)(2,1)}, bf16[2,32,4096]{2,1,0:T(8,128)(2,1)S(1)}, u32[]{:S(2)}, u32[]{:S(2)}) %collective-permute-start.17) | collective-permute-done | bytes 524320 | tf_op jit(solution)/shard_map/ppermute | solution.py:266
  236.4 2.2 halve.7
  239.1 1.7 constant_dynamic-slice_fusion.1.embed_ref
  240.8 19.0 %collective-permute-done.18.got_ref = bf16[1,32,4096]{2,1,0:T(8,128)(2,1)S(1)} collective-permute-done((bf16[1,32,4096]{2,1,0:T(8,128)(2,1)}, bf16[1,32,4096]{2,1,0:T(8,128)(2,1)S(1)}, u32[]{:S(2)}, u32[]{:S(2)}) %collective-permute-start.18) | collective-permute-done | bytes 262176 | tf_op jit(solution)/shard_map/ppermute | solution.py:266
  260.5 2.2 finish.4
  263.4 2.2 finish.5
  266.4 2.2 finish.6
  269.4 2.2 finish.7
  271.6 1.0 copy-done.2
  272.6 3.4 %shard_map.151 = bf16[128,4096]{1,0:T(8,128)(2,1)} custom-call(bf16[16,128,256]{2,1,0:T(8,128)(2,1)} %copy-done.2), custom_call_target="tpu_custom_call" | custom-call | bytes 2097152 | tf_op jit(solution)/shard_map/pallas_call | solution.py:508
  (78 shorter events, 13.8 us)
Async XLA Ops:
  5.5 30.3 %all-to-all-start = ((bf16[16,128,256]{2,1,0:T(8,128)(2,1)}), bf16[16,128,256]{2,1,0:T(8,128)(2,1)S(1)}, u32[]{:S(2)}, u32[]{:S(2)}) async-start(bf16[16,128,256]{2,1,0:T(8,128)(2,1)} %shard_map.148), calls=%async_computation | async-start | bytes 2097152 | tf_op jit(solution)/shard_map/all_to_all | solution.py:298
  35.8 1.0 copy-start.3
  36.7 79.5 %all-to-all-start.1 = ((bf16[16,2,128,256]{3,2,1,0:T(8,128)(2,1)}), bf16[16,2,128,256]{3,2,1,0:T(8,128)(2,1)S(1)}, u32[]{:S(2)}, u32[]{:S(2)}) async-start(bf16[16,2,128,256]{3,2,1,0:T(8,128)(2,1)} %shard_map.149), calls=%async_computation.1 | async-start | bytes 4194304 | tf_op jit(solution)/shard_map/all_to_all | solution.py:284
  43.5 50.2 %copy-start.18 = (bf16[4096]{0:T(1024)(128)(2,1)S(1)}, bf16[4096]{0:T(1024)(128)(2,1)}, u32[]{:S(2)}) copy-start(bf16[4096]{0:T(1024)(128)(2,1)} %param.17) | copy-start | bytes 24580
  43.5 50.8 %copy-start.19 = (bf16[4096]{0:T(1024)(128)(2,1)S(1)}, bf16[4096]{0:T(1024)(128)(2,1)}, u32[]{:S(2)}) copy-start(bf16[4096]{0:T(1024)(128)(2,1)} %param.20) | copy-start | bytes 24580
  44.9 46.7 %collective-permute-start.4 = (bf16[128,4096]{1,0:T(8,128)(2,1)S(1)}, bf16[128,4096]{1,0:T(8,128)(2,1)S(1)}, u32[]{:S(2)}, u32[]{:S(2)}) collective-permute-start(bf16[128,4096]{1,0:T(8,128)(2,1)S(1)} %constant_dynamic-slice_fusion), channel_id=1, source_target_pairs={{0,2},{1,3},{2,0},{3,1},{4,6},{5,7},{6,4},{7,5},{8,10},{9,11},{10,... | collective-permute-start | bytes 3145736 | tf_op jit(solution)/shard_map/ppermute | solution.py:266
  91.6 15.9 %copy-start.1 = (bf16[128,4096]{1,0:T(8,128)(2,1)}, bf16[128,4096]{1,0:T(8,128)(2,1)S(1)}, u32[]{:S(2)}) copy-start(bf16[128,4096]{1,0:T(8,128)(2,1)S(1)} %collective-permute-done.4.refs_6_) | copy-start | bytes 3145732
  91.6 24.7 %collective-permute-start.5 = (bf16[128,4096]{1,0:T(8,128)(2,1)S(1)}, bf16[128,4096]{1,0:T(8,128)(2,1)}, u32[]{:S(2)}, u32[]{:S(2)}) collective-permute-start(bf16[128,4096]{1,0:T(8,128)(2,1)S(1)} %collective-permute-done.4.refs_6_), channel_id=1, source_target_pairs={{0,16},{16,0},{1,17},{17,1},{2,18},{18,2},{3,19},{19,3},{4,20},{20... | collective-permute-start | bytes 3145736 | tf_op jit(solution)/shard_map/ppermute | solution.py:307
  93.1 72.0 %collective-permute-start.3 = (bf16[256,4096]{1,0:T(8,128)(2,1)}, bf16[256,4096]{1,0:T(8,128)(2,1)}, u32[]{:S(2)}, u32[]{:S(2)}) collective-permute-start(bf16[256,4096]{1,0:T(8,128)(2,1)} %refs_4_.3), channel_id=1, source_target_pairs={{0,1},{1,0},{2,3},{3,2},{4,5},{5,4},{6,7},{7,6},{8,9},{9,8},{10,11... | collective-permute-start | bytes 6291464 | tf_op jit(solution)/shard_map/ppermute | solution.py:266
  107.4 50.7 %collective-permute-start.6 = (bf16[128,4096]{1,0:T(8,128)(2,1)S(1)}, bf16[128,4096]{1,0:T(8,128)(2,1)}, u32[]{:S(2)}, u32[]{:S(2)}) collective-permute-start(bf16[128,4096]{1,0:T(8,128)(2,1)S(1)} %collective-permute-done.4.refs_6_), channel_id=1, source_target_pairs={{0,1},{1,0},{2,3},{3,2},{4,5},{5,4},{6,7},{7,6},{8,9},{9,8},{10,11... | collective-permute-start | bytes 3145736 | tf_op jit(solution)/shard_map/ppermute | solution.py:266
  116.3 49.4 %collective-permute-start.7 = (bf16[128,4096]{1,0:T(8,128)(2,1)}, bf16[128,4096]{1,0:T(8,128)(2,1)}, u32[]{:S(2)}, u32[]{:S(2)}) collective-permute-start(bf16[128,4096]{1,0:T(8,128)(2,1)} %collective-permute-done.5.refs_7_), channel_id=1, source_target_pairs={{0,1},{1,0},{2,3},{3,2},{4,5},{5,4},{6,7},{7,6},{8,9},{9,8},{10,11... | collective-permute-start | bytes 3145736 | tf_op jit(solution)/shard_map/ppermute | solution.py:266
  116.3 1.4 copy-start
  136.8 4.9 %copy-start.21 = (s32[512]{0:T(512)S(1)}, s32[512]{0:T(512)}, u32[]{:S(2)}) copy-start(s32[512]{0:T(512)} %param.18) | copy-start | bytes 6148
  136.8 134.8 %all-to-all-start.2 = ((bf16[16,128,256]{2,1,0:T(8,128)(2,1)}), bf16[16,128,256]{2,1,0:T(8,128)(2,1)S(1)}, u32[]{:S(2)}, u32[]{:S(2)}) async-start(bf16[16,128,256]{2,1,0:T(8,128)(2,1)} %prompt_attention.5), calls=%async_computation.2 | async-start | bytes 2097152 | tf_op jit(solution)/shard_map/all_to_all | solution.py:482
  156.1 9.6 %collective-permute-start.8 = (bf16[4,2,32,256]{3,2,1,0:T(8,128)(2,1)}, bf16[4,2,32,256]{3,2,1,0:T(8,128)(2,1)S(1)}, u32[]{:S(2)}, u32[]{:S(2)}) collective-permute-start(bf16[4,2,32,256]{3,2,1,0:T(8,128)(2,1)} %get-tuple-element.57), channel_id=1, source_target_pairs={{0,1},{1,0},{2,3},{3,2},{4,5},{5,4},{6,7},{7,6},{8,9},{9,8},{10,11... | collective-permute-start | bytes 393224 | tf_op jit(solution)/shard_map/ppermute | solution.py:266
  156.5 9.4 %collective-permute-start.9 = (bf16[4,2,32,256]{3,2,1,0:T(8,128)(2,1)}, bf16[4,2,32,256]{3,2,1,0:T(8,128)(2,1)S(1)}, u32[]{:S(2)}, u32[]{:S(2)}) collective-permute-start(bf16[4,2,32,256]{3,2,1,0:T(8,128)(2,1)} %get-tuple-element.58), channel_id=1, source_target_pairs={{0,2},{1,3},{2,0},{3,1},{4,6},{5,7},{6,4},{7,5},{8,10},{9,11},{10,... | collective-permute-start | bytes 393224 | tf_op jit(solution)/shard_map/ppermute | solution.py:266
  158.1 9.2 %collective-permute-start.10 = (bf16[4,2,32,256]{3,2,1,0:T(8,128)(2,1)}, bf16[4,2,32,256]{3,2,1,0:T(8,128)(2,1)S(1)}, u32[]{:S(2)}, u32[]{:S(2)}) collective-permute-start(bf16[4,2,32,256]{3,2,1,0:T(8,128)(2,1)} %get-tuple-element.59), channel_id=1, source_target_pairs={{0,3},{1,2},{2,1},{3,0},{4,7},{5,6},{6,5},{7,4},{8,11},{9,10},{10,... | collective-permute-start | bytes 393224 | tf_op jit(solution)/shard_map/ppermute | solution.py:266
  165.1 15.2 %collective-permute-start = (bf16[4,2,32,256]{3,2,1,0:T(8,128)(2,1)}, bf16[4,2,32,256]{3,2,1,0:T(8,128)(2,1)S(1)}, u32[]{:S(2)}, u32[]{:S(2)}) collective-permute-start(bf16[4,2,32,256]{3,2,1,0:T(8,128)(2,1)} %get-tuple-element.52), channel_id=1, source_target_pairs={{0,1},{1,0},{2,3},{3,2},{4,5},{5,4},{6,7},{7,6},{8,9},{9,8},{10,11... | collective-permute-start | bytes 393224 | tf_op jit(solution)/shard_map/ppermute | solution.py:266
  165.7 1.6 copy-start.13
  165.9 1.4 copy-start.14
  167.3 0.7 copy-start.16
  168.0 12.3 %copy-start.22 = (bf16[4,2,32,256]{3,2,1,0:T(8,128)(2,1)S(1)}, bf16[4,2,32,256]{3,2,1,0:T(8,128)(2,1)}, u32[]{:S(2)}) copy-start(bf16[4,2,32,256]{3,2,1,0:T(8,128)(2,1)} %get-tuple-element.53) | copy-start | bytes 393220
  168.0 17.4 %copy-start.20 = (bf16[4096]{0:T(1024)(128)(2,1)S(1)}, bf16[4096]{0:T(1024)(128)(2,1)}, u32[]{:S(2)}) copy-start(bf16[4096]{0:T(1024)(128)(2,1)} %param.21) | copy-start | bytes 24580
  175.5 23.7 %collective-permute-start.11 = (bf16[2,32,4096]{2,1,0:T(8,128)(2,1)}, bf16[2,32,4096]{2,1,0:T(8,128)(2,1)S(1)}, u32[]{:S(2)}, u32[]{:S(2)}) collective-permute-start(bf16[2,32,4096]{2,1,0:T(8,128)(2,1)} %get-tuple-element.60), channel_id=1, source_target_pairs={{0,4},{1,5},{2,6},{3,7},{4,0},{5,1},{6,2},{7,3},{8,12},{9,13},{10,... | collective-permute-start | bytes 1572872 | tf_op jit(solution)/shard_map/ppermute | solution.py:266
  178.1 26.7 %collective-permute-start.13 = (bf16[2,32,4096]{2,1,0:T(8,128)(2,1)}, bf16[2,32,4096]{2,1,0:T(8,128)(2,1)S(1)}, u32[]{:S(2)}, u32[]{:S(2)}) collective-permute-start(bf16[2,32,4096]{2,1,0:T(8,128)(2,1)} %get-tuple-element.64), channel_id=1, source_target_pairs={{0,4},{1,5},{2,6},{3,7},{4,0},{5,1},{6,2},{7,3},{8,12},{9,13},{10,... | collective-permute-start | bytes 1572872 | tf_op jit(solution)/shard_map/ppermute | solution.py:266
  178.2 46.6 %collective-permute-start.15 = (bf16[2,32,4096]{2,1,0:T(8,128)(2,1)}, bf16[2,32,4096]{2,1,0:T(8,128)(2,1)S(1)}, u32[]{:S(2)}, u32[]{:S(2)}) collective-permute-start(bf16[2,32,4096]{2,1,0:T(8,128)(2,1)} %get-tuple-element.68), channel_id=1, source_target_pairs={{0,4},{1,5},{2,6},{3,7},{4,0},{5,1},{6,2},{7,3},{8,12},{9,13},{10,... | collective-permute-start | bytes 1572872 | tf_op jit(solution)/shard_map/ppermute | solution.py:266
  180.2 55.4 %collective-permute-start.17 = (bf16[2,32,4096]{2,1,0:T(8,128)(2,1)}, bf16[2,32,4096]{2,1,0:T(8,128)(2,1)S(1)}, u32[]{:S(2)}, u32[]{:S(2)}) collective-permute-start(bf16[2,32,4096]{2,1,0:T(8,128)(2,1)} %get-tuple-element.72), channel_id=1, source_target_pairs={{0,4},{1,5},{2,6},{3,7},{4,0},{5,1},{6,2},{7,3},{8,12},{9,13},{10,... | collective-permute-start | bytes 1572872 | tf_op jit(solution)/shard_map/ppermute | solution.py:266
  180.2 10.9 %copy-start.12 = (bf16[4,2,32,256]{3,2,1,0:T(8,128)(2,1)}, bf16[4,2,32,256]{3,2,1,0:T(8,128)(2,1)S(1)}, u32[]{:S(2)}) copy-start(bf16[4,2,32,256]{3,2,1,0:T(8,128)(2,1)S(1)} %collective-permute-done.refs_1_) | copy-start | bytes 393220
  180.3 5.0 %collective-permute-start.1 = (bf16[4,2,32,256]{3,2,1,0:T(8,128)(2,1)S(1)}, bf16[4,2,32,256]{3,2,1,0:T(8,128)(2,1)S(1)}, u32[]{:S(2)}, u32[]{:S(2)}) collective-permute-start(bf16[4,2,32,256]{3,2,1,0:T(8,128)(2,1)S(1)} %copy-done.22), channel_id=1, source_target_pairs={{0,2},{1,3},{2,0},{3,1},{4,6},{5,7},{6,4},{7,5},{8,10},{9,11},{10,... | collective-permute-start | bytes 393224 | tf_op jit(solution)/shard_map/ppermute | solution.py:266
  185.3 5.9 %copy-start.15 = (bf16[4,2,32,256]{3,2,1,0:T(8,128)(2,1)}, bf16[4,2,32,256]{3,2,1,0:T(8,128)(2,1)S(1)}, u32[]{:S(2)}) copy-start(bf16[4,2,32,256]{3,2,1,0:T(8,128)(2,1)S(1)} %collective-permute-done.1.refs_2_) | copy-start | bytes 393220
  185.3 5.9 %collective-permute-start.2 = (bf16[4,2,32,256]{3,2,1,0:T(8,128)(2,1)}, bf16[4,2,32,256]{3,2,1,0:T(8,128)(2,1)S(1)}, u32[]{:S(2)}, u32[]{:S(2)}) collective-permute-start(bf16[4,2,32,256]{3,2,1,0:T(8,128)(2,1)} %get-tuple-element.54), channel_id=1, source_target_pairs={{0,3},{1,2},{2,1},{3,0},{4,7},{5,6},{6,5},{7,4},{8,11},{9,10},{10,... | collective-permute-start | bytes 393224 | tf_op jit(solution)/shard_map/ppermute | solution.py:266
  191.2 0.7 copy-start.17
  199.2 0.8 copy-start.7
  202.2 66.4 %collective-permute-start.12 = (bf16[1,32,4096]{2,1,0:T(8,128)(2,1)}, bf16[1,32,4096]{2,1,0:T(8,128)(2,1)S(1)}, u32[]{:S(2)}, u32[]{:S(2)}) collective-permute-start(bf16[1,32,4096]{2,1,0:T(8,128)(2,1)} %get-tuple-element.62), channel_id=1, source_target_pairs={{0,8},{1,9},{2,10},{3,11},{4,12},{5,13},{6,14},{7,15},{8,0},{9,1},... | collective-permute-start | bytes 786440 | tf_op jit(solution)/shard_map/ppermute | solution.py:266
  204.8 0.8 copy-start.6
  207.9 57.8 %collective-permute-start.14 = (bf16[1,32,4096]{2,1,0:T(8,128)(2,1)}, bf16[1,32,4096]{2,1,0:T(8,128)(2,1)S(1)}, u32[]{:S(2)}, u32[]{:S(2)}) collective-permute-start(bf16[1,32,4096]{2,1,0:T(8,128)(2,1)} %get-tuple-element.66), channel_id=1, source_target_pairs={{0,8},{1,9},{2,10},{3,11},{4,12},{5,13},{6,14},{7,15},{8,0},{9,1},... | collective-permute-start | bytes 786440 | tf_op jit(solution)/shard_map/ppermute | solution.py:266
  224.8 0.8 copy-start.5
  227.8 34.9 %collective-permute-start.16 = (bf16[1,32,4096]{2,1,0:T(8,128)(2,1)}, bf16[1,32,4096]{2,1,0:T(8,128)(2,1)S(1)}, u32[]{:S(2)}, u32[]{:S(2)}) collective-permute-start(bf16[1,32,4096]{2,1,0:T(8,128)(2,1)} %get-tuple-element.70), channel_id=1, source_target_pairs={{0,8},{1,9},{2,10},{3,11},{4,12},{5,13},{6,14},{7,15},{8,0},{9,1},... | collective-permute-start | bytes 786440 | tf_op jit(solution)/shard_map/ppermute | solution.py:266
  235.6 0.8 copy-start.4
  238.6 21.2 %collective-permute-start.18 = (bf16[1,32,4096]{2,1,0:T(8,128)(2,1)}, bf16[1,32,4096]{2,1,0:T(8,128)(2,1)S(1)}, u32[]{:S(2)}, u32[]{:S(2)}) collective-permute-start(bf16[1,32,4096]{2,1,0:T(8,128)(2,1)} %get-tuple-element.74), channel_id=1, source_target_pairs={{0,8},{1,9},{2,10},{3,11},{4,12},{5,13},{6,14},{7,15},{8,0},{9,1},... | collective-permute-start | bytes 786440 | tf_op jit(solution)/shard_map/ppermute | solution.py:266
  259.8 0.7 copy-start.11
  262.7 0.7 copy-start.10
  265.7 0.7 copy-start.9
  268.7 0.7 copy-start.8
  271.6 1.0 copy-start.2
